TPU v7x, 32 devices: a whole 2x2x4 slice. The times are simulated.
32 devices in a mesh: seg: 8 (over z, x), space: 4 (over y, core).
Axes of the slice: x: 2, y: 2, z: 4, core: 2. Of those that a mesh axis runs over, the one named last changes fastest.
Arguments:
- states: float32 [8, 32, 65, 128], P('seg', 'space'), may hold values from -6 to 6
- forcing: float32 [32, 65, 128], P('space'), may hold values from -6 to 6
- wall_viscosity: float32 [65], replicated, may hold values from 0.5 to 4
Outputs:
- new_states: float32 [8, 32, 65, 128], P('seg', 'space')
- mismatch: float32 [8, 32, 65, 128], P('seg', 'space')
All inputs are finite; a program needn't handle non-finite values.
Results may differ from a plain program's by a relative error of at most 0.0075.
Values sent between devices are 32-bit elements; how exact they have to be, the bound alone decides.
No kernel may reach another device: no remote copies, remote signals or barrier semaphores. Data moves between devices by JAX's collectives and lax.ppermute only.
A program may use at most 64 MiB of HBM per device.

v0:
```python
import jax
import jax.numpy as jnp
from jax import lax
from jax.sharding import PartitionSpec as P

NY = 65
STEPS = 4
ITERS = 2


ADVECT = 0.15
SPREAD = 0.2
PUSHED = 0.25
EPSILON = 1e-06


def padded_2(shard, sides, width):
    for axis, dim in sides:
        devices, length = (lax.axis_size(axis), shard.shape[dim])
        up = [(i, (i + 1) % devices) for i in range(devices)]
        down = [(j, i) for i, j in up]
        last = lax.slice_in_dim(shard, length - width, length, axis=dim)
        initial = lax.slice_in_dim(shard, 0, width, axis=dim)
        before = lax.ppermute(last, axis, up)
        after = lax.ppermute(initial, axis, down)
        shard = jnp.concatenate([before, shard, after], axis=dim)
    return shard


def shifted(block, axis, distance):
    devices = range(lax.axis_size(axis))
    route = [((i - distance) % len(devices), i) for i in devices]
    return lax.ppermute(block, axis, route)


def inverses(viscosity):
    points = viscosity.shape[0]
    zero = jnp.zeros((1,), jnp.float32)
    negative = -viscosity
    centre = 1.0 + 2.0 * viscosity
    lower = jnp.concatenate([zero, negative[1:]])
    upper = jnp.concatenate([negative[:-1], zero])
    identity = jnp.eye(points, dtype=jnp.float32)
    return lax.linalg.tridiagonal_solve(lower[None], centre[None], upper[None], identity[None])[0]


def apply_inverse(inverse, field):
    return jnp.einsum("jk,xkz->xjz", inverse, field, precision=lax.Precision.HIGHEST)


def apply_transposed(inverse, field):
    return jnp.einsum("kj,xkz->xjz", inverse, field, precision=lax.Precision.HIGHEST)


def spanwise(field):
    return jnp.roll(field, 1, 2) + jnp.roll(field, -1, 2) - 2.0 * field


def forward_step(field, forcing, base, inverse):
    padded = padded_2(field, (("space", 0),), 1)
    slope = 0.5 * (padded[2:] - padded[:-2])
    pushed = field - ADVECT * (base + field) * slope + SPREAD * spanwise(field) + PUSHED * forcing
    return (apply_inverse(inverse, pushed), slope)


def adjoint_step(weight, field, slope, base, inverse):
    carried = apply_transposed(inverse, weight)
    flux = (base + field) * carried
    padded = padded_2(flux, (("space", 0),), 1)
    return (
        carried
        - ADVECT * carried * slope
        + ADVECT * (0.5 * (padded[2:] - padded[:-2]))
        + SPREAD * spanwise(carried)
    )


def integrate(field, forcing, base, inverse):
    saved = []
    for step in range(STEPS):
        following, slope = forward_step(field, forcing, base, inverse)
        saved.append((field, slope))
        field = following
    return (field, saved)


def adjoint(weight, saved, base, inverse):
    for step in reversed(range(len(saved))):
        weight = adjoint_step(weight, saved[step][0], saved[step][1], base, inverse)
    return weight


def per_device(states, forcing, wall_viscosity):
    current = states[0]
    base = (2.0 * jnp.arange(NY, dtype=jnp.float32) / (NY - 1) - 1.0)[None, :, None]
    inverse = inverses(wall_viscosity)
    mismatch = current
    for iteration in range(ITERS):
        ending, saved = integrate(current, forcing, base, inverse)
        prior = shifted(ending, "seg", 1)
        earlier = prior - current
        mismatch = shifted(earlier, "seg", -1)
        back = adjoint(mismatch, saved, base, inverse)
        descent = back - earlier
        total, squares = lax.psum(
            (0.5 * jnp.sum(mismatch * mismatch), jnp.sum(descent * descent)), ("seg", "space")
        )
        current = current - total / (squares + EPSILON) * descent
    return (current[None], mismatch[None])


def solution(mesh):
    placed = (P("seg", "space", None, None), P("space", None, None), P())
    return jax.shard_map(
        per_device,
        mesh=mesh,
        in_specs=placed,
        out_specs=(P("seg", "space", None, None), P("seg", "space", None, None)),
        check_vma=False,
    )
```

profile of v0, /device:TPU:0, one launch (start us, length us, event | category | flops | bytes accessed | tf_op | source)
XLA Modules:
  0.0 419.8 jit_solution(12235927826151954652)
XLA Ops:
  1.7 2.5 collective-permute-start
  5.8 170.1 %while.32 = (s32[]{:T(128)}, f32[1]{0:T(128)}, f32[1,65]{1,0:T(1,128)S(1)}, f32[2,32,1]{1,2,0:T(1,128)S(1)}, f32[2,32,1,65]{3,1,2,0:T(8,128)S(1)}, /*index=5*/f3...) while((s32[]{:T(128)}, f32[1]{0:T(128)}, ...), condition=%wide.region_1.2_spmd, body=%wide.region_0.1_spmd.sunk | while | flops 6369 | bytes 103045 | solution.py:44
  175.8 44.2 %while.33 = (s32[]{:T(128)}, f32[1,65]{1,0:T(1,128)S(1)}, f32[2,32,1,65]{3,1,2,0:T(8,128)S(1)}, f32[2,32,1,65]{3,2,1,0:T(1,128)S(1)}, f32[2,32,1]{1,2,0:T(1,128)...) while((s32[]{:T(128)}, f32[1,65]{1,0:T(1,128)S(1)}, ...), condition=%wide.region_3.4_spmd, body=%wide.region_2.3_spmd.sunk | while | flops 4193 | bytes 91485 | solution.py:44
  177.3 19.5 %constant_dynamic-update-slice_fusion.168 = (f32[32,1,65]{2,1,0:T(1,128)S(1)}, f32[1,65]{1,0:T(1,128)S(1)}, f32[1,65]{1,0:T(1,128)S(1)}, f32[1,65]{1,0:T(1,128)S...) fusion(f32[]{:T(128)} %bitcast.1400, ...), kind=kLoop, calls=%fused_computation.196.clone.1 | loop fusion | flops 4029 | bytes 24956 | tf_op jit(solution)/shard_map/vmap()/while
  199.4 19.5 %constant_dynamic-update-slice_fusion.168 = (f32[32,1,65]{2,1,0:T(1,128)S(1)}, f32[1,65]{1,0:T(1,128)S(1)}, f32[1,65]{1,0:T(1,128)S(1)}, f32[1,65]{1,0:T(1,128)S...) fusion(f32[]{:T(128)} %bitcast.1400, ...), kind=kLoop, calls=%fused_computation.196.clone.1 | loop fusion | flops 4029 | bytes 24956 | tf_op jit(solution)/shard_map/vmap()/while
  221.0 1.8 collective-permute-start.2
  222.9 1.7 collective-permute-done.2
  224.6 1.6 collective-permute-done.3
  229.4 1.7 collective-permute-done.5
  234.0 1.9 collective-permute-done.7
  237.3 1.6 collective-permute-start.8
  238.9 8.8 %collective-permute-done.8 = f32[8,65,128]{2,1,0:T(8,128)S(1)} collective-permute-done((f32[8,65,128]{2,1,0:T(8,128)S(1)}, f32[8,65,128]{2,1,0:T(8,128)S(1)}, u32[]{:S(2)}, u32[]{:S(2)}) %collective-permute-start.8) | collective-permute-done | bytes 266272 | tf_op jit(solution)/shard_map/ppermute | solution.py:33
  247.8 1.8 collective-permute-start.9
  249.6 5.0 %collective-permute-done.9 = f32[8,65,128]{2,1,0:T(8,128)S(1)} collective-permute-done((f32[8,65,128]{2,1,0:T(8,128)S(1)}, f32[8,65,128]{2,1,0:T(8,128)S(1)}, u32[]{:S(2)}, u32[]{:S(2)}) %collective-permute-start.9) | collective-permute-done | bytes 266272 | tf_op jit(solution)/shard_map/ppermute | solution.py:33
  256.7 1.6 collective-permute-start.10
  260.3 2.3 collective-permute-done.11
  262.5 1.7 add_multiply_fusion.5
  266.0 2.0 collective-permute-done.13
  270.3 2.0 collective-permute-done.15
  274.7 2.0 collective-permute-done.17
  277.5 40.1 %all-reduce.1 = (f32[]{:T(128)}, f32[]{:T(128)}) all-reduce(f32[]{:T(128)S(6)} %mul.1494, f32[]{:T(128)} %get-tuple-element.304), channel_id=1, replica_groups=mesh['seg'=8,'space'=4] {'seg','space'}, use_global_device_ids=true, to_apply=%region_5.6 | all-reduce | flops 2 | bytes 16 | tf_op jit(solution)/shard_map/psum | solution.py:105
  321.0 2.7 collective-permute-done.19
  326.2 2.0 collective-permute-done.21
  330.7 2.0 collective-permute-done.23
  335.2 2.0 collective-permute-done.25
  337.9 1.9 collective-permute-start.26
  339.8 9.8 %collective-permute-done.26 = f32[8,65,128]{2,1,0:T(8,128)S(1)} collective-permute-done((f32[8,65,128]{2,1,0:T(8,128)S(1)}, f32[8,65,128]{2,1,0:T(8,128)S(1)}, u32[]{:S(2)}, u32[]{:S(2)}) %collective-permute-start.26) | collective-permute-done | bytes 266272 | tf_op jit(solution)/shard_map/ppermute | solution.py:33
  349.8 8.2 %collective-permute-done.27 = f32[8,65,128]{2,1,0:T(8,128)S(1)} collective-permute-done((f32[8,65,128]{2,1,0:T(8,128)S(1)}, f32[8,65,128]{2,1,0:T(8,128)S(1)}, u32[]{:S(2)}, u32[]{:S(2)}) %collective-permute-start.27) | collective-permute-done | bytes 266272 | tf_op jit(solution)/shard_map/ppermute | solution.py:33
  367.3 1.7 collective-permute-done.31
  371.6 1.7 collective-permute-done.33
  376.0 1.7 collective-permute-done.35
  378.6 39.1 %all-reduce = (f32[]{:T(128)}, f32[]{:T(128)}) all-reduce(f32[]{:T(128)S(6)} %mul.1544, f32[]{:T(128)} %get-tuple-element.302), channel_id=1, replica_groups=mesh['seg'=8,'space'=4] {'seg','space'}, use_global_device_ids=true, to_apply=%region_9.10 | all-reduce | flops 2 | bytes 16 | tf_op jit(solution)/shard_map/psum | solution.py:105
  (333 shorter events, 102.7 us)
Async XLA Ops:
  1.7 218.4 %collective-permute-start = (f32[1,65,128]{2,1,0:T(8,128)S(1)}, f32[1,65,128]{2,1,0:T(8,128)S(1)}, u32[]{:S(2)}, u32[]{:S(2)}) collective-permute-start(f32[1,65,128]{2,1,0:T(8,128)S(1)} %get-tuple-element.526), channel_id=1, source_target_pairs={{1,0},{2,1},{3,2},{0,3},{5,4},{6,5},{7,6},{4,7},{9,8},{10,9},{11,1... | collective-permute-start | bytes 99848 | tf_op jit(solution)/shard_map/ppermute | solution.py:25
  4.1 216.0 %collective-permute-start.1 = (f32[1,65,128]{2,1,0:T(8,128)S(1)}, f32[1,65,128]{2,1,0:T(8,128)S(1)}, u32[]{:S(2)}, u32[]{:S(2)}) collective-permute-start(f32[1,65,128]{2,1,0:T(8,128)S(1)} %get-tuple-element.527), channel_id=1, source_target_pairs={{0,1},{1,2},{2,3},{3,0},{4,5},{5,6},{6,7},{7,4},{8,9},{9,10},{10,1... | collective-permute-start | bytes 99848 | tf_op jit(solution)/shard_map/ppermute | solution.py:24
  221.0 3.6 collective-permute-start.2
  222.8 3.4 collective-permute-start.3
  227.0 2.4 collective-permute-start.4
  227.7 3.4 collective-permute-start.5
  232.0 2.0 collective-permute-start.6
  232.3 3.5 collective-permute-start.7
  237.3 10.4 %collective-permute-start.8 = (f32[8,65,128]{2,1,0:T(8,128)S(1)}, f32[8,65,128]{2,1,0:T(8,128)S(1)}, u32[]{:S(2)}, u32[]{:S(2)}) collective-permute-start(f32[8,65,128]{2,1,0:T(8,128)S(1)} %convolution_bitcast_fusion.12), channel_id=1, source_target_pairs={{28,0},{0,4},{4,8},{8,12},{12,16},{16,20},{20,24},{24,28},{29,1},{... | collective-permute-start | bytes 798728 | tf_op jit(solution)/shard_map/ppermute | solution.py:33
  247.8 6.8 %collective-permute-start.9 = (f32[8,65,128]{2,1,0:T(8,128)S(1)}, f32[8,65,128]{2,1,0:T(8,128)S(1)}, u32[]{:S(2)}, u32[]{:S(2)}) collective-permute-start(f32[8,65,128]{2,1,0:T(8,128)S(1)} %bitcast_subtract_fusion), channel_id=1, source_target_pairs={{4,0},{8,4},{12,8},{16,12},{20,16},{24,20},{28,24},{0,28},{5,1},{9... | collective-permute-start | bytes 798728 | tf_op jit(solution)/shard_map/ppermute | solution.py:33
  256.7 3.6 collective-permute-start.10
  258.3 4.2 %collective-permute-start.11 = (f32[1,65,128]{2,1,0:T(8,128)}, f32[1,65,128]{2,1,0:T(8,128)}, u32[]{:S(2)}, u32[]{:S(2)}) collective-permute-start(f32[1,65,128]{2,1,0:T(8,128)} %get-tuple-element.507), channel_id=1, source_target_pairs={{0,1},{1,2},{2,3},{3,0},{4,5},{5,6},{6,7},{7,4},{8,9},{9,10},{10,1... | collective-permute-start | bytes 99848 | tf_op jit(solution)/shard_map/ppermute | solution.py:24
  264.3 1.7 collective-permute-start.12
  264.3 3.6 collective-permute-start.13
  268.6 1.7 collective-permute-start.14
  268.7 3.6 collective-permute-start.15
  273.0 3.6 collective-permute-start.17
  319.2 1.8 collective-permute-start.18
  319.4 4.3 %collective-permute-start.19 = (f32[1,65,128]{2,1,0:T(8,128)S(1)}, f32[1,65,128]{2,1,0:T(8,128)S(1)}, u32[]{:S(2)}, u32[]{:S(2)}) collective-permute-start(f32[1,65,128]{2,1,0:T(8,128)S(1)} %get-tuple-element.479), channel_id=1, source_target_pairs={{0,1},{1,2},{2,3},{3,0},{4,5},{5,6},{6,7},{7,4},{8,9},{9,10},{10,1... | collective-permute-start | bytes 99848 | tf_op jit(solution)/shard_map/ppermute | solution.py:24
  324.6 3.6 collective-permute-start.21
  329.1 3.6 collective-permute-start.23
  333.6 3.6 collective-permute-start.25
  337.9 11.8 %collective-permute-start.26 = (f32[8,65,128]{2,1,0:T(8,128)S(1)}, f32[8,65,128]{2,1,0:T(8,128)S(1)}, u32[]{:S(2)}, u32[]{:S(2)}) collective-permute-start(f32[8,65,128]{2,1,0:T(8,128)S(1)} %convolution_bitcast_fusion.4), channel_id=1, source_target_pairs={{28,0},{0,4},{4,8},{8,12},{12,16},{16,20},{20,24},{24,28},{29,1},{... | collective-permute-start | bytes 798728 | tf_op jit(solution)/shard_map/ppermute | solution.py:33
  349.7 8.2 %collective-permute-start.27 = (f32[8,65,128]{2,1,0:T(8,128)S(1)}, f32[8,65,128]{2,1,0:T(8,128)S(1)}, u32[]{:S(2)}, u32[]{:S(2)}) collective-permute-start(f32[8,65,128]{2,1,0:T(8,128)S(1)} %sub.738), channel_id=1, source_target_pairs={{4,0},{8,4},{12,8},{16,12},{20,16},{24,20},{28,24},{0,28},{5,1},{9... | collective-permute-start | bytes 798728 | tf_op jit(solution)/shard_map/ppermute | solution.py:33
  360.0 2.6 collective-permute-start.28
  360.0 3.7 collective-permute-start.29
  365.2 2.1 collective-permute-start.30
  365.6 3.4 collective-permute-start.31
  369.6 2.0 collective-permute-start.32
  370.0 3.4 collective-permute-start.33
  374.1 1.9 collective-permute-start.34
  374.3 3.4 collective-permute-start.35
  (22 other events, 93.2 us)
where the time goes:
time: 423 us; the launch traced here: 420 us
  loops' own time  120 us (28%)
  other arithmetic  85.2 us (20%)
  blocking collectives  79.3 us (19%)
  waiting for transfers between devices  75.2 us (18%)
  local copies, waits for them, and re-layouts  23.4 us (6%)
  starting transfers between devices  18.6 us (4%)
  matrix products  12.9 us (3%)
  between operations  5.19 us (1%)
    another operation x2, loops' own time, inverses(): lax.linalg.tridiagonal_solve(lower[None], centre[None], upper[None], iden...  120 us
    psum x2, blocking collectives, per_device(): lax.psum((0.5 * jnp.sum(mismatch * mismatch), jnp.sum(descent * descent))...  79.3 us
    while x62, other arithmetic  77.8 us
    ppermute x4, waiting for transfers between devices, shifted(): return lax.ppermute(block, axis, route)  31.9 us
    ppermute x16, waiting for transfers between devices, padded_2(): before = lax.ppermute(last, axis, up)  28.1 us
    ppermute x16, waiting for transfers between devices, padded_2(): after = lax.ppermute(initial, axis, down)  15.2 us
    slice x20, local copies, waits for them, and re-layouts, inverses(): lax.linalg.tridiagonal_solve(lower[None], centre[None], upper[None], iden...  11.7 us
    ppermute x16, starting transfers between devices, padded_2(): after = lax.ppermute(initial, axis, down)  8.5 us
  transfers between devices with their start and end apart: 36, of which 33 were waited for; matrix products, arithmetic and copies ran while one was open for 24% of the time, Pallas kernels for 0%

commit v1 on v0

v1 whole, which is shorter than its diff:
```python
import functools

import jax
import jax.numpy as jnp
from jax import lax
from jax.experimental import pallas as pl
from jax.experimental.pallas import tpu as pltpu
from jax.sharding import PartitionSpec as P

STEPS = 4
ITERS = 2
ADVECT = 0.15
SPREAD = 0.2
PUSHED = 0.25
EPSILON = 1e-06
BOTH = ("seg", "space")
VMEM = pl.BlockSpec(memory_space=pltpu.VMEM)
LANES = 128


def padded(count, step):
    return -(-count // step) * step


def call(kernel, name, outs, operands, scratch=()):
    return pl.pallas_call(
        kernel,
        name=name,
        out_shape=[jax.ShapeDtypeStruct(shape, dtype) for shape, dtype in outs],
        in_specs=[VMEM] * len(operands),
        out_specs=[VMEM] * len(outs),
        scratch_shapes=list(scratch),
        compiler_params=pltpu.CompilerParams(vmem_limit_bytes=48 * 1024 * 1024),
    )(*operands)


def inverse_kernel(points, rows, k_ref, forward_ref, backward_ref, square):
    row = lax.broadcasted_iota(jnp.int32, (LANES, LANES), 0)
    lane = lax.broadcasted_iota(jnp.int32, (LANES, LANES), 1)
    k = k_ref[...]
    zero = jnp.zeros_like(k)
    a = jnp.where((row >= 1) & (row < points), -k, zero)
    c = jnp.where(row < points - 1, -k, zero)
    b = jnp.where(row < points, 1.0 + 2.0 * k, 1.0)
    d = jnp.where((row == lane) & (row < points), 1.0, 0.0)
    step = 1
    while step < points:
        up = lambda v: pltpu.roll(v, step, 0)
        down = lambda v: pltpu.roll(v, LANES - step, 0)
        alpha = -a / up(b)
        gamma = -c / down(b)
        b = b + alpha * up(c) + gamma * down(a)
        d = d + alpha * up(d) + gamma * down(d)
        a, c = alpha * up(a), gamma * down(c)
        step *= 2
    inverse = d / b
    square[...] = inverse
    stride = padded(points, 16)
    for ref, matrix in ((forward_ref, SPREAD * inverse), (backward_ref, square[...].T)):
        head = matrix.astype(jnp.bfloat16).astype(jnp.float32)
        tail = (matrix - head).astype(jnp.bfloat16).astype(jnp.float32)
        tail = pltpu.roll(tail, stride, 1)
        left = jnp.where(lane >= stride, tail, head)
        right = jnp.where(lane < stride + points - LANES, tail, pltpu.roll(head, 2 * stride - LANES, 1))
        ref[:, :LANES] = left[:rows].astype(jnp.bfloat16)
        ref[:, LANES:] = right[: rows, : 3 * stride - LANES].astype(jnp.bfloat16)


def product(matrix, planes):
    columns = []
    for plane in planes:
        rows = plane.shape[0]
        fill = jnp.zeros((padded(rows, 16) - rows, LANES), jnp.float32)
        plane = jnp.concatenate([plane, fill], 0) if fill.shape[0] else plane
        head = plane.astype(jnp.bfloat16)
        tail = (plane - head.astype(jnp.float32)).astype(jnp.bfloat16)
        columns.append(jnp.concatenate([head, head, tail], 0))
    right = jnp.concatenate(columns, 1) if len(columns) > 1 else columns[0]
    out = jnp.dot(matrix, right, preferred_element_type=jnp.float32)
    return [out[:, i * LANES : (i + 1) * LANES] for i in range(len(planes))]


def neighbours(plane):
    return pltpu.roll(plane, 1, 1) + pltpu.roll(plane, LANES - 1, 1)


def step_size(sums):
    total = jnp.sum(sums, axis=0, keepdims=True)
    lane = lax.broadcasted_iota(jnp.int32, total.shape, 1)
    squares = jnp.sum(jnp.where(lane < LANES // 2, 0.0, total), axis=1, keepdims=True)
    residual = jnp.sum(jnp.where(lane < LANES // 2, total, 0.0), axis=1, keepdims=True)
    return 0.5 * residual / (squares + EPSILON)


def forward_kernel(nx, points, rows, updated, *refs):
    refs = list(refs)
    matrix_ref, cur, left, right, after, force, force_left, force_right = refs[:8]
    del refs[:8]
    if updated:
        d_cur, d_left, d_right, d_after, sums = refs[:5]
        del refs[:5]
        tau = step_size(sums[...])
    ending_ref, mismatch_ref, first_ref, second_ref, third_ref, low_ref, high_ref, squares_ref, edges_ref = refs[:9]
    start_ref = refs[9] if updated else None
    u0, q = refs[-2:]
    pad = rows - points
    h = STEPS

    def place(target, index, source, i, moved):
        value = source[i]
        if moved is not None:
            value = value - tau * moved[i][:points]
        target[index, :points] = value
        return value

    tail = jnp.zeros((pad, LANES), jnp.float32)
    for i in range(nx + 2 * h):
        u0[i, points:] = tail
    for i in range(nx + 2 * h - 2):
        q[i, points:] = tail
    d = (d_cur, d_left, d_right, d_after) if updated else (None,) * 4
    for i in range(h):
        place(u0, i, left, i, d[1])
        place(u0, h + nx + i, right, i, d[2])
    for i in range(nx):
        place(u0, h + i, cur, i, d[0])
    scale = PUSHED / SPREAD
    for i in range(h - 1):
        q[i, :points] = scale * force_left[i]
        q[h - 1 + nx + i, :points] = scale * force_right[i]
    for i in range(nx):
        q[h - 1 + i, :points] = scale * force[i]
    row = lax.broadcasted_iota(jnp.int32, (rows, LANES), 0).astype(jnp.float32)
    base = row * (2.0 / (points - 1)) - 1.0
    matrix = matrix_ref[...]
    fields = [u0, first_ref, second_ref, third_ref, None]
    for t in range(h):
        source, target = fields[t], fields[t + 1]
        count = nx + 2 * (h - t - 1)
        window = [source[0], source[1]]
        pending = []
        for i in range(count):
            window = window[-2:] + [source[i + 2]]
            before, here, ahead = window
            pushed = 3.0 * here + neighbours(here) + q[i + t] - (base + here) * (ahead - before) * (0.5 * ADVECT / SPREAD)
            pending.append(pushed)
            if len(pending) == 2 or i == count - 1:
                for j, plane in enumerate(product(matrix, pending)):
                    at = i - len(pending) + 1 + j
                    if target is not None:
                        target[at] = plane
                    else:
                        ending_ref[at] = plane
                pending = []
    total = jnp.zeros((rows, LANES), jnp.float32)
    for i in range(nx):
        value = after[i]
        if updated:
            value = value - tau * d_after[i][:points]
        value = ending_ref[i][:points] - value
        mismatch_ref[i] = value
        value = jnp.concatenate([value, tail], 0)
        if i < h:
            low_ref[i] = value
        if i >= nx - h:
            high_ref[i - (nx - h)] = value
        total = total + value * value
    folded = total[:8]
    for r in range(8, rows, 8):
        folded = folded + total[r : r + 8]
    squares_ref[...] = folded
    for i in range(h - 1):
        low_ref[h + i] = third_ref[1 + 1 + i]
        high_ref[h + i] = third_ref[1 + nx - h + i]
    low_ref[2 * h - 1] = second_ref[2 + 2]
    high_ref[2 * h - 1] = second_ref[2 + nx - 3]
    if updated:
        for i in range(nx):
            start_ref[i] = u0[h + i, :points]
    edges_ref[0] = u0[h - 1]
    edges_ref[1] = u0[h + nx]


def adjoint_kernel(nx, points, rows, matrix_ref, cur, edges, first, second, third, mismatch, from_left, from_right, lam_ref, a, b):
    h = STEPS
    row = lax.broadcasted_iota(jnp.int32, (rows, LANES), 0).astype(jnp.float32)
    base = row * (2.0 / (points - 1)) - 1.0
    matrix = matrix_ref[...]
    tail = jnp.zeros((rows - points, LANES), jnp.float32)

    def field(t, i):
        if t == 0:
            if i == -1:
                return edges[0]
            if i == nx:
                return edges[1]
            return jnp.concatenate([cur[i], tail], 0)
        if t == 1:
            return first[i + 3]
        if t == 2:
            if i == -3:
                return from_left[2 * h - 1]
            if i == nx + 2:
                return from_right[2 * h - 1]
            return second[i + 2]
        if i < -1:
            return from_left[h + i + 4]
        if i > nx:
            return from_right[h + i - nx - 1]
        return third[i + 1]

    def weight(i):
        if i < 0:
            return from_left[h + i]
        if i >= nx:
            return from_right[i - nx]
        return jnp.concatenate([mismatch[i], tail], 0)

    for t in reversed(range(h)):
        source, target = (a, b) if t % 2 == 0 else (b, a)
        window = []
        low, high = -(t + 1), nx + t + 1
        done = []
        for start in range(low, high, 2):
            group = list(range(start, min(start + 2, high)))
            lams = [weight(i) if t == h - 1 else source[i + h] for i in group]
            for i, mu in zip(group, product(matrix, lams)):
                u = field(t, i)
                window.append((u, mu, (base + u) * mu))
                window = window[-3:]
                if len(window) == 3:
                    (u0, _, f0), (_, m1, _), (u2, _, f2) = window
                    value = SPREAD * (3.0 * m1 + neighbours(m1)) + (0.5 * ADVECT) * ((f2 - f0) - m1 * (u2 - u0))
                    if t == 0:
                        lam_ref[i - 1] = value
                    else:
                        target[i - 1 + h] = value


def descent_kernel(nx, points, rows, devices, lam, prior, cur, squares, descent_ref, low_ref, high_ref, sums_ref):
    h = STEPS
    total = jnp.zeros((rows, LANES), jnp.float32)
    tail = jnp.zeros((rows - points, LANES), jnp.float32)
    for i in range(nx):
        value = lam[i][:points] - (prior[i][:points] - cur[i])
        value = jnp.concatenate([value, tail], 0)
        descent_ref[i] = value
        if i < h:
            low_ref[i] = value
        if i >= nx - h:
            high_ref[i - (nx - h)] = value
        total = total + value * value
    folded = total[:8]
    for r in range(8, rows, 8):
        folded = folded + total[r : r + 8]

    def fold(v):
        v = jnp.sum(v, axis=0, keepdims=True)
        return v + pltpu.roll(v, LANES // 2, 1)

    lane = lax.broadcasted_iota(jnp.int32, (1, LANES), 1)
    both = jnp.where(lane < LANES // 2, fold(squares[...]), fold(folded))
    sums_ref[...] = jnp.broadcast_to(both, (devices, LANES))


def final_kernel(nx, points, cur, descent, sums, out_ref):
    tau = step_size(sums[...])
    for i in range(nx):
        out_ref[i] = cur[i] - tau * descent[i][:points]


def shift(block, axis, distance):
    devices = lax.axis_size(axis)
    return lax.ppermute(block, axis, [((i - distance) % devices, i) for i in range(devices)])


def per_device(states, forcing, wall_viscosity):
    cur = states[0]
    nx, points, _ = cur.shape
    rows = padded(points, 8)
    depth = 3 * padded(points, 16)
    devices = lax.axis_size("seg") * lax.axis_size("space")
    h = STEPS
    f32, bf16 = jnp.float32, jnp.bfloat16
    left = shift(cur[nx - h :], "space", 1)
    right = shift(cur[:h], "space", -1)
    force_left = shift(forcing[nx - h + 1 :], "space", 1)
    force_right = shift(forcing[: h - 1], "space", -1)
    after = shift(cur, "seg", -1)
    k = jnp.broadcast_to(jnp.pad(wall_viscosity, (0, LANES - points))[:, None], (LANES, LANES))
    forward, backward = call(
        functools.partial(inverse_kernel, points, rows),
        "inverse",
        [((rows, depth), bf16)] * 2,
        [k],
        [pltpu.VMEM((LANES, LANES), f32)],
    )
    given = [cur, left, right, after, forcing, force_left, force_right]
    moved = []
    start = cur
    mismatch = None
    for iteration in range(ITERS):
        updated = iteration > 0
        outs = [
            ((nx, rows, LANES), f32),
            ((nx, points, LANES), f32),
            ((nx + 6, rows, LANES), f32),
            ((nx + 4, rows, LANES), f32),
            ((nx + 2, rows, LANES), f32),
            ((2 * h, rows, LANES), f32),
            ((2 * h, rows, LANES), f32),
            ((8, LANES), f32),
            ((2, rows, LANES), f32),
        ]
        if updated:
            outs.append(((nx, points, LANES), f32))
        ending, mismatch, first, second, third, low, high, squares, edges, *moved_start = call(
            functools.partial(forward_kernel, nx, points, rows, updated),
            "forward",
            outs,
            [forward] + given + moved,
            [pltpu.VMEM((nx + 2 * h, rows, LANES), f32), pltpu.VMEM((nx + 2 * h - 2, rows, LANES), f32)],
        )
        prior = shift(ending, "seg", 1)
        from_left = shift(high, "space", 1)
        from_right = shift(low, "space", -1)
        start = moved_start[0] if updated else cur
        lam = call(
            functools.partial(adjoint_kernel, nx, points, rows),
            "adjoint",
            [((nx, rows, LANES), f32)],
            [backward, start, edges, first, second, third, mismatch, from_left, from_right],
            [pltpu.VMEM((nx + 2 * h, rows, LANES), f32)] * 2,
        )[0]
        descent, d_low, d_high, sums = call(
            functools.partial(descent_kernel, nx, points, rows, devices),
            "descent",
            [((nx, rows, LANES), f32), ((h, rows, LANES), f32), ((h, rows, LANES), f32), ((devices, LANES), f32)],
            [lam, prior, start, squares],
        )
        if iteration < ITERS - 1:
            moved = [descent, shift(d_high, "space", 1), shift(d_low, "space", -1), shift(descent, "seg", -1)]
        sums = lax.all_to_all(sums, BOTH, 0, 0, tiled=True)
        moved = moved + [sums] if iteration < ITERS - 1 else moved
    new = call(
        functools.partial(final_kernel, nx, points),
        "final",
        [((nx, points, LANES), f32)],
        [start, descent, sums],
    )[0]
    return (new[None], mismatch[None])


def solution(mesh):
    placed = (P("seg", "space", None, None), P("space", None, None), P())
    return jax.shard_map(
        per_device,
        mesh=mesh,
        in_specs=placed,
        out_specs=(P("seg", "space", None, None), P("seg", "space", None, None)),
        check_vma=False,
    )
```

time: 423 us -> 69 us (0.16)
  loops' own time: 120 us -> 0 us
  other arithmetic: 85.2 us -> 0 us
  blocking collectives: 79.3 us -> 8.83 us
  waiting for transfers between devices: 75.2 us -> 29.8 us
  local copies, waits for them, and re-layouts: 23.4 us -> 2.7 us
  matrix products: 12.9 us -> 0 us
  Pallas kernels: 0 us -> 7.79 us
  between operations: 5.19 us -> 0.76 us
    another operation x2 -> x0, loops' own time: 120 us -> none  [inverses(): lax.linalg.tridiagonal_solve(lower[None], centre[None], upper[None], iden...]
    psum x2 -> x0, blocking collectives: 79.3 us -> none  [per_device(): lax.psum((0.5 * jnp.sum(mismatch * mismatch), jnp.sum(descent * descent))...]
    while x62 -> x0, other arithmetic: 77.8 us -> none
    ppermute x36 -> x14, waiting for transfers between devices: 75.2 us -> 23.4 us  [shift(): lax.ppermute(block, axis, [((i - distance) % devices, i) for i in range(d...]
    slice x69 -> x2, local copies, waits for them, and re-layouts: 19.1 us -> 0.04 us  [the longest x1 0.02 us: per_device(): right = shift(cur[:h], 'space', -1)]
    dot_general x16 -> x0, matrix products: 12.9 us -> none  [the longest x8 6.64 us: apply_transposed(): jnp.einsum('kj,xkz->xjz', inverse, field, precision=lax.Precision.HIGHEST)]
    all_to_all x0 -> x1, blocking collectives: none -> 8.83 us  [per_device(): sums = lax.all_to_all(sums, BOTH, 0, 0, tiled=True)]
    pallas_call x0 -> x8, Pallas kernels: none -> 7.79 us  [call(): pl.pallas_call(kernel, name=name, out_shape=[jax.ShapeDtypeStruct(shape,...]
  transfers between devices with their start and end apart: 36 -> 15, of which waited for: 33 -> 9; matrix products, arithmetic and copies ran while one was open for 24% -> 1% of each run, Pallas kernels for 0% -> 5%
where the time goes in v1:
time: 69 us; the launch traced here: 68.8 us
  waiting for transfers between devices  29.8 us (43%)
  starting transfers between devices  19 us (28%)
  blocking collectives  8.83 us (13%)
  Pallas kernels  7.79 us (11%)
  local copies, waits for them, and re-layouts  2.7 us (4%)
  between operations  0.76 us (1%)
    ppermute x14, waiting for transfers between devices, shift(): lax.ppermute(block, axis, [((i - distance) % devices, i) for i in range(d...  23.4 us
    ppermute x14, starting transfers between devices, shift(): lax.ppermute(block, axis, [((i - distance) % devices, i) for i in range(d...  16.5 us
    all_to_all x1, blocking collectives, per_device(): sums = lax.all_to_all(sums, BOTH, 0, 0, tiled=True)  8.83 us
    pallas_call x8, Pallas kernels, call(): pl.pallas_call(kernel, name=name, out_shape=[jax.ShapeDtypeStruct(shape,...  7.79 us
    all_to_all x1, waiting for transfers between devices, per_device(): sums = lax.all_to_all(sums, BOTH, 0, 0, tiled=True)  6.38 us
    unnamed x8, local copies, waits for them, and re-layouts  2.58 us
    all_to_all x1, starting transfers between devices, per_device(): sums = lax.all_to_all(sums, BOTH, 0, 0, tiled=True)  2.49 us
  transfers between devices with their start and end apart: 15, of which 9 were waited for; matrix products, arithmetic and copies ran while one was open for 1% of the time, Pallas kernels for 5%

profile of v1, /device:TPU:0, one launch (start us, length us, event | category | flops | bytes accessed | tf_op | source)
XLA Modules:
  0.0 68.8 jit_solution(3274809048715713049)
XLA Ops:
  0.6 1.0 %copy.27 = f32[1,8,65,128]{3,2,1,0:T(8,128)S(1)} copy(f32[1,8,65,128]{3,1,2,0:T(8,128)} %param.3) | data formatting | bytes 532480 | tf_op args[0]
  1.7 2.5 %collective-permute-start.1 = (f32[4,65,128]{2,1,0:T(8,128)S(1)}, f32[4,65,128]{2,1,0:T(8,128)S(1)}, u32[]{:S(2)}, u32[]{:S(2)}) collective-permute-start(f32[4,65,128]{2,1,0:T(8,128)S(1)} %get-tuple-element.62), channel_id=1, source_target_pairs={{1,0},{2,1},{3,2},{0,3},{5,4},{6,5},{7,6},{4,7},{9,8},{10,9},{11,1... | collective-permute-start | bytes 399368 | tf_op jit(solution)/shard_map/ppermute | solution.py:274
  4.1 4.5 %collective-permute-start.2 = (f32[8,65,128]{2,1,0:T(8,128)S(1)}, f32[8,65,128]{2,1,0:T(8,128)S(1)}, u32[]{:S(2)}, u32[]{:S(2)}) collective-permute-start(f32[8,65,128]{2,1,0:T(8,128)S(1)} %bitcast.16), channel_id=1, source_target_pairs={{4,0},{8,4},{12,8},{16,12},{20,16},{24,20},{28,24},{0,28},{5,1},{9... | collective-permute-start | bytes 798728 | tf_op jit(solution)/shard_map/ppermute | solution.py:274
  8.8 1.5 %collective-permute-start.4 = (f32[3,65,128]{2,1,0:T(8,128)S(1)}, f32[3,65,128]{2,1,0:T(8,128)S(1)}, u32[]{:S(2)}, u32[]{:S(2)}) collective-permute-start(f32[3,65,128]{2,1,0:T(8,128)S(1)} %get-tuple-element.60), channel_id=1, source_target_pairs={{1,0},{2,1},{3,2},{0,3},{5,4},{6,5},{7,6},{4,7},{9,8},{10,9},{11,1... | collective-permute-start | bytes 299528 | tf_op jit(solution)/shard_map/ppermute | solution.py:274
  10.4 0.4 inverse.1
  10.8 2.9 %collective-permute-done.4.refs_7_ = f32[3,65,128]{2,1,0:T(8,128)S(1)} collective-permute-done((f32[3,65,128]{2,1,0:T(8,128)S(1)}, f32[3,65,128]{2,1,0:T(8,128)S(1)}, u32[]{:S(2)}, u32[]{:S(2)}) %collective-permute-start.4) | collective-permute-done | bytes 99872 | tf_op jit(solution)/shard_map/ppermute | solution.py:274
  13.7 1.1 %collective-permute-done.3.refs_6_ = f32[3,65,128]{2,1,0:T(8,128)S(1)} collective-permute-done((f32[3,65,128]{2,1,0:T(8,128)S(1)}, f32[3,65,128]{2,1,0:T(8,128)S(1)}, u32[]{:S(2)}, u32[]{:S(2)}) %collective-permute-start.3) | collective-permute-done | bytes 99872 | tf_op jit(solution)/shard_map/ppermute | solution.py:274
  14.8 1.0 %collective-permute-done.2.refs_4_ = f32[8,65,128]{2,1,0:T(8,128)S(1)} collective-permute-done((f32[8,65,128]{2,1,0:T(8,128)S(1)}, f32[8,65,128]{2,1,0:T(8,128)S(1)}, u32[]{:S(2)}, u32[]{:S(2)}) %collective-permute-start.2) | collective-permute-done | bytes 266272 | tf_op jit(solution)/shard_map/ppermute | solution.py:274
  15.8 1.5 %forward.2 = (f32[8,72,128]{2,1,0:T(8,128)S(1)}, f32[8,65,128]{2,1,0:T(8,128)S(1)}, f32[14,72,128]{2,1,0:T(8,128)S(1)}, f32[12,72,128]{2,1,0:T(8,128)S(1)}, f32[...) custom-call(bf16[72,240]{1,0:T(8,128)(2,1)S(1)} %get-tuple-element.2, ...), custom_call_target="tpu_custom_call" | custom-call | tf_op jit(solution)/shard_map/forward/pallas_call | solution.py:26
  17.4 1.7 %collective-permute-start.6 = (f32[8,72,128]{2,1,0:T(8,128)S(1)}, f32[8,72,128]{2,1,0:T(8,128)S(1)}, u32[]{:S(2)}, u32[]{:S(2)}) collective-permute-start(f32[8,72,128]{2,1,0:T(8,128)S(1)} %get-tuple-element.37), channel_id=1, source_target_pairs={{1,0},{2,1},{3,2},{0,3},{5,4},{6,5},{7,6},{4,7},{9,8},{10,9},{11,1... | collective-permute-start | bytes 884744 | tf_op jit(solution)/shard_map/ppermute | solution.py:274
  19.2 0.3 collective-permute-start.7
  19.5 5.7 %collective-permute-done.5.from_left = f32[8,72,128]{2,1,0:T(8,128)S(1)} collective-permute-done((f32[8,72,128]{2,1,0:T(8,128)S(1)}, f32[8,72,128]{2,1,0:T(8,128)S(1)}, u32[]{:S(2)}, u32[]{:S(2)}) %collective-permute-start.5) | collective-permute-done | bytes 294944 | tf_op jit(solution)/shard_map/ppermute | solution.py:274
  25.2 0.3 collective-permute-done.6.from_right
  25.5 1.6 %adjoint.2.lam = f32[8,72,128]{2,1,0:T(8,128)S(1)} custom-call(bf16[72,240]{1,0:T(8,128)(2,1)S(1)} %get-tuple-element.30.matrix_ref, f32[8,65,128]{2,1,0:T(8,128)S(1)} %bitcast.18, f32[2,72,128]{2,1,0:T(8,128)S(1)} %get-tuple-element.31.edges, f32[14,72,128]{2,1,0:T(8,128)S(1)} %get-tuple-element.32.first, f32[12,72,128]{2,1,0:T(8,128)S(1)} %get-tuple-element.33.second, ...), custom_call_target="tpu_custom_call" | custom-call | tf_op jit(solution)/shard_map/adjoint/pallas_call | solution.py:26
  27.0 4.1 %collective-permute-done.7.prior = f32[8,72,128]{2,1,0:T(8,128)S(1)} collective-permute-done((f32[8,72,128]{2,1,0:T(8,128)S(1)}, f32[8,72,128]{2,1,0:T(8,128)S(1)}, u32[]{:S(2)}, u32[]{:S(2)}) %collective-permute-start.7) | collective-permute-done | bytes 294944 | tf_op jit(solution)/shard_map/ppermute | solution.py:274
  31.1 0.1 descent.2
  31.2 1.7 %collective-permute-start.10 = (f32[8,72,128]{2,1,0:T(8,128)S(1)}, f32[8,72,128]{2,1,0:T(8,128)S(1)}, u32[]{:S(2)}, u32[]{:S(2)}) collective-permute-start(f32[8,72,128]{2,1,0:T(8,128)S(1)} %get-tuple-element.40.refs_8_), channel_id=1, source_target_pairs={{4,0},{8,4},{12,8},{16,12},{20,16},{24,20},{28,24},{0,28},{5,1},{9... | collective-permute-start | bytes 884744 | tf_op jit(solution)/shard_map/ppermute | solution.py:274
  33.0 0.5 collective-permute-start.8
  33.5 1.2 %collective-permute-start.9 = (f32[4,72,128]{2,1,0:T(8,128)S(1)}, f32[4,72,128]{2,1,0:T(8,128)S(1)}, u32[]{:S(2)}, u32[]{:S(2)}) collective-permute-start(f32[4,72,128]{2,1,0:T(8,128)S(1)} %get-tuple-element.42), channel_id=1, source_target_pairs={{1,0},{2,1},{3,2},{0,3},{5,4},{6,5},{7,6},{4,7},{9,8},{10,9},{11,1... | collective-permute-start | bytes 442376 | tf_op jit(solution)/shard_map/ppermute | solution.py:274
  34.7 8.8 %all_to_all.22 = f32[32,1,128]{2,1,0:T(1,128)S(1)} all-to-all(f32[32,1,128]{2,1,0:T(1,128)S(1)} %bitcast.25), channel_id=1, replica_groups=mesh['seg'=8,'space'=4] {'seg','space'}, dimensions={0} | all-to-all | bytes 32768 | tf_op jit(solution)/shard_map/all_to_all | solution.py:343
  43.6 1.6 %forward.3 = (f32[8,72,128]{2,1,0:T(8,128)S(1)}, f32[8,65,128]{2,1,0:T(8,128)S(1)}, f32[14,72,128]{2,1,0:T(8,128)S(1)}, f32[12,72,128]{2,1,0:T(8,128)S(1)}, f32[...) custom-call(bf16[72,240]{1,0:T(8,128)(2,1)S(1)} %get-tuple-element.2, ...), custom_call_target="tpu_custom_call" | custom-call | tf_op jit(solution)/shard_map/forward/pallas_call | solution.py:26
  45.3 1.7 %collective-permute-start.12 = (f32[8,72,128]{2,1,0:T(8,128)S(1)}, f32[8,72,128]{2,1,0:T(8,128)S(1)}, u32[]{:S(2)}, u32[]{:S(2)}) collective-permute-start(f32[8,72,128]{2,1,0:T(8,128)S(1)} %get-tuple-element.51), channel_id=1, source_target_pairs={{1,0},{2,1},{3,2},{0,3},{5,4},{6,5},{7,6},{4,7},{9,8},{10,9},{11,1... | collective-permute-start | bytes 884744 | tf_op jit(solution)/shard_map/ppermute | solution.py:274
  47.0 0.6 collective-permute-start.13
  47.6 6.2 %collective-permute-done.11.from_left = f32[8,72,128]{2,1,0:T(8,128)S(1)} collective-permute-done((f32[8,72,128]{2,1,0:T(8,128)S(1)}, f32[8,72,128]{2,1,0:T(8,128)S(1)}, u32[]{:S(2)}, u32[]{:S(2)}) %collective-permute-start.11) | collective-permute-done | bytes 294944 | tf_op jit(solution)/shard_map/ppermute | solution.py:274
  53.8 1.6 %adjoint.3.lam = f32[8,72,128]{2,1,0:T(8,128)S(1)} custom-call(bf16[72,240]{1,0:T(8,128)(2,1)S(1)} %get-tuple-element.30.matrix_ref, f32[8,65,128]{2,1,0:T(8,128)S(1)} %get-tuple-element.44.cur, f32[2,72,128]{2,1,0:T(8,128)S(1)} %get-tuple-element.45.edges, f32[14,72,128]{2,1,0:T(8,128)S(1)} %get-tuple-element.46.first, ...), custom_call_target="tpu_custom_call" | custom-call | tf_op jit(solution)/shard_map/adjoint/pallas_call | solution.py:26
  55.3 2.2 %collective-permute-done.13.prior = f32[8,72,128]{2,1,0:T(8,128)S(1)} collective-permute-done((f32[8,72,128]{2,1,0:T(8,128)S(1)}, f32[8,72,128]{2,1,0:T(8,128)S(1)}, u32[]{:S(2)}, u32[]{:S(2)}) %collective-permute-start.13) | collective-permute-done | bytes 294944 | tf_op jit(solution)/shard_map/ppermute | solution.py:274
  57.5 0.8 %descent.3 = (f32[8,72,128]{2,1,0:T(8,128)S(1)}, f32[4,72,128]{2,1,0:T(8,128)}, f32[4,72,128]{2,1,0:T(8,128)}, f32[32,128]{1,0:T(8,128)}) custom-call(f32[8,72,128]{2,1,0:T(8,128)S(1)} %adjoint.3.lam, f32[8,72,128]{2,1,0:T(8,128)S(1)} %collective-permute-done.13.prior, f32[8,65,128]{2,1,0:T(8,128)S(1)} %get-tuple-element.44.cur, ...), custom_call_target="tpu_custom_call" | custom-call | tf_op jit(solution)/shard_map/descent/pallas_call | solution.py:26
  58.3 2.5 %all-to-all-start.1 = ((f32[32,1,128]{2,1,0:T(1,128)}), f32[32,1,128]{2,1,0:T(1,128)S(1)}, u32[]{:S(2)}, u32[]{:S(2)}) async-start(f32[32,1,128]{2,1,0:T(1,128)} %bitcast.7), calls=%async_computation.1 | async-start | bytes 32768 | tf_op jit(solution)/shard_map/all_to_all | solution.py:343
  60.8 0.8 %copy.24 = f32[1,8,65,128]{3,1,2,0:T(8,128)} copy(f32[1,8,65,128]{3,2,1,0:T(8,128)S(1)} %bitcast.22) | data formatting | bytes 532480
  61.6 6.4 %all-to-all-done.1 = f32[32,1,128]{2,1,0:T(1,128)S(1)} async-done(((f32[32,1,128]{2,1,0:T(1,128)}), f32[32,1,128]{2,1,0:T(1,128)S(1)}, u32[]{:S(2)}, u32[]{:S(2)}) %all-to-all-start.1) | async-done | bytes 16416 | tf_op jit(solution)/shard_map/all_to_all | solution.py:343
  67.9 0.1 final.1
  68.1 0.8 %copy.23 = f32[1,8,65,128]{3,1,2,0:T(8,128)} copy(f32[1,8,65,128]{3,2,1,0:T(8,128)S(1)} %bitcast.21) | data formatting | bytes 532480
  (19 shorter events, 0.3 us)
Async XLA Ops:
  1.6 7.0 %copy-start = (f32[8,65,128]{2,0,1:T(8,128)S(1)}, f32[8,65,128]{2,0,1:T(8,128)}, u32[]{:S(2)}) copy-start(f32[8,65,128]{2,0,1:T(8,128)} %param.4) | copy-start | bytes 798724
  1.7 13.1 %collective-permute-start.1 = (f32[4,65,128]{2,1,0:T(8,128)S(1)}, f32[4,65,128]{2,1,0:T(8,128)S(1)}, u32[]{:S(2)}, u32[]{:S(2)}) collective-permute-start(f32[4,65,128]{2,1,0:T(8,128)S(1)} %get-tuple-element.62), channel_id=1, source_target_pairs={{1,0},{2,1},{3,2},{0,3},{5,4},{6,5},{7,6},{4,7},{9,8},{10,9},{11,1... | collective-permute-start | bytes 399368 | tf_op jit(solution)/shard_map/ppermute | solution.py:274
  4.1 10.7 %collective-permute-start = (f32[4,65,128]{2,1,0:T(8,128)S(1)}, f32[4,65,128]{2,1,0:T(8,128)S(1)}, u32[]{:S(2)}, u32[]{:S(2)}) collective-permute-start(f32[4,65,128]{2,1,0:T(8,128)S(1)} %get-tuple-element.63), channel_id=1, source_target_pairs={{3,0},{0,1},{1,2},{2,3},{7,4},{4,5},{5,6},{6,7},{11,8},{8,9},{9,10... | collective-permute-start | bytes 399368 | tf_op jit(solution)/shard_map/ppermute | solution.py:274
  4.1 11.7 %collective-permute-start.2 = (f32[8,65,128]{2,1,0:T(8,128)S(1)}, f32[8,65,128]{2,1,0:T(8,128)S(1)}, u32[]{:S(2)}, u32[]{:S(2)}) collective-permute-start(f32[8,65,128]{2,1,0:T(8,128)S(1)} %bitcast.16), channel_id=1, source_target_pairs={{4,0},{8,4},{12,8},{16,12},{20,16},{24,20},{28,24},{0,28},{5,1},{9... | collective-permute-start | bytes 798728 | tf_op jit(solution)/shard_map/ppermute | solution.py:274
  8.8 1.5 %copy-start.1 = (f32[65]{0:T(128)S(1)}, f32[65]{0:T(128)}, u32[]{:S(2)}) copy-start(f32[65]{0:T(128)} %param.5) | copy-start | bytes 784
  8.8 4.9 %collective-permute-start.4 = (f32[3,65,128]{2,1,0:T(8,128)S(1)}, f32[3,65,128]{2,1,0:T(8,128)S(1)}, u32[]{:S(2)}, u32[]{:S(2)}) collective-permute-start(f32[3,65,128]{2,1,0:T(8,128)S(1)} %get-tuple-element.60), channel_id=1, source_target_pairs={{1,0},{2,1},{3,2},{0,3},{5,4},{6,5},{7,6},{4,7},{9,8},{10,9},{11,1... | collective-permute-start | bytes 299528 | tf_op jit(solution)/shard_map/ppermute | solution.py:274
  10.3 4.5 %collective-permute-start.3 = (f32[3,65,128]{2,1,0:T(8,128)S(1)}, f32[3,65,128]{2,1,0:T(8,128)S(1)}, u32[]{:S(2)}, u32[]{:S(2)}) collective-permute-start(f32[3,65,128]{2,1,0:T(8,128)S(1)} %get-tuple-element.61), channel_id=1, source_target_pairs={{3,0},{0,1},{1,2},{2,3},{7,4},{4,5},{5,6},{6,7},{11,8},{8,9},{9,10... | collective-permute-start | bytes 299528 | tf_op jit(solution)/shard_map/ppermute | solution.py:274
  17.4 7.8 %collective-permute-start.5 = (f32[8,72,128]{2,1,0:T(8,128)S(1)}, f32[8,72,128]{2,1,0:T(8,128)S(1)}, u32[]{:S(2)}, u32[]{:S(2)}) collective-permute-start(f32[8,72,128]{2,1,0:T(8,128)S(1)} %get-tuple-element.36), channel_id=1, source_target_pairs={{3,0},{0,1},{1,2},{2,3},{7,4},{4,5},{5,6},{6,7},{11,8},{8,9},{9,10... | collective-permute-start | bytes 884744 | tf_op jit(solution)/shard_map/ppermute | solution.py:274
  17.4 8.0 %collective-permute-start.6 = (f32[8,72,128]{2,1,0:T(8,128)S(1)}, f32[8,72,128]{2,1,0:T(8,128)S(1)}, u32[]{:S(2)}, u32[]{:S(2)}) collective-permute-start(f32[8,72,128]{2,1,0:T(8,128)S(1)} %get-tuple-element.37), channel_id=1, source_target_pairs={{1,0},{2,1},{3,2},{0,3},{5,4},{6,5},{7,6},{4,7},{9,8},{10,9},{11,1... | collective-permute-start | bytes 884744 | tf_op jit(solution)/shard_map/ppermute | solution.py:274
  19.2 11.9 %collective-permute-start.7 = (f32[8,72,128]{2,1,0:T(8,128)S(1)}, f32[8,72,128]{2,1,0:T(8,128)S(1)}, u32[]{:S(2)}, u32[]{:S(2)}) collective-permute-start(f32[8,72,128]{2,1,0:T(8,128)S(1)} %get-tuple-element.38), channel_id=1, source_target_pairs={{28,0},{0,4},{4,8},{8,12},{12,16},{16,20},{20,24},{24,28},{29,1},{... | collective-permute-start | bytes 884744 | tf_op jit(solution)/shard_map/ppermute | solution.py:274
  31.2 12.3 %collective-permute-start.10 = (f32[8,72,128]{2,1,0:T(8,128)S(1)}, f32[8,72,128]{2,1,0:T(8,128)S(1)}, u32[]{:S(2)}, u32[]{:S(2)}) collective-permute-start(f32[8,72,128]{2,1,0:T(8,128)S(1)} %get-tuple-element.40.refs_8_), channel_id=1, source_target_pairs={{4,0},{8,4},{12,8},{16,12},{20,16},{24,20},{28,24},{0,28},{5,1},{9... | collective-permute-start | bytes 884744 | tf_op jit(solution)/shard_map/ppermute | solution.py:274
  33.0 10.6 %collective-permute-start.8 = (f32[4,72,128]{2,1,0:T(8,128)S(1)}, f32[4,72,128]{2,1,0:T(8,128)S(1)}, u32[]{:S(2)}, u32[]{:S(2)}) collective-permute-start(f32[4,72,128]{2,1,0:T(8,128)S(1)} %get-tuple-element.41), channel_id=1, source_target_pairs={{3,0},{0,1},{1,2},{2,3},{7,4},{4,5},{5,6},{6,7},{11,8},{8,9},{9,10... | collective-permute-start | bytes 442376 | tf_op jit(solution)/shard_map/ppermute | solution.py:274
  33.5 10.1 %collective-permute-start.9 = (f32[4,72,128]{2,1,0:T(8,128)S(1)}, f32[4,72,128]{2,1,0:T(8,128)S(1)}, u32[]{:S(2)}, u32[]{:S(2)}) collective-permute-start(f32[4,72,128]{2,1,0:T(8,128)S(1)} %get-tuple-element.42), channel_id=1, source_target_pairs={{1,0},{2,1},{3,2},{0,3},{5,4},{6,5},{7,6},{4,7},{9,8},{10,9},{11,1... | collective-permute-start | bytes 442376 | tf_op jit(solution)/shard_map/ppermute | solution.py:274
  45.2 8.6 %collective-permute-start.11 = (f32[8,72,128]{2,1,0:T(8,128)S(1)}, f32[8,72,128]{2,1,0:T(8,128)S(1)}, u32[]{:S(2)}, u32[]{:S(2)}) collective-permute-start(f32[8,72,128]{2,1,0:T(8,128)S(1)} %get-tuple-element.50), channel_id=1, source_target_pairs={{3,0},{0,1},{1,2},{2,3},{7,4},{4,5},{5,6},{6,7},{11,8},{8,9},{9,10... | collective-permute-start | bytes 884744 | tf_op jit(solution)/shard_map/ppermute | solution.py:274
  45.3 8.5 %collective-permute-start.12 = (f32[8,72,128]{2,1,0:T(8,128)S(1)}, f32[8,72,128]{2,1,0:T(8,128)S(1)}, u32[]{:S(2)}, u32[]{:S(2)}) collective-permute-start(f32[8,72,128]{2,1,0:T(8,128)S(1)} %get-tuple-element.51), channel_id=1, source_target_pairs={{1,0},{2,1},{3,2},{0,3},{5,4},{6,5},{7,6},{4,7},{9,8},{10,9},{11,1... | collective-permute-start | bytes 884744 | tf_op jit(solution)/shard_map/ppermute | solution.py:274
  47.0 10.5 %collective-permute-start.13 = (f32[8,72,128]{2,1,0:T(8,128)S(1)}, f32[8,72,128]{2,1,0:T(8,128)S(1)}, u32[]{:S(2)}, u32[]{:S(2)}) collective-permute-start(f32[8,72,128]{2,1,0:T(8,128)S(1)} %get-tuple-element.52), channel_id=1, source_target_pairs={{28,0},{0,4},{4,8},{8,12},{12,16},{16,20},{20,24},{24,28},{29,1},{... | collective-permute-start | bytes 884744 | tf_op jit(solution)/shard_map/ppermute | solution.py:274
  58.3 9.6 %all-to-all-start.1 = ((f32[32,1,128]{2,1,0:T(1,128)}), f32[32,1,128]{2,1,0:T(1,128)S(1)}, u32[]{:S(2)}, u32[]{:S(2)}) async-start(f32[32,1,128]{2,1,0:T(1,128)} %bitcast.7), calls=%async_computation.1 | async-start | bytes 32768 | tf_op jit(solution)/shard_map/all_to_all | solution.py:343

commit v2 on v1

v2 whole, which is shorter than its diff:
```python
import functools

import jax
import jax.numpy as jnp
from jax import lax
from jax.experimental import pallas as pl
from jax.experimental.pallas import tpu as pltpu
from jax.sharding import PartitionSpec as P

STEPS = 4
ITERS = 2
ADVECT = 0.15
SPREAD = 0.2
PUSHED = 0.25
EPSILON = 1e-06
BOTH = ("seg", "space")
VMEM = pl.BlockSpec(memory_space=pltpu.VMEM)
LANES = 128


def padded(count, step):
    return -(-count // step) * step


def load(ref, i, planes):
    points = ref.shape[0] // planes
    plane = ref[pl.ds(i, points, stride=planes), :]
    return jnp.concatenate([plane, jnp.zeros((padded(points, 8) - points, LANES), jnp.float32)], 0)


def store(ref, i, planes, plane):
    points = ref.shape[0] // planes
    ref[pl.ds(i, points, stride=planes), :] = plane[:points]


def call(kernel, name, outs, operands, scratch=()):
    return pl.pallas_call(
        kernel,
        name=name,
        out_shape=[jax.ShapeDtypeStruct(shape, dtype) for shape, dtype in outs],
        in_specs=[VMEM] * len(operands),
        out_specs=[VMEM] * len(outs),
        scratch_shapes=list(scratch),
        compiler_params=pltpu.CompilerParams(vmem_limit_bytes=32 * 1024 * 1024),
    )(*operands)


def inverse_kernel(points, rows, k_ref, forward_ref, backward_ref, square):
    row = lax.broadcasted_iota(jnp.int32, (LANES, LANES), 0)
    lane = lax.broadcasted_iota(jnp.int32, (LANES, LANES), 1)
    k = k_ref[...]
    zero = jnp.zeros_like(k)
    a = jnp.where((row >= 1) & (row < points), -k, zero)
    c = jnp.where(row < points - 1, -k, zero)
    b = jnp.where(row < points, 1.0 + 2.0 * k, 1.0)
    d = jnp.where((row == lane) & (row < points), 1.0, 0.0)
    step = 1
    while step < points:
        up = lambda v: pltpu.roll(v, step, 0)
        down = lambda v: pltpu.roll(v, LANES - step, 0)
        alpha = -a / up(b)
        gamma = -c / down(b)
        b = b + alpha * up(c) + gamma * down(a)
        d = d + alpha * up(d) + gamma * down(d)
        a, c = alpha * up(a), gamma * down(c)
        step *= 2
    inverse = d / b
    square[...] = inverse
    stride = padded(points, 16)
    for ref, matrix in ((forward_ref, SPREAD * inverse), (backward_ref, square[...].T)):
        head = matrix.astype(jnp.bfloat16).astype(jnp.float32)
        tail = (matrix - head).astype(jnp.bfloat16).astype(jnp.float32)
        tail = pltpu.roll(tail, stride, 1)
        left = jnp.where(lane >= stride, tail, head)
        right = jnp.where(lane < stride + points - LANES, tail, pltpu.roll(head, 2 * stride - LANES, 1))
        ref[:, :LANES] = left[:rows].astype(jnp.bfloat16)
        ref[:, LANES:] = right[: rows, : 3 * stride - LANES].astype(jnp.bfloat16)


def product(matrix, planes):
    columns = []
    for plane in planes:
        rows = plane.shape[0]
        fill = jnp.zeros((padded(rows, 16) - rows, LANES), jnp.float32)
        plane = jnp.concatenate([plane, fill], 0) if fill.shape[0] else plane
        head = plane.astype(jnp.bfloat16)
        tail = (plane - head.astype(jnp.float32)).astype(jnp.bfloat16)
        columns.append(jnp.concatenate([head, head, tail], 0))
    right = jnp.concatenate(columns, 1) if len(columns) > 1 else columns[0]
    out = jnp.dot(matrix, right, preferred_element_type=jnp.float32)
    return [out[:, i * LANES : (i + 1) * LANES] for i in range(len(planes))]


def neighbours(plane):
    return pltpu.roll(plane, 1, 1) + pltpu.roll(plane, LANES - 1, 1)


def step_size(sums):
    total = jnp.sum(sums, axis=0, keepdims=True)
    lane = lax.broadcasted_iota(jnp.int32, total.shape, 1)
    squares = jnp.sum(jnp.where(lane < LANES // 2, 0.0, total), axis=1, keepdims=True)
    residual = jnp.sum(jnp.where(lane < LANES // 2, total, 0.0), axis=1, keepdims=True)
    return 0.5 * residual / (squares + EPSILON)


def pack_kernel(nx, states, forcing, to_left, to_right):
    h = STEPS
    for i in range(h):
        store(to_left, i, 2 * h - 1, load(states, i, nx))
        store(to_right, i, 2 * h - 1, load(states, nx - h + i, nx))
    for i in range(h - 1):
        store(to_left, h + i, 2 * h - 1, load(forcing, i, nx))
        store(to_right, h + i, 2 * h - 1, load(forcing, nx - h + 1 + i, nx))


def wall_profile(points, rows):
    row = lax.broadcasted_iota(jnp.int32, (rows, LANES), 0).astype(jnp.float32)
    return row * (2.0 / (points - 1)) - 1.0


def forward_kernel(nx, updated, *refs):
    h = STEPS
    m = 2 * h - 1
    refs = list(refs)
    matrix_ref, states, forcing, left, right = refs[:5]
    del refs[:5]
    if updated:
        descent, d_left, d_right, sums = refs[:4]
        del refs[:4]
        tau = step_size(sums[...])
    ending_ref, start_ref, first_ref, second_ref, third_ref = refs[:5]
    moved_ref = refs[5] if updated else None
    u0, q = refs[-2:]
    points = states.shape[0] // nx
    rows = padded(points, 8)
    scale = PUSHED / SPREAD
    for i in range(h):
        before, ahead = load(left, i, m), load(right, i, m)
        if updated:
            before = before - tau * load(d_left, i, h)
            ahead = ahead - tau * load(d_right, i, h)
        u0[i] = before
        u0[h + nx + i] = ahead
        if i == h - 1:
            start_ref[0] = before
        if i == 0:
            start_ref[nx + 1] = ahead
    for i in range(nx):
        here = load(states, i, nx)
        if updated:
            here = here - tau * load(descent, i, nx)
            store(moved_ref, i, nx, here)
        u0[h + i] = here
        start_ref[1 + i] = here
    for i in range(h - 1):
        q[i] = scale * load(left, h + i, m)
        q[h - 1 + nx + i] = scale * load(right, h + i, m)
    for i in range(nx):
        q[h - 1 + i] = scale * load(forcing, i, nx)
    base = wall_profile(points, rows)
    matrix = matrix_ref[...]
    fields = [u0, first_ref, second_ref, third_ref, None]
    for t in range(h):
        source, target = fields[t], fields[t + 1]
        count = nx + 2 * (h - t - 1)
        window = [source[0], source[1]]
        pending = []
        for i in range(count):
            window = window[-2:] + [source[i + 2]]
            before, here, ahead = window
            pending.append(
                3.0 * here + neighbours(here) + q[i + t] - (base + here) * (ahead - before) * (0.5 * ADVECT / SPREAD)
            )
            if len(pending) == 2 or i == count - 1:
                for j, plane in enumerate(product(matrix, pending)):
                    at = i - len(pending) + 1 + j
                    if target is not None:
                        target[at] = plane
                    else:
                        store(ending_ref, at, nx, plane)
                pending = []


def halve(total):
    row = jnp.sum(total, axis=0, keepdims=True)
    return row + pltpu.roll(row, LANES // 2, 1)


def mismatch_kernel(nx, updated, *refs):
    h = STEPS
    refs = list(refs)
    ending, after, second, third = refs[:4]
    del refs[:4]
    if updated:
        d_after, sums = refs[:2]
        del refs[:2]
        tau = step_size(sums[...])
    mismatch_ref, low_ref, high_ref, squares_ref = refs
    total = None
    for i in range(nx):
        value = load(after, i, nx)
        if updated:
            value = value - tau * load(d_after, i, nx)
        value = load(ending, i, nx) - value
        store(mismatch_ref, i, nx, value)
        if i < h:
            store(low_ref, i, 2 * h, value)
        if i >= nx - h:
            store(high_ref, i - (nx - h), 2 * h, value)
        total = value * value if total is None else total + value * value
    squares_ref[...] = halve(total)
    for i in range(h - 1):
        store(low_ref, h + i, 2 * h, third[1 + 1 + i])
        store(high_ref, h + i, 2 * h, third[1 + nx - h + i])
    store(low_ref, 2 * h - 1, 2 * h, second[2 + 2])
    store(high_ref, 2 * h - 1, 2 * h, second[2 + nx - 3])


def adjoint_kernel(nx, matrix_ref, start, first, second, third, mismatch, from_left, from_right, lam_ref, a, b):
    h = STEPS
    points = mismatch.shape[0] // nx
    base = wall_profile(points, padded(points, 8))
    matrix = matrix_ref[...]

    def field(t, i):
        if t == 0:
            return start[i + 1]
        if t == 1:
            return first[i + 3]
        if t == 2:
            if i == -3:
                return load(from_left, 2 * h - 1, 2 * h)
            if i == nx + 2:
                return load(from_right, 2 * h - 1, 2 * h)
            return second[i + 2]
        if i < -1:
            return load(from_left, h + i + 4, 2 * h)
        if i > nx:
            return load(from_right, h + i - nx - 1, 2 * h)
        return third[i + 1]

    def weight(i):
        if i < 0:
            return load(from_left, h + i, 2 * h)
        if i >= nx:
            return load(from_right, i - nx, 2 * h)
        return load(mismatch, i, nx)

    for t in reversed(range(h)):
        source, target = (a, b) if t % 2 == 0 else (b, a)
        window = []
        low, high = -(t + 1), nx + t + 1
        for start_at in range(low, high, 2):
            group = list(range(start_at, min(start_at + 2, high)))
            lams = [weight(i) if t == h - 1 else source[i + h] for i in group]
            for i, mu in zip(group, product(matrix, lams)):
                u = field(t, i)
                window.append((u, mu, (base + u) * mu))
                window = window[-3:]
                if len(window) == 3:
                    (u0, _, f0), (_, m1, _), (u2, _, f2) = window
                    value = SPREAD * (3.0 * m1 + neighbours(m1)) + (0.5 * ADVECT) * ((f2 - f0) - m1 * (u2 - u0))
                    if t == 0:
                        lam_ref[i - 1] = value
                    else:
                        target[i - 1 + h] = value


def sums_kernel(nx, devices, lam, prior, states, squares, sums_ref):
    total = None
    for i in range(nx):
        value = lam[i] - (load(prior, i, nx) - load(states, i, nx))
        total = value * value if total is None else total + value * value
    lane = lax.broadcasted_iota(jnp.int32, (1, LANES), 1)
    sums_ref[...] = jnp.broadcast_to(jnp.where(lane < LANES // 2, squares[...], halve(total)), (devices, LANES))


def descent_kernel(nx, lam, prior, states, descent_ref, low_ref, high_ref):
    h = STEPS
    for i in range(nx):
        value = lam[i] - (load(prior, i, nx) - load(states, i, nx))
        store(descent_ref, i, nx, value)
        if i < h:
            store(low_ref, i, h, value)
        if i >= nx - h:
            store(high_ref, i - (nx - h), h, value)


def final_kernel(nx, lam, prior, states, sums, out_ref):
    tau = step_size(sums[...])
    for i in range(nx):
        here = load(states, i, nx)
        store(out_ref, i, nx, here - tau * (lam[i] - (load(prior, i, nx) - here)))


def shift(block, axis, distance):
    devices = lax.axis_size(axis)
    return lax.ppermute(block, axis, [((i - distance) % devices, i) for i in range(devices)])


def per_device(states, forcing, wall_viscosity):
    nx, points, _ = forcing.shape
    rows = padded(points, 8)
    depth = 3 * padded(points, 16)
    devices = lax.axis_size("seg") * lax.axis_size("space")
    h = STEPS
    f32, bf16 = jnp.float32, jnp.bfloat16

    def flat(planes):
        return ((planes * points, LANES), f32)

    def tiles(planes):
        return ((planes, rows, LANES), f32)

    states = jnp.transpose(states[0], (1, 0, 2)).reshape(nx * points, LANES)
    forcing = jnp.transpose(forcing, (1, 0, 2)).reshape(nx * points, LANES)
    to_left, to_right = call(
        functools.partial(pack_kernel, nx), "pack", [flat(2 * h - 1)] * 2, [states, forcing]
    )
    left = shift(to_right, "space", 1)
    right = shift(to_left, "space", -1)
    after = shift(states, "seg", -1)
    k = jnp.broadcast_to(jnp.pad(wall_viscosity, (0, LANES - points))[:, None], (LANES, LANES))
    forward, backward = call(
        functools.partial(inverse_kernel, points, rows),
        "inverse",
        [((rows, depth), bf16)] * 2,
        [k],
        [pltpu.VMEM((LANES, LANES), f32)],
    )
    current = states
    moved = d_after = sums = None
    for iteration in range(ITERS):
        updated = iteration > 0
        ending, start, first, second, third, *now = call(
            functools.partial(forward_kernel, nx, updated),
            "forward",
            [flat(nx), tiles(nx + 2), tiles(nx + 6), tiles(nx + 4), tiles(nx + 2)] + [flat(nx)] * updated,
            [forward, states, forcing, left, right] + (moved + [sums] if updated else []),
            [pltpu.VMEM((nx + 2 * h, rows, LANES), f32), pltpu.VMEM((nx + 2 * h - 2, rows, LANES), f32)],
        )
        current = now[0] if updated else states
        prior = shift(ending, "seg", 1)
        mismatch, low, high, squares = call(
            functools.partial(mismatch_kernel, nx, updated),
            "mismatch",
            [flat(nx), flat(2 * h), flat(2 * h), ((1, LANES), f32)],
            [ending, after, second, third] + ([d_after, sums] if updated else []),
        )
        from_left = shift(high, "space", 1)
        from_right = shift(low, "space", -1)
        lam = call(
            functools.partial(adjoint_kernel, nx),
            "adjoint",
            [tiles(nx)],
            [backward, start, first, second, third, mismatch, from_left, from_right],
            [pltpu.VMEM((nx + 2 * h, rows, LANES), f32)] * 2,
        )[0]
        rows_of_sums = call(
            functools.partial(sums_kernel, nx, devices), "sums", [((devices, LANES), f32)], [lam, prior, current, squares]
        )[0]
        sums = lax.all_to_all(rows_of_sums, BOTH, 0, 0, tiled=True)
        if iteration < ITERS - 1:
            descent, d_low, d_high = call(
                functools.partial(descent_kernel, nx), "descent", [flat(nx), flat(h), flat(h)], [lam, prior, current]
            )
            moved = [descent, shift(d_high, "space", 1), shift(d_low, "space", -1)]
            d_after = shift(descent, "seg", -1)
    new = call(functools.partial(final_kernel, nx), "final", [flat(nx)], [lam, prior, current, sums])[0]

    def placed(block):
        return jnp.transpose(block.reshape(points, nx, LANES), (1, 0, 2))[None]

    return (placed(new), placed(mismatch))


def solution(mesh):
    placed = (P("seg", "space", None, None), P("space", None, None), P())
    return jax.shard_map(
        per_device,
        mesh=mesh,
        in_specs=placed,
        out_specs=(P("seg", "space", None, None), P("seg", "space", None, None)),
        check_vma=False,
    )
```

time: 69 us -> 66.8 us (0.968)
  blocking collectives: 8.83 us -> 18.5 us
  waiting for transfers between devices: 29.8 us -> 20.8 us
  starting transfers between devices: 19 us -> 14 us
  Pallas kernels: 7.79 us -> 9.51 us
    all_to_all x1 -> x2, blocking collectives: 8.83 us -> 18.5 us  [per_device(): sums = lax.all_to_all(rows_of_sums, BOTH, 0, 0, tiled=True)]
    all_to_all x1 -> x0, waiting for transfers between devices: 6.38 us -> none  [per_device(): sums = lax.all_to_all(sums, BOTH, 0, 0, tiled=True)]
    ppermute x14 -> x12, waiting for transfers between devices: 23.4 us -> 20.8 us  [shift(): lax.ppermute(block, axis, [((i - distance) % devices, i) for i in range(d...]
    all_to_all x1 -> x0, starting transfers between devices: 2.49 us -> none  [per_device(): sums = lax.all_to_all(sums, BOTH, 0, 0, tiled=True)]
    ppermute x14 -> x12, starting transfers between devices: 16.5 us -> 14 us  [shift(): lax.ppermute(block, axis, [((i - distance) % devices, i) for i in range(d...]
    pallas_call x8 -> x12, Pallas kernels: 7.79 us -> 9.51 us  [call(): pl.pallas_call(kernel, name=name, out_shape=[jax.ShapeDtypeStruct(shape,...]
    unnamed x8 -> x12, local copies, waits for them, and re-layouts: 2.58 us -> 2.9 us
  transfers between devices with their start and end apart: 15 -> 12, of which waited for: 9 -> 7; matrix products, arithmetic and copies ran while one was open for 1% -> 0% of each run, Pallas kernels for 5% -> 11%
where the time goes in v2:
time: 66.8 us; the launch traced here: 66.6 us
  waiting for transfers between devices  20.8 us (31%)
  blocking collectives  18.5 us (28%)
  starting transfers between devices  14 us (21%)
  Pallas kernels  9.51 us (14%)
  local copies, waits for them, and re-layouts  2.98 us (4%)
  between operations  0.74 us (1%)
    ppermute x12, waiting for transfers between devices, shift(): lax.ppermute(block, axis, [((i - distance) % devices, i) for i in range(d...  20.8 us
    all_to_all x2, blocking collectives, per_device(): sums = lax.all_to_all(rows_of_sums, BOTH, 0, 0, tiled=True)  18.5 us
    ppermute x12, starting transfers between devices, shift(): lax.ppermute(block, axis, [((i - distance) % devices, i) for i in range(d...  14 us
    pallas_call x12, Pallas kernels, call(): pl.pallas_call(kernel, name=name, out_shape=[jax.ShapeDtypeStruct(shape,...  9.51 us
    unnamed x12, local copies, waits for them, and re-layouts  2.9 us
  transfers between devices with their start and end apart: 12, of which 7 were waited for; matrix products, arithmetic and copies ran while one was open for 0% of the time, Pallas kernels for 11%

profile of v2, /device:TPU:0, one launch (start us, length us, event | category | flops | bytes accessed | tf_op | source)
XLA Modules:
  0.0 66.6 jit_solution(14614302577870292286)
XLA Ops:
  0.6 6.0 %collective-permute-start.2 = (f32[520,128]{1,0:T(8,128)}, f32[520,128]{1,0:T(8,128)S(1)}, u32[]{:S(2)}, u32[]{:S(2)}) collective-permute-start(f32[520,128]{1,0:T(8,128)} %bitcast.26), channel_id=1, source_target_pairs={{4,0},{8,4},{12,8},{16,12},{20,16},{24,20},{28,24},{0,28},{5,1},{9... | collective-permute-start | bytes 798728 | tf_op jit(solution)/shard_map/ppermute | solution.py:298
  6.7 1.0 %copy-done = f32[1,8,65,128]{3,1,2,0:T(8,128)S(1)} copy-done((f32[1,8,65,128]{3,1,2,0:T(8,128)S(1)}, f32[1,8,65,128]{3,1,2,0:T(8,128)}, u32[]{:S(2)}) %copy-start) | copy-done | bytes 266264
  7.6 0.9 %copy-done.2 = f32[8,65,128]{2,0,1:T(8,128)S(1)} copy-done((f32[8,65,128]{2,0,1:T(8,128)S(1)}, f32[8,65,128]{2,0,1:T(8,128)}, u32[]{:S(2)}) %copy-start.2) | copy-done | bytes 266264
  8.6 0.1 pack.1
  8.8 1.7 %collective-permute-start.1 = (f32[455,128]{1,0:T(8,128)S(1)}, f32[455,128]{1,0:T(8,128)S(1)}, u32[]{:S(2)}, u32[]{:S(2)}) collective-permute-start(f32[455,128]{1,0:T(8,128)S(1)} %get-tuple-element.31), channel_id=1, source_target_pairs={{1,0},{2,1},{3,2},{0,3},{5,4},{6,5},{7,6},{4,7},{9,8},{10,9},{11,1... | collective-permute-start | bytes 698888 | tf_op jit(solution)/shard_map/ppermute | solution.py:298
  10.5 0.1 broadcast_in_dim.12.k_ref
  10.6 0.4 inverse.1
  11.0 3.8 %collective-permute-done.refs_3_ = f32[455,128]{1,0:T(8,128)S(1)} collective-permute-done((f32[455,128]{1,0:T(8,128)S(1)}, f32[455,128]{1,0:T(8,128)S(1)}, u32[]{:S(2)}, u32[]{:S(2)}) %collective-permute-start) | collective-permute-done | bytes 232992 | tf_op jit(solution)/shard_map/ppermute | solution.py:298
  14.9 0.9 %collective-permute-done.1.refs_4_ = f32[455,128]{1,0:T(8,128)S(1)} collective-permute-done((f32[455,128]{1,0:T(8,128)S(1)}, f32[455,128]{1,0:T(8,128)S(1)}, u32[]{:S(2)}, u32[]{:S(2)}) %collective-permute-start.1) | collective-permute-done | bytes 232992 | tf_op jit(solution)/shard_map/ppermute | solution.py:298
  15.8 1.5 %forward.2 = (f32[520,128]{1,0:T(8,128)S(1)}, f32[10,72,128]{2,1,0:T(8,128)S(1)}, f32[14,72,128]{2,1,0:T(8,128)S(1)}, f32[12,72,128]{2,1,0:T(8,128)S(1)}, f32[10,72,128]{2,1,0:T(8,128)S(1)}) custom-call(bf16[72,240]{1,0:T(8,128)(2,1)S(1)} %get-tuple-element.29.refs_0_, f32[520,128]{1,0:T(8,128)S(1)} %bitcast.28, f32[520,128]{1,0:T(8,128)S(1)} %bitcast.33, ...), custom_call_target="tpu_custom_call" | custom-call | tf_op jit(solution)/shard_map/forward/pallas_call | solution.py:37
  17.3 0.3 mismatch.2
  17.5 0.8 %collective-permute-start.3 = (f32[520,128]{1,0:T(8,128)S(1)}, f32[520,128]{1,0:T(8,128)S(1)}, u32[]{:S(2)}, u32[]{:S(2)}) collective-permute-start(f32[520,128]{1,0:T(8,128)S(1)} %get-tuple-element.38), channel_id=1, source_target_pairs={{3,0},{0,1},{1,2},{2,3},{7,4},{4,5},{5,6},{6,7},{11,8},{8,9},{9,10... | collective-permute-start | bytes 798728 | tf_op jit(solution)/shard_map/ppermute | solution.py:298
  18.4 1.2 %collective-permute-start.4 = (f32[520,128]{1,0:T(8,128)S(1)}, f32[520,128]{1,0:T(8,128)S(1)}, u32[]{:S(2)}, u32[]{:S(2)}) collective-permute-start(f32[520,128]{1,0:T(8,128)S(1)} %get-tuple-element.39), channel_id=1, source_target_pairs={{1,0},{2,1},{3,2},{0,3},{5,4},{6,5},{7,6},{4,7},{9,8},{10,9},{11,1... | collective-permute-start | bytes 798728 | tf_op jit(solution)/shard_map/ppermute | solution.py:298
  19.6 5.0 %collective-permute-done.3.from_left = f32[520,128]{1,0:T(8,128)S(1)} collective-permute-done((f32[520,128]{1,0:T(8,128)S(1)}, f32[520,128]{1,0:T(8,128)S(1)}, u32[]{:S(2)}, u32[]{:S(2)}) %collective-permute-start.3) | collective-permute-done | bytes 266272 | tf_op jit(solution)/shard_map/ppermute | solution.py:298
  24.5 1.0 %collective-permute-done.4.from_right = f32[520,128]{1,0:T(8,128)S(1)} collective-permute-done((f32[520,128]{1,0:T(8,128)S(1)}, f32[520,128]{1,0:T(8,128)S(1)}, u32[]{:S(2)}, u32[]{:S(2)}) %collective-permute-start.4) | collective-permute-done | bytes 266272 | tf_op jit(solution)/shard_map/ppermute | solution.py:298
  25.5 1.6 %adjoint.2.lam = f32[8,72,128]{2,1,0:T(8,128)S(1)} custom-call(bf16[72,240]{1,0:T(8,128)(2,1)S(1)} %get-tuple-element.28.matrix_ref, f32[10,72,128]{2,1,0:T(8,128)S(1)} %get-tuple-element.32.start, f32[14,72,128]{2,1,0:T(8,128)S(1)} %get-tuple-element.33.first, f32[12,72,128]{2,1,0:T(8,128)S(1)} %get-tuple-element.34.refs_2_.second, ...), custom_call_target="tpu_custom_call" | custom-call | tf_op jit(solution)/shard_map/adjoint/pallas_call | solution.py:37
  27.1 3.3 %collective-permute-done.5.prior = f32[520,128]{1,0:T(8,128)S(1)} collective-permute-done((f32[520,128]{1,0:T(8,128)S(1)}, f32[520,128]{1,0:T(8,128)S(1)}, u32[]{:S(2)}, u32[]{:S(2)}) %collective-permute-start.5) | collective-permute-done | bytes 266272 | tf_op jit(solution)/shard_map/ppermute | solution.py:298
  30.4 0.1 descent.1
  30.7 1.7 %collective-permute-start.7 = (f32[260,128]{1,0:T(8,128)S(1)}, f32[260,128]{1,0:T(8,128)S(1)}, u32[]{:S(2)}, u32[]{:S(2)}) collective-permute-start(f32[260,128]{1,0:T(8,128)S(1)} %get-tuple-element.42), channel_id=1, source_target_pairs={{1,0},{2,1},{3,2},{0,3},{5,4},{6,5},{7,6},{4,7},{9,8},{10,9},{11,1... | collective-permute-start | bytes 399368 | tf_op jit(solution)/shard_map/ppermute | solution.py:298
  32.4 0.2 sums.2
  32.6 9.7 %all_to_all.22 = f32[32,1,128]{2,1,0:T(1,128)S(1)} all-to-all(f32[32,1,128]{2,1,0:T(1,128)S(1)} %bitcast.39), channel_id=1, replica_groups=mesh['seg'=8,'space'=4] {'seg','space'}, dimensions={0} | all-to-all | bytes 32768 | tf_op jit(solution)/shard_map/all_to_all | solution.py:362
  42.3 1.7 %forward.3 = (f32[520,128]{1,0:T(8,128)S(1)}, f32[10,72,128]{2,1,0:T(8,128)S(1)}, f32[14,72,128]{2,1,0:T(8,128)S(1)}, f32[12,72,128]{2,1,0:T(8,128)S(1)}, f32[10...) custom-call(bf16[72,240]{1,0:T(8,128)(2,1)S(1)} %get-tuple-element.29.refs_0_, f32[520,128]{1,0:T(8,128)S(1)} %bitcast.31, ...), custom_call_target="tpu_custom_call" | custom-call | tf_op jit(solution)/shard_map/forward/pallas_call | solution.py:37
  44.0 1.0 %mismatch.3 = (f32[520,128]{1,0:T(8,128)}, f32[520,128]{1,0:T(8,128)S(1)}, f32[520,128]{1,0:T(8,128)S(1)}, f32[1,128]{1,0:T(1,128)S(1)}) custom-call(f32[520,128]{1,0:T(8,128)S(1)} %get-tuple-element.48.refs_0_, f32[520,128]{1,0:T(8,128)S(1)} %collective-permute-done.2.refs_1_, f32[12,72,128]{2,1,0:T(8,128)S(1)} %get-tuple-element.46.refs_2_.second, ...), custom_call_target="tpu_custom_call" | custom-call | tf_op jit(solution)/shard_map/mismatch/pallas_call | solution.py:37
  45.0 1.7 %collective-permute-start.10 = (f32[520,128]{1,0:T(8,128)S(1)}, f32[520,128]{1,0:T(8,128)S(1)}, u32[]{:S(2)}, u32[]{:S(2)}) collective-permute-start(f32[520,128]{1,0:T(8,128)S(1)} %get-tuple-element.51), channel_id=1, source_target_pairs={{1,0},{2,1},{3,2},{0,3},{5,4},{6,5},{7,6},{4,7},{9,8},{10,9},{11,1... | collective-permute-start | bytes 798728 | tf_op jit(solution)/shard_map/ppermute | solution.py:298
  46.8 0.6 collective-permute-start.11
  47.3 5.6 %collective-permute-done.9.from_left = f32[520,128]{1,0:T(8,128)S(1)} collective-permute-done((f32[520,128]{1,0:T(8,128)S(1)}, f32[520,128]{1,0:T(8,128)S(1)}, u32[]{:S(2)}, u32[]{:S(2)}) %collective-permute-start.9) | collective-permute-done | bytes 266272 | tf_op jit(solution)/shard_map/ppermute | solution.py:298
  52.9 1.0 %copy-done.4 = f32[520,128]{1,0:T(8,128)S(1)} copy-done((f32[520,128]{1,0:T(8,128)S(1)}, f32[520,128]{1,0:T(8,128)}, u32[]{:S(2)}) %copy-start.4) | copy-done | bytes 266264
  53.9 1.6 %adjoint.3.lam = f32[8,72,128]{2,1,0:T(8,128)S(1)} custom-call(bf16[72,240]{1,0:T(8,128)(2,1)S(1)} %get-tuple-element.28.matrix_ref, f32[10,72,128]{2,1,0:T(8,128)S(1)} %get-tuple-element.44.start, f32[14,72,128]{2,1,0:T(8,128)S(1)} %get-tuple-element.45.first, f32[12,72,128]{2,1,0:T(8,128)S(1)} %get-tuple-element.46.refs_2_.second, ...), custom_call_target="tpu_custom_call" | custom-call | tf_op jit(solution)/shard_map/adjoint/pallas_call | solution.py:37
  55.5 1.2 %collective-permute-done.11.prior = f32[520,128]{1,0:T(8,128)S(1)} collective-permute-done((f32[520,128]{1,0:T(8,128)S(1)}, f32[520,128]{1,0:T(8,128)S(1)}, u32[]{:S(2)}, u32[]{:S(2)}) %collective-permute-start.11) | collective-permute-done | bytes 266272 | tf_op jit(solution)/shard_map/ppermute | solution.py:298
  56.7 0.2 sums.3
  56.9 8.8 %all_to_all.23 = f32[32,1,128]{2,1,0:T(1,128)S(1)} all-to-all(f32[32,1,128]{2,1,0:T(1,128)S(1)} %bitcast.40), channel_id=1, replica_groups=mesh['seg'=8,'space'=4] {'seg','space'}, dimensions={0} | all-to-all | bytes 32768 | tf_op jit(solution)/shard_map/all_to_all | solution.py:362
  65.7 0.9 %final.1 = f32[520,128]{1,0:T(8,128)} custom-call(f32[8,72,128]{2,1,0:T(8,128)S(1)} %adjoint.3.lam, f32[520,128]{1,0:T(8,128)S(1)} %collective-permute-done.11.prior, f32[520,128]{1,0:T(8,128)S(1)} %get-tuple-element.52.states, f32[32,128]{1,0:T(8,128)S(1)} %bitcast.38), custom_call_target="tpu_custom_call" | custom-call | tf_op jit(solution)/shard_map/final/pallas_call | solution.py:37
  (20 shorter events, 0.2 us)
Async XLA Ops:
  0.6 16.6 %collective-permute-start.2 = (f32[520,128]{1,0:T(8,128)}, f32[520,128]{1,0:T(8,128)S(1)}, u32[]{:S(2)}, u32[]{:S(2)}) collective-permute-start(f32[520,128]{1,0:T(8,128)} %bitcast.26), channel_id=1, source_target_pairs={{4,0},{8,4},{12,8},{16,12},{20,16},{24,20},{28,24},{0,28},{5,1},{9... | collective-permute-start | bytes 798728 | tf_op jit(solution)/shard_map/ppermute | solution.py:298
  6.7 1.0 %copy-start = (f32[1,8,65,128]{3,1,2,0:T(8,128)S(1)}, f32[1,8,65,128]{3,1,2,0:T(8,128)}, u32[]{:S(2)}) copy-start(f32[1,8,65,128]{3,1,2,0:T(8,128)} %param.3) | copy-start | bytes 798724
  7.6 1.0 %copy-start.2 = (f32[8,65,128]{2,0,1:T(8,128)S(1)}, f32[8,65,128]{2,0,1:T(8,128)}, u32[]{:S(2)}) copy-start(f32[8,65,128]{2,0,1:T(8,128)} %param.4) | copy-start | bytes 798724
  8.6 7.2 %copy-start.1 = (f32[1,8,65,128]{3,1,2,0:T(8,128)S(1)}, f32[1,8,65,128]{3,1,2,0:T(8,128)}, u32[]{:S(2)}) copy-start(f32[1,8,65,128]{3,1,2,0:T(8,128)} %param.3) | copy-start | bytes 798724
  8.7 1.8 %copy-start.5 = (f32[65]{0:T(128)S(1)}, f32[65]{0:T(128)}, u32[]{:S(2)}) copy-start(f32[65]{0:T(128)} %param.5) | copy-start | bytes 784
  8.7 6.2 %collective-permute-start = (f32[455,128]{1,0:T(8,128)S(1)}, f32[455,128]{1,0:T(8,128)S(1)}, u32[]{:S(2)}, u32[]{:S(2)}) collective-permute-start(f32[455,128]{1,0:T(8,128)S(1)} %get-tuple-element.30), channel_id=1, source_target_pairs={{3,0},{0,1},{1,2},{2,3},{7,4},{4,5},{5,6},{6,7},{11,8},{8,9},{9,10... | collective-permute-start | bytes 698888 | tf_op jit(solution)/shard_map/ppermute | solution.py:298
  8.8 7.0 %collective-permute-start.1 = (f32[455,128]{1,0:T(8,128)S(1)}, f32[455,128]{1,0:T(8,128)S(1)}, u32[]{:S(2)}, u32[]{:S(2)}) collective-permute-start(f32[455,128]{1,0:T(8,128)S(1)} %get-tuple-element.31), channel_id=1, source_target_pairs={{1,0},{2,1},{3,2},{0,3},{5,4},{6,5},{7,6},{4,7},{9,8},{10,9},{11,1... | collective-permute-start | bytes 698888 | tf_op jit(solution)/shard_map/ppermute | solution.py:298
  17.5 7.0 %collective-permute-start.3 = (f32[520,128]{1,0:T(8,128)S(1)}, f32[520,128]{1,0:T(8,128)S(1)}, u32[]{:S(2)}, u32[]{:S(2)}) collective-permute-start(f32[520,128]{1,0:T(8,128)S(1)} %get-tuple-element.38), channel_id=1, source_target_pairs={{3,0},{0,1},{1,2},{2,3},{7,4},{4,5},{5,6},{6,7},{11,8},{8,9},{9,10... | collective-permute-start | bytes 798728 | tf_op jit(solution)/shard_map/ppermute | solution.py:298
  18.4 7.1 %collective-permute-start.4 = (f32[520,128]{1,0:T(8,128)S(1)}, f32[520,128]{1,0:T(8,128)S(1)}, u32[]{:S(2)}, u32[]{:S(2)}) collective-permute-start(f32[520,128]{1,0:T(8,128)S(1)} %get-tuple-element.39), channel_id=1, source_target_pairs={{1,0},{2,1},{3,2},{0,3},{5,4},{6,5},{7,6},{4,7},{9,8},{10,9},{11,1... | collective-permute-start | bytes 798728 | tf_op jit(solution)/shard_map/ppermute | solution.py:298
  19.6 10.8 %collective-permute-start.5 = (f32[520,128]{1,0:T(8,128)S(1)}, f32[520,128]{1,0:T(8,128)S(1)}, u32[]{:S(2)}, u32[]{:S(2)}) collective-permute-start(f32[520,128]{1,0:T(8,128)S(1)} %get-tuple-element.36.refs_0_), channel_id=1, source_target_pairs={{28,0},{0,4},{4,8},{8,12},{12,16},{16,20},{20,24},{24,28},{29,1},{... | collective-permute-start | bytes 798728 | tf_op jit(solution)/shard_map/ppermute | solution.py:298
  30.6 13.4 %collective-permute-start.8 = (f32[520,128]{1,0:T(8,128)S(1)}, f32[520,128]{1,0:T(8,128)S(1)}, u32[]{:S(2)}, u32[]{:S(2)}) collective-permute-start(f32[520,128]{1,0:T(8,128)S(1)} %get-tuple-element.40.refs_5_), channel_id=1, source_target_pairs={{4,0},{8,4},{12,8},{16,12},{20,16},{24,20},{28,24},{0,28},{5,1},{9... | collective-permute-start | bytes 798728 | tf_op jit(solution)/shard_map/ppermute | solution.py:298
  30.6 11.7 %collective-permute-start.6 = (f32[260,128]{1,0:T(8,128)S(1)}, f32[260,128]{1,0:T(8,128)S(1)}, u32[]{:S(2)}, u32[]{:S(2)}) collective-permute-start(f32[260,128]{1,0:T(8,128)S(1)} %get-tuple-element.41), channel_id=1, source_target_pairs={{3,0},{0,1},{1,2},{2,3},{7,4},{4,5},{5,6},{6,7},{11,8},{8,9},{9,10... | collective-permute-start | bytes 399368 | tf_op jit(solution)/shard_map/ppermute | solution.py:298
  30.7 11.6 %collective-permute-start.7 = (f32[260,128]{1,0:T(8,128)S(1)}, f32[260,128]{1,0:T(8,128)S(1)}, u32[]{:S(2)}, u32[]{:S(2)}) collective-permute-start(f32[260,128]{1,0:T(8,128)S(1)} %get-tuple-element.42), channel_id=1, source_target_pairs={{1,0},{2,1},{3,2},{0,3},{5,4},{6,5},{7,6},{4,7},{9,8},{10,9},{11,1... | collective-permute-start | bytes 399368 | tf_op jit(solution)/shard_map/ppermute | solution.py:298
  32.4 9.9 %copy-start.3 = (f32[8,65,128]{2,0,1:T(8,128)S(1)}, f32[8,65,128]{2,0,1:T(8,128)}, u32[]{:S(2)}) copy-start(f32[8,65,128]{2,0,1:T(8,128)} %param.4) | copy-start | bytes 798724
  45.0 7.9 %collective-permute-start.9 = (f32[520,128]{1,0:T(8,128)S(1)}, f32[520,128]{1,0:T(8,128)S(1)}, u32[]{:S(2)}, u32[]{:S(2)}) collective-permute-start(f32[520,128]{1,0:T(8,128)S(1)} %get-tuple-element.50), channel_id=1, source_target_pairs={{3,0},{0,1},{1,2},{2,3},{7,4},{4,5},{5,6},{6,7},{11,8},{8,9},{9,10... | collective-permute-start | bytes 798728 | tf_op jit(solution)/shard_map/ppermute | solution.py:298
  45.0 7.9 %collective-permute-start.10 = (f32[520,128]{1,0:T(8,128)S(1)}, f32[520,128]{1,0:T(8,128)S(1)}, u32[]{:S(2)}, u32[]{:S(2)}) collective-permute-start(f32[520,128]{1,0:T(8,128)S(1)} %get-tuple-element.51), channel_id=1, source_target_pairs={{1,0},{2,1},{3,2},{0,3},{5,4},{6,5},{7,6},{4,7},{9,8},{10,9},{11,1... | collective-permute-start | bytes 798728 | tf_op jit(solution)/shard_map/ppermute | solution.py:298
  46.8 9.9 %collective-permute-start.11 = (f32[520,128]{1,0:T(8,128)S(1)}, f32[520,128]{1,0:T(8,128)S(1)}, u32[]{:S(2)}, u32[]{:S(2)}) collective-permute-start(f32[520,128]{1,0:T(8,128)S(1)} %get-tuple-element.48.refs_0_), channel_id=1, source_target_pairs={{28,0},{0,4},{4,8},{8,12},{12,16},{16,20},{20,24},{24,28},{29,1},{... | collective-permute-start | bytes 798728 | tf_op jit(solution)/shard_map/ppermute | solution.py:298
  52.9 1.0 %copy-start.4 = (f32[520,128]{1,0:T(8,128)S(1)}, f32[520,128]{1,0:T(8,128)}, u32[]{:S(2)}) copy-start(f32[520,128]{1,0:T(8,128)} %get-tuple-element.49.mismatch) | copy-start | bytes 798724

commit v3 on v2

--- a/solution.py
+++ b/solution.py
@@ -33,19 +33,20 @@
     ref[pl.ds(i, points, stride=planes), :] = plane[:points]
 
 
-def call(kernel, name, outs, operands, scratch=()):
+def call(kernel, name, outs, operands, scratch=(), spec=VMEM):
     return pl.pallas_call(
         kernel,
         name=name,
         out_shape=[jax.ShapeDtypeStruct(shape, dtype) for shape, dtype in outs],
-        in_specs=[VMEM] * len(operands),
+        in_specs=[spec] * len(operands),
         out_specs=[VMEM] * len(outs),
         scratch_shapes=list(scratch),
         compiler_params=pltpu.CompilerParams(vmem_limit_bytes=32 * 1024 * 1024),
     )(*operands)
 
 
-def inverse_kernel(points, rows, k_ref, forward_ref, backward_ref, square):
+def inverse_kernel(points, rows, k_ref, states, forward_ref, backward_ref, states_ref, square):
+    states_ref[...] = states[...]
     row = lax.broadcasted_iota(jnp.int32, (LANES, LANES), 0)
     lane = lax.broadcasted_iota(jnp.int32, (LANES, LANES), 1)
     k = k_ref[...]
@@ -103,14 +104,26 @@
     return 0.5 * residual / (squares + EPSILON)
 
 
-def pack_kernel(nx, states, forcing, to_left, to_right):
-    h = STEPS
+def pack_kernel(nx, states_hbm, forcing_hbm, to_left, to_right, states, forcing, sems):
+    h = STEPS
+    copies = [
+        pltpu.make_async_copy(states_hbm, states, sems.at[0]),
+        pltpu.make_async_copy(forcing_hbm, forcing, sems.at[1]),
+    ]
+    for copy in copies:
+        copy.start()
+    copies[0].wait()
     for i in range(h):
         store(to_left, i, 2 * h - 1, load(states, i, nx))
         store(to_right, i, 2 * h - 1, load(states, nx - h + i, nx))
+    copies[1].wait()
     for i in range(h - 1):
         store(to_left, h + i, 2 * h - 1, load(forcing, i, nx))
         store(to_right, h + i, 2 * h - 1, load(forcing, nx - h + 1 + i, nx))
+
+
+def copy_kernel(given, out):
+    out[...] = given[...]
 
 
 def wall_profile(points, rows):
@@ -129,7 +142,6 @@
         del refs[:4]
         tau = step_size(sums[...])
     ending_ref, start_ref, first_ref, second_ref, third_ref = refs[:5]
-    moved_ref = refs[5] if updated else None
     u0, q = refs[-2:]
     points = states.shape[0] // nx
     rows = padded(points, 8)
@@ -149,7 +161,6 @@
         here = load(states, i, nx)
         if updated:
             here = here - tau * load(descent, i, nx)
-            store(moved_ref, i, nx, here)
         u0[h + i] = here
         start_ref[1 + i] = here
     for i in range(h - 1):
@@ -216,7 +227,10 @@
     store(high_ref, 2 * h - 1, 2 * h, second[2 + nx - 3])
 
 
-def adjoint_kernel(nx, matrix_ref, start, first, second, third, mismatch, from_left, from_right, lam_ref, a, b):
+def adjoint_kernel(
+    nx, devices, matrix_ref, start, first, second, third, mismatch, from_left, from_right, prior, squares,
+    descent_ref, sums_ref, a, b,
+):
     h = STEPS
     points = mismatch.shape[0] // nx
     base = wall_profile(points, padded(points, 8))
@@ -246,6 +260,7 @@
             return load(from_right, i - nx, 2 * h)
         return load(mismatch, i, nx)
 
+    total = None
     for t in reversed(range(h)):
         source, target = (a, b) if t % 2 == 0 else (b, a)
         window = []
@@ -261,24 +276,19 @@
                     (u0, _, f0), (_, m1, _), (u2, _, f2) = window
                     value = SPREAD * (3.0 * m1 + neighbours(m1)) + (0.5 * ADVECT) * ((f2 - f0) - m1 * (u2 - u0))
                     if t == 0:
-                        lam_ref[i - 1] = value
+                        value = value - (load(prior, i - 1, nx) - start[i])
+                        descent_ref[i - 1] = value
+                        total = value * value if total is None else total + value * value
                     else:
                         target[i - 1 + h] = value
-
-
-def sums_kernel(nx, devices, lam, prior, states, squares, sums_ref):
-    total = None
-    for i in range(nx):
-        value = lam[i] - (load(prior, i, nx) - load(states, i, nx))
-        total = value * value if total is None else total + value * value
     lane = lax.broadcasted_iota(jnp.int32, (1, LANES), 1)
     sums_ref[...] = jnp.broadcast_to(jnp.where(lane < LANES // 2, squares[...], halve(total)), (devices, LANES))
 
 
-def descent_kernel(nx, lam, prior, states, descent_ref, low_ref, high_ref):
-    h = STEPS
-    for i in range(nx):
-        value = lam[i] - (load(prior, i, nx) - load(states, i, nx))
+def descent_kernel(nx, descent, sums, descent_ref, low_ref, high_ref):
+    h = STEPS
+    for i in range(nx):
+        value = descent[i]
         store(descent_ref, i, nx, value)
         if i < h:
             store(low_ref, i, h, value)
@@ -286,11 +296,10 @@
             store(high_ref, i - (nx - h), h, value)
 
 
-def final_kernel(nx, lam, prior, states, sums, out_ref):
+def final_kernel(nx, start, descent, sums, out_ref):
     tau = step_size(sums[...])
     for i in range(nx):
-        here = load(states, i, nx)
-        store(out_ref, i, nx, here - tau * (lam[i] - (load(prior, i, nx) - here)))
+        store(out_ref, i, nx, start[i + 1] - tau * descent[i])
 
 
 def shift(block, axis, distance):
@@ -314,32 +323,35 @@
 
     states = jnp.transpose(states[0], (1, 0, 2)).reshape(nx * points, LANES)
     forcing = jnp.transpose(forcing, (1, 0, 2)).reshape(nx * points, LANES)
-    to_left, to_right = call(
-        functools.partial(pack_kernel, nx), "pack", [flat(2 * h - 1)] * 2, [states, forcing]
+    to_left, to_right, states, forcing = call(
+        functools.partial(pack_kernel, nx),
+        "pack",
+        [flat(2 * h - 1)] * 2 + [flat(nx)] * 2,
+        [states, forcing],
+        [pltpu.SemaphoreType.DMA((2,))],
+        pl.BlockSpec(memory_space=pltpu.HBM),
     )
     left = shift(to_right, "space", 1)
     right = shift(to_left, "space", -1)
-    after = shift(states, "seg", -1)
     k = jnp.broadcast_to(jnp.pad(wall_viscosity, (0, LANES - points))[:, None], (LANES, LANES))
-    forward, backward = call(
+    forward, backward, states = call(
         functools.partial(inverse_kernel, points, rows),
         "inverse",
-        [((rows, depth), bf16)] * 2,
-        [k],
+        [((rows, depth), bf16)] * 2 + [flat(nx)],
+        [k, states],
         [pltpu.VMEM((LANES, LANES), f32)],
     )
-    current = states
+    after = shift(states, "seg", -1)
     moved = d_after = sums = None
     for iteration in range(ITERS):
         updated = iteration > 0
-        ending, start, first, second, third, *now = call(
+        ending, start, first, second, third = call(
             functools.partial(forward_kernel, nx, updated),
             "forward",
-            [flat(nx), tiles(nx + 2), tiles(nx + 6), tiles(nx + 4), tiles(nx + 2)] + [flat(nx)] * updated,
+            [flat(nx), tiles(nx + 2), tiles(nx + 6), tiles(nx + 4), tiles(nx + 2)],
             [forward, states, forcing, left, right] + (moved + [sums] if updated else []),
             [pltpu.VMEM((nx + 2 * h, rows, LANES), f32), pltpu.VMEM((nx + 2 * h - 2, rows, LANES), f32)],
         )
-        current = now[0] if updated else states
         prior = shift(ending, "seg", 1)
         mismatch, low, high, squares = call(
             functools.partial(mismatch_kernel, nx, updated),
@@ -349,24 +361,25 @@
         )
         from_left = shift(high, "space", 1)
         from_right = shift(low, "space", -1)
-        lam = call(
-            functools.partial(adjoint_kernel, nx),
+        descent, rows_of_sums = call(
+            functools.partial(adjoint_kernel, nx, devices),
             "adjoint",
-            [tiles(nx)],
-            [backward, start, first, second, third, mismatch, from_left, from_right],
+            [tiles(nx), ((devices, LANES), f32)],
+            [backward, start, first, second, third, mismatch, from_left, from_right, prior, squares],
             [pltpu.VMEM((nx + 2 * h, rows, LANES), f32)] * 2,
-        )[0]
-        rows_of_sums = call(
-            functools.partial(sums_kernel, nx, devices), "sums", [((devices, LANES), f32)], [lam, prior, current, squares]
-        )[0]
+        )
         sums = lax.all_to_all(rows_of_sums, BOTH, 0, 0, tiled=True)
         if iteration < ITERS - 1:
             descent, d_low, d_high = call(
-                functools.partial(descent_kernel, nx), "descent", [flat(nx), flat(h), flat(h)], [lam, prior, current]
+                functools.partial(descent_kernel, nx),
+                "descent",
+                [flat(nx), flat(h), flat(h)],
+                [descent, rows_of_sums],
             )
             moved = [descent, shift(d_high, "space", 1), shift(d_low, "space", -1)]
             d_after = shift(descent, "seg", -1)
-    new = call(functools.partial(final_kernel, nx), "final", [flat(nx)], [lam, prior, current, sums])[0]
+    mismatch = call(copy_kernel, "mismatch_out", [flat(nx)], [mismatch])[0]
+    new = call(functools.partial(final_kernel, nx), "final", [flat(nx)], [start, descent, sums])[0]
 
     def placed(block):
         return jnp.transpose(block.reshape(points, nx, LANES), (1, 0, 2))[None]

time: 66.8 us -> 70.1 us (1.049)
  blocking collectives: 18.5 us -> 9.25 us
  waiting for transfers between devices: 20.8 us -> 29.2 us
  starting transfers between devices: 14 us -> 18 us
    all_to_all x2 -> x1, blocking collectives: 18.5 us -> 9.25 us  [per_device(): sums = lax.all_to_all(rows_of_sums, BOTH, 0, 0, tiled=True)]
    all_to_all x0 -> x1, waiting for transfers between devices: none -> 6.35 us  [per_device(): sums = lax.all_to_all(rows_of_sums, BOTH, 0, 0, tiled=True)]
    all_to_all x0 -> x1, starting transfers between devices: none -> 2.78 us  [per_device(): sums = lax.all_to_all(rows_of_sums, BOTH, 0, 0, tiled=True)]
    ppermute x12, waiting for transfers between devices: 20.8 us -> 22.9 us  [shift(): lax.ppermute(block, axis, [((i - distance) % devices, i) for i in range(d...]
    ppermute x12, starting transfers between devices: 14 us -> 15.2 us  [shift(): lax.ppermute(block, axis, [((i - distance) % devices, i) for i in range(d...]
    unnamed x12 -> x4, local copies, waits for them, and re-layouts: 2.9 us -> 1.9 us
    pallas_call x12 -> x11, Pallas kernels: 9.51 us -> 9.99 us  [call(): pl.pallas_call(kernel, name=name, out_shape=[jax.ShapeDtypeStruct(shape,...]
  transfers between devices with their start and end apart: 12 -> 13, of which waited for: 7 -> 5; matrix products, arithmetic and copies ran while one was open for 0% -> 0% of each run, Pallas kernels for 11% -> 6%
where the time goes in v3:
time: 70.1 us; the launch traced here: 69.8 us
  waiting for transfers between devices  29.2 us (42%)
  starting transfers between devices  18 us (26%)
  Pallas kernels  9.99 us (14%)
  blocking collectives  9.25 us (13%)
  local copies, waits for them, and re-layouts  2.64 us (4%)
  between operations  0.71 us (1%)
    ppermute x12, waiting for transfers between devices, shift(): lax.ppermute(block, axis, [((i - distance) % devices, i) for i in range(d...  22.9 us
    ppermute x12, starting transfers between devices, shift(): lax.ppermute(block, axis, [((i - distance) % devices, i) for i in range(d...  15.2 us
    pallas_call x11, Pallas kernels, call(): pl.pallas_call(kernel, name=name, out_shape=[jax.ShapeDtypeStruct(shape,...  9.99 us
    all_to_all x1, blocking collectives, per_device(): sums = lax.all_to_all(rows_of_sums, BOTH, 0, 0, tiled=True)  9.25 us
    all_to_all x1, waiting for transfers between devices, per_device(): sums = lax.all_to_all(rows_of_sums, BOTH, 0, 0, tiled=True)  6.35 us
    all_to_all x1, starting transfers between devices, per_device(): sums = lax.all_to_all(rows_of_sums, BOTH, 0, 0, tiled=True)  2.78 us
    unnamed x4, local copies, waits for them, and re-layouts  1.9 us
  transfers between devices with their start and end apart: 13, of which 5 were waited for; matrix products, arithmetic and copies ran while one was open for 0% of the time, Pallas kernels for 6%

profile of v3, /device:TPU:0, one launch (start us, length us, event | category | flops | bytes accessed | tf_op | source)
XLA Modules:
  0.0 69.8 jit_solution(2768374630293954034)
XLA Ops:
  0.6 0.7 pad.4
  1.3 0.9 %copy-done = f32[1,8,65,128]{3,1,2,0:T(8,128)S(1)} copy-done((f32[1,8,65,128]{3,1,2,0:T(8,128)S(1)}, f32[1,8,65,128]{3,1,2,0:T(8,128)}, u32[]{:S(2)}) %copy-start) | copy-done | bytes 266264
  2.2 0.9 %copy-done.1 = f32[8,65,128]{2,0,1:T(8,128)S(1)} copy-done((f32[8,65,128]{2,0,1:T(8,128)S(1)}, f32[8,65,128]{2,0,1:T(8,128)}, u32[]{:S(2)}) %copy-start.1) | copy-done | bytes 266264
  3.2 0.2 pack.1
  3.4 0.1 broadcast_in_dim.12.k_ref
  3.4 0.4 inverse.1
  3.9 6.0 %collective-permute-start.2 = (f32[520,128]{1,0:T(8,128)S(1)}, f32[520,128]{1,0:T(8,128)S(1)}, u32[]{:S(2)}, u32[]{:S(2)}) collective-permute-start(f32[520,128]{1,0:T(8,128)S(1)} %get-tuple-element.36.refs_1_), channel_id=1, source_target_pairs={{4,0},{8,4},{12,8},{16,12},{20,16},{24,20},{28,24},{0,28},{5,1},{9... | collective-permute-start | bytes 798728 | tf_op jit(solution)/shard_map/ppermute | solution.py:307
  9.9 1.7 %collective-permute-start.1 = (f32[455,128]{1,0:T(8,128)S(1)}, f32[455,128]{1,0:T(8,128)S(1)}, u32[]{:S(2)}, u32[]{:S(2)}) collective-permute-start(f32[455,128]{1,0:T(8,128)S(1)} %get-tuple-element.39), channel_id=1, source_target_pairs={{1,0},{2,1},{3,2},{0,3},{5,4},{6,5},{7,6},{4,7},{9,8},{10,9},{11,1... | collective-permute-start | bytes 698888 | tf_op jit(solution)/shard_map/ppermute | solution.py:307
  11.7 4.4 %collective-permute-done.refs_3_ = f32[455,128]{1,0:T(8,128)S(1)} collective-permute-done((f32[455,128]{1,0:T(8,128)S(1)}, f32[455,128]{1,0:T(8,128)S(1)}, u32[]{:S(2)}, u32[]{:S(2)}) %collective-permute-start) | collective-permute-done | bytes 232992 | tf_op jit(solution)/shard_map/ppermute | solution.py:307
  16.0 0.9 %collective-permute-done.1.refs_4_ = f32[455,128]{1,0:T(8,128)S(1)} collective-permute-done((f32[455,128]{1,0:T(8,128)S(1)}, f32[455,128]{1,0:T(8,128)S(1)}, u32[]{:S(2)}, u32[]{:S(2)}) %collective-permute-start.1) | collective-permute-done | bytes 232992 | tf_op jit(solution)/shard_map/ppermute | solution.py:307
  16.9 1.5 %forward.2 = (f32[520,128]{1,0:T(8,128)S(1)}, f32[10,72,128]{2,1,0:T(8,128)S(1)}, f32[14,72,128]{2,1,0:T(8,128)S(1)}, f32[12,72,128]{2,1,0:T(8,128)S(1)}, f32[10,72,128]{2,1,0:T(8,128)S(1)}) custom-call(bf16[72,240]{1,0:T(8,128)(2,1)S(1)} %get-tuple-element.35.refs_0_, f32[520,128]{1,0:T(8,128)S(1)} %get-tuple-element.36.refs_1_, ...), custom_call_target="tpu_custom_call" | custom-call | tf_op jit(solution)/shard_map/forward/pallas_call | solution.py:37
  18.4 0.1 collective-permute-start.5
  18.5 0.3 mismatch.2
  18.8 0.8 %collective-permute-start.3 = (f32[520,128]{1,0:T(8,128)S(1)}, f32[520,128]{1,0:T(8,128)S(1)}, u32[]{:S(2)}, u32[]{:S(2)}) collective-permute-start(f32[520,128]{1,0:T(8,128)S(1)} %get-tuple-element.47), channel_id=1, source_target_pairs={{3,0},{0,1},{1,2},{2,3},{7,4},{4,5},{5,6},{6,7},{11,8},{8,9},{9,10... | collective-permute-start | bytes 798728 | tf_op jit(solution)/shard_map/ppermute | solution.py:307
  19.6 1.2 %collective-permute-start.4 = (f32[520,128]{1,0:T(8,128)S(1)}, f32[520,128]{1,0:T(8,128)S(1)}, u32[]{:S(2)}, u32[]{:S(2)}) collective-permute-start(f32[520,128]{1,0:T(8,128)S(1)} %get-tuple-element.48), channel_id=1, source_target_pairs={{1,0},{2,1},{3,2},{0,3},{5,4},{6,5},{7,6},{4,7},{9,8},{10,9},{11,1... | collective-permute-start | bytes 798728 | tf_op jit(solution)/shard_map/ppermute | solution.py:307
  20.8 9.5 %collective-permute-done.5.prior = f32[520,128]{1,0:T(8,128)S(1)} collective-permute-done((f32[520,128]{1,0:T(8,128)S(1)}, f32[520,128]{1,0:T(8,128)S(1)}, u32[]{:S(2)}, u32[]{:S(2)}) %collective-permute-start.5) | collective-permute-done | bytes 266272 | tf_op jit(solution)/shard_map/ppermute | solution.py:307
  30.3 1.7 %adjoint.2 = (f32[8,72,128]{2,1,0:T(8,128)S(1)}, f32[32,128]{1,0:T(8,128)S(1)}) custom-call(bf16[72,240]{1,0:T(8,128)(2,1)S(1)} %get-tuple-element.40.matrix_ref, f32[10,72,128]{2,1,0:T(8,128)S(1)} %get-tuple-element.41.start, f32[14,72,128]{2,1,0:T(8,128)S(1)} %get-tuple-element.42.first, f32[12,72,128]{2,1,0:T(8,128)S(1)} %get-tuple-element.43.refs_2_.second, ...), custom_call_target="tpu_custom_call" | custom-call | tf_op jit(solution)/shard_map/adjoint/pallas_call | solution.py:37
  31.9 0.1 descent.1
  32.0 1.2 %collective-permute-start.8 = (f32[520,128]{1,0:T(8,128)S(1)}, f32[520,128]{1,0:T(8,128)S(1)}, u32[]{:S(2)}, u32[]{:S(2)}) collective-permute-start(f32[520,128]{1,0:T(8,128)S(1)} %get-tuple-element.52.refs_5_), channel_id=1, source_target_pairs={{4,0},{8,4},{12,8},{16,12},{20,16},{24,20},{28,24},{0,28},{5,1},{9... | collective-permute-start | bytes 798728 | tf_op jit(solution)/shard_map/ppermute | solution.py:307
  33.3 0.3 collective-permute-start.6
  33.6 1.4 %collective-permute-start.7 = (f32[260,128]{1,0:T(8,128)S(1)}, f32[260,128]{1,0:T(8,128)S(1)}, u32[]{:S(2)}, u32[]{:S(2)}) collective-permute-start(f32[260,128]{1,0:T(8,128)S(1)} %get-tuple-element.54), channel_id=1, source_target_pairs={{1,0},{2,1},{3,2},{0,3},{5,4},{6,5},{7,6},{4,7},{9,8},{10,9},{11,1... | collective-permute-start | bytes 399368 | tf_op jit(solution)/shard_map/ppermute | solution.py:307
  35.0 9.3 %all_to_all.22 = f32[32,1,128]{2,1,0:T(1,128)S(1)} all-to-all(f32[32,1,128]{2,1,0:T(1,128)S(1)} %bitcast.30), channel_id=1, replica_groups=mesh['seg'=8,'space'=4] {'seg','space'}, dimensions={0} | all-to-all | bytes 32768 | tf_op jit(solution)/shard_map/all_to_all | solution.py:371
  44.3 1.6 %forward.3 = (f32[520,128]{1,0:T(8,128)S(1)}, f32[10,72,128]{2,1,0:T(8,128)S(1)}, f32[14,72,128]{2,1,0:T(8,128)S(1)}, f32[12,72,128]{2,1,0:T(8,128)S(1)}, f32[10,72,128]{2,1,0:T(8,128)S(1)}) custom-call(bf16[72,240]{1,0:T(8,128)(2,1)S(1)} %get-tuple-element.35.refs_0_, f32[520,128]{1,0:T(8,128)S(1)} %get-tuple-element.36.refs_1_, ...), custom_call_target="tpu_custom_call" | custom-call | tf_op jit(solution)/shard_map/forward/pallas_call | solution.py:37
  45.9 0.6 collective-permute-start.11
  46.5 0.4 mismatch.3
  47.0 1.7 %collective-permute-start.10 = (f32[520,128]{1,0:T(8,128)S(1)}, f32[520,128]{1,0:T(8,128)S(1)}, u32[]{:S(2)}, u32[]{:S(2)}) collective-permute-start(f32[520,128]{1,0:T(8,128)S(1)} %get-tuple-element.62), channel_id=1, source_target_pairs={{1,0},{2,1},{3,2},{0,3},{5,4},{6,5},{7,6},{4,7},{9,8},{10,9},{11,1... | collective-permute-start | bytes 798728 | tf_op jit(solution)/shard_map/ppermute | solution.py:307
  48.7 8.1 %collective-permute-done.11.prior = f32[520,128]{1,0:T(8,128)S(1)} collective-permute-done((f32[520,128]{1,0:T(8,128)S(1)}, f32[520,128]{1,0:T(8,128)S(1)}, u32[]{:S(2)}, u32[]{:S(2)}) %collective-permute-start.11) | collective-permute-done | bytes 266272 | tf_op jit(solution)/shard_map/ppermute | solution.py:307
  56.8 2.3 %adjoint.3 = (f32[8,72,128]{2,1,0:T(8,128)S(1)}, f32[32,128]{1,0:T(8,128)}) custom-call(bf16[72,240]{1,0:T(8,128)(2,1)S(1)} %get-tuple-element.40.matrix_ref, f32[10,72,128]{2,1,0:T(8,128)S(1)} %get-tuple-element.55.start, f32[14,72,128]{2,1,0:T(8,128)S(1)} %get-tuple-element.56.first, f32[12,72,128]{2,1,0:T(8,128)S(1)} %get-tuple-element.57.refs_2_.second, ...), custom_call_target="tpu_custom_call" | custom-call | tf_op jit(solution)/shard_map/adjoint/pallas_call | solution.py:37
  59.1 2.8 %all-to-all-start.1 = ((f32[32,1,128]{2,1,0:T(1,128)}), f32[32,1,128]{2,1,0:T(1,128)S(1)}, u32[]{:S(2)}, u32[]{:S(2)}) async-start(f32[32,1,128]{2,1,0:T(1,128)} %bitcast.9), calls=%async_computation.1 | async-start | bytes 32768 | tf_op jit(solution)/shard_map/all_to_all | solution.py:371
  61.9 0.7 %mismatch_out.1 = f32[520,128]{1,0:T(8,128)} custom-call(f32[520,128]{1,0:T(8,128)S(1)} %get-tuple-element.60.mismatch.given), custom_call_target="tpu_custom_call" | custom-call | tf_op jit(solution)/shard_map/mismatch_out/pallas_call | solution.py:37
  62.6 6.3 %all-to-all-done.1 = f32[32,1,128]{2,1,0:T(1,128)S(1)} async-done(((f32[32,1,128]{2,1,0:T(1,128)}), f32[32,1,128]{2,1,0:T(1,128)S(1)}, u32[]{:S(2)}, u32[]{:S(2)}) %all-to-all-start.1) | async-done | bytes 16416 | tf_op jit(solution)/shard_map/all_to_all | solution.py:371
  68.9 0.9 %final.1 = f32[520,128]{1,0:T(8,128)} custom-call(f32[10,72,128]{2,1,0:T(8,128)S(1)} %get-tuple-element.55.start, f32[8,72,128]{2,1,0:T(8,128)S(1)} %get-tuple-element.64.descent, f32[32,128]{1,0:T(8,128)S(1)} %bitcast.31), custom_call_target="tpu_custom_call" | custom-call | tf_op jit(solution)/shard_map/final/pallas_call | solution.py:37
  (12 shorter events, 0.1 us)
Async XLA Ops:
  1.3 1.0 %copy-start = (f32[1,8,65,128]{3,1,2,0:T(8,128)S(1)}, f32[1,8,65,128]{3,1,2,0:T(8,128)}, u32[]{:S(2)}) copy-start(f32[1,8,65,128]{3,1,2,0:T(8,128)} %param.3) | copy-start | bytes 798724
  2.2 1.0 %copy-start.1 = (f32[8,65,128]{2,0,1:T(8,128)S(1)}, f32[8,65,128]{2,0,1:T(8,128)}, u32[]{:S(2)}) copy-start(f32[8,65,128]{2,0,1:T(8,128)} %param.4) | copy-start | bytes 798724
  3.9 14.6 %collective-permute-start.2 = (f32[520,128]{1,0:T(8,128)S(1)}, f32[520,128]{1,0:T(8,128)S(1)}, u32[]{:S(2)}, u32[]{:S(2)}) collective-permute-start(f32[520,128]{1,0:T(8,128)S(1)} %get-tuple-element.36.refs_1_), channel_id=1, source_target_pairs={{4,0},{8,4},{12,8},{16,12},{20,16},{24,20},{28,24},{0,28},{5,1},{9... | collective-permute-start | bytes 798728 | tf_op jit(solution)/shard_map/ppermute | solution.py:307
  9.9 6.1 %collective-permute-start = (f32[455,128]{1,0:T(8,128)S(1)}, f32[455,128]{1,0:T(8,128)S(1)}, u32[]{:S(2)}, u32[]{:S(2)}) collective-permute-start(f32[455,128]{1,0:T(8,128)S(1)} %get-tuple-element.38), channel_id=1, source_target_pairs={{3,0},{0,1},{1,2},{2,3},{7,4},{4,5},{5,6},{6,7},{11,8},{8,9},{9,10... | collective-permute-start | bytes 698888 | tf_op jit(solution)/shard_map/ppermute | solution.py:307
  9.9 7.0 %collective-permute-start.1 = (f32[455,128]{1,0:T(8,128)S(1)}, f32[455,128]{1,0:T(8,128)S(1)}, u32[]{:S(2)}, u32[]{:S(2)}) collective-permute-start(f32[455,128]{1,0:T(8,128)S(1)} %get-tuple-element.39), channel_id=1, source_target_pairs={{1,0},{2,1},{3,2},{0,3},{5,4},{6,5},{7,6},{4,7},{9,8},{10,9},{11,1... | collective-permute-start | bytes 698888 | tf_op jit(solution)/shard_map/ppermute | solution.py:307
  18.4 11.8 %collective-permute-start.5 = (f32[520,128]{1,0:T(8,128)S(1)}, f32[520,128]{1,0:T(8,128)S(1)}, u32[]{:S(2)}, u32[]{:S(2)}) collective-permute-start(f32[520,128]{1,0:T(8,128)S(1)} %get-tuple-element.45.refs_0_), channel_id=1, source_target_pairs={{28,0},{0,4},{4,8},{8,12},{12,16},{16,20},{20,24},{24,28},{29,1},{... | collective-permute-start | bytes 798728 | tf_op jit(solution)/shard_map/ppermute | solution.py:307
  18.8 11.5 %collective-permute-start.3 = (f32[520,128]{1,0:T(8,128)S(1)}, f32[520,128]{1,0:T(8,128)S(1)}, u32[]{:S(2)}, u32[]{:S(2)}) collective-permute-start(f32[520,128]{1,0:T(8,128)S(1)} %get-tuple-element.47), channel_id=1, source_target_pairs={{3,0},{0,1},{1,2},{2,3},{7,4},{4,5},{5,6},{6,7},{11,8},{8,9},{9,10... | collective-permute-start | bytes 798728 | tf_op jit(solution)/shard_map/ppermute | solution.py:307
  19.6 10.7 %collective-permute-start.4 = (f32[520,128]{1,0:T(8,128)S(1)}, f32[520,128]{1,0:T(8,128)S(1)}, u32[]{:S(2)}, u32[]{:S(2)}) collective-permute-start(f32[520,128]{1,0:T(8,128)S(1)} %get-tuple-element.48), channel_id=1, source_target_pairs={{1,0},{2,1},{3,2},{0,3},{5,4},{6,5},{7,6},{4,7},{9,8},{10,9},{11,1... | collective-permute-start | bytes 798728 | tf_op jit(solution)/shard_map/ppermute | solution.py:307
  32.0 14.5 %collective-permute-start.8 = (f32[520,128]{1,0:T(8,128)S(1)}, f32[520,128]{1,0:T(8,128)S(1)}, u32[]{:S(2)}, u32[]{:S(2)}) collective-permute-start(f32[520,128]{1,0:T(8,128)S(1)} %get-tuple-element.52.refs_5_), channel_id=1, source_target_pairs={{4,0},{8,4},{12,8},{16,12},{20,16},{24,20},{28,24},{0,28},{5,1},{9... | collective-permute-start | bytes 798728 | tf_op jit(solution)/shard_map/ppermute | solution.py:307
  33.3 11.0 %collective-permute-start.6 = (f32[260,128]{1,0:T(8,128)S(1)}, f32[260,128]{1,0:T(8,128)S(1)}, u32[]{:S(2)}, u32[]{:S(2)}) collective-permute-start(f32[260,128]{1,0:T(8,128)S(1)} %get-tuple-element.53), channel_id=1, source_target_pairs={{3,0},{0,1},{1,2},{2,3},{7,4},{4,5},{5,6},{6,7},{11,8},{8,9},{9,10... | collective-permute-start | bytes 399368 | tf_op jit(solution)/shard_map/ppermute | solution.py:307
  33.6 10.7 %collective-permute-start.7 = (f32[260,128]{1,0:T(8,128)S(1)}, f32[260,128]{1,0:T(8,128)S(1)}, u32[]{:S(2)}, u32[]{:S(2)}) collective-permute-start(f32[260,128]{1,0:T(8,128)S(1)} %get-tuple-element.54), channel_id=1, source_target_pairs={{1,0},{2,1},{3,2},{0,3},{5,4},{6,5},{7,6},{4,7},{9,8},{10,9},{11,1... | collective-permute-start | bytes 399368 | tf_op jit(solution)/shard_map/ppermute | solution.py:307
  45.9 10.9 %collective-permute-start.11 = (f32[520,128]{1,0:T(8,128)S(1)}, f32[520,128]{1,0:T(8,128)S(1)}, u32[]{:S(2)}, u32[]{:S(2)}) collective-permute-start(f32[520,128]{1,0:T(8,128)S(1)} %get-tuple-element.59.refs_0_), channel_id=1, source_target_pairs={{28,0},{0,4},{4,8},{8,12},{12,16},{16,20},{20,24},{24,28},{29,1},{... | collective-permute-start | bytes 798728 | tf_op jit(solution)/shard_map/ppermute | solution.py:307
  46.9 9.9 %collective-permute-start.9 = (f32[520,128]{1,0:T(8,128)S(1)}, f32[520,128]{1,0:T(8,128)S(1)}, u32[]{:S(2)}, u32[]{:S(2)}) collective-permute-start(f32[520,128]{1,0:T(8,128)S(1)} %get-tuple-element.61), channel_id=1, source_target_pairs={{3,0},{0,1},{1,2},{2,3},{7,4},{4,5},{5,6},{6,7},{11,8},{8,9},{9,10... | collective-permute-start | bytes 798728 | tf_op jit(solution)/shard_map/ppermute | solution.py:307
  47.0 9.9 %collective-permute-start.10 = (f32[520,128]{1,0:T(8,128)S(1)}, f32[520,128]{1,0:T(8,128)S(1)}, u32[]{:S(2)}, u32[]{:S(2)}) collective-permute-start(f32[520,128]{1,0:T(8,128)S(1)} %get-tuple-element.62), channel_id=1, source_target_pairs={{1,0},{2,1},{3,2},{0,3},{5,4},{6,5},{7,6},{4,7},{9,8},{10,9},{11,1... | collective-permute-start | bytes 798728 | tf_op jit(solution)/shard_map/ppermute | solution.py:307
  59.1 9.9 %all-to-all-start.1 = ((f32[32,1,128]{2,1,0:T(1,128)}), f32[32,1,128]{2,1,0:T(1,128)S(1)}, u32[]{:S(2)}, u32[]{:S(2)}) async-start(f32[32,1,128]{2,1,0:T(1,128)} %bitcast.9), calls=%async_computation.1 | async-start | bytes 32768 | tf_op jit(solution)/shard_map/all_to_all | solution.py:371

commit v4 on v2

--- a/solution.py
+++ b/solution.py
@@ -16,6 +16,7 @@
 BOTH = ("seg", "space")
 VMEM = pl.BlockSpec(memory_space=pltpu.VMEM)
 LANES = 128
+PARTS = 4
 
 
 def padded(count, step):
@@ -33,14 +34,18 @@
     ref[pl.ds(i, points, stride=planes), :] = plane[:points]
 
 
-def call(kernel, name, outs, operands, scratch=()):
+WORK = {"forward": 4e9, "inverse": 1e9}
+
+
+def call(kernel, name, outs, operands, scratch=(), specs=None, fast=False):
     return pl.pallas_call(
         kernel,
         name=name,
         out_shape=[jax.ShapeDtypeStruct(shape, dtype) for shape, dtype in outs],
-        in_specs=[VMEM] * len(operands),
+        in_specs=specs or [VMEM] * len(operands),
         out_specs=[VMEM] * len(outs),
         scratch_shapes=list(scratch),
+        cost_estimate=pl.CostEstimate(flops=int(WORK[name]), transcendentals=0, bytes_accessed=1 << 20) if name in WORK and not fast else None,
         compiler_params=pltpu.CompilerParams(vmem_limit_bytes=32 * 1024 * 1024),
     )(*operands)
 
@@ -48,7 +53,10 @@
 def inverse_kernel(points, rows, k_ref, forward_ref, backward_ref, square):
     row = lax.broadcasted_iota(jnp.int32, (LANES, LANES), 0)
     lane = lax.broadcasted_iota(jnp.int32, (LANES, LANES), 1)
-    k = k_ref[...]
+    square[0:1, :] = jnp.zeros((1, LANES), jnp.float32)
+    square[0:1, :points] = k_ref[...]
+    k = jnp.sum(jnp.where(row == lane, square[0:1, :], 0.0), axis=1, keepdims=True)
+    k = jnp.broadcast_to(k, (LANES, LANES))
     zero = jnp.zeros_like(k)
     a = jnp.where((row >= 1) & (row < points), -k, zero)
     c = jnp.where(row < points - 1, -k, zero)
@@ -103,14 +111,33 @@
     return 0.5 * residual / (squares + EPSILON)
 
 
-def pack_kernel(nx, states, forcing, to_left, to_right):
-    h = STEPS
+def parts(ref):
+    size = padded(-(-ref.shape[0] // PARTS), 8)
+    return [pl.ds(at, min(size, ref.shape[0] - at)) for at in range(0, ref.shape[0], size)]
+
+
+def pack_kernel(nx, states_hbm, forcing_hbm, to_left, to_right, states, forcing, sems):
+    h = STEPS
+    copies = [
+        [pltpu.make_async_copy(source.at[rows], target.at[rows], sems.at[k, j]) for j, rows in enumerate(parts(source))]
+        for k, (source, target) in enumerate(((states_hbm, states), (forcing_hbm, forcing)))
+    ]
+    for copy in copies[0] + copies[1]:
+        copy.start()
+    for copy in copies[0]:
+        copy.wait()
     for i in range(h):
         store(to_left, i, 2 * h - 1, load(states, i, nx))
         store(to_right, i, 2 * h - 1, load(states, nx - h + i, nx))
+    for copy in copies[1]:
+        copy.wait()
     for i in range(h - 1):
         store(to_left, h + i, 2 * h - 1, load(forcing, i, nx))
         store(to_right, h + i, 2 * h - 1, load(forcing, nx - h + 1 + i, nx))
+
+
+def copy_kernel(given, out):
+    out[...] = given[...]
 
 
 def wall_profile(points, rows):
@@ -128,8 +155,7 @@
         descent, d_left, d_right, sums = refs[:4]
         del refs[:4]
         tau = step_size(sums[...])
-    ending_ref, start_ref, first_ref, second_ref, third_ref = refs[:5]
-    moved_ref = refs[5] if updated else None
+    ending_ref, start_ref, first_ref, second_ref, third_ref, low_ref, high_ref = refs[:7]
     u0, q = refs[-2:]
     points = states.shape[0] // nx
     rows = padded(points, 8)
@@ -149,7 +175,6 @@
         here = load(states, i, nx)
         if updated:
             here = here - tau * load(descent, i, nx)
-            store(moved_ref, i, nx, here)
         u0[h + i] = here
         start_ref[1 + i] = here
     for i in range(h - 1):
@@ -179,6 +204,11 @@
                     else:
                         store(ending_ref, at, nx, plane)
                 pending = []
+    for i in range(h - 1):
+        store(low_ref, i, h, third_ref[1 + 1 + i])
+        store(high_ref, i, h, third_ref[1 + nx - h + i])
+    store(low_ref, h - 1, h, second_ref[2 + 2])
+    store(high_ref, h - 1, h, second_ref[2 + nx - 3])
 
 
 def halve(total):
@@ -189,8 +219,8 @@
 def mismatch_kernel(nx, updated, *refs):
     h = STEPS
     refs = list(refs)
-    ending, after, second, third = refs[:4]
-    del refs[:4]
+    ending, after = refs[:2]
+    del refs[:2]
     if updated:
         d_after, sums = refs[:2]
         del refs[:2]
@@ -204,19 +234,14 @@
         value = load(ending, i, nx) - value
         store(mismatch_ref, i, nx, value)
         if i < h:
-            store(low_ref, i, 2 * h, value)
+            store(low_ref, i, h, value)
         if i >= nx - h:
-            store(high_ref, i - (nx - h), 2 * h, value)
+            store(high_ref, i - (nx - h), h, value)
         total = value * value if total is None else total + value * value
     squares_ref[...] = halve(total)
-    for i in range(h - 1):
-        store(low_ref, h + i, 2 * h, third[1 + 1 + i])
-        store(high_ref, h + i, 2 * h, third[1 + nx - h + i])
-    store(low_ref, 2 * h - 1, 2 * h, second[2 + 2])
-    store(high_ref, 2 * h - 1, 2 * h, second[2 + nx - 3])
-
-
-def adjoint_kernel(nx, matrix_ref, start, first, second, third, mismatch, from_left, from_right, lam_ref, a, b):
+
+
+def adjoint_kernel(nx, matrix_ref, start, first, second, third, mismatch, left_fields, right_fields, left, right, lam_ref, a, b):
     h = STEPS
     points = mismatch.shape[0] // nx
     base = wall_profile(points, padded(points, 8))
@@ -229,21 +254,21 @@
             return first[i + 3]
         if t == 2:
             if i == -3:
-                return load(from_left, 2 * h - 1, 2 * h)
+                return load(left_fields, h - 1, h)
             if i == nx + 2:
-                return load(from_right, 2 * h - 1, 2 * h)
+                return load(right_fields, h - 1, h)
             return second[i + 2]
         if i < -1:
-            return load(from_left, h + i + 4, 2 * h)
+            return load(left_fields, i + h, h)
         if i > nx:
-            return load(from_right, h + i - nx - 1, 2 * h)
+            return load(right_fields, i - nx - 1, h)
         return third[i + 1]
 
     def weight(i):
         if i < 0:
-            return load(from_left, h + i, 2 * h)
+            return load(left, h + i, h)
         if i >= nx:
-            return load(from_right, i - nx, 2 * h)
+            return load(right, i - nx, h)
         return load(mismatch, i, nx)
 
     for t in reversed(range(h)):
@@ -265,32 +290,29 @@
                     else:
                         target[i - 1 + h] = value
 
-
-def sums_kernel(nx, devices, lam, prior, states, squares, sums_ref):
+def descent_kernel(nx, devices, sent, lam, prior, start, squares, *refs):
+    sums_ref, descent_ref, *edges = refs if sent else refs[1:]
+    h = STEPS
     total = None
     for i in range(nx):
-        value = lam[i] - (load(prior, i, nx) - load(states, i, nx))
+        value = lam[i] - (load(prior, i, nx) - start[i + 1])
+        if sent:
+            store(descent_ref, i, nx, value)
+            if i < h:
+                store(edges[0], i, h, value)
+            if i >= nx - h:
+                store(edges[1], i - (nx - h), h, value)
+        else:
+            descent_ref[i] = value
         total = value * value if total is None else total + value * value
     lane = lax.broadcasted_iota(jnp.int32, (1, LANES), 1)
     sums_ref[...] = jnp.broadcast_to(jnp.where(lane < LANES // 2, squares[...], halve(total)), (devices, LANES))
 
 
-def descent_kernel(nx, lam, prior, states, descent_ref, low_ref, high_ref):
-    h = STEPS
-    for i in range(nx):
-        value = lam[i] - (load(prior, i, nx) - load(states, i, nx))
-        store(descent_ref, i, nx, value)
-        if i < h:
-            store(low_ref, i, h, value)
-        if i >= nx - h:
-            store(high_ref, i - (nx - h), h, value)
-
-
-def final_kernel(nx, lam, prior, states, sums, out_ref):
+def final_kernel(nx, start, descent, sums, out_ref):
     tau = step_size(sums[...])
     for i in range(nx):
-        here = load(states, i, nx)
-        store(out_ref, i, nx, here - tau * (lam[i] - (load(prior, i, nx) - here)))
+        store(out_ref, i, nx, start[i + 1] - tau * descent[i])
 
 
 def shift(block, axis, distance):
@@ -314,64 +336,71 @@
 
     states = jnp.transpose(states[0], (1, 0, 2)).reshape(nx * points, LANES)
     forcing = jnp.transpose(forcing, (1, 0, 2)).reshape(nx * points, LANES)
-    to_left, to_right = call(
-        functools.partial(pack_kernel, nx), "pack", [flat(2 * h - 1)] * 2, [states, forcing]
+    to_left, to_right, states, forcing = call(
+        functools.partial(pack_kernel, nx),
+        "pack",
+        [flat(2 * h - 1)] * 2 + [flat(nx)] * 2,
+        [pltpu.with_memory_space_constraint(v, pltpu.HBM) for v in (states, forcing)],
+        [pltpu.SemaphoreType.DMA((2, PARTS))],
+        [pl.BlockSpec(memory_space=pltpu.HBM)] * 2,
     )
     left = shift(to_right, "space", 1)
     right = shift(to_left, "space", -1)
     after = shift(states, "seg", -1)
-    k = jnp.broadcast_to(jnp.pad(wall_viscosity, (0, LANES - points))[:, None], (LANES, LANES))
     forward, backward = call(
         functools.partial(inverse_kernel, points, rows),
         "inverse",
         [((rows, depth), bf16)] * 2,
-        [k],
+        [wall_viscosity.reshape(1, points)],
         [pltpu.VMEM((LANES, LANES), f32)],
     )
-    current = states
     moved = d_after = sums = None
     for iteration in range(ITERS):
         updated = iteration > 0
-        ending, start, first, second, third, *now = call(
+        ending, start, first, second, third, low, high = call(
             functools.partial(forward_kernel, nx, updated),
             "forward",
-            [flat(nx), tiles(nx + 2), tiles(nx + 6), tiles(nx + 4), tiles(nx + 2)] + [flat(nx)] * updated,
+            [flat(nx), tiles(nx + 2), tiles(nx + 6), tiles(nx + 4), tiles(nx + 2), flat(h), flat(h)],
             [forward, states, forcing, left, right] + (moved + [sums] if updated else []),
             [pltpu.VMEM((nx + 2 * h, rows, LANES), f32), pltpu.VMEM((nx + 2 * h - 2, rows, LANES), f32)],
+            fast=updated,
         )
-        current = now[0] if updated else states
         prior = shift(ending, "seg", 1)
+        sides = [shift(high, "space", 1), shift(low, "space", -1)]
         mismatch, low, high, squares = call(
             functools.partial(mismatch_kernel, nx, updated),
             "mismatch",
-            [flat(nx), flat(2 * h), flat(2 * h), ((1, LANES), f32)],
-            [ending, after, second, third] + ([d_after, sums] if updated else []),
+            [flat(nx), flat(h), flat(h), ((1, LANES), f32)],
+            [ending, after] + ([d_after, sums] if updated else []),
         )
-        from_left = shift(high, "space", 1)
-        from_right = shift(low, "space", -1)
+        sides += [shift(high, "space", 1), shift(low, "space", -1)]
         lam = call(
             functools.partial(adjoint_kernel, nx),
             "adjoint",
             [tiles(nx)],
-            [backward, start, first, second, third, mismatch, from_left, from_right],
+            [backward, start, first, second, third, mismatch] + sides,
             [pltpu.VMEM((nx + 2 * h, rows, LANES), f32)] * 2,
         )[0]
-        rows_of_sums = call(
-            functools.partial(sums_kernel, nx, devices), "sums", [((devices, LANES), f32)], [lam, prior, current, squares]
-        )[0]
-        sums = lax.all_to_all(rows_of_sums, BOTH, 0, 0, tiled=True)
-        if iteration < ITERS - 1:
-            descent, d_low, d_high = call(
-                functools.partial(descent_kernel, nx), "descent", [flat(nx), flat(h), flat(h)], [lam, prior, current]
-            )
-            moved = [descent, shift(d_high, "space", 1), shift(d_low, "space", -1)]
+        sent = iteration < ITERS - 1
+        if not sent:
+            kept = call(copy_kernel, "kept", [flat(nx)], [mismatch])[0]
+        sums, descent, *edges = call(
+            functools.partial(descent_kernel, nx, devices, sent),
+            "descent",
+            [((devices, LANES), f32)] + ([flat(nx), flat(h), flat(h)] if sent else [tiles(nx)]),
+            [lam, prior, start, squares] + ([] if sent else [kept]),
+            specs=[VMEM] * 4 + ([] if sent else [pl.BlockSpec(memory_space=pl.ANY)]),
+        )
+        sums = lax.all_to_all(sums, BOTH, 0, 0, tiled=True)
+        if sent:
+            moved = [descent, shift(edges[1], "space", 1), shift(edges[0], "space", -1)]
             d_after = shift(descent, "seg", -1)
-    new = call(functools.partial(final_kernel, nx), "final", [flat(nx)], [lam, prior, current, sums])[0]
+    new = call(functools.partial(final_kernel, nx), "final", [flat(nx)], [start, descent, sums])[0]
 
     def placed(block):
         return jnp.transpose(block.reshape(points, nx, LANES), (1, 0, 2))[None]
 
-    return (placed(new), placed(mismatch))
+    return (placed(new), placed(kept))
 
 
 def solution(mesh):

time: 66.8 us -> 63.8 us (0.955)
  waiting for transfers between devices: 20.8 us -> 9.26 us
  starting transfers between devices: 14 us -> 22.7 us
  local copies, waits for them, and re-layouts: 2.98 us -> 0.01 us
  blocking collectives: 18.5 us -> 20.4 us
  Pallas kernels: 9.51 us -> 10.6 us
    ppermute x12 -> x16, waiting for transfers between devices: 20.8 us -> 9.26 us  [shift(): lax.ppermute(block, axis, [((i - distance) % devices, i) for i in range(d...]
    ppermute x12 -> x16, starting transfers between devices: 14 us -> 22.7 us  [shift(): lax.ppermute(block, axis, [((i - distance) % devices, i) for i in range(d...]
    unnamed x12 -> x4, local copies, waits for them, and re-layouts: 2.9 us -> 0.01 us
    all_to_all x2, blocking collectives: 18.5 us -> 20.4 us  [per_device(): sums = lax.all_to_all(sums, BOTH, 0, 0, tiled=True)]
    pallas_call x12, Pallas kernels: 9.51 us -> 10.6 us  [call(): pl.pallas_call(kernel, name=name, out_shape=[jax.ShapeDtypeStruct(shape,...]
  transfers between devices with their start and end apart: 12 -> 16, of which waited for: 7 -> 9; matrix products, arithmetic and copies ran while one was open for 0% -> 0% of each run, Pallas kernels for 11% -> 13%
where the time goes in v4:
time: 63.8 us; the launch traced here: 63.6 us
  starting transfers between devices  22.7 us (36%)
  blocking collectives  20.4 us (32%)
  Pallas kernels  10.6 us (17%)
  waiting for transfers between devices  9.26 us (15%)
  between operations  0.69 us (1%)
    ppermute x16, starting transfers between devices, shift(): lax.ppermute(block, axis, [((i - distance) % devices, i) for i in range(d...  22.7 us
    all_to_all x2, blocking collectives, per_device(): sums = lax.all_to_all(sums, BOTH, 0, 0, tiled=True)  20.4 us
    pallas_call x12, Pallas kernels, call(): pl.pallas_call(kernel, name=name, out_shape=[jax.ShapeDtypeStruct(shape,...  10.6 us
    ppermute x16, waiting for transfers between devices, shift(): lax.ppermute(block, axis, [((i - distance) % devices, i) for i in range(d...  9.26 us
  transfers between devices with their start and end apart: 16, of which 9 were waited for; matrix products, arithmetic and copies ran while one was open for 0% of the time, Pallas kernels for 13%

profile of v4, /device:TPU:0, one launch (start us, length us, event | category | flops | bytes accessed | tf_op | source)
XLA Modules:
  0.0 63.6 jit_solution(16488117304752105468)
XLA Ops:
  0.6 1.2 %pack.1 = (f32[455,128]{1,0:T(8,128)S(1)}, f32[455,128]{1,0:T(8,128)S(1)}, f32[520,128]{1,0:T(8,128)S(1)}, f32[520,128]{1,0:T(8,128)S(1)}) custom-call(f32[520,128]{1,0:T(8,128)} %bitcast.34, f32[520,128]{1,0:T(8,128)} %bitcast.35), custom_call_target="tpu_custom_call" | custom-call | tf_op jit(solution)/shard_map/pack/pallas_call | solution.py:41
  1.8 0.5 collective-permute-start
  2.3 2.0 %collective-permute-start.1 = (f32[455,128]{1,0:T(8,128)S(1)}, f32[455,128]{1,0:T(8,128)S(1)}, u32[]{:S(2)}, u32[]{:S(2)}) collective-permute-start(f32[455,128]{1,0:T(8,128)S(1)} %get-tuple-element.40), channel_id=1, source_target_pairs={{1,0},{2,1},{3,2},{0,3},{5,4},{6,5},{7,6},{4,7},{9,8},{10,9},{11,1... | collective-permute-start | bytes 698888 | tf_op jit(solution)/shard_map/ppermute | solution.py:320
  4.4 5.3 %collective-permute-start.2 = (f32[520,128]{1,0:T(8,128)S(1)}, f32[520,128]{1,0:T(8,128)S(1)}, u32[]{:S(2)}, u32[]{:S(2)}) collective-permute-start(f32[520,128]{1,0:T(8,128)S(1)} %get-tuple-element.37.refs_1_), channel_id=1, source_target_pairs={{4,0},{8,4},{12,8},{16,12},{20,16},{24,20},{28,24},{0,28},{5,1},{9... | collective-permute-start | bytes 798728 | tf_op jit(solution)/shard_map/ppermute | solution.py:320
  9.6 0.5 inverse.1
  10.4 1.5 %forward.2 = (f32[520,128]{1,0:T(8,128)S(1)}, f32[10,72,128]{2,1,0:T(8,128)S(1)}, f32[14,72,128]{2,1,0:T(8,128)S(1)}, f32[12,72,128]{2,1,0:T(8,128)S(1)}, f32[10...) custom-call(bf16[72,240]{1,0:T(8,128)(2,1)S(1)} %get-tuple-element.36.refs_0_, ...), custom_call_target="tpu_custom_call" | custom-call | flops 4000000000 | bytes 1048576 | tf_op jit(solution)/shard_map/forward/pallas_call | solution.py:41
  11.8 1.5 %collective-permute-start.7 = (f32[520,128]{1,0:T(8,128)S(1)}, f32[520,128]{1,0:T(8,128)S(1)}, u32[]{:S(2)}, u32[]{:S(2)}) collective-permute-start(f32[520,128]{1,0:T(8,128)S(1)} %get-tuple-element.46.refs_0_), channel_id=1, source_target_pairs={{28,0},{0,4},{4,8},{8,12},{12,16},{16,20},{20,24},{24,28},{29,1},{... | collective-permute-start | bytes 798728 | tf_op jit(solution)/shard_map/ppermute | solution.py:320
  13.4 0.8 %collective-permute-start.3 = (f32[260,128]{1,0:T(8,128)S(1)}, f32[260,128]{1,0:T(8,128)S(1)}, u32[]{:S(2)}, u32[]{:S(2)}) collective-permute-start(f32[260,128]{1,0:T(8,128)S(1)} %get-tuple-element.48), channel_id=1, source_target_pairs={{3,0},{0,1},{1,2},{2,3},{7,4},{4,5},{5,6},{6,7},{11,8},{8,9},{9,10... | collective-permute-start | bytes 399368 | tf_op jit(solution)/shard_map/ppermute | solution.py:320
  14.2 1.1 %collective-permute-start.4 = (f32[260,128]{1,0:T(8,128)S(1)}, f32[260,128]{1,0:T(8,128)S(1)}, u32[]{:S(2)}, u32[]{:S(2)}) collective-permute-start(f32[260,128]{1,0:T(8,128)S(1)} %get-tuple-element.49), channel_id=1, source_target_pairs={{1,0},{2,1},{3,2},{0,3},{5,4},{6,5},{7,6},{4,7},{9,8},{10,9},{11,1... | collective-permute-start | bytes 399368 | tf_op jit(solution)/shard_map/ppermute | solution.py:320
  15.3 0.2 mismatch.2
  15.6 1.8 %collective-permute-start.6 = (f32[260,128]{1,0:T(8,128)S(1)}, f32[260,128]{1,0:T(8,128)S(1)}, u32[]{:S(2)}, u32[]{:S(2)}) collective-permute-start(f32[260,128]{1,0:T(8,128)S(1)} %get-tuple-element.51), channel_id=1, source_target_pairs={{1,0},{2,1},{3,2},{0,3},{5,4},{6,5},{7,6},{4,7},{9,8},{10,9},{11,1... | collective-permute-start | bytes 399368 | tf_op jit(solution)/shard_map/ppermute | solution.py:320
  17.3 0.7 %collective-permute-done.3.left_fields = f32[260,128]{1,0:T(8,128)S(1)} collective-permute-done((f32[260,128]{1,0:T(8,128)S(1)}, f32[260,128]{1,0:T(8,128)S(1)}, u32[]{:S(2)}, u32[]{:S(2)}) %collective-permute-start.3) | collective-permute-done | bytes 133152 | tf_op jit(solution)/shard_map/ppermute | solution.py:320
  18.0 1.3 %collective-permute-done.4.right_fields = f32[260,128]{1,0:T(8,128)S(1)} collective-permute-done((f32[260,128]{1,0:T(8,128)S(1)}, f32[260,128]{1,0:T(8,128)S(1)}, u32[]{:S(2)}, u32[]{:S(2)}) %collective-permute-start.4) | collective-permute-done | bytes 133152 | tf_op jit(solution)/shard_map/ppermute | solution.py:320
  19.3 2.2 %collective-permute-done.5.left = f32[260,128]{1,0:T(8,128)S(1)} collective-permute-done((f32[260,128]{1,0:T(8,128)S(1)}, f32[260,128]{1,0:T(8,128)S(1)}, u32[]{:S(2)}, u32[]{:S(2)}) %collective-permute-start.5) | collective-permute-done | bytes 133152 | tf_op jit(solution)/shard_map/ppermute | solution.py:320
  21.5 1.6 %adjoint.2.lam = f32[8,72,128]{2,1,0:T(8,128)S(1)} custom-call(bf16[72,240]{1,0:T(8,128)(2,1)S(1)} %get-tuple-element.41.matrix_ref, f32[10,72,128]{2,1,0:T(8,128)S(1)} %get-tuple-element.42.start, f32[14,72,128]{2,1,0:T(8,128)S(1)} %get-tuple-element.43.first, f32[12,72,128]{2,1,0:T(8,128)S(1)} %get-tuple-element.44.second, ...), custom_call_target="tpu_custom_call" | custom-call | tf_op jit(solution)/shard_map/adjoint/pallas_call | solution.py:41
  23.0 0.8 %collective-permute-done.7.prior = f32[520,128]{1,0:T(8,128)S(1)} collective-permute-done((f32[520,128]{1,0:T(8,128)S(1)}, f32[520,128]{1,0:T(8,128)S(1)}, u32[]{:S(2)}, u32[]{:S(2)}) %collective-permute-start.7) | collective-permute-done | bytes 266272 | tf_op jit(solution)/shard_map/ppermute | solution.py:320
  24.0 3.8 %collective-permute-start.10 = (f32[520,128]{1,0:T(8,128)S(1)}, f32[520,128]{1,0:T(8,128)S(1)}, u32[]{:S(2)}, u32[]{:S(2)}) collective-permute-start(f32[520,128]{1,0:T(8,128)S(1)} %get-tuple-element.53.refs_5_), channel_id=1, source_target_pairs={{4,0},{8,4},{12,8},{16,12},{20,16},{24,20},{28,24},{0,28},{5,1},{9... | collective-permute-start | bytes 798728 | tf_op jit(solution)/shard_map/ppermute | solution.py:320
  28.1 1.5 %collective-permute-start.9 = (f32[260,128]{1,0:T(8,128)S(1)}, f32[260,128]{1,0:T(8,128)S(1)}, u32[]{:S(2)}, u32[]{:S(2)}) collective-permute-start(f32[260,128]{1,0:T(8,128)S(1)} %get-tuple-element.55), channel_id=1, source_target_pairs={{1,0},{2,1},{3,2},{0,3},{5,4},{6,5},{7,6},{4,7},{9,8},{10,9},{11,1... | collective-permute-start | bytes 399368 | tf_op jit(solution)/shard_map/ppermute | solution.py:320
  29.6 9.1 %all_to_all.22 = f32[32,1,128]{2,1,0:T(1,128)S(1)} all-to-all(f32[32,1,128]{2,1,0:T(1,128)S(1)} %bitcast.31), channel_id=1, replica_groups=mesh['seg'=8,'space'=4] {'seg','space'}, dimensions={0} | all-to-all | bytes 32768 | tf_op jit(solution)/shard_map/all_to_all | solution.py:394
  38.7 1.6 %forward.3 = (f32[520,128]{1,0:T(8,128)S(1)}, f32[10,72,128]{2,1,0:T(8,128)S(1)}, f32[14,72,128]{2,1,0:T(8,128)S(1)}, f32[12,72,128]{2,1,0:T(8,128)S(1)}, f32[10...) custom-call(bf16[72,240]{1,0:T(8,128)(2,1)S(1)} %get-tuple-element.36.refs_0_, ...), custom_call_target="tpu_custom_call" | custom-call | tf_op jit(solution)/shard_map/forward/pallas_call | solution.py:41
  40.3 0.6 collective-permute-start.15
  41.0 1.7 %collective-permute-start.12 = (f32[260,128]{1,0:T(8,128)S(1)}, f32[260,128]{1,0:T(8,128)S(1)}, u32[]{:S(2)}, u32[]{:S(2)}) collective-permute-start(f32[260,128]{1,0:T(8,128)S(1)} %get-tuple-element.64), channel_id=1, source_target_pairs={{1,0},{2,1},{3,2},{0,3},{5,4},{6,5},{7,6},{4,7},{9,8},{10,9},{11,1... | collective-permute-start | bytes 399368 | tf_op jit(solution)/shard_map/ppermute | solution.py:320
  42.7 0.4 mismatch.3
  43.1 1.8 %collective-permute-start.14 = (f32[260,128]{1,0:T(8,128)S(1)}, f32[260,128]{1,0:T(8,128)S(1)}, u32[]{:S(2)}, u32[]{:S(2)}) collective-permute-start(f32[260,128]{1,0:T(8,128)S(1)} %get-tuple-element.66), channel_id=1, source_target_pairs={{1,0},{2,1},{3,2},{0,3},{5,4},{6,5},{7,6},{4,7},{9,8},{10,9},{11,1... | collective-permute-start | bytes 399368 | tf_op jit(solution)/shard_map/ppermute | solution.py:320
  44.8 0.7 %kept.1.refs_0_ = f32[520,128]{1,0:T(8,128)} custom-call(f32[520,128]{1,0:T(8,128)S(1)} %get-tuple-element.62.mismatch.given), custom_call_target="tpu_custom_call" | custom-call | tf_op jit(solution)/shard_map/kept/pallas_call | solution.py:41
  45.6 0.4 collective-permute-done.11.left_fields
  46.0 0.4 collective-permute-done.12.right_fields
  46.4 2.6 %collective-permute-done.13.left = f32[260,128]{1,0:T(8,128)S(1)} collective-permute-done((f32[260,128]{1,0:T(8,128)S(1)}, f32[260,128]{1,0:T(8,128)S(1)}, u32[]{:S(2)}, u32[]{:S(2)}) %collective-permute-start.13) | collective-permute-done | bytes 133152 | tf_op jit(solution)/shard_map/ppermute | solution.py:320
  49.0 1.6 %adjoint.3.lam = f32[8,72,128]{2,1,0:T(8,128)S(1)} custom-call(bf16[72,240]{1,0:T(8,128)(2,1)S(1)} %get-tuple-element.41.matrix_ref, f32[10,72,128]{2,1,0:T(8,128)S(1)} %get-tuple-element.57.start, f32[14,72,128]{2,1,0:T(8,128)S(1)} %get-tuple-element.58.first, f32[12,72,128]{2,1,0:T(8,128)S(1)} %get-tuple-element.59.second, ...), custom_call_target="tpu_custom_call" | custom-call | tf_op jit(solution)/shard_map/adjoint/pallas_call | solution.py:41
  50.6 0.7 %collective-permute-done.15.prior = f32[520,128]{1,0:T(8,128)S(1)} collective-permute-done((f32[520,128]{1,0:T(8,128)S(1)}, f32[520,128]{1,0:T(8,128)S(1)}, u32[]{:S(2)}, u32[]{:S(2)}) %collective-permute-start.15) | collective-permute-done | bytes 266272 | tf_op jit(solution)/shard_map/ppermute | solution.py:320
  51.4 11.3 %all_to_all.23 = f32[32,1,128]{2,1,0:T(1,128)S(1)} all-to-all(f32[32,1,128]{2,1,0:T(1,128)S(1)} %bitcast.32), channel_id=1, replica_groups=mesh['seg'=8,'space'=4] {'seg','space'}, dimensions={0} | all-to-all | bytes 32768 | tf_op jit(solution)/shard_map/all_to_all | solution.py:394
  62.7 0.9 %final.1 = f32[520,128]{1,0:T(8,128)} custom-call(f32[10,72,128]{2,1,0:T(8,128)S(1)} %get-tuple-element.57.start, f32[8,72,128]{2,1,0:T(8,128)S(1)} %get-tuple-element.68.descent, f32[32,128]{1,0:T(8,128)S(1)} %bitcast.30), custom_call_target="tpu_custom_call" | custom-call | tf_op jit(solution)/shard_map/final/pallas_call | solution.py:41
  (18 shorter events, 0.9 us)
Async XLA Ops:
  1.8 8.3 %collective-permute-start = (f32[455,128]{1,0:T(8,128)S(1)}, f32[455,128]{1,0:T(8,128)S(1)}, u32[]{:S(2)}, u32[]{:S(2)}) collective-permute-start(f32[455,128]{1,0:T(8,128)S(1)} %get-tuple-element.39), channel_id=1, source_target_pairs={{3,0},{0,1},{1,2},{2,3},{7,4},{4,5},{5,6},{6,7},{11,8},{8,9},{9,10... | collective-permute-start | bytes 698888 | tf_op jit(solution)/shard_map/ppermute | solution.py:320
  2.3 8.0 %collective-permute-start.1 = (f32[455,128]{1,0:T(8,128)S(1)}, f32[455,128]{1,0:T(8,128)S(1)}, u32[]{:S(2)}, u32[]{:S(2)}) collective-permute-start(f32[455,128]{1,0:T(8,128)S(1)} %get-tuple-element.40), channel_id=1, source_target_pairs={{1,0},{2,1},{3,2},{0,3},{5,4},{6,5},{7,6},{4,7},{9,8},{10,9},{11,1... | collective-permute-start | bytes 698888 | tf_op jit(solution)/shard_map/ppermute | solution.py:320
  4.4 5.3 %copy-start.1 = (f32[65]{0:T(128)S(1)}, f32[65]{0:T(128)}, u32[]{:S(2)}) copy-start(f32[65]{0:T(128)} %param.5) | copy-start | bytes 784
  4.4 11.0 %collective-permute-start.2 = (f32[520,128]{1,0:T(8,128)S(1)}, f32[520,128]{1,0:T(8,128)S(1)}, u32[]{:S(2)}, u32[]{:S(2)}) collective-permute-start(f32[520,128]{1,0:T(8,128)S(1)} %get-tuple-element.37.refs_1_), channel_id=1, source_target_pairs={{4,0},{8,4},{12,8},{16,12},{20,16},{24,20},{28,24},{0,28},{5,1},{9... | collective-permute-start | bytes 798728 | tf_op jit(solution)/shard_map/ppermute | solution.py:320
  11.8 11.9 %collective-permute-start.7 = (f32[520,128]{1,0:T(8,128)S(1)}, f32[520,128]{1,0:T(8,128)S(1)}, u32[]{:S(2)}, u32[]{:S(2)}) collective-permute-start(f32[520,128]{1,0:T(8,128)S(1)} %get-tuple-element.46.refs_0_), channel_id=1, source_target_pairs={{28,0},{0,4},{4,8},{8,12},{12,16},{16,20},{20,24},{24,28},{29,1},{... | collective-permute-start | bytes 798728 | tf_op jit(solution)/shard_map/ppermute | solution.py:320
  13.4 4.6 %collective-permute-start.3 = (f32[260,128]{1,0:T(8,128)S(1)}, f32[260,128]{1,0:T(8,128)S(1)}, u32[]{:S(2)}, u32[]{:S(2)}) collective-permute-start(f32[260,128]{1,0:T(8,128)S(1)} %get-tuple-element.48), channel_id=1, source_target_pairs={{3,0},{0,1},{1,2},{2,3},{7,4},{4,5},{5,6},{6,7},{11,8},{8,9},{9,10... | collective-permute-start | bytes 399368 | tf_op jit(solution)/shard_map/ppermute | solution.py:320
  14.2 5.1 %collective-permute-start.4 = (f32[260,128]{1,0:T(8,128)S(1)}, f32[260,128]{1,0:T(8,128)S(1)}, u32[]{:S(2)}, u32[]{:S(2)}) collective-permute-start(f32[260,128]{1,0:T(8,128)S(1)} %get-tuple-element.49), channel_id=1, source_target_pairs={{1,0},{2,1},{3,2},{0,3},{5,4},{6,5},{7,6},{4,7},{9,8},{10,9},{11,1... | collective-permute-start | bytes 399368 | tf_op jit(solution)/shard_map/ppermute | solution.py:320
  15.6 5.9 %collective-permute-start.5 = (f32[260,128]{1,0:T(8,128)S(1)}, f32[260,128]{1,0:T(8,128)S(1)}, u32[]{:S(2)}, u32[]{:S(2)}) collective-permute-start(f32[260,128]{1,0:T(8,128)S(1)} %get-tuple-element.50), channel_id=1, source_target_pairs={{3,0},{0,1},{1,2},{2,3},{7,4},{4,5},{5,6},{6,7},{11,8},{8,9},{9,10... | collective-permute-start | bytes 399368 | tf_op jit(solution)/shard_map/ppermute | solution.py:320
  15.6 5.9 %collective-permute-start.6 = (f32[260,128]{1,0:T(8,128)S(1)}, f32[260,128]{1,0:T(8,128)S(1)}, u32[]{:S(2)}, u32[]{:S(2)}) collective-permute-start(f32[260,128]{1,0:T(8,128)S(1)} %get-tuple-element.51), channel_id=1, source_target_pairs={{1,0},{2,1},{3,2},{0,3},{5,4},{6,5},{7,6},{4,7},{9,8},{10,9},{11,1... | collective-permute-start | bytes 399368 | tf_op jit(solution)/shard_map/ppermute | solution.py:320
  24.0 18.7 %collective-permute-start.10 = (f32[520,128]{1,0:T(8,128)S(1)}, f32[520,128]{1,0:T(8,128)S(1)}, u32[]{:S(2)}, u32[]{:S(2)}) collective-permute-start(f32[520,128]{1,0:T(8,128)S(1)} %get-tuple-element.53.refs_5_), channel_id=1, source_target_pairs={{4,0},{8,4},{12,8},{16,12},{20,16},{24,20},{28,24},{0,28},{5,1},{9... | collective-permute-start | bytes 798728 | tf_op jit(solution)/shard_map/ppermute | solution.py:320
  27.8 10.9 %collective-permute-start.8 = (f32[260,128]{1,0:T(8,128)S(1)}, f32[260,128]{1,0:T(8,128)S(1)}, u32[]{:S(2)}, u32[]{:S(2)}) collective-permute-start(f32[260,128]{1,0:T(8,128)S(1)} %get-tuple-element.54), channel_id=1, source_target_pairs={{3,0},{0,1},{1,2},{2,3},{7,4},{4,5},{5,6},{6,7},{11,8},{8,9},{9,10... | collective-permute-start | bytes 399368 | tf_op jit(solution)/shard_map/ppermute | solution.py:320
  28.1 10.6 %collective-permute-start.9 = (f32[260,128]{1,0:T(8,128)S(1)}, f32[260,128]{1,0:T(8,128)S(1)}, u32[]{:S(2)}, u32[]{:S(2)}) collective-permute-start(f32[260,128]{1,0:T(8,128)S(1)} %get-tuple-element.55), channel_id=1, source_target_pairs={{1,0},{2,1},{3,2},{0,3},{5,4},{6,5},{7,6},{4,7},{9,8},{10,9},{11,1... | collective-permute-start | bytes 399368 | tf_op jit(solution)/shard_map/ppermute | solution.py:320
  40.3 10.9 %collective-permute-start.15 = (f32[520,128]{1,0:T(8,128)S(1)}, f32[520,128]{1,0:T(8,128)S(1)}, u32[]{:S(2)}, u32[]{:S(2)}) collective-permute-start(f32[520,128]{1,0:T(8,128)S(1)} %get-tuple-element.61.refs_0_), channel_id=1, source_target_pairs={{28,0},{0,4},{4,8},{8,12},{12,16},{16,20},{20,24},{24,28},{29,1},{... | collective-permute-start | bytes 798728 | tf_op jit(solution)/shard_map/ppermute | solution.py:320
  41.0 5.0 %collective-permute-start.11 = (f32[260,128]{1,0:T(8,128)S(1)}, f32[260,128]{1,0:T(8,128)S(1)}, u32[]{:S(2)}, u32[]{:S(2)}) collective-permute-start(f32[260,128]{1,0:T(8,128)S(1)} %get-tuple-element.63), channel_id=1, source_target_pairs={{3,0},{0,1},{1,2},{2,3},{7,4},{4,5},{5,6},{6,7},{11,8},{8,9},{9,10... | collective-permute-start | bytes 399368 | tf_op jit(solution)/shard_map/ppermute | solution.py:320
  41.0 5.4 %collective-permute-start.12 = (f32[260,128]{1,0:T(8,128)S(1)}, f32[260,128]{1,0:T(8,128)S(1)}, u32[]{:S(2)}, u32[]{:S(2)}) collective-permute-start(f32[260,128]{1,0:T(8,128)S(1)} %get-tuple-element.64), channel_id=1, source_target_pairs={{1,0},{2,1},{3,2},{0,3},{5,4},{6,5},{7,6},{4,7},{9,8},{10,9},{11,1... | collective-permute-start | bytes 399368 | tf_op jit(solution)/shard_map/ppermute | solution.py:320
  43.1 5.9 %collective-permute-start.13 = (f32[260,128]{1,0:T(8,128)S(1)}, f32[260,128]{1,0:T(8,128)S(1)}, u32[]{:S(2)}, u32[]{:S(2)}) collective-permute-start(f32[260,128]{1,0:T(8,128)S(1)} %get-tuple-element.65), channel_id=1, source_target_pairs={{3,0},{0,1},{1,2},{2,3},{7,4},{4,5},{5,6},{6,7},{11,8},{8,9},{9,10... | collective-permute-start | bytes 399368 | tf_op jit(solution)/shard_map/ppermute | solution.py:320
  43.1 5.9 %collective-permute-start.14 = (f32[260,128]{1,0:T(8,128)S(1)}, f32[260,128]{1,0:T(8,128)S(1)}, u32[]{:S(2)}, u32[]{:S(2)}) collective-permute-start(f32[260,128]{1,0:T(8,128)S(1)} %get-tuple-element.66), channel_id=1, source_target_pairs={{1,0},{2,1},{3,2},{0,3},{5,4},{6,5},{7,6},{4,7},{9,8},{10,9},{11,1... | collective-permute-start | bytes 399368 | tf_op jit(solution)/shard_map/ppermute | solution.py:320
  49.0 2.3 %copy-start = (f32[520,128]{1,0:T(8,128)S(1)}, f32[520,128]{1,0:T(8,128)}, u32[]{:S(2)}) copy-start(f32[520,128]{1,0:T(8,128)} %kept.1.refs_0_) | copy-start | bytes 798724

commit v5 on v4

--- a/solution.py
+++ b/solution.py
@@ -34,7 +34,7 @@
     ref[pl.ds(i, points, stride=planes), :] = plane[:points]
 
 
-WORK = {"forward": 4e9, "inverse": 1e9}
+WORK = {"forward": 4e9, "adjoint": 4e9, "inverse": 1e9}
 
 
 def call(kernel, name, outs, operands, scratch=(), specs=None, fast=False):
@@ -136,13 +136,18 @@
         store(to_right, h + i, 2 * h - 1, load(forcing, nx - h + 1 + i, nx))
 
 
-def copy_kernel(given, out):
+def copy_kernel(given, order, out):
     out[...] = given[...]
 
 
 def wall_profile(points, rows):
     row = lax.broadcasted_iota(jnp.int32, (rows, LANES), 0).astype(jnp.float32)
     return row * (2.0 / (points - 1)) - 1.0
+
+
+def halve(total):
+    row = jnp.sum(total, axis=0, keepdims=True)
+    return row + pltpu.roll(row, LANES // 2, 1)
 
 
 def forward_kernel(nx, updated, *refs):
@@ -152,8 +157,8 @@
     matrix_ref, states, forcing, left, right = refs[:5]
     del refs[:5]
     if updated:
-        descent, d_left, d_right, sums = refs[:4]
-        del refs[:4]
+        descent, d_left, d_right, sums, after, d_after = refs[:6]
+        del refs[:6]
         tau = step_size(sums[...])
     ending_ref, start_ref, first_ref, second_ref, third_ref, low_ref, high_ref = refs[:7]
     u0, q = refs[-2:]
@@ -204,34 +209,31 @@
                     else:
                         store(ending_ref, at, nx, plane)
                 pending = []
+    sent = 2 * h if updated else h
     for i in range(h - 1):
-        store(low_ref, i, h, third_ref[1 + 1 + i])
-        store(high_ref, i, h, third_ref[1 + nx - h + i])
-    store(low_ref, h - 1, h, second_ref[2 + 2])
-    store(high_ref, h - 1, h, second_ref[2 + nx - 3])
-
-
-def halve(total):
-    row = jnp.sum(total, axis=0, keepdims=True)
-    return row + pltpu.roll(row, LANES // 2, 1)
-
-
-def mismatch_kernel(nx, updated, *refs):
-    h = STEPS
-    refs = list(refs)
-    ending, after = refs[:2]
-    del refs[:2]
+        store(low_ref, i, sent, third_ref[1 + 1 + i])
+        store(high_ref, i, sent, third_ref[1 + nx - h + i])
+    store(low_ref, h - 1, sent, second_ref[2 + 2])
+    store(high_ref, h - 1, sent, second_ref[2 + nx - 3])
     if updated:
-        d_after, sums = refs[:2]
-        del refs[:2]
-        tau = step_size(sums[...])
-    mismatch_ref, low_ref, high_ref, squares_ref = refs
+        mismatch_ref, squares_ref = refs[7:9]
+        total = None
+        for i in range(nx):
+            value = load(ending_ref, i, nx) - (load(after, i, nx) - tau * load(d_after, i, nx))
+            store(mismatch_ref, i, nx, value)
+            if i < h:
+                store(low_ref, h + i, sent, value)
+            if i >= nx - h:
+                store(high_ref, h + i - (nx - h), sent, value)
+            total = value * value if total is None else total + value * value
+        squares_ref[...] = halve(total)
+
+
+def mismatch_kernel(nx, ending, after, mismatch_ref, low_ref, high_ref, squares_ref):
+    h = STEPS
     total = None
     for i in range(nx):
-        value = load(after, i, nx)
-        if updated:
-            value = value - tau * load(d_after, i, nx)
-        value = load(ending, i, nx) - value
+        value = load(ending, i, nx) - load(after, i, nx)
         store(mismatch_ref, i, nx, value)
         if i < h:
             store(low_ref, i, h, value)
@@ -241,9 +243,13 @@
     squares_ref[...] = halve(total)
 
 
-def adjoint_kernel(nx, matrix_ref, start, first, second, third, mismatch, left_fields, right_fields, left, right, lam_ref, a, b):
-    h = STEPS
+def adjoint_kernel(nx, matrix_ref, start, first, second, third, mismatch, *refs):
+    h = STEPS
+    *sides, lam_ref, a, b = refs
     points = mismatch.shape[0] // nx
+    sent = sides[0].shape[0] // points
+    left_fields, right_fields = sides[:2]
+    left, right = sides[-2:]
     base = wall_profile(points, padded(points, 8))
     matrix = matrix_ref[...]
 
@@ -254,21 +260,21 @@
             return first[i + 3]
         if t == 2:
             if i == -3:
-                return load(left_fields, h - 1, h)
+                return load(left_fields, h - 1, sent)
             if i == nx + 2:
-                return load(right_fields, h - 1, h)
+                return load(right_fields, h - 1, sent)
             return second[i + 2]
         if i < -1:
-            return load(left_fields, i + h, h)
+            return load(left_fields, i + h, sent)
         if i > nx:
-            return load(right_fields, i - nx - 1, h)
+            return load(right_fields, i - nx - 1, sent)
         return third[i + 1]
 
     def weight(i):
         if i < 0:
-            return load(left, h + i, h)
+            return load(left, sent + i, sent)
         if i >= nx:
-            return load(right, i - nx, h)
+            return load(right, sent - h + i - nx, sent)
         return load(mismatch, i, nx)
 
     for t in reversed(range(h)):
@@ -357,39 +363,45 @@
     moved = d_after = sums = None
     for iteration in range(ITERS):
         updated = iteration > 0
-        ending, start, first, second, third, low, high = call(
+        sent = 2 * h if updated else h
+        ending, start, first, second, third, low, high, *rest = call(
             functools.partial(forward_kernel, nx, updated),
             "forward",
-            [flat(nx), tiles(nx + 2), tiles(nx + 6), tiles(nx + 4), tiles(nx + 2), flat(h), flat(h)],
-            [forward, states, forcing, left, right] + (moved + [sums] if updated else []),
+            [flat(nx), tiles(nx + 2), tiles(nx + 6), tiles(nx + 4), tiles(nx + 2), flat(sent), flat(sent)]
+            + ([flat(nx), ((1, LANES), f32)] if updated else []),
+            [forward, states, forcing, left, right] + (moved + [sums, after, d_after] if updated else []),
             [pltpu.VMEM((nx + 2 * h, rows, LANES), f32), pltpu.VMEM((nx + 2 * h - 2, rows, LANES), f32)],
             fast=updated,
         )
         prior = shift(ending, "seg", 1)
         sides = [shift(high, "space", 1), shift(low, "space", -1)]
-        mismatch, low, high, squares = call(
-            functools.partial(mismatch_kernel, nx, updated),
-            "mismatch",
-            [flat(nx), flat(h), flat(h), ((1, LANES), f32)],
-            [ending, after] + ([d_after, sums] if updated else []),
-        )
-        sides += [shift(high, "space", 1), shift(low, "space", -1)]
+        if updated:
+            mismatch, squares = rest
+        else:
+            mismatch, low, high, squares = call(
+                functools.partial(mismatch_kernel, nx),
+                "mismatch",
+                [flat(nx), flat(h), flat(h), ((1, LANES), f32)],
+                [ending, after],
+            )
+            sides += [shift(high, "space", 1), shift(low, "space", -1)]
         lam = call(
             functools.partial(adjoint_kernel, nx),
             "adjoint",
             [tiles(nx)],
             [backward, start, first, second, third, mismatch] + sides,
             [pltpu.VMEM((nx + 2 * h, rows, LANES), f32)] * 2,
+            fast=not updated,
         )[0]
         sent = iteration < ITERS - 1
         if not sent:
-            kept = call(copy_kernel, "kept", [flat(nx)], [mismatch])[0]
+            kept = call(copy_kernel, "kept", [flat(nx)], [mismatch, lam], specs=[VMEM, pl.BlockSpec(memory_space=pl.ANY)])[0]
         sums, descent, *edges = call(
             functools.partial(descent_kernel, nx, devices, sent),
             "descent",
             [((devices, LANES), f32)] + ([flat(nx), flat(h), flat(h)] if sent else [tiles(nx)]),
-            [lam, prior, start, squares] + ([] if sent else [kept]),
-            specs=[VMEM] * 4 + ([] if sent else [pl.BlockSpec(memory_space=pl.ANY)]),
+            [lam, prior, start, squares] + ([] if sent else [pltpu.with_memory_space_constraint(kept, pltpu.HBM)]),
+            specs=[VMEM] * 4 + ([] if sent else [pl.BlockSpec(memory_space=pltpu.HBM)]),
         )
         sums = lax.all_to_all(sums, BOTH, 0, 0, tiled=True)
         if sent:

time: 63.8 us -> 62.3 us (0.976)
  waiting for transfers between devices: 9.26 us -> 12.1 us
  blocking collectives: 20.4 us -> 17.9 us
  starting transfers between devices: 22.7 us -> 20.9 us
    ppermute x16 -> x14, waiting for transfers between devices: 9.26 us -> 12.1 us  [shift(): lax.ppermute(block, axis, [((i - distance) % devices, i) for i in range(d...]
    all_to_all x2, blocking collectives: 20.4 us -> 17.9 us  [per_device(): sums = lax.all_to_all(sums, BOTH, 0, 0, tiled=True)]
    ppermute x16 -> x14, starting transfers between devices: 22.7 us -> 20.9 us  [shift(): lax.ppermute(block, axis, [((i - distance) % devices, i) for i in range(d...]
    pallas_call x12 -> x11, Pallas kernels: 10.6 us -> 10.4 us  [call(): pl.pallas_call(kernel, name=name, out_shape=[jax.ShapeDtypeStruct(shape,...]
  transfers between devices with their start and end apart: 16 -> 14, of which waited for: 9 -> 7; matrix products, arithmetic and copies ran while one was open for 0% -> 0% of each run, Pallas kernels for 13% -> 10%
where the time goes in v5:
time: 62.3 us; the launch traced here: 62.1 us
  starting transfers between devices  20.9 us (34%)
  blocking collectives  17.9 us (29%)
  waiting for transfers between devices  12.1 us (19%)
  Pallas kernels  10.4 us (17%)
  between operations  0.69 us (1%)
    ppermute x14, starting transfers between devices, shift(): lax.ppermute(block, axis, [((i - distance) % devices, i) for i in range(d...  20.9 us
    all_to_all x2, blocking collectives, per_device(): sums = lax.all_to_all(sums, BOTH, 0, 0, tiled=True)  17.9 us
    ppermute x14, waiting for transfers between devices, shift(): lax.ppermute(block, axis, [((i - distance) % devices, i) for i in range(d...  12.1 us
    pallas_call x11, Pallas kernels, call(): pl.pallas_call(kernel, name=name, out_shape=[jax.ShapeDtypeStruct(shape,...  10.4 us
  transfers between devices with their start and end apart: 14, of which 7 were waited for; matrix products, arithmetic and copies ran while one was open for 0% of the time, Pallas kernels for 10%

profile of v5, /device:TPU:0, one launch (start us, length us, event | category | flops | bytes accessed | tf_op | source)
XLA Modules:
  0.0 62.1 jit_solution(11752013415950513816)
XLA Ops:
  0.6 1.2 %pack.1 = (f32[455,128]{1,0:T(8,128)S(1)}, f32[455,128]{1,0:T(8,128)S(1)}, f32[520,128]{1,0:T(8,128)S(1)}, f32[520,128]{1,0:T(8,128)S(1)}) custom-call(f32[520,128]{1,0:T(8,128)} %bitcast.33, f32[520,128]{1,0:T(8,128)} %bitcast.34), custom_call_target="tpu_custom_call" | custom-call | tf_op jit(solution)/shard_map/pack/pallas_call | solution.py:41
  1.8 0.5 collective-permute-start
  2.3 2.0 %collective-permute-start.1 = (f32[455,128]{1,0:T(8,128)S(1)}, f32[455,128]{1,0:T(8,128)S(1)}, u32[]{:S(2)}, u32[]{:S(2)}) collective-permute-start(f32[455,128]{1,0:T(8,128)S(1)} %get-tuple-element.38), channel_id=1, source_target_pairs={{1,0},{2,1},{3,2},{0,3},{5,4},{6,5},{7,6},{4,7},{9,8},{10,9},{11,1... | collective-permute-start | bytes 698888 | tf_op jit(solution)/shard_map/ppermute | solution.py:326
  4.4 5.3 %collective-permute-start.2 = (f32[520,128]{1,0:T(8,128)S(1)}, f32[520,128]{1,0:T(8,128)S(1)}, u32[]{:S(2)}, u32[]{:S(2)}) collective-permute-start(f32[520,128]{1,0:T(8,128)S(1)} %get-tuple-element.35.refs_1_), channel_id=1, source_target_pairs={{4,0},{8,4},{12,8},{16,12},{20,16},{24,20},{28,24},{0,28},{5,1},{9... | collective-permute-start | bytes 798728 | tf_op jit(solution)/shard_map/ppermute | solution.py:326
  9.6 0.5 inverse.1
  10.1 0.2 collective-permute-done.1.refs_4_
  10.4 1.5 %forward.2 = (f32[520,128]{1,0:T(8,128)S(1)}, f32[10,72,128]{2,1,0:T(8,128)S(1)}, f32[14,72,128]{2,1,0:T(8,128)S(1)}, f32[12,72,128]{2,1,0:T(8,128)S(1)}, f32[10...) custom-call(bf16[72,240]{1,0:T(8,128)(2,1)S(1)} %get-tuple-element.34.refs_0_, ...), custom_call_target="tpu_custom_call" | custom-call | flops 4000000000 | bytes 1048576 | tf_op jit(solution)/shard_map/forward/pallas_call | solution.py:41
  11.9 1.5 %collective-permute-start.7 = (f32[520,128]{1,0:T(8,128)S(1)}, f32[520,128]{1,0:T(8,128)S(1)}, u32[]{:S(2)}, u32[]{:S(2)}) collective-permute-start(f32[520,128]{1,0:T(8,128)S(1)} %get-tuple-element.44.ending), channel_id=1, source_target_pairs={{28,0},{0,4},{4,8},{8,12},{12,16},{16,20},{20,24},{24,28},{29,1},{... | collective-permute-start | bytes 798728 | tf_op jit(solution)/shard_map/ppermute | solution.py:326
  13.4 0.8 %collective-permute-start.3 = (f32[260,128]{1,0:T(8,128)S(1)}, f32[260,128]{1,0:T(8,128)S(1)}, u32[]{:S(2)}, u32[]{:S(2)}) collective-permute-start(f32[260,128]{1,0:T(8,128)S(1)} %get-tuple-element.46), channel_id=1, source_target_pairs={{3,0},{0,1},{1,2},{2,3},{7,4},{4,5},{5,6},{6,7},{11,8},{8,9},{9,10... | collective-permute-start | bytes 399368 | tf_op jit(solution)/shard_map/ppermute | solution.py:326
  14.2 1.1 %collective-permute-start.4 = (f32[260,128]{1,0:T(8,128)S(1)}, f32[260,128]{1,0:T(8,128)S(1)}, u32[]{:S(2)}, u32[]{:S(2)}) collective-permute-start(f32[260,128]{1,0:T(8,128)S(1)} %get-tuple-element.47), channel_id=1, source_target_pairs={{1,0},{2,1},{3,2},{0,3},{5,4},{6,5},{7,6},{4,7},{9,8},{10,9},{11,1... | collective-permute-start | bytes 399368 | tf_op jit(solution)/shard_map/ppermute | solution.py:326
  15.3 0.2 mismatch.1
  15.6 1.8 %collective-permute-start.6 = (f32[260,128]{1,0:T(8,128)S(1)}, f32[260,128]{1,0:T(8,128)S(1)}, u32[]{:S(2)}, u32[]{:S(2)}) collective-permute-start(f32[260,128]{1,0:T(8,128)S(1)} %get-tuple-element.49), channel_id=1, source_target_pairs={{1,0},{2,1},{3,2},{0,3},{5,4},{6,5},{7,6},{4,7},{9,8},{10,9},{11,1... | collective-permute-start | bytes 399368 | tf_op jit(solution)/shard_map/ppermute | solution.py:326
  17.3 0.7 %collective-permute-done.3.refs_0_ = f32[260,128]{1,0:T(8,128)S(1)} collective-permute-done((f32[260,128]{1,0:T(8,128)S(1)}, f32[260,128]{1,0:T(8,128)S(1)}, u32[]{:S(2)}, u32[]{:S(2)}) %collective-permute-start.3) | collective-permute-done | bytes 133152 | tf_op jit(solution)/shard_map/ppermute | solution.py:326
  18.0 1.3 %collective-permute-done.4.refs_1_ = f32[260,128]{1,0:T(8,128)S(1)} collective-permute-done((f32[260,128]{1,0:T(8,128)S(1)}, f32[260,128]{1,0:T(8,128)S(1)}, u32[]{:S(2)}, u32[]{:S(2)}) %collective-permute-start.4) | collective-permute-done | bytes 133152 | tf_op jit(solution)/shard_map/ppermute | solution.py:326
  19.3 2.2 %collective-permute-done.5.refs_2_ = f32[260,128]{1,0:T(8,128)S(1)} collective-permute-done((f32[260,128]{1,0:T(8,128)S(1)}, f32[260,128]{1,0:T(8,128)S(1)}, u32[]{:S(2)}, u32[]{:S(2)}) %collective-permute-start.5) | collective-permute-done | bytes 133152 | tf_op jit(solution)/shard_map/ppermute | solution.py:326
  21.5 1.6 %adjoint.2.lam = f32[8,72,128]{2,1,0:T(8,128)S(1)} custom-call(bf16[72,240]{1,0:T(8,128)(2,1)S(1)} %get-tuple-element.39.matrix_ref, f32[10,72,128]{2,1,0:T(8,128)S(1)} %get-tuple-element.40.start, f32[14,72,128]{2,1,0:T(8,128)S(1)} %get-tuple-element.41.first, f32[12,72,128]{2,1,0:T(8,128)S(1)} %get-tuple-element.42.second, ...), custom_call_target="tpu_custom_call" | custom-call | tf_op jit(solution)/shard_map/adjoint/pallas_call | solution.py:41
  23.0 0.7 %collective-permute-done.7.prior = f32[520,128]{1,0:T(8,128)S(1)} collective-permute-done((f32[520,128]{1,0:T(8,128)S(1)}, f32[520,128]{1,0:T(8,128)S(1)}, u32[]{:S(2)}, u32[]{:S(2)}) %collective-permute-start.7) | collective-permute-done | bytes 266272 | tf_op jit(solution)/shard_map/ppermute | solution.py:326
  23.8 0.2 descent.2
  24.0 3.8 %collective-permute-start.10 = (f32[520,128]{1,0:T(8,128)S(1)}, f32[520,128]{1,0:T(8,128)S(1)}, u32[]{:S(2)}, u32[]{:S(2)}) collective-permute-start(f32[520,128]{1,0:T(8,128)S(1)} %get-tuple-element.51.refs_5_), channel_id=1, source_target_pairs={{4,0},{8,4},{12,8},{16,12},{20,16},{24,20},{28,24},{0,28},{5,1},{9... | collective-permute-start | bytes 798728 | tf_op jit(solution)/shard_map/ppermute | solution.py:326
  27.8 0.2 collective-permute-start.8
  28.1 1.5 %collective-permute-start.9 = (f32[260,128]{1,0:T(8,128)S(1)}, f32[260,128]{1,0:T(8,128)S(1)}, u32[]{:S(2)}, u32[]{:S(2)}) collective-permute-start(f32[260,128]{1,0:T(8,128)S(1)} %get-tuple-element.53), channel_id=1, source_target_pairs={{1,0},{2,1},{3,2},{0,3},{5,4},{6,5},{7,6},{4,7},{9,8},{10,9},{11,1... | collective-permute-start | bytes 399368 | tf_op jit(solution)/shard_map/ppermute | solution.py:326
  29.6 9.1 %all_to_all.22 = f32[32,1,128]{2,1,0:T(1,128)S(1)} all-to-all(f32[32,1,128]{2,1,0:T(1,128)S(1)} %bitcast.29), channel_id=1, replica_groups=mesh['seg'=8,'space'=4] {'seg','space'}, dimensions={0} | all-to-all | bytes 32768 | tf_op jit(solution)/shard_map/all_to_all | solution.py:406
  38.7 1.8 %forward.3 = (f32[520,128]{1,0:T(8,128)S(1)}, f32[10,72,128]{2,1,0:T(8,128)S(1)}, f32[14,72,128]{2,1,0:T(8,128)S(1)}, f32[12,72,128]{2,1,0:T(8,128)S(1)}, f32[10...) custom-call(bf16[72,240]{1,0:T(8,128)(2,1)S(1)} %get-tuple-element.3, ...), custom_call_target="tpu_custom_call" | custom-call | tf_op jit(solution)/shard_map/forward/pallas_call | solution.py:41
  40.5 1.7 %collective-permute-start.12 = (f32[520,128]{1,0:T(8,128)S(1)}, f32[520,128]{1,0:T(8,128)S(1)}, u32[]{:S(2)}, u32[]{:S(2)}) collective-permute-start(f32[520,128]{1,0:T(8,128)S(1)} %get-tuple-element.61), channel_id=1, source_target_pairs={{1,0},{2,1},{3,2},{0,3},{5,4},{6,5},{7,6},{4,7},{9,8},{10,9},{11,1... | collective-permute-start | bytes 798728 | tf_op jit(solution)/shard_map/ppermute | solution.py:326
  42.3 0.6 collective-permute-start.13
  42.9 5.6 %collective-permute-done.11.refs_0_ = f32[520,128]{1,0:T(8,128)S(1)} collective-permute-done((f32[520,128]{1,0:T(8,128)S(1)}, f32[520,128]{1,0:T(8,128)S(1)}, u32[]{:S(2)}, u32[]{:S(2)}) %collective-permute-start.11) | collective-permute-done | bytes 266272 | tf_op jit(solution)/shard_map/ppermute | solution.py:326
  48.4 1.6 %adjoint.3.order.lam = f32[8,72,128]{2,1,0:T(8,128)S(1)} custom-call(bf16[72,240]{1,0:T(8,128)(2,1)S(1)} %get-tuple-element.39.matrix_ref, f32[10,72,128]{2,1,0:T(8,128)S(1)} %get-tuple-element.55.start, f32[14,72,128]{2,1,0:T(8,128)S(1)} %get-tuple-element.56.first, f32[12,72,128]{2,1,0:T(8,128)S(1)} %get-tuple-element.57.second, ...), custom_call_target="tpu_custom_call" | custom-call | flops 4000000000 | bytes 1048576 | tf_op jit(solution)/shard_map/adjoint/pallas_call | solution.py:41
  50.1 0.7 %kept.1.refs_0_ = f32[520,128]{1,0:T(8,128)} custom-call(f32[520,128]{1,0:T(8,128)S(1)} %get-tuple-element.59.mismatch.given, f32[8,72,128]{2,1,0:T(8,128)S(1)} %adjoint.3.order.lam), custom_call_target="tpu_custom_call" | custom-call | tf_op jit(solution)/shard_map/kept/pallas_call | solution.py:41
  50.8 1.4 %collective-permute-done.13.prior = f32[520,128]{1,0:T(8,128)S(1)} collective-permute-done((f32[520,128]{1,0:T(8,128)S(1)}, f32[520,128]{1,0:T(8,128)S(1)}, u32[]{:S(2)}, u32[]{:S(2)}) %collective-permute-start.13) | collective-permute-done | bytes 266272 | tf_op jit(solution)/shard_map/ppermute | solution.py:326
  52.2 0.2 descent.3
  52.4 8.8 %all_to_all.23 = f32[32,1,128]{2,1,0:T(1,128)S(1)} all-to-all(f32[32,1,128]{2,1,0:T(1,128)S(1)} %bitcast.30), channel_id=1, replica_groups=mesh['seg'=8,'space'=4] {'seg','space'}, dimensions={0} | all-to-all | bytes 32768 | tf_op jit(solution)/shard_map/all_to_all | solution.py:406
  61.2 0.9 %final.1 = f32[520,128]{1,0:T(8,128)} custom-call(f32[10,72,128]{2,1,0:T(8,128)S(1)} %get-tuple-element.55.start, f32[8,72,128]{2,1,0:T(8,128)S(1)} %get-tuple-element.64.descent, f32[32,128]{1,0:T(8,128)S(1)} %bitcast.28), custom_call_target="tpu_custom_call" | custom-call | tf_op jit(solution)/shard_map/final/pallas_call | solution.py:41
  (11 shorter events, 0.0 us)
Async XLA Ops:
  1.8 8.3 %collective-permute-start = (f32[455,128]{1,0:T(8,128)S(1)}, f32[455,128]{1,0:T(8,128)S(1)}, u32[]{:S(2)}, u32[]{:S(2)}) collective-permute-start(f32[455,128]{1,0:T(8,128)S(1)} %get-tuple-element.37), channel_id=1, source_target_pairs={{3,0},{0,1},{1,2},{2,3},{7,4},{4,5},{5,6},{6,7},{11,8},{8,9},{9,10... | collective-permute-start | bytes 698888 | tf_op jit(solution)/shard_map/ppermute | solution.py:326
  2.3 8.0 %collective-permute-start.1 = (f32[455,128]{1,0:T(8,128)S(1)}, f32[455,128]{1,0:T(8,128)S(1)}, u32[]{:S(2)}, u32[]{:S(2)}) collective-permute-start(f32[455,128]{1,0:T(8,128)S(1)} %get-tuple-element.38), channel_id=1, source_target_pairs={{1,0},{2,1},{3,2},{0,3},{5,4},{6,5},{7,6},{4,7},{9,8},{10,9},{11,1... | collective-permute-start | bytes 698888 | tf_op jit(solution)/shard_map/ppermute | solution.py:326
  4.4 5.3 %copy-start = (f32[65]{0:T(128)S(1)}, f32[65]{0:T(128)}, u32[]{:S(2)}) copy-start(f32[65]{0:T(128)} %param.5) | copy-start | bytes 784
  4.4 11.0 %collective-permute-start.2 = (f32[520,128]{1,0:T(8,128)S(1)}, f32[520,128]{1,0:T(8,128)S(1)}, u32[]{:S(2)}, u32[]{:S(2)}) collective-permute-start(f32[520,128]{1,0:T(8,128)S(1)} %get-tuple-element.35.refs_1_), channel_id=1, source_target_pairs={{4,0},{8,4},{12,8},{16,12},{20,16},{24,20},{28,24},{0,28},{5,1},{9... | collective-permute-start | bytes 798728 | tf_op jit(solution)/shard_map/ppermute | solution.py:326
  11.9 11.9 %collective-permute-start.7 = (f32[520,128]{1,0:T(8,128)S(1)}, f32[520,128]{1,0:T(8,128)S(1)}, u32[]{:S(2)}, u32[]{:S(2)}) collective-permute-start(f32[520,128]{1,0:T(8,128)S(1)} %get-tuple-element.44.ending), channel_id=1, source_target_pairs={{28,0},{0,4},{4,8},{8,12},{12,16},{16,20},{20,24},{24,28},{29,1},{... | collective-permute-start | bytes 798728 | tf_op jit(solution)/shard_map/ppermute | solution.py:326
  13.4 4.6 %collective-permute-start.3 = (f32[260,128]{1,0:T(8,128)S(1)}, f32[260,128]{1,0:T(8,128)S(1)}, u32[]{:S(2)}, u32[]{:S(2)}) collective-permute-start(f32[260,128]{1,0:T(8,128)S(1)} %get-tuple-element.46), channel_id=1, source_target_pairs={{3,0},{0,1},{1,2},{2,3},{7,4},{4,5},{5,6},{6,7},{11,8},{8,9},{9,10... | collective-permute-start | bytes 399368 | tf_op jit(solution)/shard_map/ppermute | solution.py:326
  14.2 5.1 %collective-permute-start.4 = (f32[260,128]{1,0:T(8,128)S(1)}, f32[260,128]{1,0:T(8,128)S(1)}, u32[]{:S(2)}, u32[]{:S(2)}) collective-permute-start(f32[260,128]{1,0:T(8,128)S(1)} %get-tuple-element.47), channel_id=1, source_target_pairs={{1,0},{2,1},{3,2},{0,3},{5,4},{6,5},{7,6},{4,7},{9,8},{10,9},{11,1... | collective-permute-start | bytes 399368 | tf_op jit(solution)/shard_map/ppermute | solution.py:326
  15.6 5.9 %collective-permute-start.5 = (f32[260,128]{1,0:T(8,128)S(1)}, f32[260,128]{1,0:T(8,128)S(1)}, u32[]{:S(2)}, u32[]{:S(2)}) collective-permute-start(f32[260,128]{1,0:T(8,128)S(1)} %get-tuple-element.48), channel_id=1, source_target_pairs={{3,0},{0,1},{1,2},{2,3},{7,4},{4,5},{5,6},{6,7},{11,8},{8,9},{9,10... | collective-permute-start | bytes 399368 | tf_op jit(solution)/shard_map/ppermute | solution.py:326
  15.6 5.9 %collective-permute-start.6 = (f32[260,128]{1,0:T(8,128)S(1)}, f32[260,128]{1,0:T(8,128)S(1)}, u32[]{:S(2)}, u32[]{:S(2)}) collective-permute-start(f32[260,128]{1,0:T(8,128)S(1)} %get-tuple-element.49), channel_id=1, source_target_pairs={{1,0},{2,1},{3,2},{0,3},{5,4},{6,5},{7,6},{4,7},{9,8},{10,9},{11,1... | collective-permute-start | bytes 399368 | tf_op jit(solution)/shard_map/ppermute | solution.py:326
  24.0 14.7 %collective-permute-start.10 = (f32[520,128]{1,0:T(8,128)S(1)}, f32[520,128]{1,0:T(8,128)S(1)}, u32[]{:S(2)}, u32[]{:S(2)}) collective-permute-start(f32[520,128]{1,0:T(8,128)S(1)} %get-tuple-element.51.refs_5_), channel_id=1, source_target_pairs={{4,0},{8,4},{12,8},{16,12},{20,16},{24,20},{28,24},{0,28},{5,1},{9... | collective-permute-start | bytes 798728 | tf_op jit(solution)/shard_map/ppermute | solution.py:326
  27.8 10.9 %collective-permute-start.8 = (f32[260,128]{1,0:T(8,128)S(1)}, f32[260,128]{1,0:T(8,128)S(1)}, u32[]{:S(2)}, u32[]{:S(2)}) collective-permute-start(f32[260,128]{1,0:T(8,128)S(1)} %get-tuple-element.52), channel_id=1, source_target_pairs={{3,0},{0,1},{1,2},{2,3},{7,4},{4,5},{5,6},{6,7},{11,8},{8,9},{9,10... | collective-permute-start | bytes 399368 | tf_op jit(solution)/shard_map/ppermute | solution.py:326
  28.1 10.6 %collective-permute-start.9 = (f32[260,128]{1,0:T(8,128)S(1)}, f32[260,128]{1,0:T(8,128)S(1)}, u32[]{:S(2)}, u32[]{:S(2)}) collective-permute-start(f32[260,128]{1,0:T(8,128)S(1)} %get-tuple-element.53), channel_id=1, source_target_pairs={{1,0},{2,1},{3,2},{0,3},{5,4},{6,5},{7,6},{4,7},{9,8},{10,9},{11,1... | collective-permute-start | bytes 399368 | tf_op jit(solution)/shard_map/ppermute | solution.py:326
  40.5 7.9 %collective-permute-start.11 = (f32[520,128]{1,0:T(8,128)S(1)}, f32[520,128]{1,0:T(8,128)S(1)}, u32[]{:S(2)}, u32[]{:S(2)}) collective-permute-start(f32[520,128]{1,0:T(8,128)S(1)} %get-tuple-element.60), channel_id=1, source_target_pairs={{3,0},{0,1},{1,2},{2,3},{7,4},{4,5},{5,6},{6,7},{11,8},{8,9},{9,10... | collective-permute-start | bytes 798728 | tf_op jit(solution)/shard_map/ppermute | solution.py:326
  40.5 7.9 %collective-permute-start.12 = (f32[520,128]{1,0:T(8,128)S(1)}, f32[520,128]{1,0:T(8,128)S(1)}, u32[]{:S(2)}, u32[]{:S(2)}) collective-permute-start(f32[520,128]{1,0:T(8,128)S(1)} %get-tuple-element.61), channel_id=1, source_target_pairs={{1,0},{2,1},{3,2},{0,3},{5,4},{6,5},{7,6},{4,7},{9,8},{10,9},{11,1... | collective-permute-start | bytes 798728 | tf_op jit(solution)/shard_map/ppermute | solution.py:326
  42.3 9.9 %collective-permute-start.13 = (f32[520,128]{1,0:T(8,128)S(1)}, f32[520,128]{1,0:T(8,128)S(1)}, u32[]{:S(2)}, u32[]{:S(2)}) collective-permute-start(f32[520,128]{1,0:T(8,128)S(1)} %get-tuple-element.62), channel_id=1, source_target_pairs={{28,0},{0,4},{4,8},{8,12},{12,16},{16,20},{20,24},{24,28},{29,1},{... | collective-permute-start | bytes 798728 | tf_op jit(solution)/shard_map/ppermute | solution.py:326

commit v6 on v5

--- a/solution.py
+++ b/solution.py
@@ -34,7 +34,7 @@
     ref[pl.ds(i, points, stride=planes), :] = plane[:points]
 
 
-WORK = {"forward": 4e9, "adjoint": 4e9, "inverse": 1e9}
+WORK = {"forward": 4e9, "inverse": 1e9}
 
 
 def call(kernel, name, outs, operands, scratch=(), specs=None, fast=False):
@@ -243,10 +243,46 @@
     squares_ref[...] = halve(total)
 
 
-def adjoint_kernel(nx, matrix_ref, start, first, second, third, mismatch, *refs):
-    h = STEPS
-    *sides, lam_ref, a, b = refs
+def adjoint_value(before, here, ahead):
+    (u0, _, f0), (_, m1, _), (u2, _, f2) = before, here, ahead
+    return SPREAD * (3.0 * m1 + neighbours(m1)) + (0.5 * ADVECT) * ((f2 - f0) - m1 * (u2 - u0))
+
+
+def own_field(start, first, second, third, t, i):
+    return ((start, 1), (first, 3), (second, 2), (third, 1))[t][0][i + (1, 3, 2, 1)[t]]
+
+
+def inner_range(nx, t):
+    low = STEPS - 1 - t
+    return low, nx - low, sum(nx - 2 * j for j in range(low))
+
+
+def adjoint_inner_kernel(nx, matrix_ref, start, first, second, third, mismatch, mu_ref, flux_ref, a, b):
+    h = STEPS
     points = mismatch.shape[0] // nx
+    base = wall_profile(points, padded(points, 8))
+    matrix = matrix_ref[...]
+    for t in reversed(range(h)):
+        source, target = (a, b) if t % 2 == 0 else (b, a)
+        low, high, at = inner_range(nx, t)
+        window = []
+        for begin in range(low, high, 2):
+            group = list(range(begin, min(begin + 2, high)))
+            lams = [load(mismatch, i, nx) if t == h - 1 else source[i] for i in group]
+            for i, mu in zip(group, product(matrix, lams)):
+                u = own_field(start, first, second, third, t, i)
+                flux = (base + u) * mu
+                mu_ref[at + i - low] = mu
+                flux_ref[at + i - low] = flux
+                window = window[-2:] + [(u, mu, flux)]
+                if len(window) == 3 and t > 0:
+                    target[i - 1] = adjoint_value(*window)
+
+
+def adjoint_outer_kernel(nx, matrix_ref, start, first, second, third, mu_ref, flux_ref, *refs):
+    h = STEPS
+    *sides, lam_ref, lams, mus, fluxes = refs
+    points = sides[0].shape[0] // (2 * h) if len(sides) == 2 else sides[0].shape[0] // h
     sent = sides[0].shape[0] // points
     left_fields, right_fields = sides[:2]
     left, right = sides[-2:]
@@ -254,47 +290,44 @@
     matrix = matrix_ref[...]
 
     def field(t, i):
-        if t == 0:
-            return start[i + 1]
-        if t == 1:
-            return first[i + 3]
-        if t == 2:
-            if i == -3:
-                return load(left_fields, h - 1, sent)
-            if i == nx + 2:
-                return load(right_fields, h - 1, sent)
-            return second[i + 2]
-        if i < -1:
+        if t == 2 and i == -3:
+            return load(left_fields, h - 1, sent)
+        if t == 2 and i == nx + 2:
+            return load(right_fields, h - 1, sent)
+        if t == 3 and i < -1:
             return load(left_fields, i + h, sent)
-        if i > nx:
+        if t == 3 and i > nx:
             return load(right_fields, i - nx - 1, sent)
-        return third[i + 1]
-
-    def weight(i):
-        if i < 0:
-            return load(left, sent + i, sent)
-        if i >= nx:
-            return load(right, sent - h + i - nx, sent)
-        return load(mismatch, i, nx)
+        return own_field(start, first, second, third, t, i)
 
     for t in reversed(range(h)):
-        source, target = (a, b) if t % 2 == 0 else (b, a)
-        window = []
-        low, high = -(t + 1), nx + t + 1
-        for start_at in range(low, high, 2):
-            group = list(range(start_at, min(start_at + 2, high)))
-            lams = [weight(i) if t == h - 1 else source[i + h] for i in group]
-            for i, mu in zip(group, product(matrix, lams)):
-                u = field(t, i)
-                window.append((u, mu, (base + u) * mu))
-                window = window[-3:]
-                if len(window) == 3:
-                    (u0, _, f0), (_, m1, _), (u2, _, f2) = window
-                    value = SPREAD * (3.0 * m1 + neighbours(m1)) + (0.5 * ADVECT) * ((f2 - f0) - m1 * (u2 - u0))
-                    if t == 0:
-                        lam_ref[i - 1] = value
-                    else:
-                        target[i - 1 + h] = value
+        low, high, at = inner_range(nx, t)
+        planes = list(range(low - h, low)) + list(range(high, high + h))
+        for begin in range(0, 2 * h, 2):
+            group = planes[begin : begin + 2]
+            if t < h - 1:
+                given = [lams[begin + j] for j in range(2)]
+            elif begin < h:
+                given = [load(left, sent + i, sent) for i in group]
+            else:
+                given = [load(right, sent - h + i - nx, sent) for i in group]
+            for j, mu in enumerate(product(matrix, given)):
+                mus[begin + j] = mu
+                fluxes[begin + j] = (base + field(t, group[j])) * mu
+
+        def known(i, t=t, planes=planes, low=low, at=at):
+            if i in planes:
+                j = planes.index(i)
+                return field(t, i), mus[j], fluxes[j]
+            return field(t, i), mu_ref[at + i - low], flux_ref[at + i - low]
+
+        for j, i in enumerate(list(range(low - h + 1, low + 1)) + list(range(high - 1, high + h - 1))):
+            value = adjoint_value(known(i - 1), known(i), known(i + 1))
+            if t == 0:
+                lam_ref[i] = value
+            else:
+                lams[j] = value
+
 
 def descent_kernel(nx, devices, sent, lam, prior, start, squares, *refs):
     sums_ref, descent_ref, *edges = refs if sent else refs[1:]
@@ -385,17 +418,25 @@
                 [ending, after],
             )
             sides += [shift(high, "space", 1), shift(low, "space", -1)]
+        fields = [start, first, second, third]
+        planes = sum(nx - 2 * j for j in range(h))
+        inner = call(
+            functools.partial(adjoint_inner_kernel, nx),
+            "adjoint_inner",
+            [tiles(planes)] * 2,
+            [backward, *fields, mismatch],
+            [pltpu.VMEM((nx, rows, LANES), f32)] * 2,
+        )
         lam = call(
-            functools.partial(adjoint_kernel, nx),
-            "adjoint",
+            functools.partial(adjoint_outer_kernel, nx),
+            "adjoint_outer",
             [tiles(nx)],
-            [backward, start, first, second, third, mismatch] + sides,
-            [pltpu.VMEM((nx + 2 * h, rows, LANES), f32)] * 2,
-            fast=not updated,
+            [backward, *fields, *inner, *sides],
+            [pltpu.VMEM((2 * h, rows, LANES), f32)] * 3,
         )[0]
         sent = iteration < ITERS - 1
         if not sent:
-            kept = call(copy_kernel, "kept", [flat(nx)], [mismatch, lam], specs=[VMEM, pl.BlockSpec(memory_space=pl.ANY)])[0]
+            kept = call(copy_kernel, "kept", [flat(nx)], [mismatch, inner[0]], specs=[VMEM, pl.BlockSpec(memory_space=pl.ANY)])[0]
         sums, descent, *edges = call(
             functools.partial(descent_kernel, nx, devices, sent),
             "descent",

time: 62.3 us -> 62 us (level)
  Pallas kernels: 10.4 us -> 11.9 us
  waiting for transfers between devices: 12.1 us -> 10.7 us
    ppermute x14, waiting for transfers between devices: 12.1 us -> 10.7 us  [shift(): lax.ppermute(block, axis, [((i - distance) % devices, i) for i in range(d...]
    pallas_call x11 -> x13, Pallas kernels: 10.4 us -> 11.9 us  [call(): pl.pallas_call(kernel, name=name, out_shape=[jax.ShapeDtypeStruct(shape,...]
  transfers between devices with their start and end apart: 14 -> 14, of which waited for: 7 -> 6; matrix products, arithmetic and copies ran while one was open for 0% -> 0% of each run, Pallas kernels for 10% -> 12%
where the time goes in v6:
time: 62 us; the launch traced here: 61.8 us
  starting transfers between devices  20.5 us (33%)
  blocking collectives  18 us (29%)
  Pallas kernels  11.9 us (19%)
  waiting for transfers between devices  10.7 us (17%)
  between operations  0.7 us (1%)
    ppermute x14, starting transfers between devices, shift(): lax.ppermute(block, axis, [((i - distance) % devices, i) for i in range(d...  20.5 us
    all_to_all x2, blocking collectives, per_device(): sums = lax.all_to_all(sums, BOTH, 0, 0, tiled=True)  18 us
    pallas_call x13, Pallas kernels, call(): pl.pallas_call(kernel, name=name, out_shape=[jax.ShapeDtypeStruct(shape,...  11.9 us
    ppermute x14, waiting for transfers between devices, shift(): lax.ppermute(block, axis, [((i - distance) % devices, i) for i in range(d...  10.7 us
  transfers between devices with their start and end apart: 14, of which 6 were waited for; matrix products, arithmetic and copies ran while one was open for 0% of the time, Pallas kernels for 12%

profile of v6, /device:TPU:0, one launch (start us, length us, event | category | flops | bytes accessed | tf_op | source)
XLA Modules:
  0.0 61.8 jit_solution(6604103650604403165)
XLA Ops:
  0.6 1.2 %pack.1 = (f32[455,128]{1,0:T(8,128)S(1)}, f32[455,128]{1,0:T(8,128)S(1)}, f32[520,128]{1,0:T(8,128)S(1)}, f32[520,128]{1,0:T(8,128)S(1)}) custom-call(f32[520,128]{1,0:T(8,128)} %bitcast.33, f32[520,128]{1,0:T(8,128)} %bitcast.34), custom_call_target="tpu_custom_call" | custom-call | tf_op jit(solution)/shard_map/pack/pallas_call | solution.py:41
  1.8 0.5 collective-permute-start
  2.3 2.0 %collective-permute-start.1 = (f32[455,128]{1,0:T(8,128)S(1)}, f32[455,128]{1,0:T(8,128)S(1)}, u32[]{:S(2)}, u32[]{:S(2)}) collective-permute-start(f32[455,128]{1,0:T(8,128)S(1)} %get-tuple-element.42), channel_id=1, source_target_pairs={{1,0},{2,1},{3,2},{0,3},{5,4},{6,5},{7,6},{4,7},{9,8},{10,9},{11,1... | collective-permute-start | bytes 698888 | tf_op jit(solution)/shard_map/ppermute | solution.py:359
  4.4 5.3 %collective-permute-start.2 = (f32[520,128]{1,0:T(8,128)S(1)}, f32[520,128]{1,0:T(8,128)S(1)}, u32[]{:S(2)}, u32[]{:S(2)}) collective-permute-start(f32[520,128]{1,0:T(8,128)S(1)} %get-tuple-element.39.refs_1_), channel_id=1, source_target_pairs={{4,0},{8,4},{12,8},{16,12},{20,16},{24,20},{28,24},{0,28},{5,1},{9... | collective-permute-start | bytes 798728 | tf_op jit(solution)/shard_map/ppermute | solution.py:359
  9.6 0.5 inverse.1
  10.1 0.2 collective-permute-done.1.refs_4_
  10.4 1.5 %forward.2 = (f32[520,128]{1,0:T(8,128)S(1)}, f32[10,72,128]{2,1,0:T(8,128)S(1)}, f32[14,72,128]{2,1,0:T(8,128)S(1)}, f32[12,72,128]{2,1,0:T(8,128)S(1)}, f32[10...) custom-call(bf16[72,240]{1,0:T(8,128)(2,1)S(1)} %get-tuple-element.38.refs_0_, ...), custom_call_target="tpu_custom_call" | custom-call | flops 4000000000 | bytes 1048576 | tf_op jit(solution)/shard_map/forward/pallas_call | solution.py:41
  11.9 1.5 %collective-permute-start.7 = (f32[520,128]{1,0:T(8,128)S(1)}, f32[520,128]{1,0:T(8,128)S(1)}, u32[]{:S(2)}, u32[]{:S(2)}) collective-permute-start(f32[520,128]{1,0:T(8,128)S(1)} %get-tuple-element.48.ending), channel_id=1, source_target_pairs={{28,0},{0,4},{4,8},{8,12},{12,16},{16,20},{20,24},{24,28},{29,1},{... | collective-permute-start | bytes 798728 | tf_op jit(solution)/shard_map/ppermute | solution.py:359
  13.4 0.8 %collective-permute-start.3 = (f32[260,128]{1,0:T(8,128)S(1)}, f32[260,128]{1,0:T(8,128)S(1)}, u32[]{:S(2)}, u32[]{:S(2)}) collective-permute-start(f32[260,128]{1,0:T(8,128)S(1)} %get-tuple-element.52), channel_id=1, source_target_pairs={{3,0},{0,1},{1,2},{2,3},{7,4},{4,5},{5,6},{6,7},{11,8},{8,9},{9,10... | collective-permute-start | bytes 399368 | tf_op jit(solution)/shard_map/ppermute | solution.py:359
  14.2 1.1 %collective-permute-start.4 = (f32[260,128]{1,0:T(8,128)S(1)}, f32[260,128]{1,0:T(8,128)S(1)}, u32[]{:S(2)}, u32[]{:S(2)}) collective-permute-start(f32[260,128]{1,0:T(8,128)S(1)} %get-tuple-element.53), channel_id=1, source_target_pairs={{1,0},{2,1},{3,2},{0,3},{5,4},{6,5},{7,6},{4,7},{9,8},{10,9},{11,1... | collective-permute-start | bytes 399368 | tf_op jit(solution)/shard_map/ppermute | solution.py:359
  15.3 0.2 mismatch.1
  15.6 1.8 %collective-permute-start.6 = (f32[260,128]{1,0:T(8,128)S(1)}, f32[260,128]{1,0:T(8,128)S(1)}, u32[]{:S(2)}, u32[]{:S(2)}) collective-permute-start(f32[260,128]{1,0:T(8,128)S(1)} %get-tuple-element.55), channel_id=1, source_target_pairs={{1,0},{2,1},{3,2},{0,3},{5,4},{6,5},{7,6},{4,7},{9,8},{10,9},{11,1... | collective-permute-start | bytes 399368 | tf_op jit(solution)/shard_map/ppermute | solution.py:359
  17.3 1.0 %adjoint_inner.2 = (f32[20,72,128]{2,1,0:T(8,128)S(1)}, f32[20,72,128]{2,1,0:T(8,128)S(1)}) custom-call(bf16[72,240]{1,0:T(8,128)(2,1)S(1)} %get-tuple-element.43.matrix_ref, f32[10,72,128]{2,1,0:T(8,128)S(1)} %get-tuple-element.44.start, f32[14,72,128]{2,1,0:T(8,128)S(1)} %get-tuple-element.45.first, f32[12,72,128]{2,1,0:T(8,128)S(1)} %get-tuple-element.46.second, ...), custom_call_target="tpu_custom_call" | custom-call | tf_op jit(solution)/shard_map/adjoint_inner/pallas_call | solution.py:41
  18.4 0.9 %collective-permute-done.4.refs_1_ = f32[260,128]{1,0:T(8,128)S(1)} collective-permute-done((f32[260,128]{1,0:T(8,128)S(1)}, f32[260,128]{1,0:T(8,128)S(1)}, u32[]{:S(2)}, u32[]{:S(2)}) %collective-permute-start.4) | collective-permute-done | bytes 133152 | tf_op jit(solution)/shard_map/ppermute | solution.py:359
  19.3 2.2 %collective-permute-done.5.refs_2_ = f32[260,128]{1,0:T(8,128)S(1)} collective-permute-done((f32[260,128]{1,0:T(8,128)S(1)}, f32[260,128]{1,0:T(8,128)S(1)}, u32[]{:S(2)}, u32[]{:S(2)}) %collective-permute-start.5) | collective-permute-done | bytes 133152 | tf_op jit(solution)/shard_map/ppermute | solution.py:359
  21.5 1.2 %adjoint_outer.2.lam = f32[8,72,128]{2,1,0:T(8,128)S(1)} custom-call(bf16[72,240]{1,0:T(8,128)(2,1)S(1)} %get-tuple-element.43.matrix_ref, f32[10,72,128]{2,1,0:T(8,128)S(1)} %get-tuple-element.44.start, f32[14,72,128]{2,1,0:T(8,128)S(1)} %get-tuple-element.45.first, f32[12,72,128]{2,1,0:T(8,128)S(1)} %get-tuple-element.46.second, ...), custom_call_target="tpu_custom_call" | custom-call | tf_op jit(solution)/shard_map/adjoint_outer/pallas_call | solution.py:41
  22.7 1.1 %collective-permute-done.7.prior = f32[520,128]{1,0:T(8,128)S(1)} collective-permute-done((f32[520,128]{1,0:T(8,128)S(1)}, f32[520,128]{1,0:T(8,128)S(1)}, u32[]{:S(2)}, u32[]{:S(2)}) %collective-permute-start.7) | collective-permute-done | bytes 266272 | tf_op jit(solution)/shard_map/ppermute | solution.py:359
  23.8 0.2 descent.2
  24.0 3.5 %collective-permute-start.10 = (f32[520,128]{1,0:T(8,128)S(1)}, f32[520,128]{1,0:T(8,128)S(1)}, u32[]{:S(2)}, u32[]{:S(2)}) collective-permute-start(f32[520,128]{1,0:T(8,128)S(1)} %get-tuple-element.57.refs_5_), channel_id=1, source_target_pairs={{4,0},{8,4},{12,8},{16,12},{20,16},{24,20},{28,24},{0,28},{5,1},{9... | collective-permute-start | bytes 798728 | tf_op jit(solution)/shard_map/ppermute | solution.py:359
  27.5 0.2 collective-permute-start.8
  27.7 1.5 %collective-permute-start.9 = (f32[260,128]{1,0:T(8,128)S(1)}, f32[260,128]{1,0:T(8,128)S(1)}, u32[]{:S(2)}, u32[]{:S(2)}) collective-permute-start(f32[260,128]{1,0:T(8,128)S(1)} %get-tuple-element.59), channel_id=1, source_target_pairs={{1,0},{2,1},{3,2},{0,3},{5,4},{6,5},{7,6},{4,7},{9,8},{10,9},{11,1... | collective-permute-start | bytes 399368 | tf_op jit(solution)/shard_map/ppermute | solution.py:359
  29.3 9.1 %all_to_all.22 = f32[32,1,128]{2,1,0:T(1,128)S(1)} all-to-all(f32[32,1,128]{2,1,0:T(1,128)S(1)} %bitcast.29), channel_id=1, replica_groups=mesh['seg'=8,'space'=4] {'seg','space'}, dimensions={0} | all-to-all | bytes 32768 | tf_op jit(solution)/shard_map/all_to_all | solution.py:447
  38.4 1.8 %forward.3 = (f32[520,128]{1,0:T(8,128)S(1)}, f32[10,72,128]{2,1,0:T(8,128)S(1)}, f32[14,72,128]{2,1,0:T(8,128)S(1)}, f32[12,72,128]{2,1,0:T(8,128)S(1)}, f32[10...) custom-call(bf16[72,240]{1,0:T(8,128)(2,1)S(1)} %get-tuple-element.3, ...), custom_call_target="tpu_custom_call" | custom-call | tf_op jit(solution)/shard_map/forward/pallas_call | solution.py:41
  40.2 1.7 %collective-permute-start.12 = (f32[520,128]{1,0:T(8,128)S(1)}, f32[520,128]{1,0:T(8,128)S(1)}, u32[]{:S(2)}, u32[]{:S(2)}) collective-permute-start(f32[520,128]{1,0:T(8,128)S(1)} %get-tuple-element.69), channel_id=1, source_target_pairs={{1,0},{2,1},{3,2},{0,3},{5,4},{6,5},{7,6},{4,7},{9,8},{10,9},{11,1... | collective-permute-start | bytes 798728 | tf_op jit(solution)/shard_map/ppermute | solution.py:359
  42.0 0.6 collective-permute-start.13
  42.5 1.0 %adjoint_inner.3 = (f32[20,72,128]{2,1,0:T(8,128)S(1)}, f32[20,72,128]{2,1,0:T(8,128)S(1)}) custom-call(bf16[72,240]{1,0:T(8,128)(2,1)S(1)} %get-tuple-element.43.matrix_ref, f32[10,72,128]{2,1,0:T(8,128)S(1)} %get-tuple-element.61.start, f32[14,72,128]{2,1,0:T(8,128)S(1)} %get-tuple-element.62.first, f32[12,72,128]{2,1,0:T(8,128)S(1)} %get-tuple-element.63.second, ...), custom_call_target="tpu_custom_call" | custom-call | tf_op jit(solution)/shard_map/adjoint_inner/pallas_call | solution.py:41
  43.6 0.7 %kept.1.refs_0_ = f32[520,128]{1,0:T(8,128)} custom-call(f32[520,128]{1,0:T(8,128)S(1)} %get-tuple-element.65.mismatch.given, f32[20,72,128]{2,1,0:T(8,128)S(1)} %get-tuple-element.66.mu_ref.order), custom_call_target="tpu_custom_call" | custom-call | tf_op jit(solution)/shard_map/kept/pallas_call | solution.py:41
  44.3 3.8 %collective-permute-done.11.refs_0_ = f32[520,128]{1,0:T(8,128)S(1)} collective-permute-done((f32[520,128]{1,0:T(8,128)S(1)}, f32[520,128]{1,0:T(8,128)S(1)}, u32[]{:S(2)}, u32[]{:S(2)}) %collective-permute-start.11) | collective-permute-done | bytes 266272 | tf_op jit(solution)/shard_map/ppermute | solution.py:359
  48.1 1.3 %adjoint_outer.3.lam = f32[8,72,128]{2,1,0:T(8,128)S(1)} custom-call(bf16[72,240]{1,0:T(8,128)(2,1)S(1)} %get-tuple-element.43.matrix_ref, f32[10,72,128]{2,1,0:T(8,128)S(1)} %get-tuple-element.61.start, f32[14,72,128]{2,1,0:T(8,128)S(1)} %get-tuple-element.62.first, f32[12,72,128]{2,1,0:T(8,128)S(1)} %get-tuple-element.63.second, ...), custom_call_target="tpu_custom_call" | custom-call | tf_op jit(solution)/shard_map/adjoint_outer/pallas_call | solution.py:41
  49.4 2.5 %collective-permute-done.13.prior = f32[520,128]{1,0:T(8,128)S(1)} collective-permute-done((f32[520,128]{1,0:T(8,128)S(1)}, f32[520,128]{1,0:T(8,128)S(1)}, u32[]{:S(2)}, u32[]{:S(2)}) %collective-permute-start.13) | collective-permute-done | bytes 266272 | tf_op jit(solution)/shard_map/ppermute | solution.py:359
  52.1 8.8 %all_to_all.23 = f32[32,1,128]{2,1,0:T(1,128)S(1)} all-to-all(f32[32,1,128]{2,1,0:T(1,128)S(1)} %bitcast.30), channel_id=1, replica_groups=mesh['seg'=8,'space'=4] {'seg','space'}, dimensions={0} | all-to-all | bytes 32768 | tf_op jit(solution)/shard_map/all_to_all | solution.py:447
  60.9 0.9 %final.1 = f32[520,128]{1,0:T(8,128)} custom-call(f32[10,72,128]{2,1,0:T(8,128)S(1)} %get-tuple-element.61.start, f32[8,72,128]{2,1,0:T(8,128)S(1)} %get-tuple-element.72.descent, f32[32,128]{1,0:T(8,128)S(1)} %bitcast.28), custom_call_target="tpu_custom_call" | custom-call | tf_op jit(solution)/shard_map/final/pallas_call | solution.py:41
  (13 shorter events, 0.2 us)
Async XLA Ops:
  1.8 8.3 %collective-permute-start = (f32[455,128]{1,0:T(8,128)S(1)}, f32[455,128]{1,0:T(8,128)S(1)}, u32[]{:S(2)}, u32[]{:S(2)}) collective-permute-start(f32[455,128]{1,0:T(8,128)S(1)} %get-tuple-element.41), channel_id=1, source_target_pairs={{3,0},{0,1},{1,2},{2,3},{7,4},{4,5},{5,6},{6,7},{11,8},{8,9},{9,10... | collective-permute-start | bytes 698888 | tf_op jit(solution)/shard_map/ppermute | solution.py:359
  2.3 8.0 %collective-permute-start.1 = (f32[455,128]{1,0:T(8,128)S(1)}, f32[455,128]{1,0:T(8,128)S(1)}, u32[]{:S(2)}, u32[]{:S(2)}) collective-permute-start(f32[455,128]{1,0:T(8,128)S(1)} %get-tuple-element.42), channel_id=1, source_target_pairs={{1,0},{2,1},{3,2},{0,3},{5,4},{6,5},{7,6},{4,7},{9,8},{10,9},{11,1... | collective-permute-start | bytes 698888 | tf_op jit(solution)/shard_map/ppermute | solution.py:359
  4.4 5.3 %copy-start = (f32[65]{0:T(128)S(1)}, f32[65]{0:T(128)}, u32[]{:S(2)}) copy-start(f32[65]{0:T(128)} %param.5) | copy-start | bytes 784
  4.4 11.0 %collective-permute-start.2 = (f32[520,128]{1,0:T(8,128)S(1)}, f32[520,128]{1,0:T(8,128)S(1)}, u32[]{:S(2)}, u32[]{:S(2)}) collective-permute-start(f32[520,128]{1,0:T(8,128)S(1)} %get-tuple-element.39.refs_1_), channel_id=1, source_target_pairs={{4,0},{8,4},{12,8},{16,12},{20,16},{24,20},{28,24},{0,28},{5,1},{9... | collective-permute-start | bytes 798728 | tf_op jit(solution)/shard_map/ppermute | solution.py:359
  11.9 11.9 %collective-permute-start.7 = (f32[520,128]{1,0:T(8,128)S(1)}, f32[520,128]{1,0:T(8,128)S(1)}, u32[]{:S(2)}, u32[]{:S(2)}) collective-permute-start(f32[520,128]{1,0:T(8,128)S(1)} %get-tuple-element.48.ending), channel_id=1, source_target_pairs={{28,0},{0,4},{4,8},{8,12},{12,16},{16,20},{20,24},{24,28},{29,1},{... | collective-permute-start | bytes 798728 | tf_op jit(solution)/shard_map/ppermute | solution.py:359
  13.4 5.0 %collective-permute-start.3 = (f32[260,128]{1,0:T(8,128)S(1)}, f32[260,128]{1,0:T(8,128)S(1)}, u32[]{:S(2)}, u32[]{:S(2)}) collective-permute-start(f32[260,128]{1,0:T(8,128)S(1)} %get-tuple-element.52), channel_id=1, source_target_pairs={{3,0},{0,1},{1,2},{2,3},{7,4},{4,5},{5,6},{6,7},{11,8},{8,9},{9,10... | collective-permute-start | bytes 399368 | tf_op jit(solution)/shard_map/ppermute | solution.py:359
  14.2 5.1 %collective-permute-start.4 = (f32[260,128]{1,0:T(8,128)S(1)}, f32[260,128]{1,0:T(8,128)S(1)}, u32[]{:S(2)}, u32[]{:S(2)}) collective-permute-start(f32[260,128]{1,0:T(8,128)S(1)} %get-tuple-element.53), channel_id=1, source_target_pairs={{1,0},{2,1},{3,2},{0,3},{5,4},{6,5},{7,6},{4,7},{9,8},{10,9},{11,1... | collective-permute-start | bytes 399368 | tf_op jit(solution)/shard_map/ppermute | solution.py:359
  15.6 5.9 %collective-permute-start.5 = (f32[260,128]{1,0:T(8,128)S(1)}, f32[260,128]{1,0:T(8,128)S(1)}, u32[]{:S(2)}, u32[]{:S(2)}) collective-permute-start(f32[260,128]{1,0:T(8,128)S(1)} %get-tuple-element.54), channel_id=1, source_target_pairs={{3,0},{0,1},{1,2},{2,3},{7,4},{4,5},{5,6},{6,7},{11,8},{8,9},{9,10... | collective-permute-start | bytes 399368 | tf_op jit(solution)/shard_map/ppermute | solution.py:359
  15.6 5.9 %collective-permute-start.6 = (f32[260,128]{1,0:T(8,128)S(1)}, f32[260,128]{1,0:T(8,128)S(1)}, u32[]{:S(2)}, u32[]{:S(2)}) collective-permute-start(f32[260,128]{1,0:T(8,128)S(1)} %get-tuple-element.55), channel_id=1, source_target_pairs={{1,0},{2,1},{3,2},{0,3},{5,4},{6,5},{7,6},{4,7},{9,8},{10,9},{11,1... | collective-permute-start | bytes 399368 | tf_op jit(solution)/shard_map/ppermute | solution.py:359
  24.0 14.4 %collective-permute-start.10 = (f32[520,128]{1,0:T(8,128)S(1)}, f32[520,128]{1,0:T(8,128)S(1)}, u32[]{:S(2)}, u32[]{:S(2)}) collective-permute-start(f32[520,128]{1,0:T(8,128)S(1)} %get-tuple-element.57.refs_5_), channel_id=1, source_target_pairs={{4,0},{8,4},{12,8},{16,12},{20,16},{24,20},{28,24},{0,28},{5,1},{9... | collective-permute-start | bytes 798728 | tf_op jit(solution)/shard_map/ppermute | solution.py:359
  27.5 10.9 %collective-permute-start.8 = (f32[260,128]{1,0:T(8,128)S(1)}, f32[260,128]{1,0:T(8,128)S(1)}, u32[]{:S(2)}, u32[]{:S(2)}) collective-permute-start(f32[260,128]{1,0:T(8,128)S(1)} %get-tuple-element.58), channel_id=1, source_target_pairs={{3,0},{0,1},{1,2},{2,3},{7,4},{4,5},{5,6},{6,7},{11,8},{8,9},{9,10... | collective-permute-start | bytes 399368 | tf_op jit(solution)/shard_map/ppermute | solution.py:359
  27.7 10.6 %collective-permute-start.9 = (f32[260,128]{1,0:T(8,128)S(1)}, f32[260,128]{1,0:T(8,128)S(1)}, u32[]{:S(2)}, u32[]{:S(2)}) collective-permute-start(f32[260,128]{1,0:T(8,128)S(1)} %get-tuple-element.59), channel_id=1, source_target_pairs={{1,0},{2,1},{3,2},{0,3},{5,4},{6,5},{7,6},{4,7},{9,8},{10,9},{11,1... | collective-permute-start | bytes 399368 | tf_op jit(solution)/shard_map/ppermute | solution.py:359
  40.2 7.9 %collective-permute-start.11 = (f32[520,128]{1,0:T(8,128)S(1)}, f32[520,128]{1,0:T(8,128)S(1)}, u32[]{:S(2)}, u32[]{:S(2)}) collective-permute-start(f32[520,128]{1,0:T(8,128)S(1)} %get-tuple-element.68), channel_id=1, source_target_pairs={{3,0},{0,1},{1,2},{2,3},{7,4},{4,5},{5,6},{6,7},{11,8},{8,9},{9,10... | collective-permute-start | bytes 798728 | tf_op jit(solution)/shard_map/ppermute | solution.py:359
  40.2 7.9 %collective-permute-start.12 = (f32[520,128]{1,0:T(8,128)S(1)}, f32[520,128]{1,0:T(8,128)S(1)}, u32[]{:S(2)}, u32[]{:S(2)}) collective-permute-start(f32[520,128]{1,0:T(8,128)S(1)} %get-tuple-element.69), channel_id=1, source_target_pairs={{1,0},{2,1},{3,2},{0,3},{5,4},{6,5},{7,6},{4,7},{9,8},{10,9},{11,1... | collective-permute-start | bytes 798728 | tf_op jit(solution)/shard_map/ppermute | solution.py:359
  42.0 9.9 %collective-permute-start.13 = (f32[520,128]{1,0:T(8,128)S(1)}, f32[520,128]{1,0:T(8,128)S(1)}, u32[]{:S(2)}, u32[]{:S(2)}) collective-permute-start(f32[520,128]{1,0:T(8,128)S(1)} %get-tuple-element.70), channel_id=1, source_target_pairs={{28,0},{0,4},{4,8},{8,12},{12,16},{16,20},{20,24},{24,28},{29,1},{... | collective-permute-start | bytes 798728 | tf_op jit(solution)/shard_map/ppermute | solution.py:359

commit v7 on v6

--- a/solution.py
+++ b/solution.py
@@ -150,12 +150,18 @@
     return row + pltpu.roll(row, LANES // 2, 1)
 
 
+def halo_widths(updated):
+    return (7, 6, 5, 4, 0) if updated else (4, 3, 2, 1, 0)
+
+
 def forward_kernel(nx, updated, *refs):
     h = STEPS
     m = 2 * h - 1
     refs = list(refs)
     matrix_ref, states, forcing, left, right = refs[:5]
     del refs[:5]
+    widths = halo_widths(updated)
+    wide, reach = widths[0], widths[1]
     if updated:
         descent, d_left, d_right, sums, after, d_after = refs[:6]
         del refs[:6]
@@ -165,41 +171,52 @@
     points = states.shape[0] // nx
     rows = padded(points, 8)
     scale = PUSHED / SPREAD
-    for i in range(h):
-        before, ahead = load(left, i, m), load(right, i, m)
+    more = wide - h
+    parts = wide + 2 * more
+    for j in range(wide):
+        if j < h:
+            before, ahead = load(left, h - 1 - j, m), load(right, j, m)
+        else:
+            before, ahead = load(d_left, wide + wide - 1 - j, parts), load(d_right, wide + j - h, parts)
         if updated:
-            before = before - tau * load(d_left, i, h)
-            ahead = ahead - tau * load(d_right, i, h)
-        u0[i] = before
-        u0[h + nx + i] = ahead
-        if i == h - 1:
+            before = before - tau * load(d_left, wide - 1 - j, parts)
+            ahead = ahead - tau * load(d_right, j, parts)
+        u0[wide - 1 - j] = before
+        u0[wide + nx + j] = ahead
+        if j == 0:
             start_ref[0] = before
-        if i == 0:
             start_ref[nx + 1] = ahead
     for i in range(nx):
         here = load(states, i, nx)
         if updated:
             here = here - tau * load(descent, i, nx)
-        u0[h + i] = here
+        u0[wide + i] = here
         start_ref[1 + i] = here
-    for i in range(h - 1):
-        q[i] = scale * load(left, h + i, m)
-        q[h - 1 + nx + i] = scale * load(right, h + i, m)
+    for j in range(reach):
+        if j < h - 1:
+            before, ahead = load(left, m - 1 - j, m), load(right, h + j, m)
+        else:
+            before = load(d_left, parts - 1 - (j - h + 1), parts)
+            ahead = load(d_right, wide + more + j - h + 1, parts)
+        q[reach - 1 - j] = scale * before
+        q[reach + nx + j] = scale * ahead
     for i in range(nx):
-        q[h - 1 + i] = scale * load(forcing, i, nx)
+        q[reach + i] = scale * load(forcing, i, nx)
     base = wall_profile(points, rows)
     matrix = matrix_ref[...]
     fields = [u0, first_ref, second_ref, third_ref, None]
     for t in range(h):
         source, target = fields[t], fields[t + 1]
-        count = nx + 2 * (h - t - 1)
-        window = [source[0], source[1]]
+        count = nx + 2 * widths[t + 1]
+        inset = widths[t] - widths[t + 1]
+        window = [source[inset - 1], source[inset]]
         pending = []
         for i in range(count):
-            window = window[-2:] + [source[i + 2]]
+            window = window[-2:] + [source[inset + i + 1]]
             before, here, ahead = window
+            force = q[i + reach - widths[t + 1]]
             pending.append(
-                3.0 * here + neighbours(here) + q[i + t] - (base + here) * (ahead - before) * (0.5 * ADVECT / SPREAD)
+                3.0 * here + neighbours(here) + force - (base + here) * (ahead - before) * (0.5 * ADVECT / SPREAD)
             )
             if len(pending) == 2 or i == count - 1:
                 for j, plane in enumerate(product(matrix, pending)):
@@ -209,12 +226,6 @@
                     else:
                         store(ending_ref, at, nx, plane)
                 pending = []
-    sent = 2 * h if updated else h
-    for i in range(h - 1):
-        store(low_ref, i, sent, third_ref[1 + 1 + i])
-        store(high_ref, i, sent, third_ref[1 + nx - h + i])
-    store(low_ref, h - 1, sent, second_ref[2 + 2])
-    store(high_ref, h - 1, sent, second_ref[2 + nx - 3])
     if updated:
         mismatch_ref, squares_ref = refs[7:9]
         total = None
@@ -222,11 +233,17 @@
             value = load(ending_ref, i, nx) - (load(after, i, nx) - tau * load(d_after, i, nx))
             store(mismatch_ref, i, nx, value)
             if i < h:
-                store(low_ref, h + i, sent, value)
+                store(low_ref, i, h, value)
             if i >= nx - h:
-                store(high_ref, h + i - (nx - h), sent, value)
+                store(high_ref, i - (nx - h), h, value)
             total = value * value if total is None else total + value * value
         squares_ref[...] = halve(total)
+    else:
+        for i in range(h - 1):
+            store(low_ref, i, h, third_ref[1 + 1 + i])
+            store(high_ref, i, h, third_ref[1 + nx - h + i])
+        store(low_ref, h - 1, h, second_ref[2 + 2])
+        store(high_ref, h - 1, h, second_ref[2 + nx - 3])
 
 
 def mismatch_kernel(nx, ending, after, mismatch_ref, low_ref, high_ref, squares_ref):
@@ -248,8 +265,8 @@
     return SPREAD * (3.0 * m1 + neighbours(m1)) + (0.5 * ADVECT) * ((f2 - f0) - m1 * (u2 - u0))
 
 
-def own_field(start, first, second, third, t, i):
-    return ((start, 1), (first, 3), (second, 2), (third, 1))[t][0][i + (1, 3, 2, 1)[t]]
+def own_field(fields, widths, t, i):
+    return fields[t][i + (widths[t] if t else 1)]
 
 
 def inner_range(nx, t):
@@ -257,7 +274,7 @@
     return low, nx - low, sum(nx - 2 * j for j in range(low))
 
 
-def adjoint_inner_kernel(nx, matrix_ref, start, first, second, third, mismatch, mu_ref, flux_ref, a, b):
+def adjoint_inner_kernel(nx, widths, matrix_ref, start, first, second, third, mismatch, mu_ref, flux_ref, a, b):
     h = STEPS
     points = mismatch.shape[0] // nx
     base = wall_profile(points, padded(points, 8))
@@ -270,7 +287,7 @@
             group = list(range(begin, min(begin + 2, high)))
             lams = [load(mismatch, i, nx) if t == h - 1 else source[i] for i in group]
             for i, mu in zip(group, product(matrix, lams)):
-                u = own_field(start, first, second, third, t, i)
+                u = own_field((start, first, second, third), widths, t, i)
                 flux = (base + u) * mu
                 mu_ref[at + i - low] = mu
                 flux_ref[at + i - low] = flux
@@ -279,26 +296,26 @@
                     target[i - 1] = adjoint_value(*window)
 
 
-def adjoint_outer_kernel(nx, matrix_ref, start, first, second, third, mu_ref, flux_ref, *refs):
+def adjoint_outer_kernel(nx, widths, matrix_ref, start, first, second, third, mu_ref, flux_ref, *refs):
     h = STEPS
     *sides, lam_ref, lams, mus, fluxes = refs
-    points = sides[0].shape[0] // (2 * h) if len(sides) == 2 else sides[0].shape[0] // h
-    sent = sides[0].shape[0] // points
-    left_fields, right_fields = sides[:2]
+    points = sides[0].shape[0] // h
     left, right = sides[-2:]
     base = wall_profile(points, padded(points, 8))
     matrix = matrix_ref[...]
 
     def field(t, i):
-        if t == 2 and i == -3:
-            return load(left_fields, h - 1, sent)
-        if t == 2 and i == nx + 2:
-            return load(right_fields, h - 1, sent)
-        if t == 3 and i < -1:
-            return load(left_fields, i + h, sent)
-        if t == 3 and i > nx:
-            return load(right_fields, i - nx - 1, sent)
-        return own_field(start, first, second, third, t, i)
+        if len(sides) > 2:
+            left_fields, right_fields = sides[:2]
+            if t == 2 and i == -3:
+                return load(left_fields, h - 1, h)
+            if t == 2 and i == nx + 2:
+                return load(right_fields, h - 1, h)
+            if t == 3 and i < -1:
+                return load(left_fields, i + h, h)
+            if t == 3 and i > nx:
+                return load(right_fields, i - nx - 1, h)
+        return own_field((start, first, second, third), widths, t, i)
 
     for t in reversed(range(h)):
         low, high, at = inner_range(nx, t)
@@ -308,9 +325,9 @@
             if t < h - 1:
                 given = [lams[begin + j] for j in range(2)]
             elif begin < h:
-                given = [load(left, sent + i, sent) for i in group]
+                given = [load(left, h + i, h) for i in group]
             else:
-                given = [load(right, sent - h + i - nx, sent) for i in group]
+                given = [load(right, i - nx, h) for i in group]
             for j, mu in enumerate(product(matrix, given)):
                 mus[begin + j] = mu
                 fluxes[begin + j] = (base + field(t, group[j])) * mu
@@ -330,20 +347,29 @@
 
 
 def descent_kernel(nx, devices, sent, lam, prior, start, squares, *refs):
-    sums_ref, descent_ref, *edges = refs if sent else refs[1:]
-    h = STEPS
+    h = STEPS
+    states, forcing = refs[:2] if sent else (None, None)
+    sums_ref, descent_ref, *edges = refs[2:] if sent else refs[1:]
+    wide = halo_widths(True)[0]
+    more = wide - h
+    parts = wide + 2 * more
     total = None
     for i in range(nx):
         value = lam[i] - (load(prior, i, nx) - start[i + 1])
         if sent:
             store(descent_ref, i, nx, value)
-            if i < h:
-                store(edges[0], i, h, value)
-            if i >= nx - h:
-                store(edges[1], i - (nx - h), h, value)
+            if i < wide:
+                store(edges[0], i, parts, value)
+            if i >= nx - wide:
+                store(edges[1], i - (nx - wide), parts, value)
         else:
             descent_ref[i] = value
         total = value * value if total is None else total + value * value
+    for j in range(more if sent else 0):
+        store(edges[0], wide + j, parts, load(states, h + j, nx))
+        store(edges[1], wide + j, parts, load(states, nx - wide + j, nx))
+        store(edges[0], wide + more + j, parts, load(forcing, h - 1 + j, nx))
+        store(edges[1], wide + more + j, parts, load(forcing, nx - wide + 1 + j, nx))
     lane = lax.broadcasted_iota(jnp.int32, (1, LANES), 1)
     sums_ref[...] = jnp.broadcast_to(jnp.where(lane < LANES // 2, squares[...], halve(total)), (devices, LANES))
 
@@ -396,18 +422,18 @@
     moved = d_after = sums = None
     for iteration in range(ITERS):
         updated = iteration > 0
-        sent = 2 * h if updated else h
+        widths = halo_widths(updated)
         ending, start, first, second, third, low, high, *rest = call(
             functools.partial(forward_kernel, nx, updated),
             "forward",
-            [flat(nx), tiles(nx + 2), tiles(nx + 6), tiles(nx + 4), tiles(nx + 2), flat(sent), flat(sent)]
+            [flat(nx), tiles(nx + 2)] + [tiles(nx + 2 * width) for width in widths[1:-1]] + [flat(h)] * 2
             + ([flat(nx), ((1, LANES), f32)] if updated else []),
             [forward, states, forcing, left, right] + (moved + [sums, after, d_after] if updated else []),
-            [pltpu.VMEM((nx + 2 * h, rows, LANES), f32), pltpu.VMEM((nx + 2 * h - 2, rows, LANES), f32)],
+            [pltpu.VMEM((nx + 2 * width, rows, LANES), f32) for width in widths[:2]],
             fast=updated,
         )
         prior = shift(ending, "seg", 1)
-        sides = [shift(high, "space", 1), shift(low, "space", -1)]
+        sides = [] if updated else [shift(high, "space", 1), shift(low, "space", -1)]
         if updated:
             mismatch, squares = rest
         else:
@@ -417,18 +443,18 @@
                 [flat(nx), flat(h), flat(h), ((1, LANES), f32)],
                 [ending, after],
             )
-            sides += [shift(high, "space", 1), shift(low, "space", -1)]
+        sides += [shift(high, "space", 1), shift(low, "space", -1)]
         fields = [start, first, second, third]
         planes = sum(nx - 2 * j for j in range(h))
         inner = call(
-            functools.partial(adjoint_inner_kernel, nx),
+            functools.partial(adjoint_inner_kernel, nx, widths),
             "adjoint_inner",
             [tiles(planes)] * 2,
             [backward, *fields, mismatch],
             [pltpu.VMEM((nx, rows, LANES), f32)] * 2,
         )
         lam = call(
-            functools.partial(adjoint_outer_kernel, nx),
+            functools.partial(adjoint_outer_kernel, nx, widths),
             "adjoint_outer",
             [tiles(nx)],
             [backward, *fields, *inner, *sides],
@@ -437,12 +463,15 @@
         sent = iteration < ITERS - 1
         if not sent:
             kept = call(copy_kernel, "kept", [flat(nx)], [mismatch, inner[0]], specs=[VMEM, pl.BlockSpec(memory_space=pl.ANY)])[0]
+        wide = halo_widths(True)[0]
+        side = flat(wide + 2 * (wide - h))
         sums, descent, *edges = call(
             functools.partial(descent_kernel, nx, devices, sent),
             "descent",
-            [((devices, LANES), f32)] + ([flat(nx), flat(h), flat(h)] if sent else [tiles(nx)]),
-            [lam, prior, start, squares] + ([] if sent else [pltpu.with_memory_space_constraint(kept, pltpu.HBM)]),
-            specs=[VMEM] * 4 + ([] if sent else [pl.BlockSpec(memory_space=pltpu.HBM)]),
+            [((devices, LANES), f32)] + ([flat(nx), side, side] if sent else [tiles(nx)]),
+            [lam, prior, start, squares]
+            + ([states, forcing] if sent else [pltpu.with_memory_space_constraint(kept, pltpu.HBM)]),
+            specs=[VMEM] * 4 + ([VMEM] * 2 if sent else [pl.BlockSpec(memory_space=pltpu.HBM)]),
         )
         sums = lax.all_to_all(sums, BOTH, 0, 0, tiled=True)
         if sent:

time: 62 us -> 61.4 us (level)
  waiting for transfers between devices: 10.7 us -> 9.89 us
    ppermute x14, waiting for transfers between devices: 10.7 us -> 9.89 us  [shift(): lax.ppermute(block, axis, [((i - distance) % devices, i) for i in range(d...]
where the time goes in v7:
time: 61.4 us; the launch traced here: 61.2 us
  starting transfers between devices  20.6 us (34%)
  blocking collectives  18 us (29%)
  Pallas kernels  12.1 us (20%)
  waiting for transfers between devices  9.89 us (16%)
  between operations  0.7 us (1%)
    ppermute x14, starting transfers between devices, shift(): lax.ppermute(block, axis, [((i - distance) % devices, i) for i in range(d...  20.6 us
    all_to_all x2, blocking collectives, per_device(): sums = lax.all_to_all(sums, BOTH, 0, 0, tiled=True)  18 us
    pallas_call x13, Pallas kernels, call(): pl.pallas_call(kernel, name=name, out_shape=[jax.ShapeDtypeStruct(shape,...  12.1 us
    ppermute x14, waiting for transfers between devices, shift(): lax.ppermute(block, axis, [((i - distance) % devices, i) for i in range(d...  9.89 us
  transfers between devices with their start and end apart: 14, of which 6 were waited for; matrix products, arithmetic and copies ran while one was open for 0% of the time, Pallas kernels for 12%

profile of v7, /device:TPU:0, one launch (start us, length us, event | category | flops | bytes accessed | tf_op | source)
XLA Modules:
  0.0 61.2 jit_solution(15396239272017892258)
XLA Ops:
  0.6 1.2 %pack.1 = (f32[455,128]{1,0:T(8,128)S(1)}, f32[455,128]{1,0:T(8,128)S(1)}, f32[520,128]{1,0:T(8,128)S(1)}, f32[520,128]{1,0:T(8,128)S(1)}) custom-call(f32[520,128]{1,0:T(8,128)} %bitcast.33, f32[520,128]{1,0:T(8,128)} %bitcast.34), custom_call_target="tpu_custom_call" | custom-call | tf_op jit(solution)/shard_map/pack/pallas_call | solution.py:41
  1.8 0.5 collective-permute-start
  2.3 2.0 %collective-permute-start.1 = (f32[455,128]{1,0:T(8,128)S(1)}, f32[455,128]{1,0:T(8,128)S(1)}, u32[]{:S(2)}, u32[]{:S(2)}) collective-permute-start(f32[455,128]{1,0:T(8,128)S(1)} %get-tuple-element.42), channel_id=1, source_target_pairs={{1,0},{2,1},{3,2},{0,3},{5,4},{6,5},{7,6},{4,7},{9,8},{10,9},{11,1... | collective-permute-start | bytes 698888 | tf_op jit(solution)/shard_map/ppermute | solution.py:385
  4.4 5.3 %collective-permute-start.2 = (f32[520,128]{1,0:T(8,128)S(1)}, f32[520,128]{1,0:T(8,128)S(1)}, u32[]{:S(2)}, u32[]{:S(2)}) collective-permute-start(f32[520,128]{1,0:T(8,128)S(1)} %get-tuple-element.39.refs_1_.refs_0_), channel_id=1, source_target_pairs={{4,0},{8,4},{12,8},{16,12},{20,16},{24,20},{28,24},{0,28},{5,1},{9... | collective-permute-start | bytes 798728 | tf_op jit(solution)/shard_map/ppermute | solution.py:385
  9.6 0.5 inverse.1
  10.1 0.2 collective-permute-done.1.refs_4_
  10.4 1.5 %forward.2 = (f32[520,128]{1,0:T(8,128)S(1)}, f32[10,72,128]{2,1,0:T(8,128)S(1)}, f32[14,72,128]{2,1,0:T(8,128)S(1)}, f32[12,72,128]{2,1,0:T(8,128)S(1)}, f32[10...) custom-call(bf16[72,240]{1,0:T(8,128)(2,1)S(1)} %get-tuple-element.38.refs_0_, ...), custom_call_target="tpu_custom_call" | custom-call | flops 4000000000 | bytes 1048576 | tf_op jit(solution)/shard_map/forward/pallas_call | solution.py:41
  11.9 1.5 %collective-permute-start.7 = (f32[520,128]{1,0:T(8,128)S(1)}, f32[520,128]{1,0:T(8,128)S(1)}, u32[]{:S(2)}, u32[]{:S(2)}) collective-permute-start(f32[520,128]{1,0:T(8,128)S(1)} %get-tuple-element.48.ending), channel_id=1, source_target_pairs={{28,0},{0,4},{4,8},{8,12},{12,16},{16,20},{20,24},{24,28},{29,1},{... | collective-permute-start | bytes 798728 | tf_op jit(solution)/shard_map/ppermute | solution.py:385
  13.4 0.8 %collective-permute-start.3 = (f32[260,128]{1,0:T(8,128)S(1)}, f32[260,128]{1,0:T(8,128)S(1)}, u32[]{:S(2)}, u32[]{:S(2)}) collective-permute-start(f32[260,128]{1,0:T(8,128)S(1)} %get-tuple-element.52), channel_id=1, source_target_pairs={{3,0},{0,1},{1,2},{2,3},{7,4},{4,5},{5,6},{6,7},{11,8},{8,9},{9,10... | collective-permute-start | bytes 399368 | tf_op jit(solution)/shard_map/ppermute | solution.py:385
  14.2 1.1 %collective-permute-start.4 = (f32[260,128]{1,0:T(8,128)S(1)}, f32[260,128]{1,0:T(8,128)S(1)}, u32[]{:S(2)}, u32[]{:S(2)}) collective-permute-start(f32[260,128]{1,0:T(8,128)S(1)} %get-tuple-element.53), channel_id=1, source_target_pairs={{1,0},{2,1},{3,2},{0,3},{5,4},{6,5},{7,6},{4,7},{9,8},{10,9},{11,1... | collective-permute-start | bytes 399368 | tf_op jit(solution)/shard_map/ppermute | solution.py:385
  15.3 0.2 mismatch.1
  15.6 1.8 %collective-permute-start.6 = (f32[260,128]{1,0:T(8,128)S(1)}, f32[260,128]{1,0:T(8,128)S(1)}, u32[]{:S(2)}, u32[]{:S(2)}) collective-permute-start(f32[260,128]{1,0:T(8,128)S(1)} %get-tuple-element.55), channel_id=1, source_target_pairs={{1,0},{2,1},{3,2},{0,3},{5,4},{6,5},{7,6},{4,7},{9,8},{10,9},{11,1... | collective-permute-start | bytes 399368 | tf_op jit(solution)/shard_map/ppermute | solution.py:385
  17.3 1.0 %adjoint_inner.2 = (f32[20,72,128]{2,1,0:T(8,128)S(1)}, f32[20,72,128]{2,1,0:T(8,128)S(1)}) custom-call(bf16[72,240]{1,0:T(8,128)(2,1)S(1)} %get-tuple-element.43.matrix_ref, f32[10,72,128]{2,1,0:T(8,128)S(1)} %get-tuple-element.44.start, f32[14,72,128]{2,1,0:T(8,128)S(1)} %get-tuple-element.45.first, f32[12,72,128]{2,1,0:T(8,128)S(1)} %get-tuple-element.46.second, ...), custom_call_target="tpu_custom_call" | custom-call | tf_op jit(solution)/shard_map/adjoint_inner/pallas_call | solution.py:41
  18.4 0.9 %collective-permute-done.4.refs_1_ = f32[260,128]{1,0:T(8,128)S(1)} collective-permute-done((f32[260,128]{1,0:T(8,128)S(1)}, f32[260,128]{1,0:T(8,128)S(1)}, u32[]{:S(2)}, u32[]{:S(2)}) %collective-permute-start.4) | collective-permute-done | bytes 133152 | tf_op jit(solution)/shard_map/ppermute | solution.py:385
  19.3 2.2 %collective-permute-done.5.refs_2_ = f32[260,128]{1,0:T(8,128)S(1)} collective-permute-done((f32[260,128]{1,0:T(8,128)S(1)}, f32[260,128]{1,0:T(8,128)S(1)}, u32[]{:S(2)}, u32[]{:S(2)}) %collective-permute-start.5) | collective-permute-done | bytes 133152 | tf_op jit(solution)/shard_map/ppermute | solution.py:385
  21.5 1.2 %adjoint_outer.2.lam = f32[8,72,128]{2,1,0:T(8,128)S(1)} custom-call(bf16[72,240]{1,0:T(8,128)(2,1)S(1)} %get-tuple-element.43.matrix_ref, f32[10,72,128]{2,1,0:T(8,128)S(1)} %get-tuple-element.44.start, f32[14,72,128]{2,1,0:T(8,128)S(1)} %get-tuple-element.45.first, f32[12,72,128]{2,1,0:T(8,128)S(1)} %get-tuple-element.46.second, ...), custom_call_target="tpu_custom_call" | custom-call | tf_op jit(solution)/shard_map/adjoint_outer/pallas_call | solution.py:41
  22.7 1.1 %collective-permute-done.7.prior = f32[520,128]{1,0:T(8,128)S(1)} collective-permute-done((f32[520,128]{1,0:T(8,128)S(1)}, f32[520,128]{1,0:T(8,128)S(1)}, u32[]{:S(2)}, u32[]{:S(2)}) %collective-permute-start.7) | collective-permute-done | bytes 266272 | tf_op jit(solution)/shard_map/ppermute | solution.py:385
  23.8 0.2 descent.2
  24.0 0.4 collective-permute-start.8
  24.4 1.4 %collective-permute-start.9 = (f32[845,128]{1,0:T(8,128)S(1)}, f32[845,128]{1,0:T(8,128)S(1)}, u32[]{:S(2)}, u32[]{:S(2)}) collective-permute-start(f32[845,128]{1,0:T(8,128)S(1)} %get-tuple-element.59), channel_id=1, source_target_pairs={{1,0},{2,1},{3,2},{0,3},{5,4},{6,5},{7,6},{4,7},{9,8},{10,9},{11,1... | collective-permute-start | bytes 1297928 | tf_op jit(solution)/shard_map/ppermute | solution.py:385
  25.8 3.5 %collective-permute-start.10 = (f32[520,128]{1,0:T(8,128)S(1)}, f32[520,128]{1,0:T(8,128)S(1)}, u32[]{:S(2)}, u32[]{:S(2)}) collective-permute-start(f32[520,128]{1,0:T(8,128)S(1)} %get-tuple-element.57.refs_5_), channel_id=1, source_target_pairs={{4,0},{8,4},{12,8},{16,12},{20,16},{24,20},{28,24},{0,28},{5,1},{9... | collective-permute-start | bytes 798728 | tf_op jit(solution)/shard_map/ppermute | solution.py:385
  29.3 9.1 %all_to_all.22 = f32[32,1,128]{2,1,0:T(1,128)S(1)} all-to-all(f32[32,1,128]{2,1,0:T(1,128)S(1)} %bitcast.29), channel_id=1, replica_groups=mesh['seg'=8,'space'=4] {'seg','space'}, dimensions={0} | all-to-all | bytes 32768 | tf_op jit(solution)/shard_map/all_to_all | solution.py:476
  38.4 2.0 %forward.3 = (f32[520,128]{1,0:T(8,128)S(1)}, f32[10,72,128]{2,1,0:T(8,128)S(1)}, f32[20,72,128]{2,1,0:T(8,128)S(1)}, f32[18,72,128]{2,1,0:T(8,128)S(1)}, f32[16...) custom-call(bf16[72,240]{1,0:T(8,128)(2,1)S(1)} %get-tuple-element.3, ...), custom_call_target="tpu_custom_call" | custom-call | tf_op jit(solution)/shard_map/forward/pallas_call | solution.py:41
  40.5 0.6 collective-permute-start.13
  41.0 1.7 %collective-permute-start.12 = (f32[260,128]{1,0:T(8,128)S(1)}, f32[260,128]{1,0:T(8,128)S(1)}, u32[]{:S(2)}, u32[]{:S(2)}) collective-permute-start(f32[260,128]{1,0:T(8,128)S(1)} %get-tuple-element.69), channel_id=1, source_target_pairs={{1,0},{2,1},{3,2},{0,3},{5,4},{6,5},{7,6},{4,7},{9,8},{10,9},{11,1... | collective-permute-start | bytes 399368 | tf_op jit(solution)/shard_map/ppermute | solution.py:385
  42.8 1.0 %adjoint_inner.3 = (f32[20,72,128]{2,1,0:T(8,128)S(1)}, f32[20,72,128]{2,1,0:T(8,128)S(1)}) custom-call(bf16[72,240]{1,0:T(8,128)(2,1)S(1)} %get-tuple-element.43.matrix_ref, f32[10,72,128]{2,1,0:T(8,128)S(1)} %get-tuple-element.61.start, f32[20,72,128]{2,1,0:T(8,128)S(1)} %get-tuple-element.62.first, f32[18,72,128]{2,1,0:T(8,128)S(1)} %get-tuple-element.63.second, ...), custom_call_target="tpu_custom_call" | custom-call | tf_op jit(solution)/shard_map/adjoint_inner/pallas_call | solution.py:41
  43.8 0.7 %kept.1.refs_0_ = f32[520,128]{1,0:T(8,128)} custom-call(f32[520,128]{1,0:T(8,128)S(1)} %get-tuple-element.65.mismatch.given, f32[20,72,128]{2,1,0:T(8,128)S(1)} %get-tuple-element.66.mu_ref.order), custom_call_target="tpu_custom_call" | custom-call | tf_op jit(solution)/shard_map/kept/pallas_call | solution.py:41
  44.6 1.5 %collective-permute-done.11.refs_0_ = f32[260,128]{1,0:T(8,128)S(1)} collective-permute-done((f32[260,128]{1,0:T(8,128)S(1)}, f32[260,128]{1,0:T(8,128)S(1)}, u32[]{:S(2)}, u32[]{:S(2)}) %collective-permute-start.11) | collective-permute-done | bytes 133152 | tf_op jit(solution)/shard_map/ppermute | solution.py:385
  46.1 1.3 %adjoint_outer.3.lam = f32[8,72,128]{2,1,0:T(8,128)S(1)} custom-call(bf16[72,240]{1,0:T(8,128)(2,1)S(1)} %get-tuple-element.43.matrix_ref, f32[10,72,128]{2,1,0:T(8,128)S(1)} %get-tuple-element.61.start, f32[20,72,128]{2,1,0:T(8,128)S(1)} %get-tuple-element.62.first, f32[18,72,128]{2,1,0:T(8,128)S(1)} %get-tuple-element.63.second, ...), custom_call_target="tpu_custom_call" | custom-call | tf_op jit(solution)/shard_map/adjoint_outer/pallas_call | solution.py:41
  47.3 4.0 %collective-permute-done.13.prior = f32[520,128]{1,0:T(8,128)S(1)} collective-permute-done((f32[520,128]{1,0:T(8,128)S(1)}, f32[520,128]{1,0:T(8,128)S(1)}, u32[]{:S(2)}, u32[]{:S(2)}) %collective-permute-start.13) | collective-permute-done | bytes 266272 | tf_op jit(solution)/shard_map/ppermute | solution.py:385
  51.5 8.8 %all_to_all.23 = f32[32,1,128]{2,1,0:T(1,128)S(1)} all-to-all(f32[32,1,128]{2,1,0:T(1,128)S(1)} %bitcast.30), channel_id=1, replica_groups=mesh['seg'=8,'space'=4] {'seg','space'}, dimensions={0} | all-to-all | bytes 32768 | tf_op jit(solution)/shard_map/all_to_all | solution.py:476
  60.4 0.9 %final.1 = f32[520,128]{1,0:T(8,128)} custom-call(f32[10,72,128]{2,1,0:T(8,128)S(1)} %get-tuple-element.61.start, f32[8,72,128]{2,1,0:T(8,128)S(1)} %get-tuple-element.72.descent, f32[32,128]{1,0:T(8,128)S(1)} %bitcast.28), custom_call_target="tpu_custom_call" | custom-call | tf_op jit(solution)/shard_map/final/pallas_call | solution.py:41
  (13 shorter events, 0.2 us)
Async XLA Ops:
  1.8 8.3 %collective-permute-start = (f32[455,128]{1,0:T(8,128)S(1)}, f32[455,128]{1,0:T(8,128)S(1)}, u32[]{:S(2)}, u32[]{:S(2)}) collective-permute-start(f32[455,128]{1,0:T(8,128)S(1)} %get-tuple-element.41), channel_id=1, source_target_pairs={{3,0},{0,1},{1,2},{2,3},{7,4},{4,5},{5,6},{6,7},{11,8},{8,9},{9,10... | collective-permute-start | bytes 698888 | tf_op jit(solution)/shard_map/ppermute | solution.py:385
  2.3 8.0 %collective-permute-start.1 = (f32[455,128]{1,0:T(8,128)S(1)}, f32[455,128]{1,0:T(8,128)S(1)}, u32[]{:S(2)}, u32[]{:S(2)}) collective-permute-start(f32[455,128]{1,0:T(8,128)S(1)} %get-tuple-element.42), channel_id=1, source_target_pairs={{1,0},{2,1},{3,2},{0,3},{5,4},{6,5},{7,6},{4,7},{9,8},{10,9},{11,1... | collective-permute-start | bytes 698888 | tf_op jit(solution)/shard_map/ppermute | solution.py:385
  4.4 5.3 %copy-start = (f32[65]{0:T(128)S(1)}, f32[65]{0:T(128)}, u32[]{:S(2)}) copy-start(f32[65]{0:T(128)} %param.5) | copy-start | bytes 784
  4.4 11.0 %collective-permute-start.2 = (f32[520,128]{1,0:T(8,128)S(1)}, f32[520,128]{1,0:T(8,128)S(1)}, u32[]{:S(2)}, u32[]{:S(2)}) collective-permute-start(f32[520,128]{1,0:T(8,128)S(1)} %get-tuple-element.39.refs_1_.refs_0_), channel_id=1, source_target_pairs={{4,0},{8,4},{12,8},{16,12},{20,16},{24,20},{28,24},{0,28},{5,1},{9... | collective-permute-start | bytes 798728 | tf_op jit(solution)/shard_map/ppermute | solution.py:385
  11.9 11.9 %collective-permute-start.7 = (f32[520,128]{1,0:T(8,128)S(1)}, f32[520,128]{1,0:T(8,128)S(1)}, u32[]{:S(2)}, u32[]{:S(2)}) collective-permute-start(f32[520,128]{1,0:T(8,128)S(1)} %get-tuple-element.48.ending), channel_id=1, source_target_pairs={{28,0},{0,4},{4,8},{8,12},{12,16},{16,20},{20,24},{24,28},{29,1},{... | collective-permute-start | bytes 798728 | tf_op jit(solution)/shard_map/ppermute | solution.py:385
  13.4 5.0 %collective-permute-start.3 = (f32[260,128]{1,0:T(8,128)S(1)}, f32[260,128]{1,0:T(8,128)S(1)}, u32[]{:S(2)}, u32[]{:S(2)}) collective-permute-start(f32[260,128]{1,0:T(8,128)S(1)} %get-tuple-element.52), channel_id=1, source_target_pairs={{3,0},{0,1},{1,2},{2,3},{7,4},{4,5},{5,6},{6,7},{11,8},{8,9},{9,10... | collective-permute-start | bytes 399368 | tf_op jit(solution)/shard_map/ppermute | solution.py:385
  14.2 5.1 %collective-permute-start.4 = (f32[260,128]{1,0:T(8,128)S(1)}, f32[260,128]{1,0:T(8,128)S(1)}, u32[]{:S(2)}, u32[]{:S(2)}) collective-permute-start(f32[260,128]{1,0:T(8,128)S(1)} %get-tuple-element.53), channel_id=1, source_target_pairs={{1,0},{2,1},{3,2},{0,3},{5,4},{6,5},{7,6},{4,7},{9,8},{10,9},{11,1... | collective-permute-start | bytes 399368 | tf_op jit(solution)/shard_map/ppermute | solution.py:385
  15.6 5.9 %collective-permute-start.5 = (f32[260,128]{1,0:T(8,128)S(1)}, f32[260,128]{1,0:T(8,128)S(1)}, u32[]{:S(2)}, u32[]{:S(2)}) collective-permute-start(f32[260,128]{1,0:T(8,128)S(1)} %get-tuple-element.54), channel_id=1, source_target_pairs={{3,0},{0,1},{1,2},{2,3},{7,4},{4,5},{5,6},{6,7},{11,8},{8,9},{9,10... | collective-permute-start | bytes 399368 | tf_op jit(solution)/shard_map/ppermute | solution.py:385
  15.6 5.9 %collective-permute-start.6 = (f32[260,128]{1,0:T(8,128)S(1)}, f32[260,128]{1,0:T(8,128)S(1)}, u32[]{:S(2)}, u32[]{:S(2)}) collective-permute-start(f32[260,128]{1,0:T(8,128)S(1)} %get-tuple-element.55), channel_id=1, source_target_pairs={{1,0},{2,1},{3,2},{0,3},{5,4},{6,5},{7,6},{4,7},{9,8},{10,9},{11,1... | collective-permute-start | bytes 399368 | tf_op jit(solution)/shard_map/ppermute | solution.py:385
  24.0 14.4 %collective-permute-start.8 = (f32[845,128]{1,0:T(8,128)S(1)}, f32[845,128]{1,0:T(8,128)S(1)}, u32[]{:S(2)}, u32[]{:S(2)}) collective-permute-start(f32[845,128]{1,0:T(8,128)S(1)} %get-tuple-element.58), channel_id=1, source_target_pairs={{3,0},{0,1},{1,2},{2,3},{7,4},{4,5},{5,6},{6,7},{11,8},{8,9},{9,10... | collective-permute-start | bytes 1297928 | tf_op jit(solution)/shard_map/ppermute | solution.py:385
  24.4 14.0 %collective-permute-start.9 = (f32[845,128]{1,0:T(8,128)S(1)}, f32[845,128]{1,0:T(8,128)S(1)}, u32[]{:S(2)}, u32[]{:S(2)}) collective-permute-start(f32[845,128]{1,0:T(8,128)S(1)} %get-tuple-element.59), channel_id=1, source_target_pairs={{1,0},{2,1},{3,2},{0,3},{5,4},{6,5},{7,6},{4,7},{9,8},{10,9},{11,1... | collective-permute-start | bytes 1297928 | tf_op jit(solution)/shard_map/ppermute | solution.py:385
  25.8 12.6 %collective-permute-start.10 = (f32[520,128]{1,0:T(8,128)S(1)}, f32[520,128]{1,0:T(8,128)S(1)}, u32[]{:S(2)}, u32[]{:S(2)}) collective-permute-start(f32[520,128]{1,0:T(8,128)S(1)} %get-tuple-element.57.refs_5_), channel_id=1, source_target_pairs={{4,0},{8,4},{12,8},{16,12},{20,16},{24,20},{28,24},{0,28},{5,1},{9... | collective-permute-start | bytes 798728 | tf_op jit(solution)/shard_map/ppermute | solution.py:385
  40.5 10.9 %collective-permute-start.13 = (f32[520,128]{1,0:T(8,128)S(1)}, f32[520,128]{1,0:T(8,128)S(1)}, u32[]{:S(2)}, u32[]{:S(2)}) collective-permute-start(f32[520,128]{1,0:T(8,128)S(1)} %get-tuple-element.70), channel_id=1, source_target_pairs={{28,0},{0,4},{4,8},{8,12},{12,16},{16,20},{20,24},{24,28},{29,1},{... | collective-permute-start | bytes 798728 | tf_op jit(solution)/shard_map/ppermute | solution.py:385
  41.0 5.0 %collective-permute-start.11 = (f32[260,128]{1,0:T(8,128)S(1)}, f32[260,128]{1,0:T(8,128)S(1)}, u32[]{:S(2)}, u32[]{:S(2)}) collective-permute-start(f32[260,128]{1,0:T(8,128)S(1)} %get-tuple-element.68), channel_id=1, source_target_pairs={{3,0},{0,1},{1,2},{2,3},{7,4},{4,5},{5,6},{6,7},{11,8},{8,9},{9,10... | collective-permute-start | bytes 399368 | tf_op jit(solution)/shard_map/ppermute | solution.py:385
  41.0 5.0 %collective-permute-start.12 = (f32[260,128]{1,0:T(8,128)S(1)}, f32[260,128]{1,0:T(8,128)S(1)}, u32[]{:S(2)}, u32[]{:S(2)}) collective-permute-start(f32[260,128]{1,0:T(8,128)S(1)} %get-tuple-element.69), channel_id=1, source_target_pairs={{1,0},{2,1},{3,2},{0,3},{5,4},{6,5},{7,6},{4,7},{9,8},{10,9},{11,1... | collective-permute-start | bytes 399368 | tf_op jit(solution)/shard_map/ppermute | solution.py:385

commit v8 on v7

--- a/solution.py
+++ b/solution.py
@@ -150,8 +150,8 @@
     return row + pltpu.roll(row, LANES // 2, 1)
 
 
-def halo_widths(updated):
-    return (7, 6, 5, 4, 0) if updated else (4, 3, 2, 1, 0)
+WIDTHS = (4, 3, 2, 1, 0)
+WIDE = 7
 
 
 def forward_kernel(nx, updated, *refs):
@@ -160,29 +160,24 @@
     refs = list(refs)
     matrix_ref, states, forcing, left, right = refs[:5]
     del refs[:5]
-    widths = halo_widths(updated)
-    wide, reach = widths[0], widths[1]
+    reach = WIDTHS[1]
     if updated:
-        descent, d_left, d_right, sums, after, d_after = refs[:6]
-        del refs[:6]
+        descent, d_left, d_right, sums = refs[:4]
+        del refs[:4]
         tau = step_size(sums[...])
-    ending_ref, start_ref, first_ref, second_ref, third_ref, low_ref, high_ref = refs[:7]
+    ending_ref, start_ref, first_ref, second_ref, third_ref = refs[:5]
     u0, q = refs[-2:]
     points = states.shape[0] // nx
     rows = padded(points, 8)
     scale = PUSHED / SPREAD
-    more = wide - h
-    parts = wide + 2 * more
-    for j in range(wide):
-        if j < h:
-            before, ahead = load(left, h - 1 - j, m), load(right, j, m)
-        else:
-            before, ahead = load(d_left, wide + wide - 1 - j, parts), load(d_right, wide + j - h, parts)
+    parts = WIDE + 2 * (WIDE - h)
+    for j in range(h):
+        before, ahead = load(left, h - 1 - j, m), load(right, j, m)
         if updated:
-            before = before - tau * load(d_left, wide - 1 - j, parts)
+            before = before - tau * load(d_left, WIDE - 1 - j, parts)
             ahead = ahead - tau * load(d_right, j, parts)
-        u0[wide - 1 - j] = before
-        u0[wide + nx + j] = ahead
+        u0[h - 1 - j] = before
+        u0[h + nx + j] = ahead
         if j == 0:
             start_ref[0] = before
             start_ref[nx + 1] = ahead
@@ -190,16 +185,11 @@
         here = load(states, i, nx)
         if updated:
             here = here - tau * load(descent, i, nx)
-        u0[wide + i] = here
+        u0[h + i] = here
         start_ref[1 + i] = here
     for j in range(reach):
-        if j < h - 1:
-            before, ahead = load(left, m - 1 - j, m), load(right, h + j, m)
-        else:
-            before = load(d_left, parts - 1 - (j - h + 1), parts)
-            ahead = load(d_right, wide + more + j - h + 1, parts)
-        q[reach - 1 - j] = scale * before
-        q[reach + nx + j] = scale * ahead
+        q[reach - 1 - j] = scale * load(left, m - 1 - j, m)
+        q[reach + nx + j] = scale * load(right, h + j, m)
     for i in range(nx):
         q[reach + i] = scale * load(forcing, i, nx)
     base = wall_profile(points, rows)
@@ -207,14 +197,14 @@
     fields = [u0, first_ref, second_ref, third_ref, None]
     for t in range(h):
         source, target = fields[t], fields[t + 1]
-        count = nx + 2 * widths[t + 1]
-        inset = widths[t] - widths[t + 1]
+        count = nx + 2 * WIDTHS[t + 1]
+        inset = WIDTHS[t] - WIDTHS[t + 1]
         window = [source[inset - 1], source[inset]]
         pending = []
         for i in range(count):
             window = window[-2:] + [source[inset + i + 1]]
             before, here, ahead = window
-            force = q[i + reach - widths[t + 1]]
+            force = q[i + reach - WIDTHS[t + 1]]
             pending.append(
                 3.0 * here + neighbours(here) + force - (base + here) * (ahead - before) * (0.5 * ADVECT / SPREAD)
             )
@@ -226,19 +216,8 @@
                     else:
                         store(ending_ref, at, nx, plane)
                 pending = []
-    if updated:
-        mismatch_ref, squares_ref = refs[7:9]
-        total = None
-        for i in range(nx):
-            value = load(ending_ref, i, nx) - (load(after, i, nx) - tau * load(d_after, i, nx))
-            store(mismatch_ref, i, nx, value)
-            if i < h:
-                store(low_ref, i, h, value)
-            if i >= nx - h:
-                store(high_ref, i - (nx - h), h, value)
-            total = value * value if total is None else total + value * value
-        squares_ref[...] = halve(total)
-    else:
+    if not updated:
+        low_ref, high_ref = refs[5:7]
         for i in range(h - 1):
             store(low_ref, i, h, third_ref[1 + 1 + i])
             store(high_ref, i, h, third_ref[1 + nx - h + i])
@@ -246,11 +225,72 @@
         store(high_ref, h - 1, h, second_ref[2 + nx - 3])
 
 
-def mismatch_kernel(nx, ending, after, mismatch_ref, low_ref, high_ref, squares_ref):
-    h = STEPS
+def wide_kernel(nx, matrix_ref, left, right, d_left, d_right, sums, first, second, left_fields, right_fields):
+    h = STEPS
+    m = 2 * h - 1
+    more = WIDE - h
+    parts = WIDE + 2 * more
+    points = left.shape[0] // m
+    base = wall_profile(points, padded(points, 8))
+    matrix = matrix_ref[...]
+    tau = step_size(sums[...])
+    scale = PUSHED / SPREAD
+
+    def state(side, d):
+        if side == 0:
+            value = load(left, h - d, m) if d <= h else load(d_left, WIDE + WIDE - d, parts)
+            return value - tau * load(d_left, WIDE - d, parts)
+        value = load(right, d - 1, m) if d <= h else load(d_right, WIDE + d - 1 - h, parts)
+        return value - tau * load(d_right, d - 1, parts)
+
+    def push(side, d):
+        if side == 0:
+            return scale * (load(left, m - d, m) if d < h else load(d_left, parts - 1 - (d - h), parts))
+        return scale * (load(right, h + d - 1, m) if d < h else load(d_right, WIDE + more + d - h, parts))
+
+    u = [{d: state(side, d) for d in range(h - 1, WIDE + 1)} for side in range(2)]
+    for t in range(3):
+        reach = WIDE - t
+        pushed, places = [], []
+        for side in range(2):
+            sign = 1.0 if side else -1.0
+            for d in range(reach - 3, reach):
+                here = u[side][d]
+                slope = sign * (u[side][d + 1] - u[side][d - 1])
+                pushed.append(
+                    3.0 * here + neighbours(here) + push(side, d) - (base + here) * slope * (0.5 * ADVECT / SPREAD)
+                )
+                places.append((side, d))
+        out = [{}, {}]
+        for k in range(0, len(places), 2):
+            for (side, d), plane in zip(places[k : k + 2], product(matrix, pushed[k : k + 2])):
+                out[side][d] = plane
+        for d in range(reach - 5, reach - 3):
+            if t == 0:
+                out[0][d], out[1][d] = first[WIDTHS[1] - d], first[WIDTHS[1] + nx - 1 + d]
+            elif t == 1:
+                out[0][d], out[1][d] = second[WIDTHS[2] - d], second[WIDTHS[2] + nx - 1 + d]
+        u = out
+        if t == 1:
+            store(left_fields, h - 1, h, u[0][3])
+            store(right_fields, h - 1, h, u[1][3])
+    for d in range(2, h + 1):
+        store(left_fields, h - d, h, u[0][d])
+        store(right_fields, d - 2, h, u[1][d])
+
+
+def mismatch_kernel(nx, updated, *refs):
+    h = STEPS
+    ending, after, *given = refs[:-4]
+    mismatch_ref, low_ref, high_ref, squares_ref = refs[-4:]
+    if updated:
+        tau = step_size(given[1][...])
     total = None
     for i in range(nx):
-        value = load(ending, i, nx) - load(after, i, nx)
+        value = load(after, i, nx)
+        if updated:
+            value = value - tau * load(given[0], i, nx)
+        value = load(ending, i, nx) - value
         store(mismatch_ref, i, nx, value)
         if i < h:
             store(low_ref, i, h, value)
@@ -265,8 +305,8 @@
     return SPREAD * (3.0 * m1 + neighbours(m1)) + (0.5 * ADVECT) * ((f2 - f0) - m1 * (u2 - u0))
 
 
-def own_field(fields, widths, t, i):
-    return fields[t][i + (widths[t] if t else 1)]
+def own_field(fields, t, i):
+    return fields[t][i + (WIDTHS[t] if t else 1)]
 
 
 def inner_range(nx, t):
@@ -274,7 +314,7 @@
     return low, nx - low, sum(nx - 2 * j for j in range(low))
 
 
-def adjoint_inner_kernel(nx, widths, matrix_ref, start, first, second, third, mismatch, mu_ref, flux_ref, a, b):
+def adjoint_inner_kernel(nx, matrix_ref, start, first, second, third, mismatch, mu_ref, flux_ref, a, b):
     h = STEPS
     points = mismatch.shape[0] // nx
     base = wall_profile(points, padded(points, 8))
@@ -287,7 +327,7 @@
             group = list(range(begin, min(begin + 2, high)))
             lams = [load(mismatch, i, nx) if t == h - 1 else source[i] for i in group]
             for i, mu in zip(group, product(matrix, lams)):
-                u = own_field((start, first, second, third), widths, t, i)
+                u = own_field((start, first, second, third), t, i)
                 flux = (base + u) * mu
                 mu_ref[at + i - low] = mu
                 flux_ref[at + i - low] = flux
@@ -296,26 +336,24 @@
                     target[i - 1] = adjoint_value(*window)
 
 
-def adjoint_outer_kernel(nx, widths, matrix_ref, start, first, second, third, mu_ref, flux_ref, *refs):
+def adjoint_outer_kernel(nx, matrix_ref, start, first, second, third, mu_ref, flux_ref, *refs):
     h = STEPS
     *sides, lam_ref, lams, mus, fluxes = refs
     points = sides[0].shape[0] // h
-    left, right = sides[-2:]
+    left_fields, right_fields, left, right = sides
     base = wall_profile(points, padded(points, 8))
     matrix = matrix_ref[...]
 
     def field(t, i):
-        if len(sides) > 2:
-            left_fields, right_fields = sides[:2]
-            if t == 2 and i == -3:
-                return load(left_fields, h - 1, h)
-            if t == 2 and i == nx + 2:
-                return load(right_fields, h - 1, h)
-            if t == 3 and i < -1:
-                return load(left_fields, i + h, h)
-            if t == 3 and i > nx:
-                return load(right_fields, i - nx - 1, h)
-        return own_field((start, first, second, third), widths, t, i)
+        if t == 2 and i == -3:
+            return load(left_fields, h - 1, h)
+        if t == 2 and i == nx + 2:
+            return load(right_fields, h - 1, h)
+        if t == 3 and i < -1:
+            return load(left_fields, i + h, h)
+        if t == 3 and i > nx:
+            return load(right_fields, i - nx - 1, h)
+        return own_field((start, first, second, third), t, i)
 
     for t in reversed(range(h)):
         low, high, at = inner_range(nx, t)
@@ -350,7 +388,7 @@
     h = STEPS
     states, forcing = refs[:2] if sent else (None, None)
     sums_ref, descent_ref, *edges = refs[2:] if sent else refs[1:]
-    wide = halo_widths(True)[0]
+    wide = WIDE
     more = wide - h
     parts = wide + 2 * more
     total = None
@@ -422,39 +460,44 @@
     moved = d_after = sums = None
     for iteration in range(ITERS):
         updated = iteration > 0
-        widths = halo_widths(updated)
-        ending, start, first, second, third, low, high, *rest = call(
+        ending, start, first, second, third, *sides = call(
             functools.partial(forward_kernel, nx, updated),
             "forward",
-            [flat(nx), tiles(nx + 2)] + [tiles(nx + 2 * width) for width in widths[1:-1]] + [flat(h)] * 2
-            + ([flat(nx), ((1, LANES), f32)] if updated else []),
-            [forward, states, forcing, left, right] + (moved + [sums, after, d_after] if updated else []),
-            [pltpu.VMEM((nx + 2 * width, rows, LANES), f32) for width in widths[:2]],
+            [flat(nx), tiles(nx + 2)]
+            + [tiles(nx + 2 * width) for width in WIDTHS[1:-1]]
+            + ([] if updated else [flat(h)] * 2),
+            [forward, states, forcing, left, right] + (moved + [sums] if updated else []),
+            [pltpu.VMEM((nx + 2 * width, rows, LANES), f32) for width in WIDTHS[:2]],
             fast=updated,
         )
         prior = shift(ending, "seg", 1)
-        sides = [] if updated else [shift(high, "space", 1), shift(low, "space", -1)]
         if updated:
-            mismatch, squares = rest
+            sides = call(
+                functools.partial(wide_kernel, nx),
+                "wide",
+                [flat(h)] * 2,
+                [forward, left, right, *moved[1:], sums, first, second],
+            )
         else:
-            mismatch, low, high, squares = call(
-                functools.partial(mismatch_kernel, nx),
-                "mismatch",
-                [flat(nx), flat(h), flat(h), ((1, LANES), f32)],
-                [ending, after],
-            )
-        sides += [shift(high, "space", 1), shift(low, "space", -1)]
+            sides = [shift(sides[1], "space", 1), shift(sides[0], "space", -1)]
+        mismatch, low, high, squares = call(
+            functools.partial(mismatch_kernel, nx, updated),
+            "mismatch",
+            [flat(nx), flat(h), flat(h), ((1, LANES), f32)],
+            [ending, after] + ([d_after, sums] if updated else []),
+        )
+        sides = [*sides, shift(high, "space", 1), shift(low, "space", -1)]
         fields = [start, first, second, third]
         planes = sum(nx - 2 * j for j in range(h))
         inner = call(
-            functools.partial(adjoint_inner_kernel, nx, widths),
+            functools.partial(adjoint_inner_kernel, nx),
             "adjoint_inner",
             [tiles(planes)] * 2,
             [backward, *fields, mismatch],
             [pltpu.VMEM((nx, rows, LANES), f32)] * 2,
         )
         lam = call(
-            functools.partial(adjoint_outer_kernel, nx, widths),
+            functools.partial(adjoint_outer_kernel, nx),
             "adjoint_outer",
             [tiles(nx)],
             [backward, *fields, *inner, *sides],
@@ -463,8 +506,7 @@
         sent = iteration < ITERS - 1
         if not sent:
             kept = call(copy_kernel, "kept", [flat(nx)], [mismatch, inner[0]], specs=[VMEM, pl.BlockSpec(memory_space=pl.ANY)])[0]
-        wide = halo_widths(True)[0]
-        side = flat(wide + 2 * (wide - h))
+        side = flat(WIDE + 2 * (WIDE - h))
         sums, descent, *edges = call(
             functools.partial(descent_kernel, nx, devices, sent),
             "descent",

time: 61.4 us -> 61.1 us (level)
  waiting for transfers between devices: 9.89 us -> 8.51 us
  Pallas kernels: 12.1 us -> 13.1 us
    ppermute x14, waiting for transfers between devices: 9.89 us -> 8.51 us  [shift(): lax.ppermute(block, axis, [((i - distance) % devices, i) for i in range(d...]
    pallas_call x13 -> x15, Pallas kernels: 12.1 us -> 13.1 us  [call(): pl.pallas_call(kernel, name=name, out_shape=[jax.ShapeDtypeStruct(shape,...]
  transfers between devices with their start and end apart: 14 -> 14, of which waited for: 6 -> 6; matrix products, arithmetic and copies ran while one was open for 0% -> 0% of each run, Pallas kernels for 12% -> 17%
where the time goes in v8:
time: 61.1 us; the launch traced here: 60.9 us
  starting transfers between devices  20.6 us (34%)
  blocking collectives  18 us (29%)
  Pallas kernels  13.1 us (21%)
  waiting for transfers between devices  8.51 us (14%)
  between operations  0.71 us (1%)
    ppermute x14, starting transfers between devices, shift(): lax.ppermute(block, axis, [((i - distance) % devices, i) for i in range(d...  20.6 us
    all_to_all x2, blocking collectives, per_device(): sums = lax.all_to_all(sums, BOTH, 0, 0, tiled=True)  18 us
    pallas_call x15, Pallas kernels, call(): pl.pallas_call(kernel, name=name, out_shape=[jax.ShapeDtypeStruct(shape,...  13.1 us
    ppermute x14, waiting for transfers between devices, shift(): lax.ppermute(block, axis, [((i - distance) % devices, i) for i in range(d...  8.51 us
  transfers between devices with their start and end apart: 14, of which 6 were waited for; matrix products, arithmetic and copies ran while one was open for 0% of the time, Pallas kernels for 17%

profile of v8, /device:TPU:0, one launch (start us, length us, event | category | flops | bytes accessed | tf_op | source)
XLA Modules:
  0.0 60.9 jit_solution(8085049874841148100)
XLA Ops:
  0.6 1.2 %pack.1 = (f32[455,128]{1,0:T(8,128)S(1)}, f32[455,128]{1,0:T(8,128)S(1)}, f32[520,128]{1,0:T(8,128)S(1)}, f32[520,128]{1,0:T(8,128)S(1)}) custom-call(f32[520,128]{1,0:T(8,128)} %bitcast.35, f32[520,128]{1,0:T(8,128)} %bitcast.36), custom_call_target="tpu_custom_call" | custom-call | tf_op jit(solution)/shard_map/pack/pallas_call | solution.py:41
  1.8 0.5 collective-permute-start
  2.3 2.0 %collective-permute-start.1 = (f32[455,128]{1,0:T(8,128)S(1)}, f32[455,128]{1,0:T(8,128)S(1)}, u32[]{:S(2)}, u32[]{:S(2)}) collective-permute-start(f32[455,128]{1,0:T(8,128)S(1)} %get-tuple-element.44), channel_id=1, source_target_pairs={{1,0},{2,1},{3,2},{0,3},{5,4},{6,5},{7,6},{4,7},{9,8},{10,9},{11,1... | collective-permute-start | bytes 698888 | tf_op jit(solution)/shard_map/ppermute | solution.py:423
  4.4 5.3 %collective-permute-start.2 = (f32[520,128]{1,0:T(8,128)S(1)}, f32[520,128]{1,0:T(8,128)S(1)}, u32[]{:S(2)}, u32[]{:S(2)}) collective-permute-start(f32[520,128]{1,0:T(8,128)S(1)} %get-tuple-element.41.refs_1_.refs_0_), channel_id=1, source_target_pairs={{4,0},{8,4},{12,8},{16,12},{20,16},{24,20},{28,24},{0,28},{5,1},{9... | collective-permute-start | bytes 798728 | tf_op jit(solution)/shard_map/ppermute | solution.py:423
  9.6 0.5 inverse.1
  10.4 1.5 %forward.2 = (f32[520,128]{1,0:T(8,128)S(1)}, f32[10,72,128]{2,1,0:T(8,128)S(1)}, f32[14,72,128]{2,1,0:T(8,128)S(1)}, f32[12,72,128]{2,1,0:T(8,128)S(1)}, f32[10...) custom-call(bf16[72,240]{1,0:T(8,128)(2,1)S(1)} %get-tuple-element.40.refs_0_.matrix_ref, ...), custom_call_target="tpu_custom_call" | custom-call | flops 4000000000 | bytes 1048576 | tf_op jit(solution)/shard_map/forward/pallas_call | solution.py:41
  11.9 1.5 %collective-permute-start.7 = (f32[520,128]{1,0:T(8,128)S(1)}, f32[520,128]{1,0:T(8,128)S(1)}, u32[]{:S(2)}, u32[]{:S(2)}) collective-permute-start(f32[520,128]{1,0:T(8,128)S(1)} %get-tuple-element.50.refs_0_), channel_id=1, source_target_pairs={{28,0},{0,4},{4,8},{8,12},{12,16},{16,20},{20,24},{24,28},{29,1},{... | collective-permute-start | bytes 798728 | tf_op jit(solution)/shard_map/ppermute | solution.py:423
  13.4 0.8 %collective-permute-start.3 = (f32[260,128]{1,0:T(8,128)S(1)}, f32[260,128]{1,0:T(8,128)S(1)}, u32[]{:S(2)}, u32[]{:S(2)}) collective-permute-start(f32[260,128]{1,0:T(8,128)S(1)} %get-tuple-element.54), channel_id=1, source_target_pairs={{3,0},{0,1},{1,2},{2,3},{7,4},{4,5},{5,6},{6,7},{11,8},{8,9},{9,10... | collective-permute-start | bytes 399368 | tf_op jit(solution)/shard_map/ppermute | solution.py:423
  14.2 1.1 %collective-permute-start.4 = (f32[260,128]{1,0:T(8,128)S(1)}, f32[260,128]{1,0:T(8,128)S(1)}, u32[]{:S(2)}, u32[]{:S(2)}) collective-permute-start(f32[260,128]{1,0:T(8,128)S(1)} %get-tuple-element.55), channel_id=1, source_target_pairs={{1,0},{2,1},{3,2},{0,3},{5,4},{6,5},{7,6},{4,7},{9,8},{10,9},{11,1... | collective-permute-start | bytes 399368 | tf_op jit(solution)/shard_map/ppermute | solution.py:423
  15.3 0.2 mismatch.2
  15.6 1.8 %collective-permute-start.6 = (f32[260,128]{1,0:T(8,128)S(1)}, f32[260,128]{1,0:T(8,128)S(1)}, u32[]{:S(2)}, u32[]{:S(2)}) collective-permute-start(f32[260,128]{1,0:T(8,128)S(1)} %get-tuple-element.57), channel_id=1, source_target_pairs={{1,0},{2,1},{3,2},{0,3},{5,4},{6,5},{7,6},{4,7},{9,8},{10,9},{11,1... | collective-permute-start | bytes 399368 | tf_op jit(solution)/shard_map/ppermute | solution.py:423
  17.3 1.1 %adjoint_inner.2 = (f32[20,72,128]{2,1,0:T(8,128)S(1)}, f32[20,72,128]{2,1,0:T(8,128)S(1)}) custom-call(bf16[72,240]{1,0:T(8,128)(2,1)S(1)} %get-tuple-element.45.matrix_ref, f32[10,72,128]{2,1,0:T(8,128)S(1)} %get-tuple-element.46.start, f32[14,72,128]{2,1,0:T(8,128)S(1)} %get-tuple-element.47.first, f32[12,72,128]{2,1,0:T(8,128)S(1)} %get-tuple-element.48.second, ...), custom_call_target="tpu_custom_call" | custom-call | tf_op jit(solution)/shard_map/adjoint_inner/pallas_call | solution.py:41
  18.4 0.9 %collective-permute-done.4.refs_1_ = f32[260,128]{1,0:T(8,128)S(1)} collective-permute-done((f32[260,128]{1,0:T(8,128)S(1)}, f32[260,128]{1,0:T(8,128)S(1)}, u32[]{:S(2)}, u32[]{:S(2)}) %collective-permute-start.4) | collective-permute-done | bytes 133152 | tf_op jit(solution)/shard_map/ppermute | solution.py:423
  19.3 2.2 %collective-permute-done.5.refs_2_ = f32[260,128]{1,0:T(8,128)S(1)} collective-permute-done((f32[260,128]{1,0:T(8,128)S(1)}, f32[260,128]{1,0:T(8,128)S(1)}, u32[]{:S(2)}, u32[]{:S(2)}) %collective-permute-start.5) | collective-permute-done | bytes 133152 | tf_op jit(solution)/shard_map/ppermute | solution.py:423
  21.5 1.2 %adjoint_outer.2.lam = f32[8,72,128]{2,1,0:T(8,128)S(1)} custom-call(bf16[72,240]{1,0:T(8,128)(2,1)S(1)} %get-tuple-element.45.matrix_ref, f32[10,72,128]{2,1,0:T(8,128)S(1)} %get-tuple-element.46.start, f32[14,72,128]{2,1,0:T(8,128)S(1)} %get-tuple-element.47.first, f32[12,72,128]{2,1,0:T(8,128)S(1)} %get-tuple-element.48.second, ...), custom_call_target="tpu_custom_call" | custom-call | tf_op jit(solution)/shard_map/adjoint_outer/pallas_call | solution.py:41
  22.7 1.1 %collective-permute-done.7.prior = f32[520,128]{1,0:T(8,128)S(1)} collective-permute-done((f32[520,128]{1,0:T(8,128)S(1)}, f32[520,128]{1,0:T(8,128)S(1)}, u32[]{:S(2)}, u32[]{:S(2)}) %collective-permute-start.7) | collective-permute-done | bytes 266272 | tf_op jit(solution)/shard_map/ppermute | solution.py:423
  24.0 0.4 collective-permute-start.8
  24.4 1.4 %collective-permute-start.9 = (f32[845,128]{1,0:T(8,128)S(1)}, f32[845,128]{1,0:T(8,128)S(1)}, u32[]{:S(2)}, u32[]{:S(2)}) collective-permute-start(f32[845,128]{1,0:T(8,128)S(1)} %get-tuple-element.61), channel_id=1, source_target_pairs={{1,0},{2,1},{3,2},{0,3},{5,4},{6,5},{7,6},{4,7},{9,8},{10,9},{11,1... | collective-permute-start | bytes 1297928 | tf_op jit(solution)/shard_map/ppermute | solution.py:423
  25.8 3.5 %collective-permute-start.10 = (f32[520,128]{1,0:T(8,128)S(1)}, f32[520,128]{1,0:T(8,128)S(1)}, u32[]{:S(2)}, u32[]{:S(2)}) collective-permute-start(f32[520,128]{1,0:T(8,128)S(1)} %get-tuple-element.59.refs_5_), channel_id=1, source_target_pairs={{4,0},{8,4},{12,8},{16,12},{20,16},{24,20},{28,24},{0,28},{5,1},{9... | collective-permute-start | bytes 798728 | tf_op jit(solution)/shard_map/ppermute | solution.py:423
  29.3 9.1 %all_to_all.22 = f32[32,1,128]{2,1,0:T(1,128)S(1)} all-to-all(f32[32,1,128]{2,1,0:T(1,128)S(1)} %bitcast.31), channel_id=1, replica_groups=mesh['seg'=8,'space'=4] {'seg','space'}, dimensions={0} | all-to-all | bytes 32768 | tf_op jit(solution)/shard_map/all_to_all | solution.py:518
  38.4 1.7 %forward.3 = (f32[520,128]{1,0:T(8,128)S(1)}, f32[10,72,128]{2,1,0:T(8,128)S(1)}, f32[14,72,128]{2,1,0:T(8,128)S(1)}, f32[12,72,128]{2,1,0:T(8,128)S(1)}, f32[10,72,128]{2,1,0:T(8,128)S(1)}) custom-call(bf16[72,240]{1,0:T(8,128)(2,1)S(1)} %get-tuple-element.40.refs_0_.matrix_ref, f32[520,128]{1,0:T(8,128)S(1)} %get-tuple-element.41.refs_1_.refs_0_, ...), custom_call_target="tpu_custom_call" | custom-call | tf_op jit(solution)/shard_map/forward/pallas_call | solution.py:41
  40.1 0.6 %collective-permute-start.13 = (f32[520,128]{1,0:T(8,128)S(1)}, f32[520,128]{1,0:T(8,128)S(1)}, u32[]{:S(2)}, u32[]{:S(2)}) collective-permute-start(f32[520,128]{1,0:T(8,128)S(1)} %get-tuple-element.67.refs_0_), channel_id=1, source_target_pairs={{28,0},{0,4},{4,8},{8,12},{12,16},{16,20},{20,24},{24,28},{29,1},{... | collective-permute-start | bytes 798728 | tf_op jit(solution)/shard_map/ppermute | solution.py:423
  40.7 0.4 mismatch.3
  41.1 1.8 %collective-permute-start.12 = (f32[260,128]{1,0:T(8,128)S(1)}, f32[260,128]{1,0:T(8,128)S(1)}, u32[]{:S(2)}, u32[]{:S(2)}) collective-permute-start(f32[260,128]{1,0:T(8,128)S(1)} %get-tuple-element.74), channel_id=1, source_target_pairs={{1,0},{2,1},{3,2},{0,3},{5,4},{6,5},{7,6},{4,7},{9,8},{10,9},{11,1... | collective-permute-start | bytes 399368 | tf_op jit(solution)/shard_map/ppermute | solution.py:423
  42.8 1.1 %adjoint_inner.3 = (f32[20,72,128]{2,1,0:T(8,128)S(1)}, f32[20,72,128]{2,1,0:T(8,128)S(1)}) custom-call(bf16[72,240]{1,0:T(8,128)(2,1)S(1)} %get-tuple-element.45.matrix_ref, f32[10,72,128]{2,1,0:T(8,128)S(1)} %get-tuple-element.63.start, f32[14,72,128]{2,1,0:T(8,128)S(1)} %get-tuple-element.64.first, f32[12,72,128]{2,1,0:T(8,128)S(1)} %get-tuple-element.65.second, ...), custom_call_target="tpu_custom_call" | custom-call | tf_op jit(solution)/shard_map/adjoint_inner/pallas_call | solution.py:41
  43.9 0.7 %kept.1.refs_0_ = f32[520,128]{1,0:T(8,128)} custom-call(f32[520,128]{1,0:T(8,128)S(1)} %get-tuple-element.68.mismatch.given, f32[20,72,128]{2,1,0:T(8,128)S(1)} %get-tuple-element.69.mu_ref.order), custom_call_target="tpu_custom_call" | custom-call | tf_op jit(solution)/shard_map/kept/pallas_call | solution.py:41
  44.6 1.0 %wide.1 = (f32[260,128]{1,0:T(8,128)S(1)}, f32[260,128]{1,0:T(8,128)S(1)}) custom-call(bf16[72,240]{1,0:T(8,128)(2,1)S(1)} %get-tuple-element.40.refs_0_.matrix_ref, f32[455,128]{1,0:T(8,128)S(1)} %collective-permute-done.refs_3_.left, f32[455,128]{1,0:T(8,128)S(1)} %collective-permute-done.1.refs_4_.right, ...), custom_call_target="tpu_custom_call" | custom-call | tf_op jit(solution)/shard_map/wide/pallas_call | solution.py:41
  45.6 0.5 collective-permute-done.11.refs_2_
  46.1 1.2 %adjoint_outer.3.lam = f32[8,72,128]{2,1,0:T(8,128)S(1)} custom-call(bf16[72,240]{1,0:T(8,128)(2,1)S(1)} %get-tuple-element.45.matrix_ref, f32[10,72,128]{2,1,0:T(8,128)S(1)} %get-tuple-element.63.start, f32[14,72,128]{2,1,0:T(8,128)S(1)} %get-tuple-element.64.first, f32[12,72,128]{2,1,0:T(8,128)S(1)} %get-tuple-element.65.second, ...), custom_call_target="tpu_custom_call" | custom-call | tf_op jit(solution)/shard_map/adjoint_outer/pallas_call | solution.py:41
  47.3 3.7 %collective-permute-done.13.prior = f32[520,128]{1,0:T(8,128)S(1)} collective-permute-done((f32[520,128]{1,0:T(8,128)S(1)}, f32[520,128]{1,0:T(8,128)S(1)}, u32[]{:S(2)}, u32[]{:S(2)}) %collective-permute-start.13) | collective-permute-done | bytes 266272 | tf_op jit(solution)/shard_map/ppermute | solution.py:423
  51.2 8.8 %all_to_all.23 = f32[32,1,128]{2,1,0:T(1,128)S(1)} all-to-all(f32[32,1,128]{2,1,0:T(1,128)S(1)} %bitcast.32), channel_id=1, replica_groups=mesh['seg'=8,'space'=4] {'seg','space'}, dimensions={0} | all-to-all | bytes 32768 | tf_op jit(solution)/shard_map/all_to_all | solution.py:518
  60.0 0.9 %final.1 = f32[520,128]{1,0:T(8,128)} custom-call(f32[10,72,128]{2,1,0:T(8,128)S(1)} %get-tuple-element.63.start, f32[8,72,128]{2,1,0:T(8,128)S(1)} %get-tuple-element.76.descent, f32[32,128]{1,0:T(8,128)S(1)} %bitcast.30), custom_call_target="tpu_custom_call" | custom-call | tf_op jit(solution)/shard_map/final/pallas_call | solution.py:41
  (15 shorter events, 0.7 us)
Async XLA Ops:
  1.8 8.3 %collective-permute-start = (f32[455,128]{1,0:T(8,128)S(1)}, f32[455,128]{1,0:T(8,128)S(1)}, u32[]{:S(2)}, u32[]{:S(2)}) collective-permute-start(f32[455,128]{1,0:T(8,128)S(1)} %get-tuple-element.43), channel_id=1, source_target_pairs={{3,0},{0,1},{1,2},{2,3},{7,4},{4,5},{5,6},{6,7},{11,8},{8,9},{9,10... | collective-permute-start | bytes 698888 | tf_op jit(solution)/shard_map/ppermute | solution.py:423
  2.3 8.0 %collective-permute-start.1 = (f32[455,128]{1,0:T(8,128)S(1)}, f32[455,128]{1,0:T(8,128)S(1)}, u32[]{:S(2)}, u32[]{:S(2)}) collective-permute-start(f32[455,128]{1,0:T(8,128)S(1)} %get-tuple-element.44), channel_id=1, source_target_pairs={{1,0},{2,1},{3,2},{0,3},{5,4},{6,5},{7,6},{4,7},{9,8},{10,9},{11,1... | collective-permute-start | bytes 698888 | tf_op jit(solution)/shard_map/ppermute | solution.py:423
  4.4 5.3 %copy-start = (f32[65]{0:T(128)S(1)}, f32[65]{0:T(128)}, u32[]{:S(2)}) copy-start(f32[65]{0:T(128)} %param.5) | copy-start | bytes 784
  4.4 11.0 %collective-permute-start.2 = (f32[520,128]{1,0:T(8,128)S(1)}, f32[520,128]{1,0:T(8,128)S(1)}, u32[]{:S(2)}, u32[]{:S(2)}) collective-permute-start(f32[520,128]{1,0:T(8,128)S(1)} %get-tuple-element.41.refs_1_.refs_0_), channel_id=1, source_target_pairs={{4,0},{8,4},{12,8},{16,12},{20,16},{24,20},{28,24},{0,28},{5,1},{9... | collective-permute-start | bytes 798728 | tf_op jit(solution)/shard_map/ppermute | solution.py:423
  11.9 11.9 %collective-permute-start.7 = (f32[520,128]{1,0:T(8,128)S(1)}, f32[520,128]{1,0:T(8,128)S(1)}, u32[]{:S(2)}, u32[]{:S(2)}) collective-permute-start(f32[520,128]{1,0:T(8,128)S(1)} %get-tuple-element.50.refs_0_), channel_id=1, source_target_pairs={{28,0},{0,4},{4,8},{8,12},{12,16},{16,20},{20,24},{24,28},{29,1},{... | collective-permute-start | bytes 798728 | tf_op jit(solution)/shard_map/ppermute | solution.py:423
  13.4 5.0 %collective-permute-start.3 = (f32[260,128]{1,0:T(8,128)S(1)}, f32[260,128]{1,0:T(8,128)S(1)}, u32[]{:S(2)}, u32[]{:S(2)}) collective-permute-start(f32[260,128]{1,0:T(8,128)S(1)} %get-tuple-element.54), channel_id=1, source_target_pairs={{3,0},{0,1},{1,2},{2,3},{7,4},{4,5},{5,6},{6,7},{11,8},{8,9},{9,10... | collective-permute-start | bytes 399368 | tf_op jit(solution)/shard_map/ppermute | solution.py:423
  14.2 5.1 %collective-permute-start.4 = (f32[260,128]{1,0:T(8,128)S(1)}, f32[260,128]{1,0:T(8,128)S(1)}, u32[]{:S(2)}, u32[]{:S(2)}) collective-permute-start(f32[260,128]{1,0:T(8,128)S(1)} %get-tuple-element.55), channel_id=1, source_target_pairs={{1,0},{2,1},{3,2},{0,3},{5,4},{6,5},{7,6},{4,7},{9,8},{10,9},{11,1... | collective-permute-start | bytes 399368 | tf_op jit(solution)/shard_map/ppermute | solution.py:423
  15.6 5.9 %collective-permute-start.5 = (f32[260,128]{1,0:T(8,128)S(1)}, f32[260,128]{1,0:T(8,128)S(1)}, u32[]{:S(2)}, u32[]{:S(2)}) collective-permute-start(f32[260,128]{1,0:T(8,128)S(1)} %get-tuple-element.56), channel_id=1, source_target_pairs={{3,0},{0,1},{1,2},{2,3},{7,4},{4,5},{5,6},{6,7},{11,8},{8,9},{9,10... | collective-permute-start | bytes 399368 | tf_op jit(solution)/shard_map/ppermute | solution.py:423
  15.6 5.9 %collective-permute-start.6 = (f32[260,128]{1,0:T(8,128)S(1)}, f32[260,128]{1,0:T(8,128)S(1)}, u32[]{:S(2)}, u32[]{:S(2)}) collective-permute-start(f32[260,128]{1,0:T(8,128)S(1)} %get-tuple-element.57), channel_id=1, source_target_pairs={{1,0},{2,1},{3,2},{0,3},{5,4},{6,5},{7,6},{4,7},{9,8},{10,9},{11,1... | collective-permute-start | bytes 399368 | tf_op jit(solution)/shard_map/ppermute | solution.py:423
  24.0 14.4 %collective-permute-start.8 = (f32[845,128]{1,0:T(8,128)S(1)}, f32[845,128]{1,0:T(8,128)S(1)}, u32[]{:S(2)}, u32[]{:S(2)}) collective-permute-start(f32[845,128]{1,0:T(8,128)S(1)} %get-tuple-element.60), channel_id=1, source_target_pairs={{3,0},{0,1},{1,2},{2,3},{7,4},{4,5},{5,6},{6,7},{11,8},{8,9},{9,10... | collective-permute-start | bytes 1297928 | tf_op jit(solution)/shard_map/ppermute | solution.py:423
  24.4 14.0 %collective-permute-start.9 = (f32[845,128]{1,0:T(8,128)S(1)}, f32[845,128]{1,0:T(8,128)S(1)}, u32[]{:S(2)}, u32[]{:S(2)}) collective-permute-start(f32[845,128]{1,0:T(8,128)S(1)} %get-tuple-element.61), channel_id=1, source_target_pairs={{1,0},{2,1},{3,2},{0,3},{5,4},{6,5},{7,6},{4,7},{9,8},{10,9},{11,1... | collective-permute-start | bytes 1297928 | tf_op jit(solution)/shard_map/ppermute | solution.py:423
  25.8 14.9 %collective-permute-start.10 = (f32[520,128]{1,0:T(8,128)S(1)}, f32[520,128]{1,0:T(8,128)S(1)}, u32[]{:S(2)}, u32[]{:S(2)}) collective-permute-start(f32[520,128]{1,0:T(8,128)S(1)} %get-tuple-element.59.refs_5_), channel_id=1, source_target_pairs={{4,0},{8,4},{12,8},{16,12},{20,16},{24,20},{28,24},{0,28},{5,1},{9... | collective-permute-start | bytes 798728 | tf_op jit(solution)/shard_map/ppermute | solution.py:423
  40.1 10.9 %collective-permute-start.13 = (f32[520,128]{1,0:T(8,128)S(1)}, f32[520,128]{1,0:T(8,128)S(1)}, u32[]{:S(2)}, u32[]{:S(2)}) collective-permute-start(f32[520,128]{1,0:T(8,128)S(1)} %get-tuple-element.67.refs_0_), channel_id=1, source_target_pairs={{28,0},{0,4},{4,8},{8,12},{12,16},{16,20},{20,24},{24,28},{29,1},{... | collective-permute-start | bytes 798728 | tf_op jit(solution)/shard_map/ppermute | solution.py:423
  41.1 5.0 %collective-permute-start.11 = (f32[260,128]{1,0:T(8,128)S(1)}, f32[260,128]{1,0:T(8,128)S(1)}, u32[]{:S(2)}, u32[]{:S(2)}) collective-permute-start(f32[260,128]{1,0:T(8,128)S(1)} %get-tuple-element.73), channel_id=1, source_target_pairs={{3,0},{0,1},{1,2},{2,3},{7,4},{4,5},{5,6},{6,7},{11,8},{8,9},{9,10... | collective-permute-start | bytes 399368 | tf_op jit(solution)/shard_map/ppermute | solution.py:423
  41.1 5.0 %collective-permute-start.12 = (f32[260,128]{1,0:T(8,128)S(1)}, f32[260,128]{1,0:T(8,128)S(1)}, u32[]{:S(2)}, u32[]{:S(2)}) collective-permute-start(f32[260,128]{1,0:T(8,128)S(1)} %get-tuple-element.74), channel_id=1, source_target_pairs={{1,0},{2,1},{3,2},{0,3},{5,4},{6,5},{7,6},{4,7},{9,8},{10,9},{11,1... | collective-permute-start | bytes 399368 | tf_op jit(solution)/shard_map/ppermute | solution.py:423

commit v9 on v8

--- a/solution.py
+++ b/solution.py
@@ -34,10 +34,10 @@
     ref[pl.ds(i, points, stride=planes), :] = plane[:points]
 
 
-WORK = {"forward": 4e9, "inverse": 1e9}
-
-
-def call(kernel, name, outs, operands, scratch=(), specs=None, fast=False):
+WORK = {"forward_outer": 4e9, "inverse": 1e9}
+
+
+def call(kernel, name, outs, operands, scratch=(), specs=None, fast=False, aliases=None):
     return pl.pallas_call(
         kernel,
         name=name,
@@ -45,6 +45,7 @@
         in_specs=specs or [VMEM] * len(operands),
         out_specs=[VMEM] * len(outs),
         scratch_shapes=list(scratch),
+        input_output_aliases=aliases or {},
         cost_estimate=pl.CostEstimate(flops=int(WORK[name]), transcendentals=0, bytes_accessed=1 << 20) if name in WORK and not fast else None,
         compiler_params=pltpu.CompilerParams(vmem_limit_bytes=32 * 1024 * 1024),
     )(*operands)
@@ -154,75 +155,113 @@
 WIDE = 7
 
 
-def forward_kernel(nx, updated, *refs):
+def pushed_plane(base, before, here, ahead, force):
+    return 3.0 * here + neighbours(here) + force - (base + here) * (ahead - before) * (0.5 * ADVECT / SPREAD)
+
+
+def field_plane(nx, u0, start, fields, t, i):
+    if t == 0:
+        return u0[STEPS + i] if i < 0 else u0[STEPS + i - nx] if i >= nx else start[1 + i]
+    return fields[t - 1][WIDTHS[t] + i]
+
+
+def force_plane(nx, left, right, q_own, i):
+    m = 2 * STEPS - 1
+    if i < 0:
+        return (PUSHED / SPREAD) * load(left, m + i, m)
+    if i >= nx:
+        return (PUSHED / SPREAD) * load(right, STEPS + i - nx, m)
+    return q_own[i]
+
+
+def forward_kernel(nx, matrix_ref, left, right, q_own, old, descent, d_left, d_right, sums, ending_ref, start, first, second, third, u0):
     h = STEPS
     m = 2 * h - 1
-    refs = list(refs)
-    matrix_ref, states, forcing, left, right = refs[:5]
-    del refs[:5]
-    reach = WIDTHS[1]
-    if updated:
-        descent, d_left, d_right, sums = refs[:4]
-        del refs[:4]
-        tau = step_size(sums[...])
-    ending_ref, start_ref, first_ref, second_ref, third_ref = refs[:5]
-    u0, q = refs[-2:]
+    parts = WIDE + 2 * (WIDE - h)
+    points = left.shape[0] // m
+    base = wall_profile(points, padded(points, 8))
+    matrix = matrix_ref[...]
+    tau = step_size(sums[...])
+    for j in range(h):
+        before = load(left, h - 1 - j, m) - tau * load(d_left, WIDE - 1 - j, parts)
+        ahead = load(right, j, m) - tau * load(d_right, j, parts)
+        if j == 0:
+            start[0] = before
+            start[nx + 1] = ahead
+        u0[h - 1 - j] = before
+        u0[h + j] = ahead
+    for i in range(nx):
+        start[1 + i] = old[1 + i] - tau * load(descent, i, nx)
+    value = functools.partial(field_plane, nx, u0, start, (first, second, third))
+    for t in range(h):
+        planes = list(range(-WIDTHS[t + 1], nx + WIDTHS[t + 1]))
+        for begin in range(0, len(planes), 2):
+            group = planes[begin : begin + 2]
+            pushed = [
+                pushed_plane(base, value(t, i - 1), value(t, i), value(t, i + 1), force_plane(nx, left, right, q_own, i))
+                for i in group
+            ]
+            for i, plane in zip(group, product(matrix, pushed)):
+                if t == h - 1:
+                    store(ending_ref, i, nx, plane)
+                else:
+                    (first, second, third)[t][WIDTHS[t + 1] + i] = plane
+
+
+def forward_inner_kernel(nx, matrix_ref, states, forcing, start_ref, q_ref, first_ref, second_ref, third_ref):
+    h = STEPS
     points = states.shape[0] // nx
-    rows = padded(points, 8)
-    scale = PUSHED / SPREAD
-    parts = WIDE + 2 * (WIDE - h)
+    base = wall_profile(points, padded(points, 8))
+    matrix = matrix_ref[...]
+    for i in range(nx):
+        start_ref[1 + i] = load(states, i, nx)
+        q_ref[i] = (PUSHED / SPREAD) * load(forcing, i, nx)
+    fields = ((start_ref, 1), (first_ref, WIDTHS[1]), (second_ref, WIDTHS[2]), (third_ref, WIDTHS[3]))
+    for t in range(h - 1):
+        (source, a), (target, b) = fields[t], fields[t + 1]
+        planes = list(range(t + 1, nx - t - 1))
+        for begin in range(0, len(planes), 2):
+            group = planes[begin : begin + 2]
+            pushed = [
+                pushed_plane(base, source[a + i - 1], source[a + i], source[a + i + 1], q_ref[i]) for i in group
+            ]
+            for i, plane in zip(group, product(matrix, pushed)):
+                target[b + i] = plane
+
+
+def forward_outer_kernel(nx, matrix_ref, left, right, q_own, start_in, first_in, second_in, third_in, ending_ref, start, first, second, third, low_ref, high_ref, u0):
+    h = STEPS
+    m = 2 * h - 1
+    points = left.shape[0] // m
+    base = wall_profile(points, padded(points, 8))
+    matrix = matrix_ref[...]
     for j in range(h):
         before, ahead = load(left, h - 1 - j, m), load(right, j, m)
-        if updated:
-            before = before - tau * load(d_left, WIDE - 1 - j, parts)
-            ahead = ahead - tau * load(d_right, j, parts)
+        if j == 0:
+            start[0] = before
+            start[nx + 1] = ahead
         u0[h - 1 - j] = before
-        u0[h + nx + j] = ahead
-        if j == 0:
-            start_ref[0] = before
-            start_ref[nx + 1] = ahead
-    for i in range(nx):
-        here = load(states, i, nx)
-        if updated:
-            here = here - tau * load(descent, i, nx)
-        u0[h + i] = here
-        start_ref[1 + i] = here
-    for j in range(reach):
-        q[reach - 1 - j] = scale * load(left, m - 1 - j, m)
-        q[reach + nx + j] = scale * load(right, h + j, m)
-    for i in range(nx):
-        q[reach + i] = scale * load(forcing, i, nx)
-    base = wall_profile(points, rows)
-    matrix = matrix_ref[...]
-    fields = [u0, first_ref, second_ref, third_ref, None]
+        u0[h + j] = ahead
+
+    value = functools.partial(field_plane, nx, u0, start, (first, second, third))
     for t in range(h):
-        source, target = fields[t], fields[t + 1]
-        count = nx + 2 * WIDTHS[t + 1]
-        inset = WIDTHS[t] - WIDTHS[t + 1]
-        window = [source[inset - 1], source[inset]]
-        pending = []
-        for i in range(count):
-            window = window[-2:] + [source[inset + i + 1]]
-            before, here, ahead = window
-            force = q[i + reach - WIDTHS[t + 1]]
-            pending.append(
-                3.0 * here + neighbours(here) + force - (base + here) * (ahead - before) * (0.5 * ADVECT / SPREAD)
-            )
-            if len(pending) == 2 or i == count - 1:
-                for j, plane in enumerate(product(matrix, pending)):
-                    at = i - len(pending) + 1 + j
-                    if target is not None:
-                        target[at] = plane
-                    else:
-                        store(ending_ref, at, nx, plane)
-                pending = []
-    if not updated:
-        low_ref, high_ref = refs[5:7]
-        for i in range(h - 1):
-            store(low_ref, i, h, third_ref[1 + 1 + i])
-            store(high_ref, i, h, third_ref[1 + nx - h + i])
-        store(low_ref, h - 1, h, second_ref[2 + 2])
-        store(high_ref, h - 1, h, second_ref[2 + nx - 3])
+        planes = list(range(t + 1 - h, t + 1)) + list(range(nx - 1 - t, nx - 1 - t + h))
+        for begin in range(0, 2 * h, 2):
+            group = planes[begin : begin + 2]
+            pushed = [
+                pushed_plane(base, value(t, i - 1), value(t, i), value(t, i + 1), force_plane(nx, left, right, q_own, i))
+                for i in group
+            ]
+            for i, plane in zip(group, product(matrix, pushed)):
+                if t == h - 1:
+                    store(ending_ref, i, nx, plane)
+                else:
+                    (first, second, third)[t][WIDTHS[t + 1] + i] = plane
+    for i in range(h - 1):
+        store(low_ref, i, h, third[WIDTHS[3] + 1 + i])
+        store(high_ref, i, h, third[WIDTHS[3] + nx - h + i])
+    store(low_ref, h - 1, h, second[WIDTHS[2] + 2])
+    store(high_ref, h - 1, h, second[WIDTHS[2] + nx - 3])
 
 
 def wide_kernel(nx, matrix_ref, left, right, d_left, d_right, sums, first, second, left_fields, right_fields):
@@ -460,16 +499,31 @@
     moved = d_after = sums = None
     for iteration in range(ITERS):
         updated = iteration > 0
-        ending, start, first, second, third, *sides = call(
-            functools.partial(forward_kernel, nx, updated),
-            "forward",
-            [flat(nx), tiles(nx + 2)]
-            + [tiles(nx + 2 * width) for width in WIDTHS[1:-1]]
-            + ([] if updated else [flat(h)] * 2),
-            [forward, states, forcing, left, right] + (moved + [sums] if updated else []),
-            [pltpu.VMEM((nx + 2 * width, rows, LANES), f32) for width in WIDTHS[:2]],
-            fast=updated,
-        )
+        kept_fields = [tiles(nx + 2)] + [tiles(nx + 2 * width) for width in WIDTHS[1:-1]]
+        if updated:
+            ending, start, first, second, third = call(
+                functools.partial(forward_kernel, nx),
+                "forward",
+                [flat(nx)] + kept_fields,
+                [forward, left, right, q, start, *moved, sums],
+                [pltpu.VMEM((2 * h, rows, LANES), f32)],
+                fast=True,
+            )
+        else:
+            start, q, first, second, third = call(
+                functools.partial(forward_inner_kernel, nx),
+                "forward_inner",
+                [kept_fields[0], tiles(nx)] + kept_fields[1:],
+                [forward, states, forcing],
+            )
+            ending, start, first, second, third, *sides = call(
+                functools.partial(forward_outer_kernel, nx),
+                "forward_outer",
+                [flat(nx)] + kept_fields + [flat(h)] * 2,
+                [forward, left, right, q, start, first, second, third],
+                [pltpu.VMEM((2 * h, rows, LANES), f32)],
+                aliases={4: 1, 5: 2, 6: 3, 7: 4},
+            )
         prior = shift(ending, "seg", 1)
         if updated:
             sides = call(

time: 61.1 us -> 60.8 us (level)
    pallas_call x15 -> x16, Pallas kernels: 13.1 us -> 13.7 us  [call(): pl.pallas_call(kernel, name=name, out_shape=[jax.ShapeDtypeStruct(shape,...]
  transfers between devices with their start and end apart: 14 -> 14, of which waited for: 6 -> 6; matrix products, arithmetic and copies ran while one was open for 0% -> 0% of each run, Pallas kernels for 17% -> 19%
where the time goes in v9:
time: 60.8 us; the launch traced here: 60.6 us
  starting transfers between devices  20.2 us (33%)
  blocking collectives  17.7 us (29%)
  Pallas kernels  13.7 us (23%)
  waiting for transfers between devices  8.3 us (14%)
  between operations  0.73 us (1%)
    ppermute x14, starting transfers between devices, shift(): lax.ppermute(block, axis, [((i - distance) % devices, i) for i in range(d...  20.2 us
    all_to_all x2, blocking collectives, per_device(): sums = lax.all_to_all(sums, BOTH, 0, 0, tiled=True)  17.7 us
    pallas_call x16, Pallas kernels, call(): pl.pallas_call(kernel, name=name, out_shape=[jax.ShapeDtypeStruct(shape,...  13.7 us
    ppermute x14, waiting for transfers between devices, shift(): lax.ppermute(block, axis, [((i - distance) % devices, i) for i in range(d...  8.3 us
  transfers between devices with their start and end apart: 14, of which 6 were waited for; matrix products, arithmetic and copies ran while one was open for 0% of the time, Pallas kernels for 19%

profile of v9, /device:TPU:0, one launch (start us, length us, event | category | flops | bytes accessed | tf_op | source)
XLA Modules:
  0.0 60.6 jit_solution(5168785300512932381)
XLA Ops:
  0.6 1.2 %pack.1 = (f32[455,128]{1,0:T(8,128)S(1)}, f32[455,128]{1,0:T(8,128)S(1)}, f32[520,128]{1,0:T(8,128)S(1)}, f32[520,128]{1,0:T(8,128)S(1)}) custom-call(f32[520,128]{1,0:T(8,128)} %bitcast.35, f32[520,128]{1,0:T(8,128)} %bitcast.36), custom_call_target="tpu_custom_call" | custom-call | tf_op jit(solution)/shard_map/pack/pallas_call | solution.py:41
  1.8 0.5 collective-permute-start
  2.3 2.0 %collective-permute-start.1 = (f32[455,128]{1,0:T(8,128)S(1)}, f32[455,128]{1,0:T(8,128)S(1)}, u32[]{:S(2)}, u32[]{:S(2)}) collective-permute-start(f32[455,128]{1,0:T(8,128)S(1)} %get-tuple-element.47), channel_id=1, source_target_pairs={{1,0},{2,1},{3,2},{0,3},{5,4},{6,5},{7,6},{4,7},{9,8},{10,9},{11,1... | collective-permute-start | bytes 698888 | tf_op jit(solution)/shard_map/ppermute | solution.py:462
  4.4 5.3 %collective-permute-start.2 = (f32[520,128]{1,0:T(8,128)S(1)}, f32[520,128]{1,0:T(8,128)S(1)}, u32[]{:S(2)}, u32[]{:S(2)}) collective-permute-start(f32[520,128]{1,0:T(8,128)S(1)} %get-tuple-element.48.states.refs_0_), channel_id=1, source_target_pairs={{4,0},{8,4},{12,8},{16,12},{20,16},{24,20},{28,24},{0,28},{5,1},{9... | collective-permute-start | bytes 798728 | tf_op jit(solution)/shard_map/ppermute | solution.py:462
  9.6 0.5 inverse.1
  10.1 0.9 %forward_inner.1 = (f32[10,72,128]{2,1,0:T(8,128)S(1)}, f32[8,72,128]{2,1,0:T(8,128)S(1)}, f32[14,72,128]{2,1,0:T(8,128)S(1)}, f32[12,72,128]{2,1,0:T(8,128)S(1)}, f32[10,72,128]{2,1,0:T(8,128)S(1)}) custom-call(bf16[72,240]{1,0:T(8,128)(2,1)S(1)} %get-tuple-element.45.matrix_ref, f32[520,128]{1,0:T(8,128)S(1)} %get-tuple-element.48.states.refs_0_, ...), custom_call_target="tpu_custom_call" | custom-call | tf_op jit(solution)/shard_map/forward_inner/pallas_call | solution.py:41
  11.0 1.3 %forward_outer.1 = (f32[520,128]{1,0:T(8,128)S(1)}, f32[10,72,128]{2,1,0:T(8,128)S(1)}, f32[14,72,128]{2,1,0:T(8,128)S(1)}, f32[12,72,128]{2,1,0:T(8,128)S(1)}, ...) custom-call(bf16[72,240]{1,0:T(8,128)(2,1)S(1)} %get-tuple-element.4, ...), custom_call_target="tpu_custom_call", output_to_operand_aliasing={{1}: (4, {}), {2}: (5, {}), {3}: (6, {}), {4}: (7, {})} | custom-call | flops 4000000000 | bytes 1048576 | tf_op jit(solution)/shard_map/forward_outer/pallas_call | solution.py:41
  12.3 0.9 %collective-permute-start.7 = (f32[520,128]{1,0:T(8,128)S(1)}, f32[520,128]{1,0:T(8,128)S(1)}, u32[]{:S(2)}, u32[]{:S(2)}) collective-permute-start(f32[520,128]{1,0:T(8,128)S(1)} %get-tuple-element.60.refs_0_), channel_id=1, source_target_pairs={{28,0},{0,4},{4,8},{8,12},{12,16},{16,20},{20,24},{24,28},{29,1},{... | collective-permute-start | bytes 798728 | tf_op jit(solution)/shard_map/ppermute | solution.py:462
  13.2 0.8 %collective-permute-start.3 = (f32[260,128]{1,0:T(8,128)S(1)}, f32[260,128]{1,0:T(8,128)S(1)}, u32[]{:S(2)}, u32[]{:S(2)}) collective-permute-start(f32[260,128]{1,0:T(8,128)S(1)} %get-tuple-element.64), channel_id=1, source_target_pairs={{3,0},{0,1},{1,2},{2,3},{7,4},{4,5},{5,6},{6,7},{11,8},{8,9},{9,10... | collective-permute-start | bytes 399368 | tf_op jit(solution)/shard_map/ppermute | solution.py:462
  14.0 1.1 %collective-permute-start.4 = (f32[260,128]{1,0:T(8,128)S(1)}, f32[260,128]{1,0:T(8,128)S(1)}, u32[]{:S(2)}, u32[]{:S(2)}) collective-permute-start(f32[260,128]{1,0:T(8,128)S(1)} %get-tuple-element.65), channel_id=1, source_target_pairs={{1,0},{2,1},{3,2},{0,3},{5,4},{6,5},{7,6},{4,7},{9,8},{10,9},{11,1... | collective-permute-start | bytes 399368 | tf_op jit(solution)/shard_map/ppermute | solution.py:462
  15.6 1.8 %collective-permute-start.6 = (f32[260,128]{1,0:T(8,128)S(1)}, f32[260,128]{1,0:T(8,128)S(1)}, u32[]{:S(2)}, u32[]{:S(2)}) collective-permute-start(f32[260,128]{1,0:T(8,128)S(1)} %get-tuple-element.67), channel_id=1, source_target_pairs={{1,0},{2,1},{3,2},{0,3},{5,4},{6,5},{7,6},{4,7},{9,8},{10,9},{11,1... | collective-permute-start | bytes 399368 | tf_op jit(solution)/shard_map/ppermute | solution.py:462
  17.3 1.1 %adjoint_inner.2 = (f32[20,72,128]{2,1,0:T(8,128)S(1)}, f32[20,72,128]{2,1,0:T(8,128)S(1)}) custom-call(bf16[72,240]{1,0:T(8,128)(2,1)S(1)} %get-tuple-element.56.matrix_ref, f32[10,72,128]{2,1,0:T(8,128)S(1)} %get-tuple-element.55.start.old, f32[14,72,128]{2,1,0:T(8,128)S(1)} %get-tuple-element.57.first, f32[12,72,128]{2,1,0:T(8,128)S(1)} %get-tuple-element.58.second, ...), custom_call_target="tpu_custom_call" | custom-call | tf_op jit(solution)/shard_map/adjoint_inner/pallas_call | solution.py:41
  18.4 0.7 %collective-permute-done.4.refs_1_ = f32[260,128]{1,0:T(8,128)S(1)} collective-permute-done((f32[260,128]{1,0:T(8,128)S(1)}, f32[260,128]{1,0:T(8,128)S(1)}, u32[]{:S(2)}, u32[]{:S(2)}) %collective-permute-start.4) | collective-permute-done | bytes 133152 | tf_op jit(solution)/shard_map/ppermute | solution.py:462
  19.1 2.3 %collective-permute-done.5.refs_2_ = f32[260,128]{1,0:T(8,128)S(1)} collective-permute-done((f32[260,128]{1,0:T(8,128)S(1)}, f32[260,128]{1,0:T(8,128)S(1)}, u32[]{:S(2)}, u32[]{:S(2)}) %collective-permute-start.5) | collective-permute-done | bytes 133152 | tf_op jit(solution)/shard_map/ppermute | solution.py:462
  21.4 1.2 %adjoint_outer.2.lam = f32[8,72,128]{2,1,0:T(8,128)S(1)} custom-call(bf16[72,240]{1,0:T(8,128)(2,1)S(1)} %get-tuple-element.56.matrix_ref, f32[10,72,128]{2,1,0:T(8,128)S(1)} %get-tuple-element.55.start.old, f32[14,72,128]{2,1,0:T(8,128)S(1)} %get-tuple-element.57.first, f32[12,72,128]{2,1,0:T(8,128)S(1)} %get-tuple-element.58.second, ...), custom_call_target="tpu_custom_call" | custom-call | tf_op jit(solution)/shard_map/adjoint_outer/pallas_call | solution.py:41
  22.6 1.0 %collective-permute-done.7.prior = f32[520,128]{1,0:T(8,128)S(1)} collective-permute-done((f32[520,128]{1,0:T(8,128)S(1)}, f32[520,128]{1,0:T(8,128)S(1)}, u32[]{:S(2)}, u32[]{:S(2)}) %collective-permute-start.7) | collective-permute-done | bytes 266272 | tf_op jit(solution)/shard_map/ppermute | solution.py:462
  23.8 0.4 collective-permute-start.8
  24.2 1.4 %collective-permute-start.9 = (f32[845,128]{1,0:T(8,128)S(1)}, f32[845,128]{1,0:T(8,128)S(1)}, u32[]{:S(2)}, u32[]{:S(2)}) collective-permute-start(f32[845,128]{1,0:T(8,128)S(1)} %get-tuple-element.71), channel_id=1, source_target_pairs={{1,0},{2,1},{3,2},{0,3},{5,4},{6,5},{7,6},{4,7},{9,8},{10,9},{11,1... | collective-permute-start | bytes 1297928 | tf_op jit(solution)/shard_map/ppermute | solution.py:462
  25.6 3.7 %collective-permute-start.10 = (f32[520,128]{1,0:T(8,128)S(1)}, f32[520,128]{1,0:T(8,128)S(1)}, u32[]{:S(2)}, u32[]{:S(2)}) collective-permute-start(f32[520,128]{1,0:T(8,128)S(1)} %get-tuple-element.69.descent), channel_id=1, source_target_pairs={{4,0},{8,4},{12,8},{16,12},{20,16},{24,20},{28,24},{0,28},{5,1},{9... | collective-permute-start | bytes 798728 | tf_op jit(solution)/shard_map/ppermute | solution.py:462
  29.4 8.9 %all_to_all.22 = f32[32,1,128]{2,1,0:T(1,128)S(1)} all-to-all(f32[32,1,128]{2,1,0:T(1,128)S(1)} %bitcast.31), channel_id=1, replica_groups=mesh['seg'=8,'space'=4] {'seg','space'}, dimensions={0} | all-to-all | bytes 32768 | tf_op jit(solution)/shard_map/all_to_all | solution.py:572
  38.2 1.6 %forward.1 = (f32[520,128]{1,0:T(8,128)S(1)}, f32[10,72,128]{2,1,0:T(8,128)S(1)}, f32[14,72,128]{2,1,0:T(8,128)S(1)}, f32[12,72,128]{2,1,0:T(8,128)S(1)}, f32[10,72,128]{2,1,0:T(8,128)S(1)}) custom-call(bf16[72,240]{1,0:T(8,128)(2,1)S(1)} %get-tuple-element.45.matrix_ref, f32[455,128]{1,0:T(8,128)S(1)} %collective-permute-done.left, ...), custom_call_target="tpu_custom_call" | custom-call | tf_op jit(solution)/shard_map/forward/pallas_call | solution.py:41
  39.8 0.6 %collective-permute-start.13 = (f32[520,128]{1,0:T(8,128)S(1)}, f32[520,128]{1,0:T(8,128)S(1)}, u32[]{:S(2)}, u32[]{:S(2)}) collective-permute-start(f32[520,128]{1,0:T(8,128)S(1)} %get-tuple-element.77.refs_0_), channel_id=1, source_target_pairs={{28,0},{0,4},{4,8},{8,12},{12,16},{16,20},{20,24},{24,28},{29,1},{... | collective-permute-start | bytes 798728 | tf_op jit(solution)/shard_map/ppermute | solution.py:462
  40.5 0.4 mismatch.3
  40.8 1.8 %collective-permute-start.12 = (f32[260,128]{1,0:T(8,128)S(1)}, f32[260,128]{1,0:T(8,128)S(1)}, u32[]{:S(2)}, u32[]{:S(2)}) collective-permute-start(f32[260,128]{1,0:T(8,128)S(1)} %get-tuple-element.84), channel_id=1, source_target_pairs={{1,0},{2,1},{3,2},{0,3},{5,4},{6,5},{7,6},{4,7},{9,8},{10,9},{11,1... | collective-permute-start | bytes 399368 | tf_op jit(solution)/shard_map/ppermute | solution.py:462
  42.6 1.0 %adjoint_inner.3 = (f32[20,72,128]{2,1,0:T(8,128)S(1)}, f32[20,72,128]{2,1,0:T(8,128)S(1)}) custom-call(bf16[72,240]{1,0:T(8,128)(2,1)S(1)} %get-tuple-element.56.matrix_ref, f32[10,72,128]{2,1,0:T(8,128)S(1)} %get-tuple-element.73.start, f32[14,72,128]{2,1,0:T(8,128)S(1)} %get-tuple-element.74.first, f32[12,72,128]{2,1,0:T(8,128)S(1)} %get-tuple-element.75.second, ...), custom_call_target="tpu_custom_call" | custom-call | tf_op jit(solution)/shard_map/adjoint_inner/pallas_call | solution.py:41
  43.6 0.7 %kept.1.refs_0_ = f32[520,128]{1,0:T(8,128)} custom-call(f32[520,128]{1,0:T(8,128)S(1)} %get-tuple-element.78.mismatch.given, f32[20,72,128]{2,1,0:T(8,128)S(1)} %get-tuple-element.79.mu_ref.order), custom_call_target="tpu_custom_call" | custom-call | tf_op jit(solution)/shard_map/kept/pallas_call | solution.py:41
  44.4 1.0 %wide.1 = (f32[260,128]{1,0:T(8,128)S(1)}, f32[260,128]{1,0:T(8,128)S(1)}) custom-call(bf16[72,240]{1,0:T(8,128)(2,1)S(1)} %get-tuple-element.45.matrix_ref, f32[455,128]{1,0:T(8,128)S(1)} %collective-permute-done.left, f32[455,128]{1,0:T(8,128)S(1)} %collective-permute-done.1.right, f32[845,128]{1,0:T(8,128)S(1)} %collective-permute-done.8.d_left, ...), custom_call_target="tpu_custom_call" | custom-call | tf_op jit(solution)/shard_map/wide/pallas_call | solution.py:41
  45.4 0.5 collective-permute-done.11.refs_2_
  45.8 1.2 %adjoint_outer.3.lam = f32[8,72,128]{2,1,0:T(8,128)S(1)} custom-call(bf16[72,240]{1,0:T(8,128)(2,1)S(1)} %get-tuple-element.56.matrix_ref, f32[10,72,128]{2,1,0:T(8,128)S(1)} %get-tuple-element.73.start, f32[14,72,128]{2,1,0:T(8,128)S(1)} %get-tuple-element.74.first, f32[12,72,128]{2,1,0:T(8,128)S(1)} %get-tuple-element.75.second, ...), custom_call_target="tpu_custom_call" | custom-call | tf_op jit(solution)/shard_map/adjoint_outer/pallas_call | solution.py:41
  47.1 3.7 %collective-permute-done.13.prior = f32[520,128]{1,0:T(8,128)S(1)} collective-permute-done((f32[520,128]{1,0:T(8,128)S(1)}, f32[520,128]{1,0:T(8,128)S(1)}, u32[]{:S(2)}, u32[]{:S(2)}) %collective-permute-start.13) | collective-permute-done | bytes 266272 | tf_op jit(solution)/shard_map/ppermute | solution.py:462
  50.9 8.8 %all_to_all.23 = f32[32,1,128]{2,1,0:T(1,128)S(1)} all-to-all(f32[32,1,128]{2,1,0:T(1,128)S(1)} %bitcast.32), channel_id=1, replica_groups=mesh['seg'=8,'space'=4] {'seg','space'}, dimensions={0} | all-to-all | bytes 32768 | tf_op jit(solution)/shard_map/all_to_all | solution.py:572
  59.8 0.9 %final.1 = f32[520,128]{1,0:T(8,128)} custom-call(f32[10,72,128]{2,1,0:T(8,128)S(1)} %get-tuple-element.73.start, f32[8,72,128]{2,1,0:T(8,128)S(1)} %get-tuple-element.86.descent, f32[32,128]{1,0:T(8,128)S(1)} %bitcast.30), custom_call_target="tpu_custom_call" | custom-call | tf_op jit(solution)/shard_map/final/pallas_call | solution.py:41
  (16 shorter events, 0.9 us)
Async XLA Ops:
  1.8 9.2 %collective-permute-start = (f32[455,128]{1,0:T(8,128)S(1)}, f32[455,128]{1,0:T(8,128)S(1)}, u32[]{:S(2)}, u32[]{:S(2)}) collective-permute-start(f32[455,128]{1,0:T(8,128)S(1)} %get-tuple-element.46), channel_id=1, source_target_pairs={{3,0},{0,1},{1,2},{2,3},{7,4},{4,5},{5,6},{6,7},{11,8},{8,9},{9,10... | collective-permute-start | bytes 698888 | tf_op jit(solution)/shard_map/ppermute | solution.py:462
  2.3 8.7 %collective-permute-start.1 = (f32[455,128]{1,0:T(8,128)S(1)}, f32[455,128]{1,0:T(8,128)S(1)}, u32[]{:S(2)}, u32[]{:S(2)}) collective-permute-start(f32[455,128]{1,0:T(8,128)S(1)} %get-tuple-element.47), channel_id=1, source_target_pairs={{1,0},{2,1},{3,2},{0,3},{5,4},{6,5},{7,6},{4,7},{9,8},{10,9},{11,1... | collective-permute-start | bytes 698888 | tf_op jit(solution)/shard_map/ppermute | solution.py:462
  4.4 5.3 %copy-start = (f32[65]{0:T(128)S(1)}, f32[65]{0:T(128)}, u32[]{:S(2)}) copy-start(f32[65]{0:T(128)} %param.5) | copy-start | bytes 784
  4.4 11.0 %collective-permute-start.2 = (f32[520,128]{1,0:T(8,128)S(1)}, f32[520,128]{1,0:T(8,128)S(1)}, u32[]{:S(2)}, u32[]{:S(2)}) collective-permute-start(f32[520,128]{1,0:T(8,128)S(1)} %get-tuple-element.48.states.refs_0_), channel_id=1, source_target_pairs={{4,0},{8,4},{12,8},{16,12},{20,16},{24,20},{28,24},{0,28},{5,1},{9... | collective-permute-start | bytes 798728 | tf_op jit(solution)/shard_map/ppermute | solution.py:462
  12.3 11.2 %collective-permute-start.7 = (f32[520,128]{1,0:T(8,128)S(1)}, f32[520,128]{1,0:T(8,128)S(1)}, u32[]{:S(2)}, u32[]{:S(2)}) collective-permute-start(f32[520,128]{1,0:T(8,128)S(1)} %get-tuple-element.60.refs_0_), channel_id=1, source_target_pairs={{28,0},{0,4},{4,8},{8,12},{12,16},{16,20},{20,24},{24,28},{29,1},{... | collective-permute-start | bytes 798728 | tf_op jit(solution)/shard_map/ppermute | solution.py:462
  13.2 5.2 %collective-permute-start.3 = (f32[260,128]{1,0:T(8,128)S(1)}, f32[260,128]{1,0:T(8,128)S(1)}, u32[]{:S(2)}, u32[]{:S(2)}) collective-permute-start(f32[260,128]{1,0:T(8,128)S(1)} %get-tuple-element.64), channel_id=1, source_target_pairs={{3,0},{0,1},{1,2},{2,3},{7,4},{4,5},{5,6},{6,7},{11,8},{8,9},{9,10... | collective-permute-start | bytes 399368 | tf_op jit(solution)/shard_map/ppermute | solution.py:462
  14.0 5.1 %collective-permute-start.4 = (f32[260,128]{1,0:T(8,128)S(1)}, f32[260,128]{1,0:T(8,128)S(1)}, u32[]{:S(2)}, u32[]{:S(2)}) collective-permute-start(f32[260,128]{1,0:T(8,128)S(1)} %get-tuple-element.65), channel_id=1, source_target_pairs={{1,0},{2,1},{3,2},{0,3},{5,4},{6,5},{7,6},{4,7},{9,8},{10,9},{11,1... | collective-permute-start | bytes 399368 | tf_op jit(solution)/shard_map/ppermute | solution.py:462
  15.6 5.8 %collective-permute-start.5 = (f32[260,128]{1,0:T(8,128)S(1)}, f32[260,128]{1,0:T(8,128)S(1)}, u32[]{:S(2)}, u32[]{:S(2)}) collective-permute-start(f32[260,128]{1,0:T(8,128)S(1)} %get-tuple-element.66), channel_id=1, source_target_pairs={{3,0},{0,1},{1,2},{2,3},{7,4},{4,5},{5,6},{6,7},{11,8},{8,9},{9,10... | collective-permute-start | bytes 399368 | tf_op jit(solution)/shard_map/ppermute | solution.py:462
  15.6 5.8 %collective-permute-start.6 = (f32[260,128]{1,0:T(8,128)S(1)}, f32[260,128]{1,0:T(8,128)S(1)}, u32[]{:S(2)}, u32[]{:S(2)}) collective-permute-start(f32[260,128]{1,0:T(8,128)S(1)} %get-tuple-element.67), channel_id=1, source_target_pairs={{1,0},{2,1},{3,2},{0,3},{5,4},{6,5},{7,6},{4,7},{9,8},{10,9},{11,1... | collective-permute-start | bytes 399368 | tf_op jit(solution)/shard_map/ppermute | solution.py:462
  23.8 14.4 %collective-permute-start.8 = (f32[845,128]{1,0:T(8,128)S(1)}, f32[845,128]{1,0:T(8,128)S(1)}, u32[]{:S(2)}, u32[]{:S(2)}) collective-permute-start(f32[845,128]{1,0:T(8,128)S(1)} %get-tuple-element.70), channel_id=1, source_target_pairs={{3,0},{0,1},{1,2},{2,3},{7,4},{4,5},{5,6},{6,7},{11,8},{8,9},{9,10... | collective-permute-start | bytes 1297928 | tf_op jit(solution)/shard_map/ppermute | solution.py:462
  24.2 14.0 %collective-permute-start.9 = (f32[845,128]{1,0:T(8,128)S(1)}, f32[845,128]{1,0:T(8,128)S(1)}, u32[]{:S(2)}, u32[]{:S(2)}) collective-permute-start(f32[845,128]{1,0:T(8,128)S(1)} %get-tuple-element.71), channel_id=1, source_target_pairs={{1,0},{2,1},{3,2},{0,3},{5,4},{6,5},{7,6},{4,7},{9,8},{10,9},{11,1... | collective-permute-start | bytes 1297928 | tf_op jit(solution)/shard_map/ppermute | solution.py:462
  25.6 14.8 %collective-permute-start.10 = (f32[520,128]{1,0:T(8,128)S(1)}, f32[520,128]{1,0:T(8,128)S(1)}, u32[]{:S(2)}, u32[]{:S(2)}) collective-permute-start(f32[520,128]{1,0:T(8,128)S(1)} %get-tuple-element.69.descent), channel_id=1, source_target_pairs={{4,0},{8,4},{12,8},{16,12},{20,16},{24,20},{28,24},{0,28},{5,1},{9... | collective-permute-start | bytes 798728 | tf_op jit(solution)/shard_map/ppermute | solution.py:462
  39.8 10.9 %collective-permute-start.13 = (f32[520,128]{1,0:T(8,128)S(1)}, f32[520,128]{1,0:T(8,128)S(1)}, u32[]{:S(2)}, u32[]{:S(2)}) collective-permute-start(f32[520,128]{1,0:T(8,128)S(1)} %get-tuple-element.77.refs_0_), channel_id=1, source_target_pairs={{28,0},{0,4},{4,8},{8,12},{12,16},{16,20},{20,24},{24,28},{29,1},{... | collective-permute-start | bytes 798728 | tf_op jit(solution)/shard_map/ppermute | solution.py:462
  40.8 5.0 %collective-permute-start.11 = (f32[260,128]{1,0:T(8,128)S(1)}, f32[260,128]{1,0:T(8,128)S(1)}, u32[]{:S(2)}, u32[]{:S(2)}) collective-permute-start(f32[260,128]{1,0:T(8,128)S(1)} %get-tuple-element.83), channel_id=1, source_target_pairs={{3,0},{0,1},{1,2},{2,3},{7,4},{4,5},{5,6},{6,7},{11,8},{8,9},{9,10... | collective-permute-start | bytes 399368 | tf_op jit(solution)/shard_map/ppermute | solution.py:462
  40.8 5.0 %collective-permute-start.12 = (f32[260,128]{1,0:T(8,128)S(1)}, f32[260,128]{1,0:T(8,128)S(1)}, u32[]{:S(2)}, u32[]{:S(2)}) collective-permute-start(f32[260,128]{1,0:T(8,128)S(1)} %get-tuple-element.84), channel_id=1, source_target_pairs={{1,0},{2,1},{3,2},{0,3},{5,4},{6,5},{7,6},{4,7},{9,8},{10,9},{11,1... | collective-permute-start | bytes 399368 | tf_op jit(solution)/shard_map/ppermute | solution.py:462

commit v10 on v9

--- a/solution.py
+++ b/solution.py
@@ -16,7 +16,7 @@
 BOTH = ("seg", "space")
 VMEM = pl.BlockSpec(memory_space=pltpu.VMEM)
 LANES = 128
-PARTS = 4
+PARTS = 1
 
 
 def padded(count, step):

time: 60.8 us -> 60.7 us (level)
  no operation moved by 1% of the time
where the time goes in v10:
time: 60.7 us; the launch traced here: 60.5 us
  starting transfers between devices  20.2 us (33%)
  blocking collectives  17.7 us (29%)
  Pallas kernels  13.6 us (22%)
  waiting for transfers between devices  8.3 us (14%)
  between operations  0.73 us (1%)
    ppermute x14, starting transfers between devices, shift(): lax.ppermute(block, axis, [((i - distance) % devices, i) for i in range(d...  20.2 us
    all_to_all x2, blocking collectives, per_device(): sums = lax.all_to_all(sums, BOTH, 0, 0, tiled=True)  17.7 us
    pallas_call x16, Pallas kernels, call(): pl.pallas_call(kernel, name=name, out_shape=[jax.ShapeDtypeStruct(shape,...  13.6 us
    ppermute x14, waiting for transfers between devices, shift(): lax.ppermute(block, axis, [((i - distance) % devices, i) for i in range(d...  8.3 us
  transfers between devices with their start and end apart: 14, of which 6 were waited for; matrix products, arithmetic and copies ran while one was open for 0% of the time, Pallas kernels for 19%

profile of v10, /device:TPU:0, one launch (start us, length us, event | category | flops | bytes accessed | tf_op | source)
XLA Modules:
  0.0 60.5 jit_solution(9123653285425114834)
XLA Ops:
  0.6 1.1 %pack.1 = (f32[455,128]{1,0:T(8,128)S(1)}, f32[455,128]{1,0:T(8,128)S(1)}, f32[520,128]{1,0:T(8,128)S(1)}, f32[520,128]{1,0:T(8,128)S(1)}) custom-call(f32[520,128]{1,0:T(8,128)} %bitcast.35, f32[520,128]{1,0:T(8,128)} %bitcast.36), custom_call_target="tpu_custom_call" | custom-call | tf_op jit(solution)/shard_map/pack/pallas_call | solution.py:41
  1.7 0.5 collective-permute-start
  2.2 2.0 %collective-permute-start.1 = (f32[455,128]{1,0:T(8,128)S(1)}, f32[455,128]{1,0:T(8,128)S(1)}, u32[]{:S(2)}, u32[]{:S(2)}) collective-permute-start(f32[455,128]{1,0:T(8,128)S(1)} %get-tuple-element.47), channel_id=1, source_target_pairs={{1,0},{2,1},{3,2},{0,3},{5,4},{6,5},{7,6},{4,7},{9,8},{10,9},{11,1... | collective-permute-start | bytes 698888 | tf_op jit(solution)/shard_map/ppermute | solution.py:462
  4.3 5.3 %collective-permute-start.2 = (f32[520,128]{1,0:T(8,128)S(1)}, f32[520,128]{1,0:T(8,128)S(1)}, u32[]{:S(2)}, u32[]{:S(2)}) collective-permute-start(f32[520,128]{1,0:T(8,128)S(1)} %get-tuple-element.48.states.refs_0_), channel_id=1, source_target_pairs={{4,0},{8,4},{12,8},{16,12},{20,16},{24,20},{28,24},{0,28},{5,1},{9... | collective-permute-start | bytes 798728 | tf_op jit(solution)/shard_map/ppermute | solution.py:462
  9.5 0.5 inverse.1
  10.0 0.9 %forward_inner.1 = (f32[10,72,128]{2,1,0:T(8,128)S(1)}, f32[8,72,128]{2,1,0:T(8,128)S(1)}, f32[14,72,128]{2,1,0:T(8,128)S(1)}, f32[12,72,128]{2,1,0:T(8,128)S(1)}, f32[10,72,128]{2,1,0:T(8,128)S(1)}) custom-call(bf16[72,240]{1,0:T(8,128)(2,1)S(1)} %get-tuple-element.45.matrix_ref, f32[520,128]{1,0:T(8,128)S(1)} %get-tuple-element.48.states.refs_0_, ...), custom_call_target="tpu_custom_call" | custom-call | tf_op jit(solution)/shard_map/forward_inner/pallas_call | solution.py:41
  10.9 1.3 %forward_outer.1 = (f32[520,128]{1,0:T(8,128)S(1)}, f32[10,72,128]{2,1,0:T(8,128)S(1)}, f32[14,72,128]{2,1,0:T(8,128)S(1)}, f32[12,72,128]{2,1,0:T(8,128)S(1)}, ...) custom-call(bf16[72,240]{1,0:T(8,128)(2,1)S(1)} %get-tuple-element.4, ...), custom_call_target="tpu_custom_call", output_to_operand_aliasing={{1}: (4, {}), {2}: (5, {}), {3}: (6, {}), {4}: (7, {})} | custom-call | flops 4000000000 | bytes 1048576 | tf_op jit(solution)/shard_map/forward_outer/pallas_call | solution.py:41
  12.2 0.9 %collective-permute-start.7 = (f32[520,128]{1,0:T(8,128)S(1)}, f32[520,128]{1,0:T(8,128)S(1)}, u32[]{:S(2)}, u32[]{:S(2)}) collective-permute-start(f32[520,128]{1,0:T(8,128)S(1)} %get-tuple-element.60.refs_0_), channel_id=1, source_target_pairs={{28,0},{0,4},{4,8},{8,12},{12,16},{16,20},{20,24},{24,28},{29,1},{... | collective-permute-start | bytes 798728 | tf_op jit(solution)/shard_map/ppermute | solution.py:462
  13.1 0.8 %collective-permute-start.3 = (f32[260,128]{1,0:T(8,128)S(1)}, f32[260,128]{1,0:T(8,128)S(1)}, u32[]{:S(2)}, u32[]{:S(2)}) collective-permute-start(f32[260,128]{1,0:T(8,128)S(1)} %get-tuple-element.64), channel_id=1, source_target_pairs={{3,0},{0,1},{1,2},{2,3},{7,4},{4,5},{5,6},{6,7},{11,8},{8,9},{9,10... | collective-permute-start | bytes 399368 | tf_op jit(solution)/shard_map/ppermute | solution.py:462
  13.9 1.1 %collective-permute-start.4 = (f32[260,128]{1,0:T(8,128)S(1)}, f32[260,128]{1,0:T(8,128)S(1)}, u32[]{:S(2)}, u32[]{:S(2)}) collective-permute-start(f32[260,128]{1,0:T(8,128)S(1)} %get-tuple-element.65), channel_id=1, source_target_pairs={{1,0},{2,1},{3,2},{0,3},{5,4},{6,5},{7,6},{4,7},{9,8},{10,9},{11,1... | collective-permute-start | bytes 399368 | tf_op jit(solution)/shard_map/ppermute | solution.py:462
  15.5 1.8 %collective-permute-start.6 = (f32[260,128]{1,0:T(8,128)S(1)}, f32[260,128]{1,0:T(8,128)S(1)}, u32[]{:S(2)}, u32[]{:S(2)}) collective-permute-start(f32[260,128]{1,0:T(8,128)S(1)} %get-tuple-element.67), channel_id=1, source_target_pairs={{1,0},{2,1},{3,2},{0,3},{5,4},{6,5},{7,6},{4,7},{9,8},{10,9},{11,1... | collective-permute-start | bytes 399368 | tf_op jit(solution)/shard_map/ppermute | solution.py:462
  17.2 1.1 %adjoint_inner.2 = (f32[20,72,128]{2,1,0:T(8,128)S(1)}, f32[20,72,128]{2,1,0:T(8,128)S(1)}) custom-call(bf16[72,240]{1,0:T(8,128)(2,1)S(1)} %get-tuple-element.56.matrix_ref, f32[10,72,128]{2,1,0:T(8,128)S(1)} %get-tuple-element.55.start.old, f32[14,72,128]{2,1,0:T(8,128)S(1)} %get-tuple-element.57.first, f32[12,72,128]{2,1,0:T(8,128)S(1)} %get-tuple-element.58.second, ...), custom_call_target="tpu_custom_call" | custom-call | tf_op jit(solution)/shard_map/adjoint_inner/pallas_call | solution.py:41
  18.3 0.7 %collective-permute-done.4.refs_1_ = f32[260,128]{1,0:T(8,128)S(1)} collective-permute-done((f32[260,128]{1,0:T(8,128)S(1)}, f32[260,128]{1,0:T(8,128)S(1)}, u32[]{:S(2)}, u32[]{:S(2)}) %collective-permute-start.4) | collective-permute-done | bytes 133152 | tf_op jit(solution)/shard_map/ppermute | solution.py:462
  19.0 2.3 %collective-permute-done.5.refs_2_ = f32[260,128]{1,0:T(8,128)S(1)} collective-permute-done((f32[260,128]{1,0:T(8,128)S(1)}, f32[260,128]{1,0:T(8,128)S(1)}, u32[]{:S(2)}, u32[]{:S(2)}) %collective-permute-start.5) | collective-permute-done | bytes 133152 | tf_op jit(solution)/shard_map/ppermute | solution.py:462
  21.3 1.2 %adjoint_outer.2.lam = f32[8,72,128]{2,1,0:T(8,128)S(1)} custom-call(bf16[72,240]{1,0:T(8,128)(2,1)S(1)} %get-tuple-element.56.matrix_ref, f32[10,72,128]{2,1,0:T(8,128)S(1)} %get-tuple-element.55.start.old, f32[14,72,128]{2,1,0:T(8,128)S(1)} %get-tuple-element.57.first, f32[12,72,128]{2,1,0:T(8,128)S(1)} %get-tuple-element.58.second, ...), custom_call_target="tpu_custom_call" | custom-call | tf_op jit(solution)/shard_map/adjoint_outer/pallas_call | solution.py:41
  22.5 1.0 %collective-permute-done.7.prior = f32[520,128]{1,0:T(8,128)S(1)} collective-permute-done((f32[520,128]{1,0:T(8,128)S(1)}, f32[520,128]{1,0:T(8,128)S(1)}, u32[]{:S(2)}, u32[]{:S(2)}) %collective-permute-start.7) | collective-permute-done | bytes 266272 | tf_op jit(solution)/shard_map/ppermute | solution.py:462
  23.7 0.4 collective-permute-start.8
  24.1 1.4 %collective-permute-start.9 = (f32[845,128]{1,0:T(8,128)S(1)}, f32[845,128]{1,0:T(8,128)S(1)}, u32[]{:S(2)}, u32[]{:S(2)}) collective-permute-start(f32[845,128]{1,0:T(8,128)S(1)} %get-tuple-element.71), channel_id=1, source_target_pairs={{1,0},{2,1},{3,2},{0,3},{5,4},{6,5},{7,6},{4,7},{9,8},{10,9},{11,1... | collective-permute-start | bytes 1297928 | tf_op jit(solution)/shard_map/ppermute | solution.py:462
  25.5 3.7 %collective-permute-start.10 = (f32[520,128]{1,0:T(8,128)S(1)}, f32[520,128]{1,0:T(8,128)S(1)}, u32[]{:S(2)}, u32[]{:S(2)}) collective-permute-start(f32[520,128]{1,0:T(8,128)S(1)} %get-tuple-element.69.descent), channel_id=1, source_target_pairs={{4,0},{8,4},{12,8},{16,12},{20,16},{24,20},{28,24},{0,28},{5,1},{9... | collective-permute-start | bytes 798728 | tf_op jit(solution)/shard_map/ppermute | solution.py:462
  29.3 8.9 %all_to_all.22 = f32[32,1,128]{2,1,0:T(1,128)S(1)} all-to-all(f32[32,1,128]{2,1,0:T(1,128)S(1)} %bitcast.31), channel_id=1, replica_groups=mesh['seg'=8,'space'=4] {'seg','space'}, dimensions={0} | all-to-all | bytes 32768 | tf_op jit(solution)/shard_map/all_to_all | solution.py:572
  38.1 1.6 %forward.1 = (f32[520,128]{1,0:T(8,128)S(1)}, f32[10,72,128]{2,1,0:T(8,128)S(1)}, f32[14,72,128]{2,1,0:T(8,128)S(1)}, f32[12,72,128]{2,1,0:T(8,128)S(1)}, f32[10,72,128]{2,1,0:T(8,128)S(1)}) custom-call(bf16[72,240]{1,0:T(8,128)(2,1)S(1)} %get-tuple-element.45.matrix_ref, f32[455,128]{1,0:T(8,128)S(1)} %collective-permute-done.left, ...), custom_call_target="tpu_custom_call" | custom-call | tf_op jit(solution)/shard_map/forward/pallas_call | solution.py:41
  39.7 0.6 %collective-permute-start.13 = (f32[520,128]{1,0:T(8,128)S(1)}, f32[520,128]{1,0:T(8,128)S(1)}, u32[]{:S(2)}, u32[]{:S(2)}) collective-permute-start(f32[520,128]{1,0:T(8,128)S(1)} %get-tuple-element.77.refs_0_), channel_id=1, source_target_pairs={{28,0},{0,4},{4,8},{8,12},{12,16},{16,20},{20,24},{24,28},{29,1},{... | collective-permute-start | bytes 798728 | tf_op jit(solution)/shard_map/ppermute | solution.py:462
  40.4 0.4 mismatch.3
  40.7 1.8 %collective-permute-start.12 = (f32[260,128]{1,0:T(8,128)S(1)}, f32[260,128]{1,0:T(8,128)S(1)}, u32[]{:S(2)}, u32[]{:S(2)}) collective-permute-start(f32[260,128]{1,0:T(8,128)S(1)} %get-tuple-element.84), channel_id=1, source_target_pairs={{1,0},{2,1},{3,2},{0,3},{5,4},{6,5},{7,6},{4,7},{9,8},{10,9},{11,1... | collective-permute-start | bytes 399368 | tf_op jit(solution)/shard_map/ppermute | solution.py:462
  42.5 1.0 %adjoint_inner.3 = (f32[20,72,128]{2,1,0:T(8,128)S(1)}, f32[20,72,128]{2,1,0:T(8,128)S(1)}) custom-call(bf16[72,240]{1,0:T(8,128)(2,1)S(1)} %get-tuple-element.56.matrix_ref, f32[10,72,128]{2,1,0:T(8,128)S(1)} %get-tuple-element.73.start, f32[14,72,128]{2,1,0:T(8,128)S(1)} %get-tuple-element.74.first, f32[12,72,128]{2,1,0:T(8,128)S(1)} %get-tuple-element.75.second, ...), custom_call_target="tpu_custom_call" | custom-call | tf_op jit(solution)/shard_map/adjoint_inner/pallas_call | solution.py:41
  43.5 0.7 %kept.1.refs_0_ = f32[520,128]{1,0:T(8,128)} custom-call(f32[520,128]{1,0:T(8,128)S(1)} %get-tuple-element.78.mismatch.given, f32[20,72,128]{2,1,0:T(8,128)S(1)} %get-tuple-element.79.mu_ref.order), custom_call_target="tpu_custom_call" | custom-call | tf_op jit(solution)/shard_map/kept/pallas_call | solution.py:41
  44.3 1.0 %wide.1 = (f32[260,128]{1,0:T(8,128)S(1)}, f32[260,128]{1,0:T(8,128)S(1)}) custom-call(bf16[72,240]{1,0:T(8,128)(2,1)S(1)} %get-tuple-element.45.matrix_ref, f32[455,128]{1,0:T(8,128)S(1)} %collective-permute-done.left, f32[455,128]{1,0:T(8,128)S(1)} %collective-permute-done.1.right, f32[845,128]{1,0:T(8,128)S(1)} %collective-permute-done.8.d_left, ...), custom_call_target="tpu_custom_call" | custom-call | tf_op jit(solution)/shard_map/wide/pallas_call | solution.py:41
  45.3 0.5 collective-permute-done.11.refs_2_
  45.7 1.2 %adjoint_outer.3.lam = f32[8,72,128]{2,1,0:T(8,128)S(1)} custom-call(bf16[72,240]{1,0:T(8,128)(2,1)S(1)} %get-tuple-element.56.matrix_ref, f32[10,72,128]{2,1,0:T(8,128)S(1)} %get-tuple-element.73.start, f32[14,72,128]{2,1,0:T(8,128)S(1)} %get-tuple-element.74.first, f32[12,72,128]{2,1,0:T(8,128)S(1)} %get-tuple-element.75.second, ...), custom_call_target="tpu_custom_call" | custom-call | tf_op jit(solution)/shard_map/adjoint_outer/pallas_call | solution.py:41
  47.0 3.7 %collective-permute-done.13.prior = f32[520,128]{1,0:T(8,128)S(1)} collective-permute-done((f32[520,128]{1,0:T(8,128)S(1)}, f32[520,128]{1,0:T(8,128)S(1)}, u32[]{:S(2)}, u32[]{:S(2)}) %collective-permute-start.13) | collective-permute-done | bytes 266272 | tf_op jit(solution)/shard_map/ppermute | solution.py:462
  50.8 8.8 %all_to_all.23 = f32[32,1,128]{2,1,0:T(1,128)S(1)} all-to-all(f32[32,1,128]{2,1,0:T(1,128)S(1)} %bitcast.32), channel_id=1, replica_groups=mesh['seg'=8,'space'=4] {'seg','space'}, dimensions={0} | all-to-all | bytes 32768 | tf_op jit(solution)/shard_map/all_to_all | solution.py:572
  59.7 0.9 %final.1 = f32[520,128]{1,0:T(8,128)} custom-call(f32[10,72,128]{2,1,0:T(8,128)S(1)} %get-tuple-element.73.start, f32[8,72,128]{2,1,0:T(8,128)S(1)} %get-tuple-element.86.descent, f32[32,128]{1,0:T(8,128)S(1)} %bitcast.30), custom_call_target="tpu_custom_call" | custom-call | tf_op jit(solution)/shard_map/final/pallas_call | solution.py:41
  (16 shorter events, 0.9 us)
Async XLA Ops:
  1.7 9.2 %collective-permute-start = (f32[455,128]{1,0:T(8,128)S(1)}, f32[455,128]{1,0:T(8,128)S(1)}, u32[]{:S(2)}, u32[]{:S(2)}) collective-permute-start(f32[455,128]{1,0:T(8,128)S(1)} %get-tuple-element.46), channel_id=1, source_target_pairs={{3,0},{0,1},{1,2},{2,3},{7,4},{4,5},{5,6},{6,7},{11,8},{8,9},{9,10... | collective-permute-start | bytes 698888 | tf_op jit(solution)/shard_map/ppermute | solution.py:462
  2.2 8.7 %collective-permute-start.1 = (f32[455,128]{1,0:T(8,128)S(1)}, f32[455,128]{1,0:T(8,128)S(1)}, u32[]{:S(2)}, u32[]{:S(2)}) collective-permute-start(f32[455,128]{1,0:T(8,128)S(1)} %get-tuple-element.47), channel_id=1, source_target_pairs={{1,0},{2,1},{3,2},{0,3},{5,4},{6,5},{7,6},{4,7},{9,8},{10,9},{11,1... | collective-permute-start | bytes 698888 | tf_op jit(solution)/shard_map/ppermute | solution.py:462
  4.3 5.3 %copy-start = (f32[65]{0:T(128)S(1)}, f32[65]{0:T(128)}, u32[]{:S(2)}) copy-start(f32[65]{0:T(128)} %param.5) | copy-start | bytes 784
  4.3 11.0 %collective-permute-start.2 = (f32[520,128]{1,0:T(8,128)S(1)}, f32[520,128]{1,0:T(8,128)S(1)}, u32[]{:S(2)}, u32[]{:S(2)}) collective-permute-start(f32[520,128]{1,0:T(8,128)S(1)} %get-tuple-element.48.states.refs_0_), channel_id=1, source_target_pairs={{4,0},{8,4},{12,8},{16,12},{20,16},{24,20},{28,24},{0,28},{5,1},{9... | collective-permute-start | bytes 798728 | tf_op jit(solution)/shard_map/ppermute | solution.py:462
  12.2 11.2 %collective-permute-start.7 = (f32[520,128]{1,0:T(8,128)S(1)}, f32[520,128]{1,0:T(8,128)S(1)}, u32[]{:S(2)}, u32[]{:S(2)}) collective-permute-start(f32[520,128]{1,0:T(8,128)S(1)} %get-tuple-element.60.refs_0_), channel_id=1, source_target_pairs={{28,0},{0,4},{4,8},{8,12},{12,16},{16,20},{20,24},{24,28},{29,1},{... | collective-permute-start | bytes 798728 | tf_op jit(solution)/shard_map/ppermute | solution.py:462
  13.1 5.2 %collective-permute-start.3 = (f32[260,128]{1,0:T(8,128)S(1)}, f32[260,128]{1,0:T(8,128)S(1)}, u32[]{:S(2)}, u32[]{:S(2)}) collective-permute-start(f32[260,128]{1,0:T(8,128)S(1)} %get-tuple-element.64), channel_id=1, source_target_pairs={{3,0},{0,1},{1,2},{2,3},{7,4},{4,5},{5,6},{6,7},{11,8},{8,9},{9,10... | collective-permute-start | bytes 399368 | tf_op jit(solution)/shard_map/ppermute | solution.py:462
  13.9 5.1 %collective-permute-start.4 = (f32[260,128]{1,0:T(8,128)S(1)}, f32[260,128]{1,0:T(8,128)S(1)}, u32[]{:S(2)}, u32[]{:S(2)}) collective-permute-start(f32[260,128]{1,0:T(8,128)S(1)} %get-tuple-element.65), channel_id=1, source_target_pairs={{1,0},{2,1},{3,2},{0,3},{5,4},{6,5},{7,6},{4,7},{9,8},{10,9},{11,1... | collective-permute-start | bytes 399368 | tf_op jit(solution)/shard_map/ppermute | solution.py:462
  15.5 5.8 %collective-permute-start.5 = (f32[260,128]{1,0:T(8,128)S(1)}, f32[260,128]{1,0:T(8,128)S(1)}, u32[]{:S(2)}, u32[]{:S(2)}) collective-permute-start(f32[260,128]{1,0:T(8,128)S(1)} %get-tuple-element.66), channel_id=1, source_target_pairs={{3,0},{0,1},{1,2},{2,3},{7,4},{4,5},{5,6},{6,7},{11,8},{8,9},{9,10... | collective-permute-start | bytes 399368 | tf_op jit(solution)/shard_map/ppermute | solution.py:462
  15.5 5.8 %collective-permute-start.6 = (f32[260,128]{1,0:T(8,128)S(1)}, f32[260,128]{1,0:T(8,128)S(1)}, u32[]{:S(2)}, u32[]{:S(2)}) collective-permute-start(f32[260,128]{1,0:T(8,128)S(1)} %get-tuple-element.67), channel_id=1, source_target_pairs={{1,0},{2,1},{3,2},{0,3},{5,4},{6,5},{7,6},{4,7},{9,8},{10,9},{11,1... | collective-permute-start | bytes 399368 | tf_op jit(solution)/shard_map/ppermute | solution.py:462
  23.7 14.4 %collective-permute-start.8 = (f32[845,128]{1,0:T(8,128)S(1)}, f32[845,128]{1,0:T(8,128)S(1)}, u32[]{:S(2)}, u32[]{:S(2)}) collective-permute-start(f32[845,128]{1,0:T(8,128)S(1)} %get-tuple-element.70), channel_id=1, source_target_pairs={{3,0},{0,1},{1,2},{2,3},{7,4},{4,5},{5,6},{6,7},{11,8},{8,9},{9,10... | collective-permute-start | bytes 1297928 | tf_op jit(solution)/shard_map/ppermute | solution.py:462
  24.1 14.0 %collective-permute-start.9 = (f32[845,128]{1,0:T(8,128)S(1)}, f32[845,128]{1,0:T(8,128)S(1)}, u32[]{:S(2)}, u32[]{:S(2)}) collective-permute-start(f32[845,128]{1,0:T(8,128)S(1)} %get-tuple-element.71), channel_id=1, source_target_pairs={{1,0},{2,1},{3,2},{0,3},{5,4},{6,5},{7,6},{4,7},{9,8},{10,9},{11,1... | collective-permute-start | bytes 1297928 | tf_op jit(solution)/shard_map/ppermute | solution.py:462
  25.5 14.8 %collective-permute-start.10 = (f32[520,128]{1,0:T(8,128)S(1)}, f32[520,128]{1,0:T(8,128)S(1)}, u32[]{:S(2)}, u32[]{:S(2)}) collective-permute-start(f32[520,128]{1,0:T(8,128)S(1)} %get-tuple-element.69.descent), channel_id=1, source_target_pairs={{4,0},{8,4},{12,8},{16,12},{20,16},{24,20},{28,24},{0,28},{5,1},{9... | collective-permute-start | bytes 798728 | tf_op jit(solution)/shard_map/ppermute | solution.py:462
  39.7 10.9 %collective-permute-start.13 = (f32[520,128]{1,0:T(8,128)S(1)}, f32[520,128]{1,0:T(8,128)S(1)}, u32[]{:S(2)}, u32[]{:S(2)}) collective-permute-start(f32[520,128]{1,0:T(8,128)S(1)} %get-tuple-element.77.refs_0_), channel_id=1, source_target_pairs={{28,0},{0,4},{4,8},{8,12},{12,16},{16,20},{20,24},{24,28},{29,1},{... | collective-permute-start | bytes 798728 | tf_op jit(solution)/shard_map/ppermute | solution.py:462
  40.7 5.0 %collective-permute-start.11 = (f32[260,128]{1,0:T(8,128)S(1)}, f32[260,128]{1,0:T(8,128)S(1)}, u32[]{:S(2)}, u32[]{:S(2)}) collective-permute-start(f32[260,128]{1,0:T(8,128)S(1)} %get-tuple-element.83), channel_id=1, source_target_pairs={{3,0},{0,1},{1,2},{2,3},{7,4},{4,5},{5,6},{6,7},{11,8},{8,9},{9,10... | collective-permute-start | bytes 399368 | tf_op jit(solution)/shard_map/ppermute | solution.py:462
  40.7 5.0 %collective-permute-start.12 = (f32[260,128]{1,0:T(8,128)S(1)}, f32[260,128]{1,0:T(8,128)S(1)}, u32[]{:S(2)}, u32[]{:S(2)}) collective-permute-start(f32[260,128]{1,0:T(8,128)S(1)} %get-tuple-element.84), channel_id=1, source_target_pairs={{1,0},{2,1},{3,2},{0,3},{5,4},{6,5},{7,6},{4,7},{9,8},{10,9},{11,1... | collective-permute-start | bytes 399368 | tf_op jit(solution)/shard_map/ppermute | solution.py:462

commit v11 on v9

--- a/solution.py
+++ b/solution.py
@@ -559,7 +559,7 @@
         )[0]
         sent = iteration < ITERS - 1
         if not sent:
-            kept = call(copy_kernel, "kept", [flat(nx)], [mismatch, inner[0]], specs=[VMEM, pl.BlockSpec(memory_space=pl.ANY)])[0]
+            kept = call(copy_kernel, "kept", [flat(nx)], [mismatch, sides[0]], specs=[VMEM, pl.BlockSpec(memory_space=pl.ANY)])[0]
         side = flat(WIDE + 2 * (WIDE - h))
         sums, descent, *edges = call(
             functools.partial(descent_kernel, nx, devices, sent),

time: 60.8 us -> 60.9 us (level)
  no operation moved by 1% of the time
where the time goes in v11:
time: 60.9 us; the launch traced here: 60.6 us
  starting transfers between devices  20.2 us (33%)
  blocking collectives  17.7 us (29%)
  Pallas kernels  13.7 us (22%)
  waiting for transfers between devices  8.3 us (14%)
  between operations  0.73 us (1%)
    ppermute x14, starting transfers between devices, shift(): lax.ppermute(block, axis, [((i - distance) % devices, i) for i in range(d...  20.2 us
    all_to_all x2, blocking collectives, per_device(): sums = lax.all_to_all(sums, BOTH, 0, 0, tiled=True)  17.7 us
    pallas_call x16, Pallas kernels, call(): pl.pallas_call(kernel, name=name, out_shape=[jax.ShapeDtypeStruct(shape,...  13.7 us
    ppermute x14, waiting for transfers between devices, shift(): lax.ppermute(block, axis, [((i - distance) % devices, i) for i in range(d...  8.3 us
  transfers between devices with their start and end apart: 14, of which 6 were waited for; matrix products, arithmetic and copies ran while one was open for 0% of the time, Pallas kernels for 19%

profile of v11, /device:TPU:0, one launch (start us, length us, event | category | flops | bytes accessed | tf_op | source)
XLA Modules:
  0.0 60.6 jit_solution(17441716007499242431)
XLA Ops:
  0.6 1.2 %pack.1 = (f32[455,128]{1,0:T(8,128)S(1)}, f32[455,128]{1,0:T(8,128)S(1)}, f32[520,128]{1,0:T(8,128)S(1)}, f32[520,128]{1,0:T(8,128)S(1)}) custom-call(f32[520,128]{1,0:T(8,128)} %bitcast.35, f32[520,128]{1,0:T(8,128)} %bitcast.36), custom_call_target="tpu_custom_call" | custom-call | tf_op jit(solution)/shard_map/pack/pallas_call | solution.py:41
  1.8 0.5 collective-permute-start
  2.3 2.0 %collective-permute-start.1 = (f32[455,128]{1,0:T(8,128)S(1)}, f32[455,128]{1,0:T(8,128)S(1)}, u32[]{:S(2)}, u32[]{:S(2)}) collective-permute-start(f32[455,128]{1,0:T(8,128)S(1)} %get-tuple-element.47), channel_id=1, source_target_pairs={{1,0},{2,1},{3,2},{0,3},{5,4},{6,5},{7,6},{4,7},{9,8},{10,9},{11,1... | collective-permute-start | bytes 698888 | tf_op jit(solution)/shard_map/ppermute | solution.py:462
  4.4 5.3 %collective-permute-start.2 = (f32[520,128]{1,0:T(8,128)S(1)}, f32[520,128]{1,0:T(8,128)S(1)}, u32[]{:S(2)}, u32[]{:S(2)}) collective-permute-start(f32[520,128]{1,0:T(8,128)S(1)} %get-tuple-element.48.states.refs_0_), channel_id=1, source_target_pairs={{4,0},{8,4},{12,8},{16,12},{20,16},{24,20},{28,24},{0,28},{5,1},{9... | collective-permute-start | bytes 798728 | tf_op jit(solution)/shard_map/ppermute | solution.py:462
  9.6 0.5 inverse.1
  10.1 0.9 %forward_inner.1 = (f32[10,72,128]{2,1,0:T(8,128)S(1)}, f32[8,72,128]{2,1,0:T(8,128)S(1)}, f32[14,72,128]{2,1,0:T(8,128)S(1)}, f32[12,72,128]{2,1,0:T(8,128)S(1)}, f32[10,72,128]{2,1,0:T(8,128)S(1)}) custom-call(bf16[72,240]{1,0:T(8,128)(2,1)S(1)} %get-tuple-element.45.matrix_ref, f32[520,128]{1,0:T(8,128)S(1)} %get-tuple-element.48.states.refs_0_, ...), custom_call_target="tpu_custom_call" | custom-call | tf_op jit(solution)/shard_map/forward_inner/pallas_call | solution.py:41
  11.0 1.3 %forward_outer.1 = (f32[520,128]{1,0:T(8,128)S(1)}, f32[10,72,128]{2,1,0:T(8,128)S(1)}, f32[14,72,128]{2,1,0:T(8,128)S(1)}, f32[12,72,128]{2,1,0:T(8,128)S(1)}, ...) custom-call(bf16[72,240]{1,0:T(8,128)(2,1)S(1)} %get-tuple-element.4, ...), custom_call_target="tpu_custom_call", output_to_operand_aliasing={{1}: (4, {}), {2}: (5, {}), {3}: (6, {}), {4}: (7, {})} | custom-call | flops 4000000000 | bytes 1048576 | tf_op jit(solution)/shard_map/forward_outer/pallas_call | solution.py:41
  12.3 0.9 %collective-permute-start.7 = (f32[520,128]{1,0:T(8,128)S(1)}, f32[520,128]{1,0:T(8,128)S(1)}, u32[]{:S(2)}, u32[]{:S(2)}) collective-permute-start(f32[520,128]{1,0:T(8,128)S(1)} %get-tuple-element.60.refs_0_), channel_id=1, source_target_pairs={{28,0},{0,4},{4,8},{8,12},{12,16},{16,20},{20,24},{24,28},{29,1},{... | collective-permute-start | bytes 798728 | tf_op jit(solution)/shard_map/ppermute | solution.py:462
  13.2 0.8 %collective-permute-start.3 = (f32[260,128]{1,0:T(8,128)S(1)}, f32[260,128]{1,0:T(8,128)S(1)}, u32[]{:S(2)}, u32[]{:S(2)}) collective-permute-start(f32[260,128]{1,0:T(8,128)S(1)} %get-tuple-element.64), channel_id=1, source_target_pairs={{3,0},{0,1},{1,2},{2,3},{7,4},{4,5},{5,6},{6,7},{11,8},{8,9},{9,10... | collective-permute-start | bytes 399368 | tf_op jit(solution)/shard_map/ppermute | solution.py:462
  14.0 1.1 %collective-permute-start.4 = (f32[260,128]{1,0:T(8,128)S(1)}, f32[260,128]{1,0:T(8,128)S(1)}, u32[]{:S(2)}, u32[]{:S(2)}) collective-permute-start(f32[260,128]{1,0:T(8,128)S(1)} %get-tuple-element.65), channel_id=1, source_target_pairs={{1,0},{2,1},{3,2},{0,3},{5,4},{6,5},{7,6},{4,7},{9,8},{10,9},{11,1... | collective-permute-start | bytes 399368 | tf_op jit(solution)/shard_map/ppermute | solution.py:462
  15.6 1.8 %collective-permute-start.6 = (f32[260,128]{1,0:T(8,128)S(1)}, f32[260,128]{1,0:T(8,128)S(1)}, u32[]{:S(2)}, u32[]{:S(2)}) collective-permute-start(f32[260,128]{1,0:T(8,128)S(1)} %get-tuple-element.67), channel_id=1, source_target_pairs={{1,0},{2,1},{3,2},{0,3},{5,4},{6,5},{7,6},{4,7},{9,8},{10,9},{11,1... | collective-permute-start | bytes 399368 | tf_op jit(solution)/shard_map/ppermute | solution.py:462
  17.3 1.1 %adjoint_inner.2 = (f32[20,72,128]{2,1,0:T(8,128)S(1)}, f32[20,72,128]{2,1,0:T(8,128)S(1)}) custom-call(bf16[72,240]{1,0:T(8,128)(2,1)S(1)} %get-tuple-element.56.matrix_ref, f32[10,72,128]{2,1,0:T(8,128)S(1)} %get-tuple-element.55.start.old, f32[14,72,128]{2,1,0:T(8,128)S(1)} %get-tuple-element.57.first, f32[12,72,128]{2,1,0:T(8,128)S(1)} %get-tuple-element.58.second, ...), custom_call_target="tpu_custom_call" | custom-call | tf_op jit(solution)/shard_map/adjoint_inner/pallas_call | solution.py:41
  18.4 0.7 %collective-permute-done.4.refs_1_ = f32[260,128]{1,0:T(8,128)S(1)} collective-permute-done((f32[260,128]{1,0:T(8,128)S(1)}, f32[260,128]{1,0:T(8,128)S(1)}, u32[]{:S(2)}, u32[]{:S(2)}) %collective-permute-start.4) | collective-permute-done | bytes 133152 | tf_op jit(solution)/shard_map/ppermute | solution.py:462
  19.1 2.3 %collective-permute-done.5.refs_2_ = f32[260,128]{1,0:T(8,128)S(1)} collective-permute-done((f32[260,128]{1,0:T(8,128)S(1)}, f32[260,128]{1,0:T(8,128)S(1)}, u32[]{:S(2)}, u32[]{:S(2)}) %collective-permute-start.5) | collective-permute-done | bytes 133152 | tf_op jit(solution)/shard_map/ppermute | solution.py:462
  21.4 1.2 %adjoint_outer.2.lam = f32[8,72,128]{2,1,0:T(8,128)S(1)} custom-call(bf16[72,240]{1,0:T(8,128)(2,1)S(1)} %get-tuple-element.56.matrix_ref, f32[10,72,128]{2,1,0:T(8,128)S(1)} %get-tuple-element.55.start.old, f32[14,72,128]{2,1,0:T(8,128)S(1)} %get-tuple-element.57.first, f32[12,72,128]{2,1,0:T(8,128)S(1)} %get-tuple-element.58.second, ...), custom_call_target="tpu_custom_call" | custom-call | tf_op jit(solution)/shard_map/adjoint_outer/pallas_call | solution.py:41
  22.6 1.0 %collective-permute-done.7.prior = f32[520,128]{1,0:T(8,128)S(1)} collective-permute-done((f32[520,128]{1,0:T(8,128)S(1)}, f32[520,128]{1,0:T(8,128)S(1)}, u32[]{:S(2)}, u32[]{:S(2)}) %collective-permute-start.7) | collective-permute-done | bytes 266272 | tf_op jit(solution)/shard_map/ppermute | solution.py:462
  23.8 0.4 collective-permute-start.8
  24.2 1.4 %collective-permute-start.9 = (f32[845,128]{1,0:T(8,128)S(1)}, f32[845,128]{1,0:T(8,128)S(1)}, u32[]{:S(2)}, u32[]{:S(2)}) collective-permute-start(f32[845,128]{1,0:T(8,128)S(1)} %get-tuple-element.71), channel_id=1, source_target_pairs={{1,0},{2,1},{3,2},{0,3},{5,4},{6,5},{7,6},{4,7},{9,8},{10,9},{11,1... | collective-permute-start | bytes 1297928 | tf_op jit(solution)/shard_map/ppermute | solution.py:462
  25.6 3.7 %collective-permute-start.10 = (f32[520,128]{1,0:T(8,128)S(1)}, f32[520,128]{1,0:T(8,128)S(1)}, u32[]{:S(2)}, u32[]{:S(2)}) collective-permute-start(f32[520,128]{1,0:T(8,128)S(1)} %get-tuple-element.69.descent), channel_id=1, source_target_pairs={{4,0},{8,4},{12,8},{16,12},{20,16},{24,20},{28,24},{0,28},{5,1},{9... | collective-permute-start | bytes 798728 | tf_op jit(solution)/shard_map/ppermute | solution.py:462
  29.3 8.9 %all_to_all.22 = f32[32,1,128]{2,1,0:T(1,128)S(1)} all-to-all(f32[32,1,128]{2,1,0:T(1,128)S(1)} %bitcast.31), channel_id=1, replica_groups=mesh['seg'=8,'space'=4] {'seg','space'}, dimensions={0} | all-to-all | bytes 32768 | tf_op jit(solution)/shard_map/all_to_all | solution.py:572
  38.2 1.6 %forward.1 = (f32[520,128]{1,0:T(8,128)S(1)}, f32[10,72,128]{2,1,0:T(8,128)S(1)}, f32[14,72,128]{2,1,0:T(8,128)S(1)}, f32[12,72,128]{2,1,0:T(8,128)S(1)}, f32[10,72,128]{2,1,0:T(8,128)S(1)}) custom-call(bf16[72,240]{1,0:T(8,128)(2,1)S(1)} %get-tuple-element.45.matrix_ref, f32[455,128]{1,0:T(8,128)S(1)} %collective-permute-done.left, ...), custom_call_target="tpu_custom_call" | custom-call | tf_op jit(solution)/shard_map/forward/pallas_call | solution.py:41
  39.8 0.6 %collective-permute-start.13 = (f32[520,128]{1,0:T(8,128)S(1)}, f32[520,128]{1,0:T(8,128)S(1)}, u32[]{:S(2)}, u32[]{:S(2)}) collective-permute-start(f32[520,128]{1,0:T(8,128)S(1)} %get-tuple-element.77.refs_0_), channel_id=1, source_target_pairs={{28,0},{0,4},{4,8},{8,12},{12,16},{16,20},{20,24},{24,28},{29,1},{... | collective-permute-start | bytes 798728 | tf_op jit(solution)/shard_map/ppermute | solution.py:462
  40.5 0.4 mismatch.3
  40.8 1.8 %collective-permute-start.12 = (f32[260,128]{1,0:T(8,128)S(1)}, f32[260,128]{1,0:T(8,128)S(1)}, u32[]{:S(2)}, u32[]{:S(2)}) collective-permute-start(f32[260,128]{1,0:T(8,128)S(1)} %get-tuple-element.84), channel_id=1, source_target_pairs={{1,0},{2,1},{3,2},{0,3},{5,4},{6,5},{7,6},{4,7},{9,8},{10,9},{11,1... | collective-permute-start | bytes 399368 | tf_op jit(solution)/shard_map/ppermute | solution.py:462
  42.6 1.0 %wide.1 = (f32[260,128]{1,0:T(8,128)S(1)}, f32[260,128]{1,0:T(8,128)S(1)}) custom-call(bf16[72,240]{1,0:T(8,128)(2,1)S(1)} %get-tuple-element.45.matrix_ref, f32[455,128]{1,0:T(8,128)S(1)} %collective-permute-done.left, f32[455,128]{1,0:T(8,128)S(1)} %collective-permute-done.1.right, f32[845,128]{1,0:T(8,128)S(1)} %collective-permute-done.8.d_left, ...), custom_call_target="tpu_custom_call" | custom-call | tf_op jit(solution)/shard_map/wide/pallas_call | solution.py:41
  43.6 0.7 %kept.1.refs_0_ = f32[520,128]{1,0:T(8,128)} custom-call(f32[520,128]{1,0:T(8,128)S(1)} %get-tuple-element.78.mismatch.given, f32[260,128]{1,0:T(8,128)S(1)} %get-tuple-element.81.refs_0_.order), custom_call_target="tpu_custom_call" | custom-call | tf_op jit(solution)/shard_map/kept/pallas_call | solution.py:41
  44.3 1.0 %adjoint_inner.3 = (f32[20,72,128]{2,1,0:T(8,128)S(1)}, f32[20,72,128]{2,1,0:T(8,128)S(1)}) custom-call(bf16[72,240]{1,0:T(8,128)(2,1)S(1)} %get-tuple-element.56.matrix_ref, f32[10,72,128]{2,1,0:T(8,128)S(1)} %get-tuple-element.73.start, f32[14,72,128]{2,1,0:T(8,128)S(1)} %get-tuple-element.74.first, f32[12,72,128]{2,1,0:T(8,128)S(1)} %get-tuple-element.75.second, ...), custom_call_target="tpu_custom_call" | custom-call | tf_op jit(solution)/shard_map/adjoint_inner/pallas_call | solution.py:41
  45.4 0.5 collective-permute-done.11.refs_2_
  45.8 1.2 %adjoint_outer.3.lam = f32[8,72,128]{2,1,0:T(8,128)S(1)} custom-call(bf16[72,240]{1,0:T(8,128)(2,1)S(1)} %get-tuple-element.56.matrix_ref, f32[10,72,128]{2,1,0:T(8,128)S(1)} %get-tuple-element.73.start, f32[14,72,128]{2,1,0:T(8,128)S(1)} %get-tuple-element.74.first, f32[12,72,128]{2,1,0:T(8,128)S(1)} %get-tuple-element.75.second, ...), custom_call_target="tpu_custom_call" | custom-call | tf_op jit(solution)/shard_map/adjoint_outer/pallas_call | solution.py:41
  47.1 3.7 %collective-permute-done.13.prior = f32[520,128]{1,0:T(8,128)S(1)} collective-permute-done((f32[520,128]{1,0:T(8,128)S(1)}, f32[520,128]{1,0:T(8,128)S(1)}, u32[]{:S(2)}, u32[]{:S(2)}) %collective-permute-start.13) | collective-permute-done | bytes 266272 | tf_op jit(solution)/shard_map/ppermute | solution.py:462
  50.9 8.8 %all_to_all.23 = f32[32,1,128]{2,1,0:T(1,128)S(1)} all-to-all(f32[32,1,128]{2,1,0:T(1,128)S(1)} %bitcast.32), channel_id=1, replica_groups=mesh['seg'=8,'space'=4] {'seg','space'}, dimensions={0} | all-to-all | bytes 32768 | tf_op jit(solution)/shard_map/all_to_all | solution.py:572
  59.8 0.9 %final.1 = f32[520,128]{1,0:T(8,128)} custom-call(f32[10,72,128]{2,1,0:T(8,128)S(1)} %get-tuple-element.73.start, f32[8,72,128]{2,1,0:T(8,128)S(1)} %get-tuple-element.86.descent, f32[32,128]{1,0:T(8,128)S(1)} %bitcast.30), custom_call_target="tpu_custom_call" | custom-call | tf_op jit(solution)/shard_map/final/pallas_call | solution.py:41
  (16 shorter events, 0.9 us)
Async XLA Ops:
  1.8 9.2 %collective-permute-start = (f32[455,128]{1,0:T(8,128)S(1)}, f32[455,128]{1,0:T(8,128)S(1)}, u32[]{:S(2)}, u32[]{:S(2)}) collective-permute-start(f32[455,128]{1,0:T(8,128)S(1)} %get-tuple-element.46), channel_id=1, source_target_pairs={{3,0},{0,1},{1,2},{2,3},{7,4},{4,5},{5,6},{6,7},{11,8},{8,9},{9,10... | collective-permute-start | bytes 698888 | tf_op jit(solution)/shard_map/ppermute | solution.py:462
  2.3 8.7 %collective-permute-start.1 = (f32[455,128]{1,0:T(8,128)S(1)}, f32[455,128]{1,0:T(8,128)S(1)}, u32[]{:S(2)}, u32[]{:S(2)}) collective-permute-start(f32[455,128]{1,0:T(8,128)S(1)} %get-tuple-element.47), channel_id=1, source_target_pairs={{1,0},{2,1},{3,2},{0,3},{5,4},{6,5},{7,6},{4,7},{9,8},{10,9},{11,1... | collective-permute-start | bytes 698888 | tf_op jit(solution)/shard_map/ppermute | solution.py:462
  4.4 5.3 %copy-start = (f32[65]{0:T(128)S(1)}, f32[65]{0:T(128)}, u32[]{:S(2)}) copy-start(f32[65]{0:T(128)} %param.5) | copy-start | bytes 784
  4.4 11.0 %collective-permute-start.2 = (f32[520,128]{1,0:T(8,128)S(1)}, f32[520,128]{1,0:T(8,128)S(1)}, u32[]{:S(2)}, u32[]{:S(2)}) collective-permute-start(f32[520,128]{1,0:T(8,128)S(1)} %get-tuple-element.48.states.refs_0_), channel_id=1, source_target_pairs={{4,0},{8,4},{12,8},{16,12},{20,16},{24,20},{28,24},{0,28},{5,1},{9... | collective-permute-start | bytes 798728 | tf_op jit(solution)/shard_map/ppermute | solution.py:462
  12.3 11.2 %collective-permute-start.7 = (f32[520,128]{1,0:T(8,128)S(1)}, f32[520,128]{1,0:T(8,128)S(1)}, u32[]{:S(2)}, u32[]{:S(2)}) collective-permute-start(f32[520,128]{1,0:T(8,128)S(1)} %get-tuple-element.60.refs_0_), channel_id=1, source_target_pairs={{28,0},{0,4},{4,8},{8,12},{12,16},{16,20},{20,24},{24,28},{29,1},{... | collective-permute-start | bytes 798728 | tf_op jit(solution)/shard_map/ppermute | solution.py:462
  13.2 5.2 %collective-permute-start.3 = (f32[260,128]{1,0:T(8,128)S(1)}, f32[260,128]{1,0:T(8,128)S(1)}, u32[]{:S(2)}, u32[]{:S(2)}) collective-permute-start(f32[260,128]{1,0:T(8,128)S(1)} %get-tuple-element.64), channel_id=1, source_target_pairs={{3,0},{0,1},{1,2},{2,3},{7,4},{4,5},{5,6},{6,7},{11,8},{8,9},{9,10... | collective-permute-start | bytes 399368 | tf_op jit(solution)/shard_map/ppermute | solution.py:462
  14.0 5.1 %collective-permute-start.4 = (f32[260,128]{1,0:T(8,128)S(1)}, f32[260,128]{1,0:T(8,128)S(1)}, u32[]{:S(2)}, u32[]{:S(2)}) collective-permute-start(f32[260,128]{1,0:T(8,128)S(1)} %get-tuple-element.65), channel_id=1, source_target_pairs={{1,0},{2,1},{3,2},{0,3},{5,4},{6,5},{7,6},{4,7},{9,8},{10,9},{11,1... | collective-permute-start | bytes 399368 | tf_op jit(solution)/shard_map/ppermute | solution.py:462
  15.6 5.8 %collective-permute-start.5 = (f32[260,128]{1,0:T(8,128)S(1)}, f32[260,128]{1,0:T(8,128)S(1)}, u32[]{:S(2)}, u32[]{:S(2)}) collective-permute-start(f32[260,128]{1,0:T(8,128)S(1)} %get-tuple-element.66), channel_id=1, source_target_pairs={{3,0},{0,1},{1,2},{2,3},{7,4},{4,5},{5,6},{6,7},{11,8},{8,9},{9,10... | collective-permute-start | bytes 399368 | tf_op jit(solution)/shard_map/ppermute | solution.py:462
  15.6 5.8 %collective-permute-start.6 = (f32[260,128]{1,0:T(8,128)S(1)}, f32[260,128]{1,0:T(8,128)S(1)}, u32[]{:S(2)}, u32[]{:S(2)}) collective-permute-start(f32[260,128]{1,0:T(8,128)S(1)} %get-tuple-element.67), channel_id=1, source_target_pairs={{1,0},{2,1},{3,2},{0,3},{5,4},{6,5},{7,6},{4,7},{9,8},{10,9},{11,1... | collective-permute-start | bytes 399368 | tf_op jit(solution)/shard_map/ppermute | solution.py:462
  23.8 14.4 %collective-permute-start.8 = (f32[845,128]{1,0:T(8,128)S(1)}, f32[845,128]{1,0:T(8,128)S(1)}, u32[]{:S(2)}, u32[]{:S(2)}) collective-permute-start(f32[845,128]{1,0:T(8,128)S(1)} %get-tuple-element.70), channel_id=1, source_target_pairs={{3,0},{0,1},{1,2},{2,3},{7,4},{4,5},{5,6},{6,7},{11,8},{8,9},{9,10... | collective-permute-start | bytes 1297928 | tf_op jit(solution)/shard_map/ppermute | solution.py:462
  24.2 14.0 %collective-permute-start.9 = (f32[845,128]{1,0:T(8,128)S(1)}, f32[845,128]{1,0:T(8,128)S(1)}, u32[]{:S(2)}, u32[]{:S(2)}) collective-permute-start(f32[845,128]{1,0:T(8,128)S(1)} %get-tuple-element.71), channel_id=1, source_target_pairs={{1,0},{2,1},{3,2},{0,3},{5,4},{6,5},{7,6},{4,7},{9,8},{10,9},{11,1... | collective-permute-start | bytes 1297928 | tf_op jit(solution)/shard_map/ppermute | solution.py:462
  25.6 14.8 %collective-permute-start.10 = (f32[520,128]{1,0:T(8,128)S(1)}, f32[520,128]{1,0:T(8,128)S(1)}, u32[]{:S(2)}, u32[]{:S(2)}) collective-permute-start(f32[520,128]{1,0:T(8,128)S(1)} %get-tuple-element.69.descent), channel_id=1, source_target_pairs={{4,0},{8,4},{12,8},{16,12},{20,16},{24,20},{28,24},{0,28},{5,1},{9... | collective-permute-start | bytes 798728 | tf_op jit(solution)/shard_map/ppermute | solution.py:462
  39.8 10.9 %collective-permute-start.13 = (f32[520,128]{1,0:T(8,128)S(1)}, f32[520,128]{1,0:T(8,128)S(1)}, u32[]{:S(2)}, u32[]{:S(2)}) collective-permute-start(f32[520,128]{1,0:T(8,128)S(1)} %get-tuple-element.77.refs_0_), channel_id=1, source_target_pairs={{28,0},{0,4},{4,8},{8,12},{12,16},{16,20},{20,24},{24,28},{29,1},{... | collective-permute-start | bytes 798728 | tf_op jit(solution)/shard_map/ppermute | solution.py:462
  40.8 5.0 %collective-permute-start.11 = (f32[260,128]{1,0:T(8,128)S(1)}, f32[260,128]{1,0:T(8,128)S(1)}, u32[]{:S(2)}, u32[]{:S(2)}) collective-permute-start(f32[260,128]{1,0:T(8,128)S(1)} %get-tuple-element.83), channel_id=1, source_target_pairs={{3,0},{0,1},{1,2},{2,3},{7,4},{4,5},{5,6},{6,7},{11,8},{8,9},{9,10... | collective-permute-start | bytes 399368 | tf_op jit(solution)/shard_map/ppermute | solution.py:462
  40.8 5.0 %collective-permute-start.12 = (f32[260,128]{1,0:T(8,128)S(1)}, f32[260,128]{1,0:T(8,128)S(1)}, u32[]{:S(2)}, u32[]{:S(2)}) collective-permute-start(f32[260,128]{1,0:T(8,128)S(1)} %get-tuple-element.84), channel_id=1, source_target_pairs={{1,0},{2,1},{3,2},{0,3},{5,4},{6,5},{7,6},{4,7},{9,8},{10,9},{11,1... | collective-permute-start | bytes 399368 | tf_op jit(solution)/shard_map/ppermute | solution.py:462
